TPU v7x, 32 devices: a whole 2x2x4 slice. The times are simulated.
32 devices in a mesh: seq: 4 (over z), ctx: 8 (over y, x, core).
Axes of the slice: x: 2, y: 2, z: 4, core: 2. Of those that a mesh axis runs over, the one named last changes fastest.
Arguments:
- tokens: bfloat16 [4, 1024, 768], P('seq', 'ctx'), may hold values from -6 to 6
- block_ids: int32 [4, 1024], P('seq', 'ctx'), may hold values from 0 to 3, as said below
- ln1_gain: bfloat16 [768], P('seq'), may hold values from 0.25 to 1.75
- ln1_bias: bfloat16 [768], P('seq'), may hold values from -3 to 3
- w_qkv: bfloat16 [768, 2304], P('seq'), may hold values from -0.3125 to 0.3125
- q_bias: bfloat16 [768], P('seq'), may hold values from -3 to 3
- v_bias: bfloat16 [768], P('seq'), may hold values from -3 to 3
- w_out: bfloat16 [768, 768], P('seq'), may hold values from -1 to 1
- out_bias: bfloat16 [768], P('seq'), may hold values from -3 to 3
- ln2_gain: bfloat16 [768], P('seq'), may hold values from 0.25 to 1.75
- ln2_bias: bfloat16 [768], P('seq'), may hold values from -3 to 3
- w_up: bfloat16 [768, 3072], P('seq'), may hold values from -0.21875 to 0.21875
- up_bias: bfloat16 [3072], P('seq'), may hold values from -3 to 3
- w_down: bfloat16 [3072, 768], P('seq'), may hold values from -0.109375 to 0.109375
- down_bias: bfloat16 [768], P('seq'), may hold values from -3 to 3
- cotangent: bfloat16 [4, 1024, 768], P('seq', 'ctx'), may hold values from -6 to 6
Outputs:
- output: bfloat16 [4, 1024, 768], P('seq', 'ctx')
- input_grad: float32 [4, 1024, 768], P('seq', 'ctx')
- grad_ln1_gain: float32 [768], P('seq')
- grad_ln1_bias: float32 [768], P('seq')
- grad_w_qkv: float32 [768, 2304], P('seq')
- grad_q_bias: float32 [768], P('seq')
- grad_v_bias: float32 [768], P('seq')
- grad_w_out: float32 [768, 768], P('seq')
- grad_out_bias: float32 [768], P('seq')
- grad_ln2_gain: float32 [768], P('seq')
- grad_ln2_bias: float32 [768], P('seq')
- grad_w_up: float32 [768, 3072], P('seq')
- grad_up_bias: float32 [3072], P('seq')
- grad_w_down: float32 [3072, 768], P('seq')
- grad_down_bias: float32 [768], P('seq')
Inputs may be any that keep to these rules, and one draw needn't show every extreme that they name: `block_ids`: along each sequence's true order of patches the block id starts at 0 and rises by 0 or 1 from one patch to the next; each sequence has exactly 4 blocks. Index c of ctx holds, in order, the 64 patches of true block of rows c and then those of true block of rows 15 - c, where true blocks of rows have 128 / 2 patches each.
All inputs are finite; a program needn't handle non-finite values.
Results may differ from a plain program's by a relative error of at most 0.017.
The roundings to bfloat16 on the way count: a program that leaves them out, or rounds other values in their place, can miss the bound.
Values may be sent and summed in bfloat16 or wider, within the bound.
No kernel may reach another device: no remote copies, remote signals or barrier semaphores. Data moves between devices by JAX's collectives and lax.ppermute only.
A program may use at most 256 MiB of HBM per device.

v0:
```python
import math

import jax
import jax.numpy as jnp
from jax import lax
from jax.sharding import PartitionSpec as P

HEADS = 12


EPSILON = 1e-06
NEGATIVE = -1e30


def layer_norm(values, gain, shift):
    center = values - jnp.mean(values, -1, keepdims=True)
    spread = jnp.mean(center * center, -1, keepdims=True)
    return center * lax.rsqrt(spread + EPSILON) * gain + shift


def block_rows(count):
    return math.gcd(count, 512)


def masked_scores(query_heads, key_heads, query_ids, key_ids, scale):
    raw = (
        jnp.einsum("qhd,khd->hqk", query_heads, key_heads, preferred_element_type=jnp.float32)
        * scale
    )
    allowed = key_ids[None, None, :] <= query_ids[None, :, None]
    return (raw, allowed)


def attend_forward(query_heads, query_ids, keys_all, values_all, ids_all, scale):
    tok_rows, heads, head_dim = query_heads.shape
    total_keys = keys_all.shape[0]
    step = block_rows(total_keys)
    blocks = total_keys // step

    def attend_visit(carry, inputs):
        running, total, accum = carry
        key_block, value_block, id_block = inputs
        raw, allowed = masked_scores(query_heads, key_block, query_ids, id_block, scale)
        masked = jnp.where(allowed, raw, NEGATIVE)
        new_top = jnp.maximum(running, jnp.max(masked, -1))
        weights = jnp.where(allowed, jnp.exp(masked - new_top[..., None]), 0.0)
        factor = jnp.exp(running - new_top)
        total = total * factor + jnp.sum(weights, -1)
        accum = accum * factor[..., None] + jnp.einsum(
            "hqk,khd->hqd",
            weights.astype(jnp.bfloat16),
            value_block,
            preferred_element_type=jnp.float32,
        )
        return ((new_top, total, accum), None)

    start_state = (
        jnp.full((heads, tok_rows), NEGATIVE, jnp.float32),
        jnp.zeros((heads, tok_rows), jnp.float32),
        jnp.zeros((heads, tok_rows, head_dim), jnp.float32),
    )
    (running, total, accum), _ = lax.scan(
        attend_visit,
        start_state,
        (
            keys_all.reshape(blocks, step, heads, head_dim),
            values_all.reshape(blocks, step, heads, head_dim),
            ids_all.reshape(blocks, step),
        ),
    )
    output_heads = jnp.transpose(accum / total[..., None], (1, 0, 2))
    return (output_heads, running + jnp.log(total))


def query_gradient(
    query_heads, grad_heads, query_ids, keys_all, values_all, ids_all, logsum, inner, scale
):
    tok_rows, heads, head_dim = query_heads.shape
    total_keys = keys_all.shape[0]
    step = block_rows(total_keys)
    blocks = total_keys // step

    def query_visit(accum, inputs):
        key_block, value_block, id_block = inputs
        raw, allowed = masked_scores(query_heads, key_block, query_ids, id_block, scale)
        probs = jnp.where(allowed, jnp.exp(raw - logsum[..., None]), 0.0)
        grad_probs = jnp.einsum(
            "qhd,khd->hqk", grad_heads, value_block, preferred_element_type=jnp.float32
        )
        grad_scores = (probs * (grad_probs - inner[..., None])).astype(jnp.bfloat16)
        accum = accum + jnp.einsum(
            "hqk,khd->qhd", grad_scores, key_block, preferred_element_type=jnp.float32
        )
        return (accum, None)

    accum, _ = lax.scan(
        query_visit,
        jnp.zeros((tok_rows, heads, head_dim), jnp.float32),
        (
            keys_all.reshape(blocks, step, heads, head_dim),
            values_all.reshape(blocks, step, heads, head_dim),
            ids_all.reshape(blocks, step),
        ),
    )
    return accum * scale


def pair_grads(
    query_heads, grad_heads, query_ids, logsum, inner, key_heads, value_heads, key_ids, scale
):
    raw, allowed = masked_scores(query_heads, key_heads, query_ids, key_ids, scale)
    probs = jnp.where(allowed, jnp.exp(raw - logsum[..., None]), 0.0)
    grad_probs = jnp.einsum(
        "qhd,khd->hqk", grad_heads, value_heads, preferred_element_type=jnp.float32
    )
    grad_scores = (probs * (grad_probs - inner[..., None])).astype(jnp.bfloat16)
    grad_keys = (
        jnp.einsum("hqk,qhd->khd", grad_scores, query_heads, preferred_element_type=jnp.float32)
        * scale
    )
    grad_values = jnp.einsum(
        "hqk,qhd->khd", probs.astype(jnp.bfloat16), grad_heads, preferred_element_type=jnp.float32
    )
    return (grad_keys, grad_values)


def shards(
    tokens,
    block_ids,
    ln1_gain,
    ln1_bias,
    w_qkv,
    q_bias,
    v_bias,
    w_out,
    out_bias,
    ln2_gain,
    ln2_bias,
    w_up,
    up_bias,
    w_down,
    down_bias,
    cotangent,
):
    gathered = (
        lax.all_gather(ln1_gain, "seq", axis=0, tiled=True),
        lax.all_gather(ln1_bias, "seq", axis=0, tiled=True),
        lax.all_gather(w_qkv, "seq", axis=0, tiled=True),
        lax.all_gather(q_bias, "seq", axis=0, tiled=True),
        lax.all_gather(v_bias, "seq", axis=0, tiled=True),
        lax.all_gather(w_out, "seq", axis=0, tiled=True),
        lax.all_gather(out_bias, "seq", axis=0, tiled=True),
        lax.all_gather(ln2_gain, "seq", axis=0, tiled=True),
        lax.all_gather(ln2_bias, "seq", axis=0, tiled=True),
        lax.all_gather(w_up, "seq", axis=0, tiled=True),
        lax.all_gather(up_bias, "seq", axis=0, tiled=True),
        lax.all_gather(w_down, "seq", axis=0, tiled=True),
        lax.all_gather(down_bias, "seq", axis=0, tiled=True),
    )
    attention_part = gathered[:7]
    feed_part = gathered[7:]
    gain_one, shift_one, weight_qkv, bias_query, bias_value, weight_out, bias_out = attention_part
    width = weight_out.shape[0]
    heads = HEADS
    head_dim = width // heads
    scale = 1.0 / math.sqrt(head_dim)
    inputs = tokens[0].astype(jnp.float32)
    tok_rows = inputs.shape[0]
    own_ids = block_ids[0]
    gain_one_f = gain_one.astype(jnp.float32)
    shift_one_f = shift_one.astype(jnp.float32)
    normed_one, norm_one_pull = jax.vjp(layer_norm, inputs, gain_one_f, shift_one_f)
    normed_low = normed_one.astype(jnp.bfloat16)
    qkv_bias = jnp.concatenate(
        [
            bias_query.astype(jnp.float32),
            jnp.zeros((width,), jnp.float32),
            bias_value.astype(jnp.float32),
        ]
    )
    projected = (
        jnp.dot(normed_low, weight_qkv, preferred_element_type=jnp.float32) + qkv_bias
    ).astype(jnp.bfloat16)
    query_low = projected[:, :width]
    key_low = projected[:, width : 2 * width]
    value_low = projected[:, 2 * width :]
    ids_all = lax.all_gather(block_ids, "ctx", axis=1, tiled=True)[0]
    keys_all, values_all = (
        lax.all_gather(key_low, "ctx", axis=0, tiled=True),
        lax.all_gather(value_low, "ctx", axis=0, tiled=True),
    )
    query_heads = query_low.reshape(tok_rows, heads, head_dim)
    output_heads, logsum = attend_forward(
        query_heads, own_ids, keys_all, values_all, ids_all, scale
    )
    mixed_low = output_heads.reshape(tok_rows, width).astype(jnp.bfloat16)
    attended = jnp.dot(mixed_low, weight_out, preferred_element_type=jnp.float32) + bias_out.astype(
        jnp.float32
    )
    middle = inputs + attended
    gain_two, shift_two, weight_up, bias_up, weight_down, bias_down = feed_part
    gain_two_f = gain_two.astype(jnp.float32)
    shift_two_f = shift_two.astype(jnp.float32)
    normed_two, norm_two_pull = jax.vjp(layer_norm, middle, gain_two_f, shift_two_f)
    normed_two_low = normed_two.astype(jnp.bfloat16)
    pre_act = jnp.dot(
        normed_two_low, weight_up, preferred_element_type=jnp.float32
    ) + bias_up.astype(jnp.float32)
    activated, gelu_pull = jax.vjp(lambda values: jax.nn.gelu(values, approximate=False), pre_act)
    activated_low = activated.astype(jnp.bfloat16)
    result = (
        middle
        + jnp.dot(activated_low, weight_down, preferred_element_type=jnp.float32)
        + bias_down.astype(jnp.float32)
    )
    grad_out = cotangent[0]
    grad_out_f = grad_out.astype(jnp.float32)
    grad_weight_down = jnp.einsum(
        "tf,td->fd", activated_low, grad_out, preferred_element_type=jnp.float32
    )
    grad_bias_down = jnp.sum(grad_out_f, 0)
    grad_hidden = jnp.einsum("td,fd->tf", grad_out, weight_down, preferred_element_type=jnp.float32)
    grad_pre_low = gelu_pull(grad_hidden)[0].astype(jnp.bfloat16)
    grad_weight_up = jnp.einsum(
        "td,tf->df", normed_two_low, grad_pre_low, preferred_element_type=jnp.float32
    )
    grad_bias_up = jnp.sum(grad_pre_low.astype(jnp.float32), 0)
    grad_normed_two = jnp.einsum(
        "tf,df->td", grad_pre_low, weight_up, preferred_element_type=jnp.float32
    )
    grad_middle_part, grad_gain_two, grad_shift_two = norm_two_pull(grad_normed_two)
    grad_middle = grad_out_f + grad_middle_part
    grad_attended = grad_middle.astype(jnp.bfloat16)
    grad_weight_out = jnp.einsum(
        "td,te->de", mixed_low, grad_attended, preferred_element_type=jnp.float32
    )
    grad_bias_out = jnp.sum(grad_attended.astype(jnp.float32), 0)
    grad_mixed = jnp.einsum(
        "te,de->td", grad_attended, weight_out, preferred_element_type=jnp.float32
    ).astype(jnp.bfloat16)
    grad_heads = grad_mixed.reshape(tok_rows, heads, head_dim)
    inner = jnp.einsum("thd,thd->ht", grad_heads.astype(jnp.float32), output_heads)
    grad_query = query_gradient(
        query_heads, grad_heads, own_ids, keys_all, values_all, ids_all, logsum, inner, scale
    )
    step = block_rows(lax.axis_size("ctx") * tok_rows)
    blocks = lax.axis_size("ctx") * tok_rows // step
    key_part = keys_all.reshape(blocks, step, heads, head_dim)
    value_part = values_all.reshape(blocks, step, heads, head_dim)
    id_part = ids_all.reshape(blocks, step)

    def key_visit(carry, inputs):
        grad_keys, grad_values = pair_grads(
            query_heads, grad_heads, own_ids, logsum, inner, inputs[0], inputs[1], inputs[2], scale
        )
        joined = jnp.concatenate(
            [grad_keys.reshape(step, width), grad_values.reshape(step, width)], 1
        )
        return (carry, joined)

    _, terms = lax.scan(key_visit, jnp.zeros((), jnp.float32), (key_part, value_part, id_part))
    key_value_grads = lax.psum_scatter(
        terms.reshape(lax.axis_size("ctx") * tok_rows, 2 * width),
        "ctx",
        scatter_dimension=0,
        tiled=True,
    )
    grad_keys_all = key_value_grads[:, :width]
    grad_values_all = key_value_grads[:, width:]
    grad_query_low = grad_query.reshape(tok_rows, width).astype(jnp.bfloat16)
    grad_value_low = grad_values_all.astype(jnp.bfloat16)
    grad_projected = jnp.concatenate(
        [grad_query_low, grad_keys_all.astype(jnp.bfloat16), grad_value_low], 1
    )
    grad_weight_qkv = jnp.einsum(
        "td,te->de", normed_low, grad_projected, preferred_element_type=jnp.float32
    )
    grad_bias_query = jnp.sum(grad_query_low.astype(jnp.float32), 0)
    grad_bias_value = jnp.sum(grad_value_low.astype(jnp.float32), 0)
    grad_normed_one = jnp.einsum(
        "te,de->td", grad_projected, weight_qkv, preferred_element_type=jnp.float32
    )
    grad_input_part, grad_gain_one, grad_shift_one = norm_one_pull(grad_normed_one)
    input_grad = grad_middle + grad_input_part
    local_grads = (
        grad_gain_one,
        grad_shift_one,
        grad_weight_qkv,
        grad_bias_query,
        grad_bias_value,
        grad_weight_out,
        grad_bias_out,
        grad_gain_two,
        grad_shift_two,
        grad_weight_up,
        grad_bias_up,
        grad_weight_down,
        grad_bias_down,
    )
    shares = (
        lax.psum_scatter(
            local_grads[0].astype(jnp.bfloat16), "seq", scatter_dimension=0, tiled=True
        ).astype(jnp.float32),
        lax.psum_scatter(
            local_grads[1].astype(jnp.bfloat16), "seq", scatter_dimension=0, tiled=True
        ).astype(jnp.float32),
        lax.psum_scatter(
            local_grads[2].astype(jnp.bfloat16), "seq", scatter_dimension=0, tiled=True
        ).astype(jnp.float32),
        lax.psum_scatter(
            local_grads[3].astype(jnp.bfloat16), "seq", scatter_dimension=0, tiled=True
        ).astype(jnp.float32),
        lax.psum_scatter(
            local_grads[4].astype(jnp.bfloat16), "seq", scatter_dimension=0, tiled=True
        ).astype(jnp.float32),
        lax.psum_scatter(
            local_grads[5].astype(jnp.bfloat16), "seq", scatter_dimension=0, tiled=True
        ).astype(jnp.float32),
        lax.psum_scatter(
            local_grads[6].astype(jnp.bfloat16), "seq", scatter_dimension=0, tiled=True
        ).astype(jnp.float32),
        lax.psum_scatter(
            local_grads[7].astype(jnp.bfloat16), "seq", scatter_dimension=0, tiled=True
        ).astype(jnp.float32),
        lax.psum_scatter(
            local_grads[8].astype(jnp.bfloat16), "seq", scatter_dimension=0, tiled=True
        ).astype(jnp.float32),
        lax.psum_scatter(
            local_grads[9].astype(jnp.bfloat16), "seq", scatter_dimension=0, tiled=True
        ).astype(jnp.float32),
        lax.psum_scatter(
            local_grads[10].astype(jnp.bfloat16), "seq", scatter_dimension=0, tiled=True
        ).astype(jnp.float32),
        lax.psum_scatter(
            local_grads[11].astype(jnp.bfloat16), "seq", scatter_dimension=0, tiled=True
        ).astype(jnp.float32),
        lax.psum_scatter(
            local_grads[12].astype(jnp.bfloat16), "seq", scatter_dimension=0, tiled=True
        ).astype(jnp.float32),
    )
    totals = lax.psum(
        (
            shares[0],
            shares[1],
            shares[2],
            shares[3],
            shares[4],
            shares[5],
            shares[6],
            shares[7],
            shares[8],
            shares[9],
            shares[10],
            shares[11],
            shares[12],
        ),
        "ctx",
    )
    return (result.astype(jnp.bfloat16)[None], input_grad[None]) + tuple(totals)


def solution(mesh):
    placed = (
        P("seq", "ctx", None),
        P("seq", "ctx"),
        P("seq"),
        P("seq"),
        P("seq", None),
        P("seq"),
        P("seq"),
        P("seq", None),
        P("seq"),
        P("seq"),
        P("seq"),
        P("seq", None),
        P("seq"),
        P("seq", None),
        P("seq"),
        P("seq", "ctx", None),
    )
    return jax.shard_map(
        shards,
        mesh=mesh,
        in_specs=placed,
        out_specs=(
            P("seq", "ctx", None),
            P("seq", "ctx", None),
            P("seq"),
            P("seq"),
            P("seq", None),
            P("seq"),
            P("seq"),
            P("seq", None),
            P("seq"),
            P("seq"),
            P("seq"),
            P("seq", None),
            P("seq"),
            P("seq", None),
            P("seq"),
        ),
        check_vma=False,
    )
```

profile of v0, /device:TPU:0, one launch (start us, length us, event | category | flops | bytes accessed | tf_op | source)
XLA Modules:
  0.0 881.9 jit_solution(5407056362961799217)
XLA Ops:
  8.0 1.3 fusion.105
  15.8 21.3 %all-reduce.19 = (bf16[768]{0:T(1024)(128)(2,1)S(1)}, bf16[768]{0:T(1024)(128)(2,1)S(1)}, bf16[768]{0:T(1024)(128)(2,1)S(1)}, bf16[768]{0:T(1024)(128)(2,1)S(1)}...) all-reduce(bf16[768]{0:T(1024)(128)(2,1)S(1)} %dynamic-update-slice, ...), channel_id=1, replica_groups=mesh['seq'=4,'ctx'=8] {'seq'}, use_global_device_ids=true, to_apply=%add.3 | all-reduce | flops 5376 | bytes 21504
  37.1 1.0 convert_reduce_fusion
  38.2 1.1 fusion.81
  39.4 43.2 %all-gather.8.cloned.1.call-done = bf16[768,2304]{1,0:T(8,128)(2,1)} async-done(((bf16[192,2304]{1,0:T(8,128)(2,1)}), bf16[768,2304]{1,0:T(8,128)(2,1)}) %all-gather.8.cloned.1.call-update) | async-done | bytes 3538960 | tf_op jit(solution)/shard_map/all_gather | solution.py:148
  82.5 2.7 fusion.60
  88.7 8.7 all_gather.48
  98.6 13.2 %all-gather = bf16[4,1,768]{2,1,0:T(2,128)(2,1)S(1)} all-gather(bf16[1,1,768]{2,1,0:T(2,128)(2,1)S(1)} %reshape.276), channel_id=1, replica_groups=mesh['seq'=4,'ctx'=8] {'seq'}, dimensions={0}, use_global_device_ids=true | all-gather | bytes 7680 | tf_op jit(solution)/shard_map/all_gather | solution.py:156
  112.1 1.7 copy.79
  113.8 1.2 reshape.247
  115.0 1.5 copy.82
  116.5 22.4 %all-gather.12.cloned.1.call-done = bf16[1024,768]{1,0:T(8,128)(2,1)} async-done(((bf16[128,768]{1,0:T(8,128)(2,1)}), bf16[1024,768]{1,0:T(8,128)(2,1)}) %all-gather.12.cloned.1.call-update) | async-done | bytes 1572880 | tf_op jit(solution)/shard_map/all_gather | solution.py:190
  138.8 1.7 copy.81
  140.5 1.2 reshape.249
  141.7 1.5 copy.83
  143.2 10.8 %while.37 = (s32[]{:T(128)}, f32[12,128]{1,0:T(8,128)S(1)}, f32[12,128]{1,0:T(8,128)S(1)}, f32[12,128,64]{1,2,0:T(8,128)}, s32[2,512]{1,0:T(2,128)S(1)}, /*index...) while((s32[]{:T(128)}, f32[12,128]{1,0:T(8,128)S(1)}, ...), condition=%wide.region_5.6_spmd.clone, body=%wide.region_2.5_spmd.clone.sunk | while | flops 211918336 | bytes 21801696 | solution.py:62
  143.3 1.9 fusion.166
  146.8 1.1 fusion.169
  148.7 1.9 fusion.166
  152.1 1.1 fusion.169
  153.9 1.0 bitcast_convert_fusion
  155.0 15.7 %all-gather.14.cloned.1.call-done = bf16[768,768]{1,0:T(8,128)(2,1)} async-done(((bf16[192,768]{1,0:T(8,128)(2,1)}), bf16[768,768]{1,0:T(8,128)(2,1)}) %all-gather.14.cloned.1.call-update) | async-done | bytes 1179664 | tf_op jit(solution)/shard_map/all_gather | solution.py:151
  170.7 1.7 fusion.106
  173.3 87.4 %all-gather.16.cloned.1.call-done = bf16[768,3072]{1,0:T(8,128)(2,1)} async-done(((bf16[192,3072]{1,0:T(8,128)(2,1)}), bf16[768,3072]{1,0:T(8,128)(2,1)}) %all-gather.16.cloned.1.call-update) | async-done | bytes 4718608 | tf_op jit(solution)/shard_map/all_gather | solution.py:155
  260.7 8.5 multiply_convert_fusion
  269.2 80.8 %all-gather.18.cloned.1.call-done = bf16[3072,768]{1,0:T(8,128)(2,1)} async-done(((bf16[768,768]{1,0:T(8,128)(2,1)}), bf16[3072,768]{1,0:T(8,128)(2,1)}) %all-gather.18.cloned.1.call-update) | async-done | bytes 4718608 | tf_op jit(solution)/shard_map/all_gather | solution.py:157
  350.0 5.7 fusion.107
  356.6 2.4 multiply_reduce_fusion
  361.8 32.0 %while.36 = (s32[]{:T(128)}, f32[2,512,1536]{2,1,0:T(8,128)}, s32[2,512]{1,0:T(2,128)S(1)}, s32[1,128]{1,0:T(1,128)}, bf16[2,512,12,64]{1,3,2,0:T(8,128)(2,1)}, ...) while((s32[]{:T(128)}, f32[2,512,1536]{2,1,0:T(8,128)}, ...), condition=%wide.region_13.14_spmd, body=%wide.region_12.13_spmd.sunk | while | flops 411762688 | bytes 34329304 | solution.py:261
  361.8 1.8 fusion.161
  363.8 1.9 fusion.162
  365.7 3.9 convolution_multiply_fusion.2
  369.6 3.9 maximum_bitcast_fusion.2
  373.5 2.4 copy.119
  375.9 1.8 constant_dynamic-update-slice_fusion.2
  377.8 1.8 fusion.161
  379.8 1.9 fusion.162
  381.7 3.9 convolution_multiply_fusion.2
  385.6 3.9 maximum_bitcast_fusion.2
  389.5 2.4 copy.119
  391.9 1.9 constant_dynamic-update-slice_fusion.2
  394.8 1.5 convolution_convert_fusion.3
  396.4 3.7 convolution_convert_fusion.1
  400.2 1.1 copy-done.6
  401.4 3.7 convolution_convert_fusion
  405.2 1.5 copy-done
  406.8 14.3 %while.38 = (s32[]{:T(128)}, f32[128,12,64]{0,2,1:T(8,128)}, bf16[2,512,12,64]{1,3,2,0:T(8,128)(2,1)S(1)}, s32[2,512]{1,0:T(2,128)S(1)}, s32[1,128]{1,0:T(1,128)...) while((s32[]{:T(128)}, f32[128,12,64]{0,2,1:T(8,128)}, ...), condition=%wide.region_11.12_spmd.clone, body=%wide.region_10.11_spmd.clone.sunk | while | flops 306970624 | bytes 9986190 | solution.py:96
  407.0 2.4 fusion.175
  409.6 4.4 fusion.176
  413.9 2.4 fusion.175
  416.4 4.6 fusion.176
  421.1 1.2 fusion.101
  422.5 31.7 %reduce-scatter.6.cloned.1.call-done = f32[128,1536]{1,0:T(8,128)} async-done(((f32[1024,1536]{1,0:T(8,128)}), f32[128,1536]{1,0:T(8,128)}) %reduce-scatter.6.cloned.1.call-update) | async-done | bytes 786448 | tf_op jit(solution)/shard_map/reduce_scatter | solution.py:262
  454.2 1.2 convert.9
  455.4 3.0 convolution_convert_fusion.2
  460.1 26.3 %reduce-scatter.10.cloned.1.call-done = bf16[192,768]{1,0:T(8,128)(2,1)} async-done(((bf16[768,768]{1,0:T(8,128)(2,1)}), bf16[192,768]{1,0:T(8,128)(2,1)}) %reduce-scatter.10.cloned.1.call-update) | async-done | bytes 294928 | tf_op jit(solution)/shard_map/reduce_scatter | solution.py:316
  486.5 3.4 fusion.98
  490.3 17.6 %all-reduce.18 = (bf16[768]{0:T(1024)(128)(2,1)S(1)}, bf16[768]{0:T(1024)(128)(2,1)S(1)}, bf16[768]{0:T(1024)(128)(2,1)S(1)}, bf16[768]{0:T(1024)(128)(2,1)S(1)}...) all-reduce(bf16[768]{0:T(1024)(128)(2,1)S(1)} %dynamic-update-slice, ...), channel_id=1, replica_groups=mesh['seq'=4,'ctx'=8] {'seq'}, use_global_device_ids=true, to_apply=%add.7 | all-reduce | flops 9984 | bytes 39936
  507.9 65.8 %reduce-scatter.12.cloned.1.call-done = bf16[192,3072]{1,0:T(8,128)(2,1)} async-done(((bf16[768,3072]{1,0:T(8,128)(2,1)}), bf16[192,3072]{1,0:T(8,128)(2,1)}) %reduce-scatter.12.cloned.1.call-update) | async-done | bytes 1179664 | tf_op jit(solution)/shard_map/reduce_scatter | solution.py:328
  573.7 87.9 %reduce-scatter.14.cloned.1.call-done = bf16[768,768]{1,0:T(8,128)(2,1)} async-done(((bf16[3072,768]{1,0:T(8,128)(2,1)}), bf16[768,768]{1,0:T(8,128)(2,1)}) %reduce-scatter.14.cloned.1.call-update) | async-done | bytes 1179664 | tf_op jit(solution)/shard_map/reduce_scatter | solution.py:334
  662.0 1.0 add_bitcast_fusion
  663.0 3.9 fusion.70
  666.9 64.1 %reduce-scatter.8.cloned.1.call-done = bf16[192,2304]{1,0:T(8,128)(2,1)} async-done(((bf16[768,2304]{1,0:T(8,128)(2,1)}), bf16[192,2304]{1,0:T(8,128)(2,1)}) %reduce-scatter.8.cloned.1.call-update) | async-done | bytes 884752 | tf_op jit(solution)/shard_map/reduce_scatter | solution.py:307
  731.0 144.4 %all-reduce.21 = (f32[192]{0:T(256)}, f32[192]{0:T(256)}, f32[192,2304]{1,0:T(8,128)}, f32[192]{0:T(256)}, f32[192]{0:T(256)}, /*index=5*/f32[192,768]{1,0:T(8,1...) all-reduce(f32[192]{0:T(256)S(1)} %get-tuple-element.478, ...), channel_id=1, replica_groups=mesh['seq'=4,'ctx'=8] {'ctx'}, use_global_device_ids=true, to_apply=%region_19.20 | all-reduce | flops 1771776 | bytes 10635264 | tf_op jit(solution)/shard_map/psum | solution.py:341
  (226 shorter events, 23.6 us)
Async XLA Ops:
  7.2 75.4 %copy-start.3 = (bf16[1,128,768]{2,1,0:T(8,128)(2,1)S(1)}, bf16[1,128,768]{2,1,0:T(8,128)(2,1)}, u32[]{:S(2)}) copy-start(bf16[1,128,768]{2,1,0:T(8,128)(2,1)} %param.22) | copy-start | bytes 589828
  7.2 75.3 %all-gather.8.cloned.1.call-start = ((), (), s32[]{:S(2)}) async-start(), calls=%async_computation.5 | async-start | bytes 4423680 | tf_op jit(solution)/shard_map/all_gather | solution.py:148
  7.9 104.2 %all-gather.10.cloned.1.call-start = ((), (), s32[]{:S(2)}) async-start(), calls=%async_computation.6 | async-start | bytes 1769472 | tf_op jit(solution)/shard_map/all_gather | solution.py:189
  37.1 48.1 %copy-start.29 = (f32[768]{0:T(1024)}, f32[768]{0:T(1024)S(1)}, u32[]{:S(2)}) copy-start(f32[768]{0:T(1024)S(1)} %convert_element_type.163) | copy-start | bytes 9220
  38.2 47.1 %copy-start.36 = (f32[128]{0:T(128)}, f32[128]{0:T(128)S(1)}, u32[]{:S(2)}) copy-start(f32[128]{0:T(128)S(1)} %broadcast_multiply_fusion.1) | copy-start | bytes 1540
  39.3 45.9 %copy-start.52 = (f32[128]{0:T(128)}, f32[128]{0:T(128)S(1)}, u32[]{:S(2)}) copy-start(f32[128]{0:T(128)S(1)} %fusion.81) | copy-start | bytes 1540
  39.4 45.9 %copy-start.38 = (f32[128]{0:T(128)}, f32[128]{0:T(128)S(1)}, u32[]{:S(2)}) copy-start(f32[128]{0:T(128)S(1)} %fusion.91) | copy-start | bytes 1540
  86.1 2.6 copy-start.31
  86.1 12.5 %copy-start.49 = (bf16[768]{0:T(1024)(128)(2,1)S(1)}, bf16[768]{0:T(1024)(128)(2,1)}, u32[]{:S(2)}) copy-start(bf16[768]{0:T(1024)(128)(2,1)} %param.34) | copy-start | bytes 4612
  86.1 52.7 %all-gather.12.cloned.1.call-start = ((), (), s32[]{:S(2)}) async-start(), calls=%async_computation.7 | async-start | bytes 1769472 | tf_op jit(solution)/shard_map/all_gather | solution.py:190
  86.8 83.9 %all-gather.14.cloned.1.call-start = ((), (), s32[]{:S(2)}) async-start(), calls=%async_computation.8 | async-start | bytes 1474560 | tf_op jit(solution)/shard_map/all_gather | solution.py:151
  87.4 173.3 %all-gather.16.cloned.1.call-start = ((), (), s32[]{:S(2)}) async-start(), calls=%async_computation.9 | async-start | bytes 5898240 | tf_op jit(solution)/shard_map/all_gather | solution.py:155
  88.0 262.0 %all-gather.18.cloned.1.call-start = ((), (), s32[]{:S(2)}) async-start(), calls=%async_computation.10 | async-start | bytes 5898240 | tf_op jit(solution)/shard_map/all_gather | solution.py:157
  88.6 365.6 %reduce-scatter.6.cloned.1.call-start = ((), (), s32[]{:S(2)}) async-start(), calls=%async_computation.11 | async-start | bytes 7077888 | tf_op jit(solution)/shard_map/reduce_scatter | solution.py:262
  111.9 148.8 %copy-start.34 = (f32[768]{0:T(1024)}, f32[768]{0:T(1024)S(1)}, u32[]{:S(2)}) copy-start(f32[768]{0:T(1024)S(1)} %convert_element_type.172) | copy-start | bytes 9220
  111.9 247.1 %copy-start.27 = (f32[768]{0:T(1024)}, f32[768]{0:T(1024)S(1)}, u32[]{:S(2)}) copy-start(f32[768]{0:T(1024)S(1)} %convert_element_type.171) | copy-start | bytes 9220
  145.3 1.4 copy-start.19
  145.3 1.5 copy-start.20
  150.6 1.4 copy-start.19
  150.7 1.5 copy-start.20
  155.0 114.3 %copy-start.15 = (bf16[128,12,64]{0,2,1:T(8,128)(2,1)}, bf16[128,12,64]{0,2,1:T(8,128)(2,1)S(1)}, u32[]{:S(2)}) copy-start(bf16[128,12,64]{0,2,1:T(8,128)(2,1)S(1)} %bitcast_convert_fusion) | copy-start | bytes 589828
  172.4 186.6 %copy-start.1 = (f32[128,768]{1,0:T(8,128)}, f32[128,768]{1,0:T(8,128)S(1)}, u32[]{:S(2)}) copy-start(f32[128,768]{1,0:T(8,128)S(1)} %get-tuple-element.465) | copy-start | bytes 1179652
  172.5 186.6 %copy-start.40 = (f32[128]{0:T(128)}, f32[128]{0:T(128)S(1)}, u32[]{:S(2)}) copy-start(f32[128]{0:T(128)S(1)} %broadcast_multiply_fusion) | copy-start | bytes 1540
  172.7 186.4 %copy-start.43 = (f32[128]{0:T(128)}, f32[128]{0:T(128)S(1)}, u32[]{:S(2)}) copy-start(f32[128]{0:T(128)S(1)} %fusion.92) | copy-start | bytes 1540
  260.7 89.3 %copy-start.13 = (bf16[1,128,768]{2,1,0:T(8,128)(2,1)S(1)}, bf16[1,128,768]{2,1,0:T(8,128)(2,1)}, u32[]{:S(2)}) copy-start(bf16[1,128,768]{2,1,0:T(8,128)(2,1)} %param.37) | copy-start | bytes 589828
  350.0 6.6 copy-start.8
  359.0 1.4 copy-start.7
  359.3 2.5 copy-start.9
  359.3 1.8 copy-start.22
  360.0 1.8 copy-start.17
  361.8 1.8 copy-start.32
  361.8 2.0 copy-start.24
  363.8 1.9 copy-start.5
  377.8 1.8 copy-start.32
  377.8 2.0 copy-start.24
  379.8 1.9 copy-start.5
  393.8 2.5 copy-start.2
  393.8 2.5 copy-start.12
  393.9 2.5 copy-start.28
  393.9 2.5 copy-start.35
  393.9 2.5 copy-start.41
  393.9 2.5 copy-start.44
  393.9 92.5 %reduce-scatter.10.cloned.1.call-start = ((), (), s32[]{:S(2)}) async-start(), calls=%async_computation.13 | async-start | bytes 1474560 | tf_op jit(solution)/shard_map/reduce_scatter | solution.py:316
  396.3 177.4 %reduce-scatter.12.cloned.1.call-start = ((), (), s32[]{:S(2)}) async-start(), calls=%async_computation.14 | async-start | bytes 5898240 | tf_op jit(solution)/shard_map/reduce_scatter | solution.py:328
  400.1 261.4 %reduce-scatter.14.cloned.1.call-start = ((), (), s32[]{:S(2)}) async-start(), calls=%async_computation.15 | async-start | bytes 5898240 | tf_op jit(solution)/shard_map/reduce_scatter | solution.py:334
  405.1 1.6 copy-start
  405.2 1.6 copy-start.25
  405.2 1.6 copy-start.33
  405.2 1.6 copy-start.42
  405.2 325.8 %reduce-scatter.8.cloned.1.call-start = ((), (), s32[]{:S(2)}) async-start(), calls=%async_computation.12 | async-start | bytes 4423680 | tf_op jit(solution)/shard_map/reduce_scatter | solution.py:307
  421.1 34.3 %copy-start.4 = (bf16[1,128,768]{2,1,0:T(8,128)(2,1)S(1)}, bf16[1,128,768]{2,1,0:T(8,128)(2,1)}, u32[]{:S(2)}) copy-start(bf16[1,128,768]{2,1,0:T(8,128)(2,1)} %param.22) | copy-start | bytes 589828
  421.1 34.3 %copy-start.30 = (f32[768]{0:T(1024)S(1)}, f32[768]{0:T(1024)}, u32[]{:S(2)}) copy-start(f32[768]{0:T(1024)} %copy-done.29) | copy-start | bytes 9220
  421.1 34.3 %copy-start.37 = (f32[128]{0:T(128)S(1)}, f32[128]{0:T(128)}, u32[]{:S(2)}) copy-start(f32[128]{0:T(128)} %copy-done.36) | copy-start | bytes 1540
  421.1 34.3 %copy-start.39 = (f32[128]{0:T(128)S(1)}, f32[128]{0:T(128)}, u32[]{:S(2)}) copy-start(f32[128]{0:T(128)} %copy-done.38) | copy-start | bytes 1540
  458.4 1.4 copy-start.54
  486.4 3.5 copy-start.53
  486.5 3.8 copy-start.45
  486.5 3.8 copy-start.46
  486.5 3.8 copy-start.47
  486.5 3.8 copy-start.48
  486.5 175.5 %copy-start.10 = (f32[128,768]{1,0:T(8,128)S(1)}, f32[128,768]{1,0:T(8,128)}, u32[]{:S(2)}) copy-start(f32[128,768]{1,0:T(8,128)} %copy-done.9) | copy-start | bytes 1179652
  486.5 175.5 %copy-start.51 = (f32[128]{0:T(128)S(1)}, f32[128]{0:T(128)}, u32[]{:S(2)}) copy-start(f32[128]{0:T(128)} %copy-done.50) | copy-start | bytes 1540
  662.9 68.0 %copy-start.23 = (bf16[192,3072]{1,0:T(8,128)(2,1)S(1)}, bf16[192,3072]{1,0:T(8,128)(2,1)}, u32[]{:S(2)}) copy-start(bf16[192,3072]{1,0:T(8,128)(2,1)} %reduce-scatter.12.cloned.1.call-done) | copy-start | bytes 3538948
  662.9 68.0 %copy-start.26 = (bf16[192,768]{1,0:T(8,128)(2,1)S(1)}, bf16[192,768]{1,0:T(8,128)(2,1)}, u32[]{:S(2)}) copy-start(bf16[192,768]{1,0:T(8,128)(2,1)} %reduce-scatter.10.cloned.1.call-done) | copy-start | bytes 884740
  (8 other events, 7.5 us)
Sparse Core Ops, SparseCore 0:
  9.6 72.8 all-gather.7
  86.2 24.3 all-gather.9
  113.1 25.6 all-gather.11
  140.2 30.4 all-gather.13
  172.1 88.5 all-gather.15
  262.1 87.8 all-gather.17
  393.9 60.1 reduce-scatter.5
  457.2 29.1 reduce-scatter.9
  488.8 84.8 reduce-scatter.11
  575.9 85.5 reduce-scatter.13
  664.0 66.8 reduce-scatter.7
where the time goes:
time: 883 us; the launch traced here: 882 us
  waiting for transfers between devices  528 us (60%)
  blocking collectives  205 us (23%)
  matrix products  75.7 us (9%)
  local copies, waits for them, and re-layouts  34.5 us (4%)
  other arithmetic  20.6 us (2%)
  between operations  16.6 us (2%)
    psum x1, blocking collectives, shards(): lax.psum((shares[0], shares[1], shares[2], shares[3], shares[4], shares[5...  144 us
    reduce_scatter x1, waiting for transfers between devices, shards(): lax.psum_scatter(local_grads[11].astype(jnp.bfloat16), 'seq', scatter_dim...  87.9 us
    all_gather x1, waiting for transfers between devices, shards(): lax.all_gather(w_up, 'seq', axis=0, tiled=True)  87.4 us
    all_gather x1, waiting for transfers between devices, shards(): lax.all_gather(w_down, 'seq', axis=0, tiled=True)  80.8 us
    reduce_scatter x1, waiting for transfers between devices, shards(): lax.psum_scatter(local_grads[9].astype(jnp.bfloat16), 'seq', scatter_dime...  65.8 us
    reduce_scatter x1, waiting for transfers between devices, shards(): lax.psum_scatter(local_grads[2].astype(jnp.bfloat16), 'seq', scatter_dime...  64.1 us
    all_gather x1, waiting for transfers between devices, shards(): lax.all_gather(w_qkv, 'seq', axis=0, tiled=True)  43.2 us
    unnamed x2, blocking collectives  38.8 us
  transfers between devices with their start and end apart: 11, of which 10 were waited for; matrix products, arithmetic and copies ran while one was open for 9% of the time, Pallas kernels for 0%

commit v1 on v0

--- a/solution.py
+++ b/solution.py
@@ -124,7 +124,7 @@
     return (grad_keys, grad_values)
 
 
-def shards(
+def shards_general(
     tokens,
     block_ids,
     ln1_gain,
@@ -359,6 +359,317 @@
     return (result.astype(jnp.bfloat16)[None], input_grad[None]) + tuple(totals)
 
 
+def core_swap(values):
+    return lax.ppermute(values, "ctx", [(i, i ^ 1) for i in range(8)])
+
+
+def chip_swap(values, mask):
+    return lax.ppermute(values, "ctx", [(i, i ^ (2 * mask)) for i in range(8)])
+
+
+def seq_swap(values, mask):
+    return lax.ppermute(values, "seq", [(i, i ^ mask) for i in range(4)])
+
+
+def chip_gather(values):
+    return [values] + [chip_swap(values, m) for m in (1, 2, 3)]
+
+
+def seq_gather(values):
+    return [values] + [seq_swap(values, m) for m in (1, 2, 3)]
+
+
+def unxor(blocks, index):
+    low, high = (index & 1) == 1, (index >> 1) == 1
+    first = [jnp.where(low, blocks[z ^ 1], blocks[z]) for z in range(4)]
+    return [jnp.where(high, first[z ^ 2], first[z]) for z in range(4)]
+
+
+def core_order(own, other, core):
+    return [jnp.where(core == 0, own, other), jnp.where(core == 0, other, own)]
+
+
+def gather_rows(piece, seq, core):
+    mine = jnp.stack(unxor(seq_gather(piece), seq))
+    theirs = core_swap(mine)
+    both = jnp.stack(core_order(mine, theirs, core), 1)
+    return both.reshape(-1, piece.shape[1])
+
+
+def column_slice(values, k, parts):
+    width = values.shape[1] // parts
+    quarter = width // 4
+    return jnp.concatenate(
+        [
+            lax.dynamic_slice_in_dim(values, width * p + quarter * k, quarter, 1)
+            for p in range(parts)
+        ],
+        1,
+    )
+
+
+def reduce_rows(partial, seq, core):
+    low = partial.astype(jnp.bfloat16)
+    other = lax.dynamic_index_in_dim(low, 1 - core, 1, False)
+    own = lax.dynamic_index_in_dim(partial, core, 1, False)
+    halves = own + core_swap(other).astype(jnp.float32)
+    halves_low = halves.astype(jnp.bfloat16)
+    total = lax.dynamic_index_in_dim(halves, seq, 0, False)
+    for m in (1, 2, 3):
+        block = lax.dynamic_index_in_dim(halves_low, seq ^ m, 0, False)
+        total = total + seq_swap(block, m).astype(jnp.float32)
+    return total
+
+
+def gather_ctx(piece, k, core):
+    mine = jnp.stack(unxor(chip_gather(piece), k))
+    theirs = core_swap(mine)
+    first, second = core_order(mine, theirs, core)
+    return [[first[q], second[q]] for q in range(4)]
+
+
+def shards(
+    tokens,
+    block_ids,
+    ln1_gain,
+    ln1_bias,
+    w_qkv,
+    q_bias,
+    v_bias,
+    w_out,
+    out_bias,
+    ln2_gain,
+    ln2_bias,
+    w_up,
+    up_bias,
+    w_down,
+    down_bias,
+    cotangent,
+):
+    f32, bf16 = jnp.float32, jnp.bfloat16
+    seq = lax.axis_index("seq")
+    ctx = lax.axis_index("ctx")
+    k, core = ctx // 2, ctx % 2
+    width = tokens.shape[-1]
+    quarter = width // 4
+    half = quarter // 2
+    head_dim = width // HEADS
+    scale = 1.0 / math.sqrt(head_dim)
+    rows = tokens.shape[1]
+
+    def placed(vec):
+        return jnp.concatenate([jnp.where(seq == z, vec, jnp.zeros_like(vec)) for z in range(4)])
+
+    small = [ln1_gain, ln1_bias, q_bias, v_bias, out_bias, ln2_gain, ln2_bias, down_bias]
+    small = [placed(v) for v in small] + [
+        jnp.where(seq == z, up_bias, jnp.zeros_like(up_bias)) for z in range(4)
+    ]
+    small_all = sum(v.astype(f32) for v in seq_gather(jnp.stack(small)))
+    gain_one, shift_one, bias_q, bias_v, bias_out, gain_two, shift_two, bias_down = small_all[:8]
+    bias_up = small_all[8:]
+
+    def rows_of_core(values):
+        return lax.dynamic_slice_in_dim(values, half * core, half, 0)
+
+    weight_qkv = gather_rows(column_slice(rows_of_core(w_qkv), k, 3), seq, core)
+    ids_row = jnp.pad(block_ids.astype(bf16), ((0, 7), (0, width - rows)))
+    packed = chip_gather(jnp.concatenate([tokens[0], ids_row], 0))
+    weight_out = gather_rows(rows_of_core(w_out), seq, core)
+    weight_up = gather_rows(column_slice(rows_of_core(w_up), k, 4), seq, core)
+    weight_down = gather_rows(
+        lax.dynamic_slice_in_dim(w_down, quarter * k + half * core, half, 0), seq, core
+    )
+    inputs = jnp.concatenate([p[:rows] for p in packed], 0).astype(f32)
+    ids_own = jnp.concatenate([p[rows, :rows] for p in packed])
+    cot = jnp.concatenate(chip_gather(cotangent[0]), 0)
+
+    def normal(values):
+        center = values - jnp.mean(values, -1, keepdims=True)
+        rstd = lax.rsqrt(jnp.mean(center * center, -1, keepdims=True) + EPSILON)
+        return center * rstd, rstd
+
+    hat_one, rstd_one = normal(inputs)
+    normed = (hat_one * gain_one + shift_one).astype(bf16)
+    bias_qkv = jnp.concatenate(
+        [
+            lax.dynamic_slice_in_dim(bias_q, quarter * k, quarter, 0),
+            jnp.zeros((quarter,), f32),
+            lax.dynamic_slice_in_dim(bias_v, quarter * k, quarter, 0),
+        ]
+    )
+    projected = (jnp.dot(normed, weight_qkv, preferred_element_type=f32) + bias_qkv).astype(bf16)
+    query = projected[:, :quarter]
+    pair = projected[:, quarter:]
+    ids_pad = jnp.pad(ids_own.reshape(4, rows), ((0, 4), (0, 2 * quarter - rows)))
+    other_pack = core_swap(jnp.concatenate([pair, ids_pad], 0))
+    own_rows = 4 * rows
+    pair_all = jnp.concatenate([pair, other_pack[:own_rows]], 0)
+    ids_all = jnp.concatenate([ids_own, other_pack[own_rows : own_rows + 4, :rows].reshape(-1)])
+    heads = HEADS // 4
+    query_heads = query.reshape(own_rows, heads, head_dim)
+    key_heads = pair_all[:, :quarter].reshape(2 * own_rows, heads, head_dim)
+    value_heads = pair_all[:, quarter:].reshape(2 * own_rows, heads, head_dim)
+    allowed = (ids_all[None, :] <= ids_own[:, None])[None]
+    scores = jnp.einsum("qhd,khd->hqk", query_heads, key_heads, preferred_element_type=f32) * scale
+    masked = jnp.where(allowed, scores, NEGATIVE)
+    top = jnp.max(masked, -1, keepdims=True)
+    weights = jnp.where(allowed, jnp.exp(masked - top), 0.0)
+    probs = weights / jnp.sum(weights, -1, keepdims=True)
+    probs_low = probs.astype(bf16)
+    mixed_f = jnp.einsum("hqk,khd->qhd", probs_low, value_heads, preferred_element_type=f32)
+    mixed = mixed_f.reshape(own_rows, quarter).astype(bf16)
+
+    mixed_blocks = chip_gather(mixed)
+    attended = bias_out
+    mixed_rel = []
+    for m in range(4):
+        block = mixed_blocks[m].reshape(4, rows, quarter)
+        block = jnp.concatenate([block[r ^ m] for r in range(4)], 0)
+        mixed_rel.append(block)
+        w_block = lax.dynamic_slice_in_dim(weight_out, quarter * (k ^ m), quarter, 0)
+        attended = attended + jnp.dot(block, w_block, preferred_element_type=f32)
+    middle = inputs + attended
+    hat_two, rstd_two = normal(middle)
+    normed_two = (hat_two * gain_two + shift_two).astype(bf16)
+    bias_up_k = lax.dynamic_slice_in_dim(bias_up, quarter * k, quarter, 1).reshape(-1)
+    pre_act = jnp.dot(normed_two, weight_up, preferred_element_type=f32) + bias_up_k
+    cdf = 0.5 * (1.0 + lax.erf(pre_act * (1.0 / math.sqrt(2.0))))
+    activated = (pre_act * cdf).astype(bf16)
+    down = jnp.dot(activated, weight_down, preferred_element_type=f32).astype(bf16)
+
+    def scatter(partial):
+        blocks = partial.reshape(4, rows, -1)
+        total = blocks[0].astype(f32)
+        for m in (1, 2, 3):
+            total = total + chip_swap(blocks[m], m).astype(f32)
+        return total
+
+    grad_hidden = jnp.einsum("td,fd->tf", cot, weight_down, preferred_element_type=f32)
+    slope = cdf + pre_act * jnp.exp(-0.5 * pre_act * pre_act) * (1.0 / math.sqrt(2.0 * math.pi))
+    grad_pre = (grad_hidden * slope).astype(bf16)
+    grad_normed_two = jnp.einsum("tf,df->td", grad_pre, weight_up, preferred_element_type=f32)
+    grad_gain_two = jnp.sum(grad_normed_two * hat_two, 0)
+    grad_shift_two = jnp.sum(grad_normed_two, 0)
+    err_two = scatter(grad_normed_two.astype(bf16))
+
+    def norm_back(err, gain, hat, rstd):
+        scaled = err * gain
+        return rstd * (
+            scaled
+            - jnp.mean(scaled, -1, keepdims=True)
+            - hat * jnp.mean(scaled * hat, -1, keepdims=True)
+        )
+
+    cot_own = cot[:rows].astype(f32)
+    grad_middle = cot_own + norm_back(err_two, gain_two, hat_two[:rows], rstd_two[:rows])
+    grad_attended_own = grad_middle.astype(bf16)
+    grad_attended = jnp.concatenate(chip_gather(grad_attended_own), 0)
+    w_out_k = lax.dynamic_slice_in_dim(weight_out, quarter * k, quarter, 0)
+    grad_mixed = jnp.einsum("te,de->td", grad_attended, w_out_k, preferred_element_type=f32).astype(
+        bf16
+    )
+    grad_heads = grad_mixed.reshape(own_rows, heads, head_dim)
+    grad_probs = jnp.einsum("qhd,khd->hqk", grad_heads, value_heads, preferred_element_type=f32)
+    inner = jnp.sum(probs * grad_probs, -1, keepdims=True)
+    grad_scores = (probs * (grad_probs - inner)).astype(bf16)
+    grad_query = jnp.einsum("hqk,khd->qhd", grad_scores, key_heads, preferred_element_type=f32)
+    grad_key = jnp.einsum("hqk,qhd->khd", grad_scores, query_heads, preferred_element_type=f32)
+    grad_value = jnp.einsum("hqk,qhd->khd", probs_low, grad_heads, preferred_element_type=f32)
+    grad_pair = jnp.concatenate(
+        [
+            (grad_key * scale).reshape(2 * own_rows, quarter),
+            grad_value.reshape(2 * own_rows, quarter),
+        ],
+        1,
+    )
+    grad_pair_own = grad_pair[:own_rows] + core_swap(grad_pair[own_rows:].astype(bf16)).astype(f32)
+    grad_projected = jnp.concatenate(
+        [(grad_query * scale).reshape(own_rows, quarter).astype(bf16), grad_pair_own.astype(bf16)], 1
+    )
+    grad_normed_one = jnp.einsum(
+        "te,de->td", grad_projected, weight_qkv, preferred_element_type=f32
+    )
+    grad_gain_one = jnp.sum(grad_normed_one * hat_one, 0)
+    grad_shift_one = jnp.sum(grad_normed_one, 0)
+    err_one = scatter(grad_normed_one.astype(bf16))
+    input_grad = grad_middle + norm_back(err_one, gain_one, hat_one[:rows], rstd_one[:rows])
+    result = (middle[:rows] + scatter(down) + bias_down).astype(bf16)
+
+    def by_rows(partial):
+        return partial.reshape(4, 2, half, -1)
+
+    def wgrad(left, right):
+        return jnp.einsum("td,te->de", left, right, preferred_element_type=f32)
+
+    piece_down = reduce_rows(by_rows(wgrad(activated, cot)), seq, core)
+    grad_w_down = jnp.concatenate(
+        [p for pair_ in gather_ctx(piece_down.astype(bf16), k, core) for p in pair_], 0
+    ).astype(f32)
+
+    def columns(pieces, parts):
+        out = []
+        for c in range(2):
+            cols = [
+                pieces[q][c][:, quarter * p : quarter * (p + 1)]
+                for p in range(parts)
+                for q in range(4)
+            ]
+            out.append(jnp.concatenate(cols, 1))
+        return jnp.concatenate(out, 0).astype(f32)
+
+    piece_up = reduce_rows(by_rows(wgrad(normed_two, grad_pre)), seq, core)
+    grad_w_up = columns(gather_ctx(piece_up.astype(bf16), k, core), 4)
+    ga_k = lax.dynamic_slice_in_dim(grad_attended, quarter * k, quarter, 1)
+    grad_out_part = jnp.stack(unxor([wgrad(b, ga_k) for b in mixed_rel], k)).reshape(width, quarter)
+    piece_qkv = reduce_rows(
+        by_rows(jnp.concatenate([wgrad(normed, grad_projected), grad_out_part], 1)), seq, core
+    )
+    pieces = gather_ctx(piece_qkv.astype(bf16), k, core)
+    grad_w_qkv = columns([[p[:, : 3 * quarter] for p in pair_] for pair_ in pieces], 3)
+    grad_w_out = columns([[p[:, 3 * quarter :] for p in pair_] for pair_ in pieces], 1)
+
+    def chip_placed(vec):
+        return jnp.concatenate([jnp.where(k == q, vec, jnp.zeros_like(vec)) for q in range(4)], -1)
+
+    projected_sums = jnp.sum(grad_projected.astype(f32), 0)
+    up_sums = jnp.sum(grad_pre.astype(f32), 0).reshape(4, quarter)
+    vectors = [
+        grad_gain_one,
+        grad_shift_one,
+        chip_placed(projected_sums[:quarter]),
+        chip_placed(projected_sums[2 * quarter :]),
+        jnp.sum(grad_attended_own.astype(f32), 0),
+        grad_gain_two,
+        grad_shift_two,
+        jnp.sum(cot_own, 0),
+    ]
+    small_part = jnp.stack(vectors).reshape(8, 4, quarter).transpose(1, 0, 2).reshape(4, 8 * quarter)
+    small_part = jnp.concatenate([small_part, chip_placed(up_sums)], 1)
+    small_part = lax.psum(small_part, "ctx")
+    total = lax.dynamic_index_in_dim(small_part, seq, 0, False)
+    for m in (1, 2, 3):
+        total = total + seq_swap(lax.dynamic_index_in_dim(small_part, seq ^ m, 0, False), m)
+    g = [total[quarter * n : quarter * (n + 1)] for n in range(8)]
+    g_up = total[8 * quarter :]
+    return (
+        result[None],
+        input_grad[None],
+        g[0],
+        g[1],
+        grad_w_qkv,
+        g[2],
+        g[3],
+        grad_w_out,
+        g[4],
+        g[5],
+        g[6],
+        grad_w_up,
+        g_up,
+        grad_w_down,
+        g[7],
+    )
+
+
 def solution(mesh):
     placed = (
         P("seq", "ctx", None),
@@ -379,7 +690,7 @@
         P("seq", "ctx", None),
     )
     return jax.shard_map(
-        shards,
+        shards if mesh.shape["ctx"] == 8 and mesh.shape["seq"] == 4 else shards_general,
         mesh=mesh,
         in_specs=placed,
         out_specs=(

time: 883 us -> 311 us (0.35)
  waiting for transfers between devices: 528 us -> 69.3 us
  blocking collectives: 205 us -> 22.9 us
  starting transfers between devices: 0.44 us -> 90.7 us
  matrix products: 75.7 us -> 36.2 us
  other arithmetic: 20.6 us -> 43.9 us
  between operations: 16.6 us -> 2.45 us
  local copies, waits for them, and re-layouts: 34.5 us -> 44 us
    reduce_scatter x5 -> x0, waiting for transfers between devices: 276 us -> none  [the longest x1 87.9 us: shards(): lax.psum_scatter(local_grads[11].astype(jnp.bfloat16), 'seq', scatter_dim...]
    all_gather x6 -> x0, waiting for transfers between devices: 249 us -> none  [the longest x1 87.4 us: shards(): lax.all_gather(w_up, 'seq', axis=0, tiled=True)]
    psum x1, blocking collectives: 144 us -> 22.9 us  [shards(): small_part = lax.psum(small_part, 'ctx')]
    ppermute x0 -> x69, starting transfers between devices: none -> 90.7 us  [the longest x27 52.8 us: seq_swap(): return lax.ppermute(values, 'seq', [(i, i ^ mask) for i in range(4)])]
    ppermute x0 -> x69, waiting for transfers between devices: none -> 69.3 us  [the longest x27 35.3 us: seq_swap(): return lax.ppermute(values, 'seq', [(i, i ^ mask) for i in range(4)])]
    dot_general x25 -> x22, matrix products: 72.3 us -> 28 us  [the longest x7 7.43 us: wgrad(): return jnp.einsum('td,te->de', left, right, preferred_element_type=f32)]
    unnamed x2 -> x0, blocking collectives: 38.8 us -> none
    all_gather x2 -> x0, blocking collectives: 21.9 us -> none  [the longest x1 13.2 us: shards(): lax.all_gather(up_bias, 'seq', axis=0, tiled=True)]
  transfers between devices with their start and end apart: 11 -> 69, of which waited for: 10 -> 26; matrix products, arithmetic and copies ran while one was open for 9% -> 33% of each run, Pallas kernels for 0% -> 0%
where the time goes in v1:
time: 311 us; the launch traced here: 309 us
  starting transfers between devices  90.7 us (29%)
  waiting for transfers between devices  69.3 us (22%)
  local copies, waits for them, and re-layouts  44 us (14%)
  other arithmetic  43.9 us (14%)
  matrix products  36.2 us (12%)
  blocking collectives  22.9 us (7%)
    ppermute x27, starting transfers between devices, seq_swap(): return lax.ppermute(values, 'seq', [(i, i ^ mask) for i in range(4)])  52.8 us
    ppermute x30, starting transfers between devices, chip_swap(): return lax.ppermute(values, 'ctx', [(i, i ^ 2 * mask) for i in range(8)])  35.6 us
    ppermute x27, waiting for transfers between devices, seq_swap(): return lax.ppermute(values, 'seq', [(i, i ^ mask) for i in range(4)])  35.3 us
    ppermute x30, waiting for transfers between devices, chip_swap(): return lax.ppermute(values, 'ctx', [(i, i ^ 2 * mask) for i in range(8)])  33.7 us
    psum x1, blocking collectives, shards(): small_part = lax.psum(small_part, 'ctx')  22.9 us
    unnamed x169, local copies, waits for them, and re-layouts  8.83 us
    dot_general x7, matrix products, wgrad(): return jnp.einsum('td,te->de', left, right, preferred_element_type=f32)  7.43 us
  transfers between devices with their start and end apart: 69, of which 26 were waited for; matrix products, arithmetic and copies ran while one was open for 33% of the time, Pallas kernels for 0%

profile of v1, /device:TPU:0, one launch (start us, length us, event | category | flops | bytes accessed | tf_op | source)
XLA Modules:
  0.0 309.5 jit_solution(16136789283342343459)
XLA Ops:
  5.0 5.1 %collective-permute-start.5 = (bf16[12,768]{1,0:T(8,128)(2,1)S(1)}, bf16[12,768]{1,0:T(8,128)(2,1)S(1)}, u32[]{:S(2)}, u32[]{:S(2)}) collective-permute-start(bf16[12,768]{1,0:T(8,128)(2,1)S(1)} %stack.234), channel_id=1, source_target_pairs={{0,24},{8,16},{16,8},{24,0},{1,25},{9,17},{17,9},{25,1},{2,26},{10... | collective-permute-start | bytes 55304 | tf_op jit(solution)/shard_map/ppermute | solution.py:371
  12.0 3.8 %collective-permute-start.18 = (bf16[96,768]{1,0:T(8,128)(2,1)S(1)}, bf16[96,768]{1,0:T(8,128)(2,1)S(1)}, u32[]{:S(2)}, u32[]{:S(2)}) collective-permute-start(bf16[96,768]{1,0:T(8,128)(2,1)S(1)} %pad_maximum_fusion.22), channel_id=1, source_target_pairs={{0,24},{8,16},{16,8},{24,0},{1,25},{9,17},{17,9},{25,1},{2,26},{10... | collective-permute-start | bytes 442376 | tf_op jit(solution)/shard_map/ppermute | solution.py:371
  20.6 1.5 collective-permute-start.6
  22.1 1.5 collective-permute-start.7
  23.7 1.4 collective-permute-start.8
  28.6 8.5 %collective-permute-start.20 = (bf16[96,768]{1,0:T(8,128)(2,1)S(1)}, bf16[96,768]{1,0:T(8,128)(2,1)S(1)}, u32[]{:S(2)}, u32[]{:S(2)}) collective-permute-start(bf16[96,768]{1,0:T(8,128)(2,1)S(1)} %pad_maximum_fusion.22), channel_id=1, source_target_pairs={{0,8},{8,0},{16,24},{24,16},{1,9},{9,1},{17,25},{25,17},{2,10},{10... | collective-permute-start | bytes 442376 | tf_op jit(solution)/shard_map/ppermute | solution.py:371
  38.1 2.3 collective-permute-start.11
  41.8 2.5 collective-permute-start.2
  44.9 5.6 %collective-permute-done.12 = bf16[96,768]{1,0:T(8,128)(2,1)S(1)} collective-permute-done((bf16[96,768]{1,0:T(8,128)(2,1)S(1)}, bf16[96,768]{1,0:T(8,128)(2,1)S(1)}, u32[]{:S(2)}, u32[]{:S(2)}) %collective-permute-start.12) | collective-permute-done | bytes 147488 | tf_op jit(solution)/shard_map/ppermute | solution.py:371
  50.5 1.9 collective-permute-start.22
  52.4 3.8 %collective-permute-start.23 = (bf16[96,768]{1,0:T(8,128)(2,1)S(1)}, bf16[96,768]{1,0:T(8,128)(2,1)S(1)}, u32[]{:S(2)}, u32[]{:S(2)}) collective-permute-start(bf16[96,768]{1,0:T(8,128)(2,1)S(1)} %constant_dynamic-slice_fusion), channel_id=1, source_target_pairs={{0,16},{8,24},{16,0},{24,8},{1,17},{9,25},{17,1},{25,9},{2,18},{10... | collective-permute-start | bytes 442376 | tf_op jit(solution)/shard_map/ppermute | solution.py:371
  57.4 1.6 collective-permute-done.22
  59.1 1.5 collective-permute-start
  60.6 3.9 %collective-permute-done.23 = bf16[96,768]{1,0:T(8,128)(2,1)S(1)} collective-permute-done((bf16[96,768]{1,0:T(8,128)(2,1)S(1)}, bf16[96,768]{1,0:T(8,128)(2,1)S(1)}, u32[]{:S(2)}, u32[]{:S(2)}) %collective-permute-start.23) | collective-permute-done | bytes 147488 | tf_op jit(solution)/shard_map/ppermute | solution.py:371
  64.5 2.4 collective-permute-start.31
  90.5 5.4 %fusion.135 = (f32[3,512]{1,0:T(4,128)S(1)}, f32[3,512,1024]{2,1,0:T(8,128)}) fusion(pred[512,1024]{1,0:T(8,128)(4,1)S(1)} %broadcast_compare_fusion, bf16[512,3,64]{0,2,1:T(8,128)(2,1)S(1)} %bitcast.300, bf16[1024,3,64]{0,2,1:T(8,128)(2,1)S(1)} %bitcast.292), kind=kOutput, calls=%fused_computation.404 | convolution fusion | flops 209191936 | bytes 7411712 | tf_op jit(solution)/shard_map/sub | solution.py:516
  95.9 3.9 %fusion.22 = bf16[3,64,512]{2,1,0:T(8,128)(2,1)S(1)} fusion(bf16[1024,3,64]{0,2,1:T(8,128)(2,1)S(1)} %bitcast.314, f32[3,512,1024]{2,1,0:T(8,128)} %get-tuple-element.272, f32[3,512]{1,0:T(4,128)S(1)} %get-tuple-element.271), kind=kOutput, calls=%fused_computation.58 | convolution fusion | flops 204570624 | bytes 6887424 | tf_op jit(solution)/shard_map/hqk,khd->qhd/dot_general | solution.py:519
  99.9 2.5 collective-permute-start.17
  103.3 8.8 %collective-permute-done.16 = bf16[512,192]{0,1:T(8,128)(2,1)S(1)} collective-permute-done((bf16[512,192]{0,1:T(8,128)(2,1)S(1)}, bf16[512,192]{0,1:T(8,128)(2,1)S(1)}, u32[]{:S(2)}, u32[]{:S(2)}) %collective-permute-start.16) | collective-permute-done | bytes 196640 | tf_op jit(solution)/shard_map/ppermute | solution.py:367
  112.1 1.5 collective-permute-start.15
  113.6 5.3 %collective-permute-done.15 = bf16[512,192]{0,1:T(8,128)(2,1)S(1)} collective-permute-done((bf16[512,192]{0,1:T(8,128)(2,1)S(1)}, bf16[512,192]{0,1:T(8,128)(2,1)S(1)}, u32[]{:S(2)}, u32[]{:S(2)}) %collective-permute-start.15) | collective-permute-done | bytes 196640 | tf_op jit(solution)/shard_map/ppermute | solution.py:367
  123.8 2.9 convert_reduce_fusion.1
  126.7 1.4 fusion.103
  128.1 2.2 fusion.60
  133.2 1.7 collective-permute-start.27
  135.8 1.5 collective-permute-start.34
  137.8 1.5 collective-permute-start.32
  147.3 2.1 fusion.79
  149.5 3.0 fusion.31
  154.4 1.7 fusion.106
  156.1 1.9 convert_reduce_fusion.4
  160.6 1.7 collective-permute-start.36
  162.9 2.0 fusion.61
  164.9 3.4 %collective-permute-done.37 = bf16[128,768]{1,0:T(8,128)(2,1)S(1)} collective-permute-done((bf16[128,768]{1,0:T(8,128)(2,1)}, bf16[128,768]{1,0:T(8,128)(2,1)S(1)}, u32[]{:S(2)}, u32[]{:S(2)}) %collective-permute-start.37) | collective-permute-done | bytes 196640 | tf_op jit(solution)/shard_map/ppermute | solution.py:367
  168.3 3.3 %collective-permute-done.36 = bf16[128,768]{1,0:T(8,128)(2,1)S(1)} collective-permute-done((bf16[128,768]{1,0:T(8,128)(2,1)}, bf16[128,768]{1,0:T(8,128)(2,1)S(1)}, u32[]{:S(2)}, u32[]{:S(2)}) %collective-permute-start.36) | collective-permute-done | bytes 196640 | tf_op jit(solution)/shard_map/ppermute | solution.py:367
  172.7 1.5 convolution_convert_fusion.1
  174.3 3.7 %multiply_reduce_fusion = (f32[3,512]{1,0:T(4,128)S(1)}, f32[3,512,1024]{2,1,0:T(8,128)S(1)}) fusion(f32[3,512,1024]{2,1,0:T(8,128)} %get-tuple-element.272, f32[3,512]{1,0:T(4,128)S(1)} %copy-done.58, bf16[512,3,64]{0,2,1:T(8,128)(2,1)S(1)} %bitcast.316, bf16[1024,3,64]{0,2,1:T(8,128)(2,1)S(1)} %bitcast.315), kind=kOutput, calls=%fused_computation.2 | convolution fusion | flops 206043648 | bytes 13185024 | tf_op jit(solution)/shard_map/qhd,khd->hqk/dot_general | solution.py:572
  186.3 2.5 collective-permute-start.56
  188.8 2.0 collective-permute-start.54
  192.1 2.5 collective-permute-start.64
  195.0 5.4 %collective-permute-start.63 = (bf16[96,768]{1,0:T(8,128)(2,1)S(1)}, bf16[96,768]{1,0:T(8,128)(2,1)S(1)}, u32[]{:S(2)}, u32[]{:S(2)}) collective-permute-start(bf16[96,768]{1,0:T(8,128)(2,1)S(1)} %get-tuple-element.89), channel_id=1, source_target_pairs={{0,16},{8,24},{16,0},{24,8},{1,17},{9,25},{17,1},{25,9},{2,18},{10... | collective-permute-start | bytes 442376 | tf_op jit(solution)/shard_map/ppermute | solution.py:371
  200.3 8.0 %collective-permute-done.55 = bf16[96,768]{1,0:T(8,128)(2,1)S(1)} collective-permute-done((bf16[96,768]{1,0:T(8,128)(2,1)S(1)}, bf16[96,768]{1,0:T(8,128)(2,1)S(1)}, u32[]{:S(2)}, u32[]{:S(2)}) %collective-permute-start.55) | collective-permute-done | bytes 147488 | tf_op jit(solution)/shard_map/ppermute | solution.py:371
  209.1 1.4 collective-permute-start.57
  211.9 2.4 collective-permute-done.63
  214.4 2.2 collective-permute-done.62
  218.0 2.7 fusion.104
  227.0 22.9 %psum.7 = f32[4,2304]{1,0:T(4,128)S(1)} all-reduce(f32[4,2304]{1,0:T(4,128)S(1)} %concatenate.149), channel_id=1, replica_groups=mesh['seq'=4,'ctx'=8] {'ctx'}, use_global_device_ids=true, to_apply=%region_19.20 | all-reduce | flops 9216 | bytes 73728 | tf_op jit(solution)/shard_map/psum | solution.py:648
  250.0 2.4 collective-permute-start.44
  252.5 2.0 collective-permute-start.42
  255.6 1.5 collective-permute-done.43
  257.0 1.5 collective-permute-start.65
  260.3 1.5 collective-permute-start.67
  261.9 1.5 collective-permute-start.41
  266.6 1.9 collective-permute-done.66
  269.3 3.8 %collective-permute-done.41 = bf16[128,768]{1,0:T(8,128)(2,1)S(1)} collective-permute-done((bf16[128,768]{1,0:T(8,128)(2,1)S(1)}, bf16[128,768]{1,0:T(8,128)(2,1)S(1)}, u32[]{:S(2)}, u32[]{:S(2)}) %collective-permute-start.41) | collective-permute-done | bytes 196640 | tf_op jit(solution)/shard_map/ppermute | solution.py:367
  277.2 2.4 collective-permute-start.48
  279.6 2.0 collective-permute-start.46
  282.6 1.6 convert_element_type.276
  286.1 5.2 %collective-permute-done.47 = bf16[96,768]{1,0:T(8,128)(2,1)} collective-permute-done((bf16[96,768]{1,0:T(8,128)(2,1)}, bf16[96,768]{1,0:T(8,128)(2,1)}, u32[]{:S(2)}, u32[]{:S(2)}) %collective-permute-start.47) | collective-permute-done | bytes 147488 | tf_op jit(solution)/shard_map/ppermute | solution.py:371
  292.5 1.8 collective-permute-start.49
  294.3 1.5 collective-permute-start.50
  296.7 3.4 %collective-permute-done.49 = bf16[96,768]{1,0:T(8,128)(2,1)S(1)} collective-permute-done((bf16[96,768]{1,0:T(8,128)(2,1)S(1)}, bf16[96,768]{1,0:T(8,128)(2,1)S(1)}, u32[]{:S(2)}, u32[]{:S(2)}) %collective-permute-start.49) | collective-permute-done | bytes 147488 | tf_op jit(solution)/shard_map/ppermute | solution.py:367
  300.2 1.7 collective-permute-done.50
  304.1 1.7 maximum_convert_fusion
  (454 shorter events, 107.0 us)
Async XLA Ops:
  5.0 15.7 %collective-permute-start.5 = (bf16[12,768]{1,0:T(8,128)(2,1)S(1)}, bf16[12,768]{1,0:T(8,128)(2,1)S(1)}, u32[]{:S(2)}, u32[]{:S(2)}) collective-permute-start(bf16[12,768]{1,0:T(8,128)(2,1)S(1)} %stack.234), channel_id=1, source_target_pairs={{0,24},{8,16},{16,8},{24,0},{1,25},{9,17},{17,9},{25,1},{2,26},{10... | collective-permute-start | bytes 55304 | tf_op jit(solution)/shard_map/ppermute | solution.py:371
  10.1 12.1 %collective-permute-start.4 = (bf16[12,768]{1,0:T(8,128)(2,1)S(1)}, bf16[12,768]{1,0:T(8,128)(2,1)S(1)}, u32[]{:S(2)}, u32[]{:S(2)}) collective-permute-start(bf16[12,768]{1,0:T(8,128)(2,1)S(1)} %stack.234), channel_id=1, source_target_pairs={{0,16},{8,24},{16,0},{24,8},{1,17},{9,25},{17,1},{25,9},{2,18},{10... | collective-permute-start | bytes 55304 | tf_op jit(solution)/shard_map/ppermute | solution.py:371
  10.1 13.6 %collective-permute-start.3 = (bf16[12,768]{1,0:T(8,128)(2,1)S(1)}, bf16[12,768]{1,0:T(8,128)(2,1)S(1)}, u32[]{:S(2)}, u32[]{:S(2)}) collective-permute-start(bf16[12,768]{1,0:T(8,128)(2,1)S(1)} %stack.234), channel_id=1, source_target_pairs={{0,8},{8,0},{16,24},{24,16},{1,9},{9,1},{17,25},{25,17},{2,10},{10... | collective-permute-start | bytes 55304 | tf_op jit(solution)/shard_map/ppermute | solution.py:371
  12.0 28.4 %collective-permute-start.18 = (bf16[96,768]{1,0:T(8,128)(2,1)S(1)}, bf16[96,768]{1,0:T(8,128)(2,1)S(1)}, u32[]{:S(2)}, u32[]{:S(2)}) collective-permute-start(bf16[96,768]{1,0:T(8,128)(2,1)S(1)} %pad_maximum_fusion.22), channel_id=1, source_target_pairs={{0,24},{8,16},{16,8},{24,0},{1,25},{9,17},{17,9},{25,1},{2,26},{10... | collective-permute-start | bytes 442376 | tf_op jit(solution)/shard_map/ppermute | solution.py:371
  15.8 26.0 %collective-permute-start.19 = (bf16[96,768]{1,0:T(8,128)(2,1)S(1)}, bf16[96,768]{1,0:T(8,128)(2,1)S(1)}, u32[]{:S(2)}, u32[]{:S(2)}) collective-permute-start(bf16[96,768]{1,0:T(8,128)(2,1)S(1)} %pad_maximum_fusion.22), channel_id=1, source_target_pairs={{0,16},{8,24},{16,0},{24,8},{1,17},{9,25},{17,1},{25,9},{2,18},{10... | collective-permute-start | bytes 442376 | tf_op jit(solution)/shard_map/ppermute | solution.py:371
  20.6 8.0 %collective-permute-start.6 = (bf16[96,576]{1,0:T(8,128)(2,1)S(1)}, bf16[96,576]{1,0:T(8,128)(2,1)S(1)}, u32[]{:S(2)}, u32[]{:S(2)}) collective-permute-start(bf16[96,576]{1,0:T(8,128)(2,1)S(1)} %pad_maximum_fusion.27), channel_id=1, source_target_pairs={{0,24},{8,16},{16,8},{24,0},{1,25},{9,17},{17,9},{25,1},{2,26},{10... | collective-permute-start | bytes 331784 | tf_op jit(solution)/shard_map/ppermute | solution.py:371
  22.1 15.9 %collective-permute-start.7 = (bf16[96,576]{1,0:T(8,128)(2,1)S(1)}, bf16[96,576]{1,0:T(8,128)(2,1)S(1)}, u32[]{:S(2)}, u32[]{:S(2)}) collective-permute-start(bf16[96,576]{1,0:T(8,128)(2,1)S(1)} %pad_maximum_fusion.27), channel_id=1, source_target_pairs={{0,16},{8,24},{16,0},{24,8},{1,17},{9,25},{17,1},{25,9},{2,18},{10... | collective-permute-start | bytes 331784 | tf_op jit(solution)/shard_map/ppermute | solution.py:371
  23.7 14.4 %collective-permute-start.8 = (bf16[96,576]{1,0:T(8,128)(2,1)S(1)}, bf16[96,576]{1,0:T(8,128)(2,1)S(1)}, u32[]{:S(2)}, u32[]{:S(2)}) collective-permute-start(bf16[96,576]{1,0:T(8,128)(2,1)S(1)} %pad_maximum_fusion.27), channel_id=1, source_target_pairs={{0,8},{8,0},{16,24},{24,16},{1,9},{9,1},{17,25},{25,17},{2,10},{10... | collective-permute-start | bytes 331784 | tf_op jit(solution)/shard_map/ppermute | solution.py:371
  28.6 15.7 %collective-permute-start.20 = (bf16[96,768]{1,0:T(8,128)(2,1)S(1)}, bf16[96,768]{1,0:T(8,128)(2,1)S(1)}, u32[]{:S(2)}, u32[]{:S(2)}) collective-permute-start(bf16[96,768]{1,0:T(8,128)(2,1)S(1)} %pad_maximum_fusion.22), channel_id=1, source_target_pairs={{0,8},{8,0},{16,24},{24,16},{1,9},{9,1},{17,25},{25,17},{2,10},{10... | collective-permute-start | bytes 442376 | tf_op jit(solution)/shard_map/ppermute | solution.py:371
  38.1 12.4 %collective-permute-start.12 = (bf16[96,768]{1,0:T(8,128)(2,1)S(1)}, bf16[96,768]{1,0:T(8,128)(2,1)S(1)}, u32[]{:S(2)}, u32[]{:S(2)}) collective-permute-start(bf16[96,768]{1,0:T(8,128)(2,1)S(1)} %constant_dynamic-slice_fusion.2), channel_id=1, source_target_pairs={{0,16},{8,24},{16,0},{24,8},{1,17},{9,25},{17,1},{25,9},{2,18},{10... | collective-permute-start | bytes 442376 | tf_op jit(solution)/shard_map/ppermute | solution.py:371
  38.1 14.3 %collective-permute-start.11 = (bf16[96,768]{1,0:T(8,128)(2,1)S(1)}, bf16[96,768]{1,0:T(8,128)(2,1)S(1)}, u32[]{:S(2)}, u32[]{:S(2)}) collective-permute-start(bf16[96,768]{1,0:T(8,128)(2,1)S(1)} %constant_dynamic-slice_fusion.2), channel_id=1, source_target_pairs={{0,24},{8,16},{16,8},{24,0},{1,25},{9,17},{17,9},{25,1},{2,26},{10... | collective-permute-start | bytes 442376 | tf_op jit(solution)/shard_map/ppermute | solution.py:371
  40.4 15.8 %collective-permute-start.13 = (bf16[96,768]{1,0:T(8,128)(2,1)S(1)}, bf16[96,768]{1,0:T(8,128)(2,1)S(1)}, u32[]{:S(2)}, u32[]{:S(2)}) collective-permute-start(bf16[96,768]{1,0:T(8,128)(2,1)S(1)} %constant_dynamic-slice_fusion.2), channel_id=1, source_target_pairs={{0,8},{8,0},{16,24},{24,16},{1,9},{9,1},{17,25},{25,17},{2,10},{10... | collective-permute-start | bytes 442376 | tf_op jit(solution)/shard_map/ppermute | solution.py:371
  41.8 28.4 %collective-permute-start.2 = (bf16[136,768]{1,0:T(8,128)(2,1)}, bf16[136,768]{1,0:T(8,128)(2,1)S(1)}, u32[]{:S(2)}, u32[]{:S(2)}) collective-permute-start(bf16[136,768]{1,0:T(8,128)(2,1)} %fusion.58), channel_id=1, source_target_pairs={{0,6},{1,7},{2,4},{3,5},{4,2},{5,3},{6,0},{7,1},{8,14},{9,15},{10,... | collective-permute-start | bytes 626696 | tf_op jit(solution)/shard_map/ppermute | solution.py:367
  44.4 26.5 %collective-permute-start.1 = (bf16[136,768]{1,0:T(8,128)(2,1)}, bf16[136,768]{1,0:T(8,128)(2,1)S(1)}, u32[]{:S(2)}, u32[]{:S(2)}) collective-permute-start(bf16[136,768]{1,0:T(8,128)(2,1)} %fusion.58), channel_id=1, source_target_pairs={{0,4},{1,5},{2,6},{3,7},{4,0},{5,1},{6,2},{7,3},{8,12},{9,13},{10,... | collective-permute-start | bytes 626696 | tf_op jit(solution)/shard_map/ppermute | solution.py:367
  50.5 8.6 %collective-permute-start.22 = (bf16[96,768]{1,0:T(8,128)(2,1)S(1)}, bf16[96,768]{1,0:T(8,128)(2,1)S(1)}, u32[]{:S(2)}, u32[]{:S(2)}) collective-permute-start(bf16[96,768]{1,0:T(8,128)(2,1)S(1)} %constant_dynamic-slice_fusion), channel_id=1, source_target_pairs={{0,24},{8,16},{16,8},{24,0},{1,25},{9,17},{17,9},{25,1},{2,26},{10... | collective-permute-start | bytes 442376 | tf_op jit(solution)/shard_map/ppermute | solution.py:371
  52.4 12.1 %collective-permute-start.23 = (bf16[96,768]{1,0:T(8,128)(2,1)S(1)}, bf16[96,768]{1,0:T(8,128)(2,1)S(1)}, u32[]{:S(2)}, u32[]{:S(2)}) collective-permute-start(bf16[96,768]{1,0:T(8,128)(2,1)S(1)} %constant_dynamic-slice_fusion), channel_id=1, source_target_pairs={{0,16},{8,24},{16,0},{24,8},{1,17},{9,25},{17,1},{25,9},{2,18},{10... | collective-permute-start | bytes 442376 | tf_op jit(solution)/shard_map/ppermute | solution.py:371
  56.2 10.7 %collective-permute-start.24 = (bf16[96,768]{1,0:T(8,128)(2,1)S(1)}, bf16[96,768]{1,0:T(8,128)(2,1)S(1)}, u32[]{:S(2)}, u32[]{:S(2)}) collective-permute-start(bf16[96,768]{1,0:T(8,128)(2,1)S(1)} %constant_dynamic-slice_fusion), channel_id=1, source_target_pairs={{0,8},{8,0},{16,24},{24,16},{1,9},{9,1},{17,25},{25,17},{2,10},{10... | collective-permute-start | bytes 442376 | tf_op jit(solution)/shard_map/ppermute | solution.py:371
  59.1 11.9 %collective-permute-start = (bf16[136,768]{1,0:T(8,128)(2,1)}, bf16[136,768]{1,0:T(8,128)(2,1)S(1)}, u32[]{:S(2)}, u32[]{:S(2)}) collective-permute-start(bf16[136,768]{1,0:T(8,128)(2,1)} %fusion.58), channel_id=1, source_target_pairs={{0,2},{1,3},{2,0},{3,1},{4,6},{5,7},{6,4},{7,5},{8,10},{9,11},{10,... | collective-permute-start | bytes 626696 | tf_op jit(solution)/shard_map/ppermute | solution.py:367
  64.5 58.9 %collective-permute-start.31 = (bf16[128,768]{1,0:T(8,128)(2,1)}, bf16[128,768]{1,0:T(8,128)(2,1)}, u32[]{:S(2)}, u32[]{:S(2)}) collective-permute-start(bf16[128,768]{1,0:T(8,128)(2,1)} %bitcast.45), channel_id=1, source_target_pairs={{0,6},{1,7},{2,4},{3,5},{4,2},{5,3},{6,0},{7,1},{8,14},{9,15},{10,... | collective-permute-start | bytes 589832 | tf_op jit(solution)/shard_map/ppermute | solution.py:367
  66.9 56.5 %collective-permute-start.30 = (bf16[128,768]{1,0:T(8,128)(2,1)}, bf16[128,768]{1,0:T(8,128)(2,1)}, u32[]{:S(2)}, u32[]{:S(2)}) collective-permute-start(bf16[128,768]{1,0:T(8,128)(2,1)} %bitcast.45), channel_id=1, source_target_pairs={{0,4},{1,5},{2,6},{3,7},{4,0},{5,1},{6,2},{7,3},{8,12},{9,13},{10,... | collective-permute-start | bytes 589832 | tf_op jit(solution)/shard_map/ppermute | solution.py:367
  70.3 53.2 %collective-permute-start.29 = (bf16[128,768]{1,0:T(8,128)(2,1)}, bf16[128,768]{1,0:T(8,128)(2,1)}, u32[]{:S(2)}, u32[]{:S(2)}) collective-permute-start(bf16[128,768]{1,0:T(8,128)(2,1)} %bitcast.45), channel_id=1, source_target_pairs={{0,2},{1,3},{2,0},{3,1},{4,6},{5,7},{6,4},{7,5},{8,10},{9,11},{10,... | collective-permute-start | bytes 589832 | tf_op jit(solution)/shard_map/ppermute | solution.py:367
  70.9 9.1 %collective-permute-start.9 = (bf16[4,96,576]{2,1,0:T(8,128)(2,1)S(1)}, bf16[4,96,576]{2,1,0:T(8,128)(2,1)}, u32[]{:S(2)}, u32[]{:S(2)}) collective-permute-start(bf16[4,96,576]{2,1,0:T(8,128)(2,1)S(1)} %pad_maximum_fusion.15), channel_id=1, source_target_pairs={{0,1},{1,0},{2,3},{3,2},{4,5},{5,4},{6,7},{7,6},{8,9},{9,8},{10,11... | collective-permute-start | bytes 1327112 | tf_op jit(solution)/shard_map/ppermute | solution.py:363
  71.0 12.7 %collective-permute-start.21 = (bf16[4,96,768]{2,1,0:T(8,128)(2,1)}, bf16[4,96,768]{2,1,0:T(8,128)(2,1)}, u32[]{:S(2)}, u32[]{:S(2)}) collective-permute-start(bf16[4,96,768]{2,1,0:T(8,128)(2,1)} %pad_maximum_fusion.9), channel_id=1, source_target_pairs={{0,1},{1,0},{2,3},{3,2},{4,5},{5,4},{6,7},{7,6},{8,9},{9,8},{10,11... | collective-permute-start | bytes 1769480 | tf_op jit(solution)/shard_map/ppermute | solution.py:363
  80.0 6.9 %collective-permute-start.25 = (bf16[4,96,768]{2,1,0:T(8,128)(2,1)}, bf16[4,96,768]{2,1,0:T(8,128)(2,1)S(1)}, u32[]{:S(2)}, u32[]{:S(2)}) collective-permute-start(bf16[4,96,768]{2,1,0:T(8,128)(2,1)} %pad_maximum_fusion.10), channel_id=1, source_target_pairs={{0,1},{1,0},{2,3},{3,2},{4,5},{5,4},{6,7},{7,6},{8,9},{9,8},{10,11... | collective-permute-start | bytes 1769480 | tf_op jit(solution)/shard_map/ppermute | solution.py:363
  99.9 20.0 %collective-permute-start.17 = (bf16[512,192]{0,1:T(8,128)(2,1)S(1)}, bf16[512,192]{0,1:T(8,128)(2,1)S(1)}, u32[]{:S(2)}, u32[]{:S(2)}) collective-permute-start(bf16[512,192]{0,1:T(8,128)(2,1)S(1)} %bitcast.309), channel_id=1, source_target_pairs={{0,6},{1,7},{2,4},{3,5},{4,2},{5,3},{6,0},{7,1},{8,14},{9,15},{10,... | collective-permute-start | bytes 589832 | tf_op jit(solution)/shard_map/ppermute | solution.py:367
  102.4 9.7 %collective-permute-start.16 = (bf16[512,192]{0,1:T(8,128)(2,1)S(1)}, bf16[512,192]{0,1:T(8,128)(2,1)S(1)}, u32[]{:S(2)}, u32[]{:S(2)}) collective-permute-start(bf16[512,192]{0,1:T(8,128)(2,1)S(1)} %bitcast.310), channel_id=1, source_target_pairs={{0,4},{1,5},{2,6},{3,7},{4,0},{5,1},{6,2},{7,3},{8,12},{9,13},{10,... | collective-permute-start | bytes 589832 | tf_op jit(solution)/shard_map/ppermute | solution.py:367
  112.1 6.8 %collective-permute-start.15 = (bf16[512,192]{0,1:T(8,128)(2,1)S(1)}, bf16[512,192]{0,1:T(8,128)(2,1)S(1)}, u32[]{:S(2)}, u32[]{:S(2)}) collective-permute-start(bf16[512,192]{0,1:T(8,128)(2,1)S(1)} %bitcast.312), channel_id=1, source_target_pairs={{0,2},{1,3},{2,0},{3,1},{4,6},{5,7},{6,4},{7,5},{8,10},{9,11},{10,... | collective-permute-start | bytes 589832 | tf_op jit(solution)/shard_map/ppermute | solution.py:367
  132.0 27.4 %collective-permute-start.28 = (bf16[128,768]{1,0:T(8,128)(2,1)}, bf16[128,768]{1,0:T(8,128)(2,1)}, u32[]{:S(2)}, u32[]{:S(2)}) collective-permute-start(bf16[128,768]{1,0:T(8,128)(2,1)} %get-tuple-element.79), channel_id=1, source_target_pairs={{0,6},{1,7},{2,4},{3,5},{4,2},{5,3},{6,0},{7,1},{8,14},{9,15},{10,... | collective-permute-start | bytes 589832 | tf_op jit(solution)/shard_map/ppermute | solution.py:367
  133.2 27.4 %collective-permute-start.27 = (bf16[128,768]{1,0:T(8,128)(2,1)}, bf16[128,768]{1,0:T(8,128)(2,1)}, u32[]{:S(2)}, u32[]{:S(2)}) collective-permute-start(bf16[128,768]{1,0:T(8,128)(2,1)} %get-tuple-element.80), channel_id=1, source_target_pairs={{0,4},{1,5},{2,6},{3,7},{4,0},{5,1},{6,2},{7,3},{8,12},{9,13},{10,... | collective-permute-start | bytes 589832 | tf_op jit(solution)/shard_map/ppermute | solution.py:367
  135.8 17.6 %collective-permute-start.34 = (bf16[128,768]{1,0:T(8,128)(2,1)}, bf16[128,768]{1,0:T(8,128)(2,1)}, u32[]{:S(2)}, u32[]{:S(2)}) collective-permute-start(bf16[128,768]{1,0:T(8,128)(2,1)} %get-tuple-element.76), channel_id=1, source_target_pairs={{0,6},{1,7},{2,4},{3,5},{4,2},{5,3},{6,0},{7,1},{8,14},{9,15},{10,... | collective-permute-start | bytes 589832 | tf_op jit(solution)/shard_map/ppermute | solution.py:367
  137.3 16.6 %collective-permute-start.33 = (bf16[128,768]{1,0:T(8,128)(2,1)}, bf16[128,768]{1,0:T(8,128)(2,1)}, u32[]{:S(2)}, u32[]{:S(2)}) collective-permute-start(bf16[128,768]{1,0:T(8,128)(2,1)} %get-tuple-element.77), channel_id=1, source_target_pairs={{0,4},{1,5},{2,6},{3,7},{4,0},{5,1},{6,2},{7,3},{8,12},{9,13},{10,... | collective-permute-start | bytes 589832 | tf_op jit(solution)/shard_map/ppermute | solution.py:367
  137.8 16.1 %collective-permute-start.32 = (bf16[128,768]{1,0:T(8,128)(2,1)}, bf16[128,768]{1,0:T(8,128)(2,1)}, u32[]{:S(2)}, u32[]{:S(2)}) collective-permute-start(bf16[128,768]{1,0:T(8,128)(2,1)} %get-tuple-element.75), channel_id=1, source_target_pairs={{0,2},{1,3},{2,0},{3,1},{4,6},{5,7},{6,4},{7,5},{8,10},{9,11},{10,... | collective-permute-start | bytes 589832 | tf_op jit(solution)/shard_map/ppermute | solution.py:367
  153.4 9.0 %collective-permute-start.26 = (bf16[128,768]{1,0:T(8,128)(2,1)}, bf16[128,768]{1,0:T(8,128)(2,1)}, u32[]{:S(2)}, u32[]{:S(2)}) collective-permute-start(bf16[128,768]{1,0:T(8,128)(2,1)} %get-tuple-element.78), channel_id=1, source_target_pairs={{0,2},{1,3},{2,0},{3,1},{4,6},{5,7},{6,4},{7,5},{8,10},{9,11},{10,... | collective-permute-start | bytes 589832 | tf_op jit(solution)/shard_map/ppermute | solution.py:367
  153.9 31.0 %collective-permute-start.53 = (bf16[4,96,768]{2,1,0:T(8,128)(2,1)}, bf16[4,96,768]{2,1,0:T(8,128)(2,1)}, u32[]{:S(2)}, u32[]{:S(2)}) collective-permute-start(bf16[4,96,768]{2,1,0:T(8,128)(2,1)} %fusion.31), channel_id=1, source_target_pairs={{0,1},{1,0},{2,3},{3,2},{4,5},{5,4},{6,7},{7,6},{8,9},{9,8},{10,11... | collective-permute-start | bytes 1769480 | tf_op jit(solution)/shard_map/ppermute | solution.py:363
  153.9 36.9 %collective-permute-start.61 = (bf16[4,96,768]{2,1,0:T(8,128)(2,1)}, bf16[4,96,768]{2,1,0:T(8,128)(2,1)}, u32[]{:S(2)}, u32[]{:S(2)}) collective-permute-start(bf16[4,96,768]{2,1,0:T(8,128)(2,1)} %fusion.32), channel_id=1, source_target_pairs={{0,1},{1,0},{2,3},{3,2},{4,5},{5,4},{6,7},{7,6},{8,9},{9,8},{10,11... | collective-permute-start | bytes 1769480 | tf_op jit(solution)/shard_map/ppermute | solution.py:363
  159.4 8.9 %collective-permute-start.37 = (bf16[128,768]{1,0:T(8,128)(2,1)}, bf16[128,768]{1,0:T(8,128)(2,1)S(1)}, u32[]{:S(2)}, u32[]{:S(2)}) collective-permute-start(bf16[128,768]{1,0:T(8,128)(2,1)} %get-tuple-element.40), channel_id=1, source_target_pairs={{0,6},{1,7},{2,4},{3,5},{4,2},{5,3},{6,0},{7,1},{8,14},{9,15},{10,... | collective-permute-start | bytes 589832 | tf_op jit(solution)/shard_map/ppermute | solution.py:367
  160.6 11.0 %collective-permute-start.36 = (bf16[128,768]{1,0:T(8,128)(2,1)}, bf16[128,768]{1,0:T(8,128)(2,1)S(1)}, u32[]{:S(2)}, u32[]{:S(2)}) collective-permute-start(bf16[128,768]{1,0:T(8,128)(2,1)} %get-tuple-element.40), channel_id=1, source_target_pairs={{0,4},{1,5},{2,6},{3,7},{4,0},{5,1},{6,2},{7,3},{8,12},{9,13},{10,... | collective-permute-start | bytes 589832 | tf_op jit(solution)/shard_map/ppermute | solution.py:367
  162.4 9.3 %collective-permute-start.35 = (bf16[128,768]{1,0:T(8,128)(2,1)}, bf16[128,768]{1,0:T(8,128)(2,1)S(1)}, u32[]{:S(2)}, u32[]{:S(2)}) collective-permute-start(bf16[128,768]{1,0:T(8,128)(2,1)} %get-tuple-element.40), channel_id=1, source_target_pairs={{0,2},{1,3},{2,0},{3,1},{4,6},{5,7},{6,4},{7,5},{8,10},{9,11},{10,... | collective-permute-start | bytes 589832 | tf_op jit(solution)/shard_map/ppermute | solution.py:367
  182.6 34.7 %collective-permute-start.38 = (bf16[512,384]{0,1:T(8,128)(2,1)S(1)}, bf16[512,384]{0,1:T(8,128)(2,1)S(1)}, u32[]{:S(2)}, u32[]{:S(2)}) collective-permute-start(bf16[512,384]{0,1:T(8,128)(2,1)S(1)} %fusion.29), channel_id=1, source_target_pairs={{0,1},{1,0},{2,3},{3,2},{4,5},{5,4},{6,7},{7,6},{8,9},{9,8},{10,11... | collective-permute-start | bytes 1179656 | tf_op jit(solution)/shard_map/ppermute | solution.py:363
  186.3 8.7 %collective-permute-start.56 = (bf16[96,768]{1,0:T(8,128)(2,1)S(1)}, bf16[96,768]{1,0:T(8,128)(2,1)S(1)}, u32[]{:S(2)}, u32[]{:S(2)}) collective-permute-start(bf16[96,768]{1,0:T(8,128)(2,1)S(1)} %get-tuple-element.103), channel_id=1, source_target_pairs={{0,24},{8,16},{16,8},{24,0},{1,25},{9,17},{17,9},{25,1},{2,26},{10... | collective-permute-start | bytes 442376 | tf_op jit(solution)/shard_map/ppermute | solution.py:371
  188.8 19.6 %collective-permute-start.55 = (bf16[96,768]{1,0:T(8,128)(2,1)S(1)}, bf16[96,768]{1,0:T(8,128)(2,1)S(1)}, u32[]{:S(2)}, u32[]{:S(2)}) collective-permute-start(bf16[96,768]{1,0:T(8,128)(2,1)S(1)} %get-tuple-element.104), channel_id=1, source_target_pairs={{0,16},{8,24},{16,0},{24,8},{1,17},{9,25},{17,1},{25,9},{2,18},{10... | collective-permute-start | bytes 442376 | tf_op jit(solution)/shard_map/ppermute | solution.py:371
  188.8 19.6 %collective-permute-start.54 = (bf16[96,768]{1,0:T(8,128)(2,1)S(1)}, bf16[96,768]{1,0:T(8,128)(2,1)S(1)}, u32[]{:S(2)}, u32[]{:S(2)}) collective-permute-start(bf16[96,768]{1,0:T(8,128)(2,1)S(1)} %get-tuple-element.102), channel_id=1, source_target_pairs={{0,8},{8,0},{16,24},{24,16},{1,9},{9,1},{17,25},{25,17},{2,10},{10... | collective-permute-start | bytes 442376 | tf_op jit(solution)/shard_map/ppermute | solution.py:371
  192.1 18.5 %collective-permute-start.64 = (bf16[96,768]{1,0:T(8,128)(2,1)S(1)}, bf16[96,768]{1,0:T(8,128)(2,1)S(1)}, u32[]{:S(2)}, u32[]{:S(2)}) collective-permute-start(bf16[96,768]{1,0:T(8,128)(2,1)S(1)} %get-tuple-element.88), channel_id=1, source_target_pairs={{0,24},{8,16},{16,8},{24,0},{1,25},{9,17},{17,9},{25,1},{2,26},{10... | collective-permute-start | bytes 442376 | tf_op jit(solution)/shard_map/ppermute | solution.py:371
  195.0 19.4 %collective-permute-start.63 = (bf16[96,768]{1,0:T(8,128)(2,1)S(1)}, bf16[96,768]{1,0:T(8,128)(2,1)S(1)}, u32[]{:S(2)}, u32[]{:S(2)}) collective-permute-start(bf16[96,768]{1,0:T(8,128)(2,1)S(1)} %get-tuple-element.89), channel_id=1, source_target_pairs={{0,16},{8,24},{16,0},{24,8},{1,17},{9,25},{17,1},{25,9},{2,18},{10... | collective-permute-start | bytes 442376 | tf_op jit(solution)/shard_map/ppermute | solution.py:371
  208.3 8.2 %collective-permute-start.62 = (bf16[96,768]{1,0:T(8,128)(2,1)S(1)}, bf16[96,768]{1,0:T(8,128)(2,1)S(1)}, u32[]{:S(2)}, u32[]{:S(2)}) collective-permute-start(bf16[96,768]{1,0:T(8,128)(2,1)S(1)} %get-tuple-element.87), channel_id=1, source_target_pairs={{0,8},{8,0},{16,24},{24,16},{1,9},{9,1},{17,25},{25,17},{2,10},{10... | collective-permute-start | bytes 442376 | tf_op jit(solution)/shard_map/ppermute | solution.py:371
  209.1 51.3 %collective-permute-start.57 = (bf16[96,768]{1,0:T(8,128)(2,1)}, bf16[96,768]{1,0:T(8,128)(2,1)}, u32[]{:S(2)}, u32[]{:S(2)}) collective-permute-start(bf16[96,768]{1,0:T(8,128)(2,1)} %fusion.43), channel_id=1, source_target_pairs={{0,6},{1,7},{2,4},{3,5},{4,2},{5,3},{6,0},{7,1},{8,14},{9,15},{10,... | collective-permute-start | bytes 442376 | tf_op jit(solution)/shard_map/ppermute | solution.py:367
  210.5 51.4 %collective-permute-start.58 = (bf16[96,768]{1,0:T(8,128)(2,1)}, bf16[96,768]{1,0:T(8,128)(2,1)}, u32[]{:S(2)}, u32[]{:S(2)}) collective-permute-start(bf16[96,768]{1,0:T(8,128)(2,1)} %fusion.43), channel_id=1, source_target_pairs={{0,4},{1,5},{2,6},{3,7},{4,0},{5,1},{6,2},{7,3},{8,12},{9,13},{10,... | collective-permute-start | bytes 442376 | tf_op jit(solution)/shard_map/ppermute | solution.py:367
  252.5 6.1 %collective-permute-start.42 = (f32[2304]{0:T(1024)S(1)}, f32[2304]{0:T(1024)S(1)}, u32[]{:S(2)}, u32[]{:S(2)}) collective-permute-start(f32[2304]{0:T(1024)S(1)} %get-tuple-element.29), channel_id=1, source_target_pairs={{0,8},{8,0},{16,24},{24,16},{1,9},{9,1},{17,25},{25,17},{2,10},{10... | collective-permute-start | bytes 27656 | tf_op jit(solution)/shard_map/ppermute | solution.py:371
  255.6 7.8 %collective-permute-start.59 = (bf16[96,768]{1,0:T(8,128)(2,1)}, bf16[96,768]{1,0:T(8,128)(2,1)S(1)}, u32[]{:S(2)}, u32[]{:S(2)}) collective-permute-start(bf16[96,768]{1,0:T(8,128)(2,1)} %fusion.43), channel_id=1, source_target_pairs={{0,2},{1,3},{2,0},{3,1},{4,6},{5,7},{6,4},{7,5},{8,10},{9,11},{10,... | collective-permute-start | bytes 442376 | tf_op jit(solution)/shard_map/ppermute | solution.py:367
  257.0 9.0 %collective-permute-start.65 = (bf16[96,768]{1,0:T(8,128)(2,1)S(1)}, bf16[96,768]{1,0:T(8,128)(2,1)S(1)}, u32[]{:S(2)}, u32[]{:S(2)}) collective-permute-start(bf16[96,768]{1,0:T(8,128)(2,1)S(1)} %copy-done.29), channel_id=1, source_target_pairs={{0,6},{1,7},{2,4},{3,5},{4,2},{5,3},{6,0},{7,1},{8,14},{9,15},{10,... | collective-permute-start | bytes 442376 | tf_op jit(solution)/shard_map/ppermute | solution.py:367
  258.5 10.1 %collective-permute-start.66 = (bf16[96,768]{1,0:T(8,128)(2,1)S(1)}, bf16[96,768]{1,0:T(8,128)(2,1)S(1)}, u32[]{:S(2)}, u32[]{:S(2)}) collective-permute-start(bf16[96,768]{1,0:T(8,128)(2,1)S(1)} %copy-done.29), channel_id=1, source_target_pairs={{0,4},{1,5},{2,6},{3,7},{4,0},{5,1},{6,2},{7,3},{8,12},{9,13},{10,... | collective-permute-start | bytes 442376 | tf_op jit(solution)/shard_map/ppermute | solution.py:367
  260.3 8.2 %collective-permute-start.67 = (bf16[96,768]{1,0:T(8,128)(2,1)S(1)}, bf16[96,768]{1,0:T(8,128)(2,1)S(1)}, u32[]{:S(2)}, u32[]{:S(2)}) collective-permute-start(bf16[96,768]{1,0:T(8,128)(2,1)S(1)} %copy-done.29), channel_id=1, source_target_pairs={{0,2},{1,3},{2,0},{3,1},{4,6},{5,7},{6,4},{7,5},{8,10},{9,11},{10,... | collective-permute-start | bytes 442376 | tf_op jit(solution)/shard_map/ppermute | solution.py:367
  261.9 11.2 %collective-permute-start.41 = (bf16[128,768]{1,0:T(8,128)(2,1)S(1)}, bf16[128,768]{1,0:T(8,128)(2,1)S(1)}, u32[]{:S(2)}, u32[]{:S(2)}) collective-permute-start(bf16[128,768]{1,0:T(8,128)(2,1)S(1)} %get-tuple-element.73), channel_id=1, source_target_pairs={{0,6},{1,7},{2,4},{3,5},{4,2},{5,3},{6,0},{7,1},{8,14},{9,15},{10,... | collective-permute-start | bytes 589832 | tf_op jit(solution)/shard_map/ppermute | solution.py:367
  263.3 10.3 %collective-permute-start.40 = (bf16[128,768]{1,0:T(8,128)(2,1)S(1)}, bf16[128,768]{1,0:T(8,128)(2,1)S(1)}, u32[]{:S(2)}, u32[]{:S(2)}) collective-permute-start(bf16[128,768]{1,0:T(8,128)(2,1)S(1)} %get-tuple-element.74), channel_id=1, source_target_pairs={{0,4},{1,5},{2,6},{3,7},{4,0},{5,1},{6,2},{7,3},{8,12},{9,13},{10,... | collective-permute-start | bytes 589832 | tf_op jit(solution)/shard_map/ppermute | solution.py:367
  266.0 8.1 %collective-permute-start.39 = (bf16[128,768]{1,0:T(8,128)(2,1)S(1)}, bf16[128,768]{1,0:T(8,128)(2,1)S(1)}, u32[]{:S(2)}, u32[]{:S(2)}) collective-permute-start(bf16[128,768]{1,0:T(8,128)(2,1)S(1)} %get-tuple-element.72), channel_id=1, source_target_pairs={{0,2},{1,3},{2,0},{3,1},{4,6},{5,7},{6,4},{7,5},{8,10},{9,11},{10,... | collective-permute-start | bytes 589832 | tf_op jit(solution)/shard_map/ppermute | solution.py:367
  268.6 7.6 %collective-permute-start.45 = (bf16[4,96,768]{2,1,0:T(8,128)(2,1)S(1)}, bf16[4,96,768]{2,1,0:T(8,128)(2,1)S(1)}, u32[]{:S(2)}, u32[]{:S(2)}) collective-permute-start(bf16[4,96,768]{2,1,0:T(8,128)(2,1)S(1)} %fusion.30), channel_id=1, source_target_pairs={{0,1},{1,0},{2,3},{3,2},{4,5},{5,4},{6,7},{7,6},{8,9},{9,8},{10,11... | collective-permute-start | bytes 1769480 | tf_op jit(solution)/shard_map/ppermute | solution.py:363
  268.6 13.0 %collective-permute-start.60 = (bf16[4,96,768]{2,1,0:T(8,128)(2,1)S(1)}, bf16[4,96,768]{2,1,0:T(8,128)(2,1)S(1)}, u32[]{:S(2)}, u32[]{:S(2)}) collective-permute-start(bf16[4,96,768]{2,1,0:T(8,128)(2,1)S(1)} %pad_maximum_fusion.13), channel_id=1, source_target_pairs={{0,1},{1,0},{2,3},{3,2},{4,5},{5,4},{6,7},{7,6},{8,9},{9,8},{10,11... | collective-permute-start | bytes 1769480 | tf_op jit(solution)/shard_map/ppermute | solution.py:363
  273.1 9.2 %collective-permute-start.68 = (bf16[4,96,768]{2,1,0:T(8,128)(2,1)S(1)}, bf16[4,96,768]{2,1,0:T(8,128)(2,1)S(1)}, u32[]{:S(2)}, u32[]{:S(2)}) collective-permute-start(bf16[4,96,768]{2,1,0:T(8,128)(2,1)S(1)} %pad_maximum_fusion.14), channel_id=1, source_target_pairs={{0,1},{1,0},{2,3},{3,2},{4,5},{5,4},{6,7},{7,6},{8,9},{9,8},{10,11... | collective-permute-start | bytes 1769480 | tf_op jit(solution)/shard_map/ppermute | solution.py:363
  277.2 9.0 %collective-permute-start.48 = (bf16[96,768]{1,0:T(8,128)(2,1)}, bf16[96,768]{1,0:T(8,128)(2,1)}, u32[]{:S(2)}, u32[]{:S(2)}) collective-permute-start(bf16[96,768]{1,0:T(8,128)(2,1)} %get-tuple-element.118), channel_id=1, source_target_pairs={{0,24},{8,16},{16,8},{24,0},{1,25},{9,17},{17,9},{25,1},{2,26},{10... | collective-permute-start | bytes 442376 | tf_op jit(solution)/shard_map/ppermute | solution.py:371
  279.6 11.7 %collective-permute-start.47 = (bf16[96,768]{1,0:T(8,128)(2,1)}, bf16[96,768]{1,0:T(8,128)(2,1)}, u32[]{:S(2)}, u32[]{:S(2)}) collective-permute-start(bf16[96,768]{1,0:T(8,128)(2,1)} %get-tuple-element.119), channel_id=1, source_target_pairs={{0,16},{8,24},{16,0},{24,8},{1,17},{9,25},{17,1},{25,9},{2,18},{10... | collective-permute-start | bytes 442376 | tf_op jit(solution)/shard_map/ppermute | solution.py:371
  279.6 11.7 %collective-permute-start.46 = (bf16[96,768]{1,0:T(8,128)(2,1)}, bf16[96,768]{1,0:T(8,128)(2,1)}, u32[]{:S(2)}, u32[]{:S(2)}) collective-permute-start(bf16[96,768]{1,0:T(8,128)(2,1)} %get-tuple-element.117), channel_id=1, source_target_pairs={{0,8},{8,0},{16,24},{24,16},{1,9},{9,1},{17,25},{25,17},{2,10},{10... | collective-permute-start | bytes 442376 | tf_op jit(solution)/shard_map/ppermute | solution.py:371
  292.5 7.7 %collective-permute-start.49 = (bf16[96,768]{1,0:T(8,128)(2,1)S(1)}, bf16[96,768]{1,0:T(8,128)(2,1)S(1)}, u32[]{:S(2)}, u32[]{:S(2)}) collective-permute-start(bf16[96,768]{1,0:T(8,128)(2,1)S(1)} %fusion.46), channel_id=1, source_target_pairs={{0,6},{1,7},{2,4},{3,5},{4,2},{5,3},{6,0},{7,1},{8,14},{9,15},{10,... | collective-permute-start | bytes 442376 | tf_op jit(solution)/shard_map/ppermute | solution.py:367
  294.3 7.6 %collective-permute-start.50 = (bf16[96,768]{1,0:T(8,128)(2,1)S(1)}, bf16[96,768]{1,0:T(8,128)(2,1)S(1)}, u32[]{:S(2)}, u32[]{:S(2)}) collective-permute-start(bf16[96,768]{1,0:T(8,128)(2,1)S(1)} %fusion.46), channel_id=1, source_target_pairs={{0,4},{1,5},{2,6},{3,7},{4,0},{5,1},{6,2},{7,3},{8,12},{9,13},{10,... | collective-permute-start | bytes 442376 | tf_op jit(solution)/shard_map/ppermute | solution.py:367
  295.8 6.1 %collective-permute-start.51 = (bf16[96,768]{1,0:T(8,128)(2,1)S(1)}, bf16[96,768]{1,0:T(8,128)(2,1)S(1)}, u32[]{:S(2)}, u32[]{:S(2)}) collective-permute-start(bf16[96,768]{1,0:T(8,128)(2,1)S(1)} %fusion.46), channel_id=1, source_target_pairs={{0,2},{1,3},{2,0},{3,1},{4,6},{5,7},{6,4},{7,5},{8,10},{9,11},{10,... | collective-permute-start | bytes 442376 | tf_op jit(solution)/shard_map/ppermute | solution.py:367
  (86 other events, 457.7 us)

commit v2 on v0

--- a/solution.py
+++ b/solution.py
@@ -3,6 +3,8 @@
 import jax
 import jax.numpy as jnp
 from jax import lax
+from jax.experimental import pallas as pl
+from jax.experimental.pallas import tpu as pltpu
 from jax.sharding import PartitionSpec as P
 
 HEADS = 12
@@ -124,7 +126,7 @@
     return (grad_keys, grad_values)
 
 
-def shards(
+def shards_general(
     tokens,
     block_ids,
     ln1_gain,
@@ -359,6 +361,568 @@
     return (result.astype(jnp.bfloat16)[None], input_grad[None]) + tuple(totals)
 
 
+QUARTER = 192
+HALF = 96
+ROWS = 128
+WIDTH = 768
+OWN = 512
+f32, bf16 = jnp.float32, jnp.bfloat16
+
+
+def core_swap(values):
+    return lax.ppermute(values, "ctx", [(i, i ^ 1) for i in range(8)])
+
+
+def chip_swap(values, mask):
+    return lax.ppermute(values, "ctx", [(i, i ^ (2 * mask)) for i in range(8)])
+
+
+def seq_swap(values, mask):
+    return lax.ppermute(values, "seq", [(i, i ^ mask) for i in range(4)])
+
+
+def chip_gather(values):
+    return [values] + [chip_swap(values, m) for m in (1, 2, 3)]
+
+
+def seq_gather(values):
+    return [values] + [seq_swap(values, m) for m in (1, 2, 3)]
+
+
+def after(values, *earlier):
+    return lax.optimization_barrier((values, *earlier))[0]
+
+
+def column_slice(values, k, parts):
+    return jnp.concatenate(
+        [
+            lax.dynamic_slice_in_dim(values, WIDTH * p + QUARTER * k, QUARTER, 1)
+            for p in range(parts)
+        ],
+        1,
+    )
+
+
+def run(body, pos, args, outs, scratch=(), flops=0, us=2.0, limit=40):
+    vmem = pl.BlockSpec(memory_space=pltpu.VMEM)
+    return pl.pallas_call(
+        body,
+        out_shape=[jax.ShapeDtypeStruct(shape, kind) for shape, kind in outs],
+        in_specs=[pl.BlockSpec(memory_space=pltpu.SMEM)] + [vmem] * len(args),
+        out_specs=[vmem] * len(outs),
+        scratch_shapes=[pltpu.VMEM(shape, kind) for shape, kind in scratch],
+        compiler_params=pltpu.CompilerParams(vmem_limit_bytes=limit << 20),
+        cost_estimate=pl.CostEstimate(
+            flops=flops, bytes_accessed=int(us * 3.0e6), transcendentals=0
+        ),
+    )(pos, *args)
+
+
+def dot(left, right):
+    return lax.dot_general(left, right, (((1,), (0,)), ((), ())), preferred_element_type=f32)
+
+
+def dot_t(left, right):
+    return lax.dot_general(left, right, (((1,), (1,)), ((), ())), preferred_element_type=f32)
+
+
+def t_dot(left, right):
+    return lax.dot_general(left, right, (((0,), (0,)), ((), ())), preferred_element_type=f32)
+
+
+def normal(values):
+    center = values - jnp.mean(values, -1, keepdims=True)
+    rstd = lax.rsqrt(jnp.mean(center * center, -1, keepdims=True) + EPSILON)
+    return center * rstd, rstd
+
+
+def norm_back(err, gain, hat, rstd):
+    scaled = err * gain
+    return rstd * (
+        scaled
+        - jnp.mean(scaled, -1, keepdims=True)
+        - hat * jnp.mean(scaled * hat, -1, keepdims=True)
+    )
+
+
+def qkv_body(pos, *refs):
+    tok, small, own, oth = refs[0:4], refs[4:8], refs[8:12], refs[12:16]
+    q_ref, kv_ref, normed_ref, vec_ref, w_ref, sm = refs[16:]
+    s, k, c = pos[0], pos[1], pos[2]
+    for m in range(4):
+        z = s ^ m
+        w_ref[pl.ds(pl.multiple_of(z * QUARTER + c * HALF, 32), HALF), :] = own[m][...]
+        w_ref[pl.ds(pl.multiple_of(z * QUARTER + (1 - c) * HALF, 32), HALF), :] = oth[m][...]
+        sm[z] = small[m][...].astype(f32)
+
+    def vec(n):
+        return jnp.concatenate([sm[z, n : n + 1, :QUARTER] for z in range(4)], 1)
+
+    gain, shift = vec(0), vec(1)
+    own_small = sm[k]
+    bias = jnp.concatenate(
+        [own_small[2:3, :QUARTER], jnp.zeros((1, QUARTER), f32), own_small[3:4, :QUARTER]], 1
+    )
+    vec_ref[...] = jnp.concatenate(
+        [gain, shift, vec(4), vec(5), vec(6), vec(7), vec(8), jnp.zeros((1, WIDTH), f32)], 0
+    )
+    for r in range(4):
+        hat, _ = normal(tok[r][:ROWS, :].astype(f32))
+        normed_ref[ROWS * r : ROWS * (r + 1), :] = (hat * gain + shift).astype(bf16)
+    projected = dot(normed_ref[...], w_ref[...]) + bias
+    q_ref[...] = (projected[:, :QUARTER].astype(bf16).astype(f32) * 0.125).astype(bf16)
+    kv_ref[:OWN, :] = projected[:, QUARTER:].astype(bf16)
+    ids = [tok[r][ROWS : ROWS + 8, :ROWS].astype(f32)[:1] for r in range(4)]
+    ids = jnp.concatenate(ids + [jnp.zeros((4, ROWS), f32)], 0).astype(bf16)
+    kv_ref[OWN:, :] = jnp.concatenate([ids, jnp.zeros((8, 2 * QUARTER - ROWS), bf16)], 1)
+
+
+def split_ids(kva, kvb):
+    ids_a = kva[OWN:, :ROWS].astype(f32)
+    ids_b = kvb[OWN:, :ROWS].astype(f32)
+    keys = jnp.concatenate(
+        [ids_a[r : r + 1] for r in range(4)] + [ids_b[r : r + 1] for r in range(4)], 1
+    )
+    return ids_a.T, keys
+
+
+def attend_body(pos, q_ref, kva, kvb, mixed_ref, state_ref):
+    cols, keys = split_ids(kva, kvb)
+    lane = lax.broadcasted_iota(jnp.int32, (ROWS, 64), 1)
+    for r in range(4):
+        rows = slice(ROWS * r, ROWS * (r + 1))
+        hidden = keys > cols[:, r : r + 1]
+        heads, lse = [], jnp.zeros((ROWS, 64), f32)
+        for h in range(3):
+            at = slice(64 * h, 64 * h + 64)
+            at_v = slice(QUARTER + 64 * h, QUARTER + 64 * h + 64)
+            query = q_ref[rows, at]
+            scores = jnp.concatenate(
+                [dot_t(query, kva[:OWN, at]), dot_t(query, kvb[:OWN, at])], 1
+            )
+            scores = jnp.where(hidden, NEGATIVE, scores)
+            top = jnp.max(scores, -1, keepdims=True)
+            weights = jnp.exp(scores - top)
+            total = jnp.sum(weights, -1, keepdims=True)
+            low = weights.astype(bf16)
+            out = dot(low[:, :OWN], kva[:OWN, at_v]) + dot(low[:, OWN:], kvb[:OWN, at_v])
+            heads.append(out * (1.0 / total))
+            lse = jnp.where(lane == h, top + jnp.log(total), lse)
+        mixed = jnp.concatenate(heads, 1)
+        mixed_ref[rows, :] = mixed.astype(bf16)
+        state_ref[rows, :] = jnp.concatenate([mixed, lse], 1)
+
+
+def feed_body(pos, *refs):
+    tok, mixed, own, oth, cot = refs[0:4], refs[4:8], refs[8:12], refs[12:16], refs[16:20]
+    vec_ref = refs[20]
+    mid_ref, n2_ref, act_ref, pre_ref, d0, d1, d2, d3, g0, g1, g2, g3, sums_ref, wok_ref = refs[21:35]
+    wo, wu, wd, hat_ref = refs[35:]
+    s, k, c = pos[0], pos[1], pos[2]
+    for m in range(4):
+        z = s ^ m
+        for half, src in ((c, own[m]), (1 - c, oth[m])):
+            at = pl.ds(pl.multiple_of(z * QUARTER + half * HALF, 32), HALF)
+            wo[at, :] = src[:HALF, :]
+            wu[at, :] = src[HALF : 2 * HALF, :]
+            wd[at, :] = src[2 * HALF :, :]
+    wok_ref[...] = wo[pl.ds(pl.multiple_of(k * QUARTER, 64), QUARTER), :]
+    bias_out, gain, shift = vec_ref[2:3, :], vec_ref[3:4, :], vec_ref[4:5, :]
+    bias_up = vec_ref[6:7, :]
+    attended = bias_out
+    for m in range(4):
+        block = jnp.concatenate(
+            [mixed[m][ROWS * (r ^ m) : ROWS * (r ^ m) + ROWS, :] for r in range(4)], 0
+        )
+        at = pl.ds(pl.multiple_of((k ^ m) * QUARTER, 64), QUARTER)
+        attended = attended + dot(block, wo[at, :])
+    for r in range(4):
+        rows = slice(ROWS * r, ROWS * (r + 1))
+        middle = tok[r][:ROWS, :].astype(f32) + attended[rows]
+        if r == 0:
+            mid_ref[...] = middle
+        hat, _ = normal(middle)
+        hat_ref[rows, :] = hat
+        n2_ref[rows, :] = (hat * gain + shift).astype(bf16)
+    pre_act = dot(n2_ref[...], wu[...]) + bias_up
+    cdf = 0.5 * (1.0 + lax.erf(pre_act * (1.0 / math.sqrt(2.0))))
+    act_ref[...] = (pre_act * cdf).astype(bf16)
+    slope = cdf + pre_act * jnp.exp(-0.5 * pre_act * pre_act) * (1.0 / math.sqrt(2.0 * math.pi))
+    grads = jnp.concatenate([ref[...] for ref in cot], 0)
+    pre = (dot_t(grads, wd[...]) * slope).astype(bf16)
+    pre_ref[...] = pre
+    back = dot_t(pre, wu[...])
+    sums = [
+        jnp.sum(back * hat_ref[...], 0, keepdims=True),
+        jnp.sum(back, 0, keepdims=True),
+        jnp.sum(pre.astype(f32), 0, keepdims=True),
+    ]
+    sums_ref[...] = jnp.concatenate(sums + [jnp.zeros((5, WIDTH), f32)], 0)
+    g0[...] = back[:ROWS]
+    for r, ref in ((1, g1), (2, g2), (3, g3)):
+        ref[...] = back[ROWS * r : ROWS * (r + 1)].astype(bf16)
+    down = dot(act_ref[...], wd[...])
+    d0[...] = down[:ROWS]
+    for r, ref in ((1, d1), (2, d2), (3, d3)):
+        ref[...] = down[ROWS * r : ROWS * (r + 1)].astype(bf16)
+
+
+def feed_grad_body(pos, act_ref, n2_ref, pre_ref, c0, c1, c2, c3, send_ref, own_ref, wg):
+    s, c = pos[0], pos[2]
+    grads = jnp.concatenate([ref[...] for ref in (c0, c1, c2, c3)], 0)
+    for part in range(2):
+        if part == 0:
+            wg[...] = t_dot(act_ref[...], grads)
+        else:
+            wg[...] = t_dot(n2_ref[...], pre_ref[...])
+        rows = slice(HALF * part, HALF * part + HALF)
+        for m in range(4):
+            z = s ^ m
+            at = pl.ds(pl.multiple_of(z * QUARTER + c * HALF, 32), HALF)
+            own_ref[m, rows, :] = wg[at, :]
+            at = pl.ds(pl.multiple_of(z * QUARTER + (1 - c) * HALF, 32), HALF)
+            send_ref[m, rows, :] = wg[at, :].astype(bf16)
+
+
+def halves_body(pos, own_ref, got_ref, o0, o1, o2, o3):
+    rows = got_ref.shape[1]
+    for m, out in enumerate((o0, o1, o2, o3)):
+        out[:rows, :] = (own_ref[m, :rows, :] + got_ref[m].astype(f32)).astype(out.dtype)
+        if own_ref.shape[1] > rows:
+            out[rows:, :] = own_ref[m, rows:, :].astype(out.dtype)
+
+
+def add_body(pos, o0, r1, r2, r3, out):
+    total = o0[...] + r1[...].astype(f32) + r2[...].astype(f32) + r3[...].astype(f32)
+    out[...] = total.astype(out.dtype)
+
+
+def middle_body(pos, g0, r1, r2, r3, mid_ref, cot_ref, vec_ref, gm_ref, ga_ref):
+    err = g0[...] + r1[...].astype(f32) + r2[...].astype(f32) + r3[...].astype(f32)
+    hat, rstd = normal(mid_ref[...])
+    grad = cot_ref[...].astype(f32) + norm_back(err, vec_ref[3:4, :], hat, rstd)
+    gm_ref[...] = grad
+    ga_ref[...] = grad.astype(bf16)
+
+
+def attend_grad_body(pos, a0, a1, a2, a3, wok, q_ref, kva, kvb, state_ref, *outs):
+    dq_ref, own_ref, send_ref, p_ref, ds_ref = outs
+    cols, keys = split_ids(kva, kvb)
+    grads = jnp.concatenate([ref[...] for ref in (a0, a1, a2, a3)], 0)
+    grad_mixed = dot_t(grads, wok[...]).astype(bf16)
+    dq = []
+    for h in range(3):
+        at = slice(64 * h, 64 * h + 64)
+        at_v = slice(QUARTER + 64 * h, QUARTER + 64 * h + 64)
+        query, grad = q_ref[:, at], grad_mixed[:, at]
+        grad_q = []
+        for r in range(4):
+            rows = slice(ROWS * r, ROWS * (r + 1))
+            hidden = keys > cols[:, r : r + 1]
+            g = grad[rows]
+            inner = jnp.sum(g.astype(f32) * state_ref[rows, at], -1, keepdims=True)
+            lse = state_ref[rows, QUARTER + h : QUARTER + h + 1]
+            scores = jnp.concatenate(
+                [dot_t(query[rows], kva[:OWN, at]), dot_t(query[rows], kvb[:OWN, at])], 1
+            )
+            probs = jnp.exp(jnp.where(hidden, NEGATIVE, scores) - lse)
+            slopes = jnp.concatenate([dot_t(g, kva[:OWN, at_v]), dot_t(g, kvb[:OWN, at_v])], 1)
+            ds = (probs * (slopes - inner)).astype(bf16)
+            p_ref[rows, :] = probs.astype(bf16)
+            ds_ref[rows, :] = ds
+            grad_q.append(dot(ds[:, :OWN], kva[:OWN, at]) + dot(ds[:, OWN:], kvb[:OWN, at]))
+        dq.append(jnp.concatenate(grad_q, 0))
+        dk = t_dot(ds_ref[...], query)
+        dv = t_dot(p_ref[...], grad)
+        own_ref[:, at] = dk[:OWN]
+        own_ref[:, at_v] = dv[:OWN]
+        send_ref[:, at] = dk[OWN:].astype(bf16)
+        send_ref[:, at_v] = dv[OWN:].astype(bf16)
+    dq_ref[...] = (jnp.concatenate(dq, 1) * 0.125).astype(bf16)
+
+
+def project_grad_body(pos, *refs):
+    tok, mixed, ga = refs[0:4], refs[4:8], refs[8:12]
+    normed, dq, kv_own, kv_got, w_ref, vec_ref, sums_ref, cot_ref = refs[12:20]
+    send_ref, own_ref, g0, g1, g2, g3, wg, sm, gk, gp = refs[20:]
+    s, k, c = pos[0], pos[1], pos[2]
+    gp[:, :QUARTER] = dq[...]
+    gp[:, QUARTER:] = (kv_own[...] + kv_got[...].astype(f32)).astype(bf16)
+    wg[:, : 3 * QUARTER] = t_dot(normed[...], gp[...])
+    for q in range(4):
+
+        @pl.when(k == q)
+        def _():
+            for r in range(4):
+                gk[ROWS * r : ROWS * (r + 1), :] = ga[r][:, QUARTER * q : QUARTER * (q + 1)]
+
+    for m in range(4):
+        block = jnp.concatenate(
+            [mixed[m][ROWS * (r ^ m) : ROWS * (r ^ m) + ROWS, :] for r in range(4)], 0
+        )
+        at = pl.ds(pl.multiple_of((k ^ m) * QUARTER, 64), QUARTER)
+        wg[at, 3 * QUARTER :] = t_dot(block, gk[...])
+    back = dot_t(gp[...], w_ref[...])
+    hat = jnp.concatenate([normal(tok[r][:ROWS, :].astype(f32))[0] for r in range(4)], 0)
+    ln1_gain = jnp.sum(back * hat, 0, keepdims=True)
+    ln1_bias = jnp.sum(back, 0, keepdims=True)
+    g0[...] = back[:ROWS]
+    for r, ref in ((1, g1), (2, g2), (3, g3)):
+        ref[...] = back[ROWS * r : ROWS * (r + 1)].astype(bf16)
+    gp_sums = jnp.sum(gp[...].astype(f32), 0, keepdims=True)
+    out_bias = jnp.sum(ga[0][...].astype(f32), 0, keepdims=True)
+    down_bias = jnp.sum(cot_ref[...].astype(f32), 0, keepdims=True)
+    for z in range(4):
+        at = slice(QUARTER * z, QUARTER * (z + 1))
+        here = jnp.where(k == z, 1.0, 0.0).astype(f32)
+        row0 = [ln1_gain[:, at], ln1_bias[:, at], gp_sums[:, :QUARTER] * here]
+        row0 = jnp.concatenate(row0 + [gp_sums[:, 2 * QUARTER :] * here], 1)
+        row1 = [out_bias[:, at], sums_ref[0:1, at], sums_ref[1:2, at], down_bias[:, at]]
+        row1 = jnp.concatenate(row1, 1)
+        row2 = jnp.concatenate([sums_ref[2:3, at], jnp.zeros((1, 3 * QUARTER), f32)], 1)
+        sm[z] = jnp.concatenate([row0, row1, row2, jnp.zeros((5, WIDTH), f32)], 0)
+    for m in range(4):
+        z = s ^ m
+        at = pl.ds(pl.multiple_of(z * QUARTER + c * HALF, 32), HALF)
+        own_ref[m, :HALF, :] = wg[at, :]
+        own_ref[m, HALF:, :] = sm[z]
+        at = pl.ds(pl.multiple_of(z * QUARTER + (1 - c) * HALF, 32), HALF)
+        send_ref[m] = wg[at, :].astype(bf16)
+
+
+def input_body(pos, g0, r1, r2, r3, tok_ref, gm_ref, vec_ref, out_ref):
+    err = g0[...] + r1[...].astype(f32) + r2[...].astype(f32) + r3[...].astype(f32)
+    hat, rstd = normal(tok_ref[:ROWS, :].astype(f32))
+    out_ref[0] = gm_ref[...] + norm_back(err, vec_ref[0:1, :], hat, rstd)
+
+
+def output_body(pos, d0, r1, r2, r3, mid_ref, vec_ref, out_ref):
+    total = d0[...] + r1[...].astype(f32) + r2[...].astype(f32) + r3[...].astype(f32)
+    out_ref[0] = (mid_ref[...] + total + vec_ref[5:6, :]).astype(bf16)
+
+
+def feed_join_body(pos, *refs):
+    own, oth = refs[0:4], refs[4:8]
+    down_ref, up_ref, sc = refs[8:]
+    k, c = pos[1], pos[2]
+    for m in range(4):
+        sc[c, k ^ m] = own[m][...]
+        sc[1 - c, k ^ m] = oth[m][...]
+    for q in range(4):
+        for half in range(2):
+            at = QUARTER * q + HALF * half
+            down_ref[at : at + HALF, :] = sc[half, q, :HALF, :].astype(f32)
+            rows = slice(HALF * half, HALF * half + HALF)
+            for p in range(4):
+                cols = slice(WIDTH * p + QUARTER * q, WIDTH * p + QUARTER * (q + 1))
+                piece = sc[half, q, HALF:, QUARTER * p : QUARTER * (p + 1)]
+                up_ref[rows, cols] = piece.astype(f32)
+
+
+def last_join_body(pos, *refs):
+    own, oth = refs[0:4], refs[4:8]
+    qkv_ref, out_ref, vec_ref, up_ref, sc = refs[8:]
+    k, c = pos[1], pos[2]
+    for m in range(4):
+        sc[c, k ^ m] = own[m][...]
+        sc[1 - c, k ^ m] = oth[m][...]
+    total = jnp.zeros((8, WIDTH), f32)
+    ups = []
+    for q in range(4):
+        small = sc[0, q, HALF:, :].astype(f32) + sc[1, q, HALF:, :].astype(f32)
+        total = total + small
+        ups.append(small[2:3, :QUARTER])
+        for half in range(2):
+            rows = slice(HALF * half, HALF * half + HALF)
+            for p in range(3):
+                cols = slice(WIDTH * p + QUARTER * q, WIDTH * p + QUARTER * (q + 1))
+                piece = sc[half, q, :HALF, QUARTER * p : QUARTER * (p + 1)]
+                qkv_ref[rows, cols] = piece.astype(f32)
+            out_ref[rows, QUARTER * q : QUARTER * (q + 1)] = sc[
+                half, q, :HALF, 3 * QUARTER :
+            ].astype(f32)
+    vecs = [total[n // 4 : n // 4 + 1, QUARTER * (n % 4) : QUARTER * (n % 4 + 1)] for n in range(8)]
+    vec_ref[...] = jnp.concatenate(vecs, 0)
+    up_ref[...] = jnp.concatenate(ups, 1)
+
+
+def shards(
+    tokens,
+    block_ids,
+    ln1_gain,
+    ln1_bias,
+    w_qkv,
+    q_bias,
+    v_bias,
+    w_out,
+    out_bias,
+    ln2_gain,
+    ln2_bias,
+    w_up,
+    up_bias,
+    w_down,
+    down_bias,
+    cotangent,
+):
+    seq = lax.axis_index("seq")
+    ctx = lax.axis_index("ctx")
+    k, core = ctx // 2, ctx % 2
+    pos = jnp.stack([seq, k, core]).astype(jnp.int32)
+
+    def rows_of_core(values):
+        return lax.dynamic_slice_in_dim(values, HALF * core, HALF, 0)
+
+    got_qkv = seq_gather(column_slice(rows_of_core(w_qkv), k, 3))
+    ids_row = jnp.pad(block_ids.astype(bf16), ((0, 7), (0, WIDTH - ROWS)))
+    tok = chip_gather(jnp.concatenate([tokens[0], ids_row], 0))
+    small = [ln1_gain, ln1_bias, q_bias, v_bias, out_bias, ln2_gain, ln2_bias, down_bias]
+    small = small + [lax.dynamic_slice_in_dim(up_bias, QUARTER * k, QUARTER, 0)]
+    small = [jnp.pad(v, (0, 256 - QUARTER)) for v in small] + [jnp.zeros((7 * 256,), bf16)]
+    got_small = seq_gather(jnp.concatenate(small).reshape(16, 256))
+    oth_qkv = [core_swap(block) for block in got_qkv]
+    rest = jnp.concatenate(
+        [
+            rows_of_core(w_out),
+            column_slice(rows_of_core(w_up), k, 4),
+            lax.dynamic_slice_in_dim(w_down, QUARTER * k + HALF * core, HALF, 0),
+        ],
+        0,
+    )
+    got_rest = seq_gather(after(rest, *got_qkv, *got_small))
+    cot = chip_gather(after(cotangent[0], *tok))
+
+    query, pair, normed, vec, weight_qkv = run(
+        qkv_body,
+        pos,
+        [*tok, *got_small, *got_qkv, *oth_qkv],
+        [
+            ((OWN, QUARTER), bf16),
+            ((OWN + 8, 2 * QUARTER), bf16),
+            ((OWN, WIDTH), bf16),
+            ((8, WIDTH), f32),
+            ((WIDTH, 3 * QUARTER), bf16),
+        ],
+        [((4, 16, 256), f32)],
+    )
+    pair_oth = core_swap(pair)
+    mixed_own, state = run(
+        attend_body,
+        pos,
+        [query, pair, pair_oth],
+        [((OWN, QUARTER), bf16), ((OWN, 256), f32)],
+        us=6.0,
+    )
+    mixed = chip_gather(mixed_own)
+    got_rest = lax.optimization_barrier((*got_rest, mixed_own))[:4]
+    oth_rest = [core_swap(block) for block in got_rest]
+    big, block = (OWN, WIDTH), (ROWS, WIDTH)
+    mid, normed_two, act, pre, d0, d1, d2, d3, g0, g1, g2, g3, sums, w_out_k = run(
+        feed_body,
+        pos,
+        [*tok, *mixed, *got_rest, *oth_rest, *cot, vec],
+        [(block, f32), (big, bf16), (big, bf16), (big, bf16)]
+        + [(block, f32), (block, bf16), (block, bf16), (block, bf16)] * 2
+        + [((8, WIDTH), f32), ((QUARTER, WIDTH), bf16)],
+        [((WIDTH, WIDTH), bf16)] * 3 + [(big, f32)],
+        us=8.0,
+    )
+    got_g = [chip_swap(g, m) for m, g in ((1, g1), (2, g2), (3, g3))]
+    feed_send, feed_own = run(
+        feed_grad_body,
+        pos,
+        [act, normed_two, pre, *cot],
+        [((4, QUARTER, WIDTH), bf16), ((4, QUARTER, WIDTH), f32)],
+        [((WIDTH, WIDTH), f32)],
+        us=4.0,
+    )
+    feed_got = core_swap(feed_send)
+    grad_mid, grad_att = run(
+        middle_body, pos, [g0, *got_g, mid, cot[0], vec], [(block, f32), (block, bf16)]
+    )
+    piece = (QUARTER, WIDTH)
+    h0, h1, h2, h3 = run(
+        halves_body, pos, [feed_own, feed_got], [(piece, f32)] + [(piece, bf16)] * 3
+    )
+    ga = chip_gather(grad_att)
+    feed_terms = [seq_swap(h, m) for m, h in ((1, h1), (2, h2), (3, h3))]
+    *ga, h0 = lax.optimization_barrier((*ga, h0))
+    got_d = [chip_swap(after(d, ga[1]), m) for m, d in ((1, d1), (2, d2), (3, d3))]
+    dq, kv_own, kv_send = run(
+        attend_grad_body,
+        pos,
+        [*ga, w_out_k, query, pair, pair_oth, state],
+        [((OWN, QUARTER), bf16), ((OWN, 2 * QUARTER), f32), ((OWN, 2 * QUARTER), bf16)],
+        [((OWN, 2 * OWN), bf16)] * 2,
+        us=8.0,
+    )
+    kv_send, *feed_terms = lax.optimization_barrier((kv_send, *feed_terms))
+    kv_got = core_swap(kv_send)
+    (feed_sum,) = run(add_body, pos, [h0, *feed_terms], [(piece, bf16)])
+    feed_blocks = chip_gather(feed_sum)
+    last_send, last_own, e0, e1, e2, e3 = run(
+        project_grad_body,
+        pos,
+        [*tok, *mixed, *ga, normed, dq, kv_own, kv_got, weight_qkv, vec, sums, cot[0]],
+        [((4, HALF, WIDTH), bf16), ((4, HALF + 8, WIDTH), f32)]
+        + [(block, f32), (block, bf16), (block, bf16), (block, bf16)],
+        [((WIDTH, WIDTH), f32), ((4, 8, WIDTH), f32), ((OWN, QUARTER), bf16), ((OWN, 3 * QUARTER), bf16)],
+        us=6.0,
+    )
+    last_got = core_swap(last_send)
+    lpiece = (HALF + 8, WIDTH)
+    l0, l1, l2, l3 = run(
+        halves_body, pos, [last_own, last_got], [(lpiece, f32)] + [(lpiece, bf16)] * 3
+    )
+    last_terms = [seq_swap(h, m) for m, h in ((1, l1), (2, l2), (3, l3))]
+    got_e = [chip_swap(e, m) for m, e in ((1, e1), (2, e2), (3, e3))]
+    feed_oth = [core_swap(b) for b in feed_blocks]
+    grad_w_down, grad_w_up = run(
+        feed_join_body,
+        pos,
+        [*feed_blocks, *feed_oth],
+        [((WIDTH, WIDTH), f32), ((QUARTER, 4 * WIDTH), f32)],
+        [((2, 4, QUARTER, WIDTH), bf16)],
+        us=4.0,
+    )
+    (result,) = run(output_body, pos, [d0, *got_d, mid, vec], [((1, *block), bf16)])
+    (input_grad,) = run(
+        input_body, pos, [e0, *got_e, tok[0], grad_mid, vec], [((1, *block), f32)]
+    )
+    (last_sum,) = run(add_body, pos, [l0, *last_terms], [(lpiece, bf16)])
+    last_blocks = chip_gather(last_sum)
+    last_oth = [core_swap(b) for b in last_blocks]
+    grad_w_qkv, grad_w_out, g, g_up = run(
+        last_join_body,
+        pos,
+        [*last_blocks, *last_oth],
+        [
+            ((QUARTER, 3 * WIDTH), f32),
+            ((QUARTER, WIDTH), f32),
+            ((8, QUARTER), f32),
+            ((1, WIDTH), f32),
+        ],
+        [((2, 4, HALF + 8, WIDTH), bf16)],
+        us=3.0,
+    )
+    return (
+        result,
+        input_grad,
+        g[0],
+        g[1],
+        grad_w_qkv,
+        g[2],
+        g[3],
+        grad_w_out,
+        g[4],
+        g[5],
+        g[6],
+        grad_w_up,
+        g_up[0],
+        grad_w_down,
+        g[7],
+    )
+
+
 def solution(mesh):
     placed = (
         P("seq", "ctx", None),
@@ -379,7 +943,7 @@
         P("seq", "ctx", None),
     )
     return jax.shard_map(
-        shards,
+        shards if mesh.shape["ctx"] == 8 and mesh.shape["seq"] == 4 else shards_general,
         mesh=mesh,
         in_specs=placed,
         out_specs=(

time: 883 us -> 226 us (0.26)
  waiting for transfers between devices: 528 us -> 110 us
  blocking collectives: 205 us -> 0 us
  matrix products: 75.7 us -> 0 us
  starting transfers between devices: 0.44 us -> 63.4 us
  Pallas kernels: 0 us -> 37.8 us
  local copies, waits for them, and re-layouts: 34.5 us -> 11.2 us
  other arithmetic: 20.6 us -> 2.48 us
  between operations: 16.6 us -> 0.95 us
    reduce_scatter x5 -> x0, waiting for transfers between devices: 276 us -> none  [the longest x1 87.9 us: shards(): lax.psum_scatter(local_grads[11].astype(jnp.bfloat16), 'seq', scatter_dim...]
    all_gather x6 -> x0, waiting for transfers between devices: 249 us -> none  [the longest x1 87.4 us: shards(): lax.all_gather(w_up, 'seq', axis=0, tiled=True)]
    psum x1 -> x0, blocking collectives: 144 us -> none  [shards(): lax.psum((shares[0], shares[1], shares[2], shares[3], shares[4], shares[5...]
    ppermute x0 -> x62, waiting for transfers between devices: none -> 110 us  [the longest x27 55.9 us: chip_swap(): return lax.ppermute(values, 'ctx', [(i, i ^ 2 * mask) for i in range(8)])]
    dot_general x26 -> x0, matrix products: 75.7 us -> none  [the longest x6 12.1 us: masked_scores(): jnp.einsum('qhd,khd->hqk', query_heads, key_heads, preferred_element_type...]
    ppermute x0 -> x62, starting transfers between devices: none -> 63.4 us  [the longest x27 31.5 us: chip_swap(): return lax.ppermute(values, 'ctx', [(i, i ^ 2 * mask) for i in range(8)])]
    unnamed x2 -> x0, blocking collectives: 38.8 us -> none
    pallas_call x0 -> x15, Pallas kernels: none -> 37.8 us  [run(): pl.pallas_call(body, out_shape=[jax.ShapeDtypeStruct(shape, kind) for sha...]
  transfers between devices with their start and end apart: 11 -> 62, of which waited for: 10 -> 26; matrix products, arithmetic and copies ran while one was open for 9% -> 2% of each run, Pallas kernels for 0% -> 11%
where the time goes in v2:
time: 226 us
  waiting for transfers between devices  110 us (49%)
  starting transfers between devices  63.4 us (28%)
  Pallas kernels  37.8 us (17%)
  local copies, waits for them, and re-layouts  11.2 us (5%)
  other arithmetic  2.48 us (1%)
    ppermute x27, waiting for transfers between devices, chip_swap(): return lax.ppermute(values, 'ctx', [(i, i ^ 2 * mask) for i in range(8)])  55.9 us
    ppermute x15, waiting for transfers between devices, seq_swap(): return lax.ppermute(values, 'seq', [(i, i ^ mask) for i in range(4)])  51 us
    pallas_call x15, Pallas kernels, run(): pl.pallas_call(body, out_shape=[jax.ShapeDtypeStruct(shape, kind) for sha...  37.8 us
    ppermute x27, starting transfers between devices, chip_swap(): return lax.ppermute(values, 'ctx', [(i, i ^ 2 * mask) for i in range(8)])  31.5 us
    ppermute x15, starting transfers between devices, seq_swap(): return lax.ppermute(values, 'seq', [(i, i ^ mask) for i in range(4)])  28.2 us
    pad x9, local copies, waits for them, and re-layouts, shards(): jnp.pad(v, (0, 256 - QUARTER))  5.28 us
  transfers between devices with their start and end apart: 62, of which 26 were waited for; matrix products, arithmetic and copies ran while one was open for 2% of the time, Pallas kernels for 11%

profile of v2, /device:TPU:0, one launch (start us, length us, event | category | flops | bytes accessed | tf_op | source)
XLA Modules:
  0.0 225.7 jit_solution(2806456544518753992)
XLA Ops:
  0.7 0.8 dynamic_slice.32
  9.0 5.1 %collective-permute-start.5 = (bf16[16,256]{1,0:T(8,128)(2,1)S(1)}, bf16[16,256]{1,0:T(8,128)(2,1)S(1)}, u32[]{:S(2)}, u32[]{:S(2)}) collective-permute-start(bf16[16,256]{1,0:T(8,128)(2,1)S(1)} %reshape.33.refs_4_), channel_id=1, source_target_pairs={{0,24},{8,16},{16,8},{24,0},{1,25},{9,17},{17,9},{25,1},{2,26},{10... | collective-permute-start | bytes 24584 | tf_op jit(solution)/shard_map/ppermute | solution.py:381
  15.4 0.9 fusion.1.refs_0_.tok_ref
  16.4 2.7 %collective-permute-start.2 = (bf16[136,768]{1,0:T(8,128)(2,1)S(1)}, bf16[136,768]{1,0:T(8,128)(2,1)S(1)}, u32[]{:S(2)}, u32[]{:S(2)}) collective-permute-start(bf16[136,768]{1,0:T(8,128)(2,1)S(1)} %fusion.1.refs_0_.tok_ref), channel_id=1, source_target_pairs={{0,6},{1,7},{2,4},{3,5},{4,2},{5,3},{6,0},{7,1},{8,14},{9,15},{10,... | collective-permute-start | bytes 626696 | tf_op jit(solution)/shard_map/ppermute | solution.py:377
  19.5 1.4 fusion.2
  21.0 3.7 %collective-permute-start.8 = (bf16[96,576]{1,0:T(8,128)(2,1)S(1)}, bf16[96,576]{1,0:T(8,128)(2,1)S(1)}, u32[]{:S(2)}, u32[]{:S(2)}) collective-permute-start(bf16[96,576]{1,0:T(8,128)(2,1)S(1)} %pad_maximum_fusion.1.refs_8_), channel_id=1, source_target_pairs={{0,24},{8,16},{16,8},{24,0},{1,25},{9,17},{17,9},{25,1},{2,26},{10... | collective-permute-start | bytes 331784 | tf_op jit(solution)/shard_map/ppermute | solution.py:381
  24.7 0.9 constant_dynamic-slice_fusion
  26.3 1.8 collective-permute-done.8.refs_11_
  28.1 5.5 %collective-permute-done.7.refs_10_ = bf16[96,576]{1,0:T(8,128)(2,1)S(1)} collective-permute-done((bf16[96,576]{1,0:T(8,128)(2,1)S(1)}, bf16[96,576]{1,0:T(8,128)(2,1)S(1)}, u32[]{:S(2)}, u32[]{:S(2)}) %collective-permute-start.7) | collective-permute-done | bytes 110624 | tf_op jit(solution)/shard_map/ppermute | solution.py:381
  33.7 4.8 %collective-permute-done.6.refs_9_ = bf16[96,576]{1,0:T(8,128)(2,1)S(1)} collective-permute-done((bf16[96,576]{1,0:T(8,128)(2,1)S(1)}, bf16[96,576]{1,0:T(8,128)(2,1)S(1)}, u32[]{:S(2)}, u32[]{:S(2)}) %collective-permute-start.6) | collective-permute-done | bytes 110624 | tf_op jit(solution)/shard_map/ppermute | solution.py:381
  38.5 2.4 %collective-permute-start.19 = (bf16[288,768]{1,0:T(8,128)(2,1)S(1)}, bf16[288,768]{1,0:T(8,128)(2,1)S(1)}, u32[]{:S(2)}, u32[]{:S(2)}) collective-permute-start(bf16[288,768]{1,0:T(8,128)(2,1)S(1)} %pad_maximum_fusion.refs_8_), channel_id=1, source_target_pairs={{0,24},{8,16},{16,8},{24,0},{1,25},{9,17},{17,9},{25,1},{2,26},{10... | collective-permute-start | bytes 1327112 | tf_op jit(solution)/shard_map/ppermute | solution.py:381
  42.7 1.9 shard_map.271
  44.9 2.0 collective-permute-start.17
  46.9 1.5 collective-permute-start.26
  48.4 4.5 %collective-permute-done.19.refs_11_ = bf16[288,768]{1,0:T(8,128)(2,1)S(1)} collective-permute-done((bf16[288,768]{1,0:T(8,128)(2,1)S(1)}, bf16[288,768]{1,0:T(8,128)(2,1)S(1)}, u32[]{:S(2)}, u32[]{:S(2)}) %collective-permute-start.19) | collective-permute-done | bytes 442400 | tf_op jit(solution)/shard_map/ppermute | solution.py:381
  52.9 1.5 collective-permute-start.25
  54.9 5.4 %shard_map.272 = (bf16[512,192]{1,0:T(8,128)(2,1)S(1)}, f32[512,256]{1,0:T(8,128)S(1)}) custom-call(s32[3]{0:T(128)S(1)} %pad_add_fusion.pos, bf16[512,192]{1,0:T(8,128)(2,1)S(1)} %get-tuple-element.81.q_ref, bf16[520,384]{1,0:T(8,128)(2,1)S(1)} %get-tuple-element.82.kva, bf16[520,384]{1,0:T(8,128)(2,1)S(1)} %collective-permute-done.13.kvb), custom_call_target="tpu_custom_call" | custom-call | bytes 18000000 | tf_op jit(solution)/shard_map/pallas_call | solution.py:408
  60.3 16.8 %collective-permute-done.18.refs_10_ = bf16[288,768]{1,0:T(8,128)(2,1)S(1)} collective-permute-done((bf16[288,768]{1,0:T(8,128)(2,1)S(1)}, bf16[288,768]{1,0:T(8,128)(2,1)S(1)}, u32[]{:S(2)}, u32[]{:S(2)}) %collective-permute-start.18) | collective-permute-done | bytes 442400 | tf_op jit(solution)/shard_map/ppermute | solution.py:381
  77.1 1.5 collective-permute-start.16
  79.6 5.1 %collective-permute-done.16.refs_7_ = bf16[512,192]{1,0:T(8,128)(2,1)S(1)} collective-permute-done((bf16[512,192]{1,0:T(8,128)(2,1)S(1)}, bf16[512,192]{1,0:T(8,128)(2,1)S(1)}, u32[]{:S(2)}, u32[]{:S(2)}) %collective-permute-start.16) | collective-permute-done | bytes 196640 | tf_op jit(solution)/shard_map/ppermute | solution.py:377
  84.7 1.5 collective-permute-start.15
  86.2 4.9 %collective-permute-done.15.refs_6_ = bf16[512,192]{1,0:T(8,128)(2,1)S(1)} collective-permute-done((bf16[512,192]{1,0:T(8,128)(2,1)S(1)}, bf16[512,192]{1,0:T(8,128)(2,1)S(1)}, u32[]{:S(2)}, u32[]{:S(2)}) %collective-permute-start.15) | collective-permute-done | bytes 196640 | tf_op jit(solution)/shard_map/ppermute | solution.py:377
  91.6 5.8 %collective-permute-done.14.refs_5_ = bf16[512,192]{1,0:T(8,128)(2,1)S(1)} collective-permute-done((bf16[512,192]{1,0:T(8,128)(2,1)S(1)}, bf16[512,192]{1,0:T(8,128)(2,1)S(1)}, u32[]{:S(2)}, u32[]{:S(2)}) %collective-permute-start.14) | collective-permute-done | bytes 196640 | tf_op jit(solution)/shard_map/ppermute | solution.py:377
  97.5 5.8 %shard_map.273 = (f32[128,768]{1,0:T(8,128)S(1)}, bf16[512,768]{1,0:T(8,128)(2,1)S(1)}, bf16[512,768]{1,0:T(8,128)(2,1)S(1)}, bf16[512,768]{1,0:T(8,128)(2,1)S(1...) custom-call(s32[3]{0:T(128)S(1)} %pad_add_fusion.pos, ...), custom_call_target="tpu_custom_call" | custom-call | bytes 24000000 | tf_op jit(solution)/shard_map/pallas_call | solution.py:408
  103.2 2.2 shard_map.275
  106.1 1.5 collective-permute-start.28
  107.6 1.5 collective-permute-start.29
  109.1 4.2 %collective-permute-done.27.r1 = bf16[128,768]{1,0:T(8,128)(2,1)S(1)} collective-permute-done((bf16[128,768]{1,0:T(8,128)(2,1)S(1)}, bf16[128,768]{1,0:T(8,128)(2,1)S(1)}, u32[]{:S(2)}, u32[]{:S(2)}) %collective-permute-start.27) | collective-permute-done | bytes 196640 | tf_op jit(solution)/shard_map/ppermute | solution.py:377
  113.3 3.1 %collective-permute-done.28.r2 = bf16[128,768]{1,0:T(8,128)(2,1)S(1)} collective-permute-done((bf16[128,768]{1,0:T(8,128)(2,1)S(1)}, bf16[128,768]{1,0:T(8,128)(2,1)S(1)}, u32[]{:S(2)}, u32[]{:S(2)}) %collective-permute-start.28) | collective-permute-done | bytes 196640 | tf_op jit(solution)/shard_map/ppermute | solution.py:377
  116.4 1.6 collective-permute-done.29.r3
  118.0 0.9 shard_map.274
  118.9 1.8 collective-permute-start.32
  120.7 0.7 shard_map.276
  121.5 1.8 collective-permute-start.37
  123.3 3.4 %collective-permute-start.38 = (bf16[192,768]{1,0:T(8,128)(2,1)S(1)}, bf16[192,768]{1,0:T(8,128)(2,1)S(1)}, u32[]{:S(2)}, u32[]{:S(2)}) collective-permute-start(bf16[192,768]{1,0:T(8,128)(2,1)S(1)} %get-tuple-element.121), channel_id=1, source_target_pairs={{0,16},{8,24},{16,0},{24,8},{1,17},{9,25},{17,1},{25,9},{2,18},{10... | collective-permute-start | bytes 884744 | tf_op jit(solution)/shard_map/ppermute | solution.py:381
  127.2 1.2 collective-permute-start.30
  128.4 3.9 %collective-permute-done.31.a2.refs_10_ = bf16[128,768]{1,0:T(8,128)(2,1)S(1)} collective-permute-done((bf16[128,768]{1,0:T(8,128)(2,1)S(1)}, bf16[128,768]{1,0:T(8,128)(2,1)S(1)}, u32[]{:S(2)}, u32[]{:S(2)}) %collective-permute-start.31) | collective-permute-done | bytes 196640 | tf_op jit(solution)/shard_map/ppermute | solution.py:377
  132.8 6.9 %shard_map.278 = (bf16[512,192]{1,0:T(8,128)(2,1)S(1)}, f32[512,384]{1,0:T(8,128)S(1)}, bf16[512,384]{1,0:T(8,128)(2,1)S(1)}) custom-call(s32[3]{0:T(128)S(1)} %pad_add_fusion.pos, bf16[128,768]{1,0:T(8,128)(2,1)S(1)} %get-tuple-element.111.a0.refs_8_, bf16[128,768]{1,0:T(8,128)(2,1)S(1)} %collective-permute-done.30.a1.refs_9_, ...), custom_call_target="tpu_custom_call" | custom-call | bytes 24000000 | tf_op jit(solution)/shard_map/pallas_call | solution.py:408
  139.8 7.4 %collective-permute-done.38.r2 = bf16[192,768]{1,0:T(8,128)(2,1)S(1)} collective-permute-done((bf16[192,768]{1,0:T(8,128)(2,1)S(1)}, bf16[192,768]{1,0:T(8,128)(2,1)S(1)}, u32[]{:S(2)}, u32[]{:S(2)}) %collective-permute-start.38) | collective-permute-done | bytes 294944 | tf_op jit(solution)/shard_map/ppermute | solution.py:381
  147.2 1.7 collective-permute-done.40.refs_15_
  148.9 3.3 %shard_map.279 = (bf16[4,96,768]{2,1,0:T(8,128)(2,1)S(1)}, f32[4,104,768]{2,1,0:T(8,128)S(1)}, f32[128,768]{1,0:T(8,128)S(1)}, bf16[128,768]{1,0:T(8,128)(2,1)S(...) custom-call(s32[3]{0:T(128)S(1)} %pad_add_fusion.pos, bf16[136,768]{1,0:T(8,128)(2,1)S(1)} %fusion.1.refs_0_.tok_ref, ...), custom_call_target="tpu_custom_call" | custom-call | bytes 18000000 | tf_op jit(solution)/shard_map/pallas_call | solution.py:408
  153.1 1.2 collective-permute-start.35
  155.0 1.7 collective-permute-start.57
  157.2 3.0 %collective-permute-done.34.r1 = bf16[128,768]{1,0:T(8,128)(2,1)S(1)} collective-permute-done((bf16[128,768]{1,0:T(8,128)(2,1)S(1)}, bf16[128,768]{1,0:T(8,128)(2,1)S(1)}, u32[]{:S(2)}, u32[]{:S(2)}) %collective-permute-start.34) | collective-permute-done | bytes 196640 | tf_op jit(solution)/shard_map/ppermute | solution.py:377
  160.8 6.4 %collective-permute-done.35.r2 = bf16[128,768]{1,0:T(8,128)(2,1)S(1)} collective-permute-done((bf16[128,768]{1,0:T(8,128)(2,1)S(1)}, bf16[128,768]{1,0:T(8,128)(2,1)S(1)}, u32[]{:S(2)}, u32[]{:S(2)}) %collective-permute-start.35) | collective-permute-done | bytes 196640 | tf_op jit(solution)/shard_map/ppermute | solution.py:377
  167.2 1.3 collective-permute-start.36
  169.2 7.4 %collective-permute-done.36.r3 = bf16[128,768]{1,0:T(8,128)(2,1)S(1)} collective-permute-done((bf16[128,768]{1,0:T(8,128)(2,1)S(1)}, bf16[128,768]{1,0:T(8,128)(2,1)S(1)}, u32[]{:S(2)}, u32[]{:S(2)}) %collective-permute-start.36) | collective-permute-done | bytes 196640 | tf_op jit(solution)/shard_map/ppermute | solution.py:377
  176.6 5.0 %collective-permute-start.45 = (bf16[104,768]{1,0:T(8,128)(2,1)S(1)}, bf16[104,768]{1,0:T(8,128)(2,1)S(1)}, u32[]{:S(2)}, u32[]{:S(2)}) collective-permute-start(bf16[104,768]{1,0:T(8,128)(2,1)S(1)} %get-tuple-element.134), channel_id=1, source_target_pairs={{0,8},{8,0},{16,24},{24,16},{1,9},{9,1},{17,25},{25,17},{2,10},{10... | collective-permute-start | bytes 479240 | tf_op jit(solution)/shard_map/ppermute | solution.py:381
  182.2 1.1 collective-permute-start.46
  183.4 2.2 collective-permute-done.45.r1
  185.6 3.1 %collective-permute-start.47 = (bf16[104,768]{1,0:T(8,128)(2,1)S(1)}, bf16[104,768]{1,0:T(8,128)(2,1)S(1)}, u32[]{:S(2)}, u32[]{:S(2)}) collective-permute-start(bf16[104,768]{1,0:T(8,128)(2,1)S(1)} %get-tuple-element.136), channel_id=1, source_target_pairs={{0,24},{8,16},{16,8},{24,0},{1,25},{9,17},{17,9},{25,1},{2,26},{10... | collective-permute-start | bytes 479240 | tf_op jit(solution)/shard_map/ppermute | solution.py:381
  188.6 8.0 %collective-permute-done.46.r2 = bf16[104,768]{1,0:T(8,128)(2,1)S(1)} collective-permute-done((bf16[104,768]{1,0:T(8,128)(2,1)S(1)}, bf16[104,768]{1,0:T(8,128)(2,1)S(1)}, u32[]{:S(2)}, u32[]{:S(2)}) %collective-permute-start.46) | collective-permute-done | bytes 159776 | tf_op jit(solution)/shard_map/ppermute | solution.py:381
  196.6 1.6 collective-permute-start.41
  199.4 1.4 collective-permute-start.50
  200.8 1.4 collective-permute-start.49
  202.3 0.7 collective-permute-start.48
  203.0 1.0 collective-permute-done.41.r1
  204.0 1.8 collective-permute-start.43
  205.8 3.7 %collective-permute-done.42.r2 = bf16[128,768]{1,0:T(8,128)(2,1)S(1)} collective-permute-done((bf16[128,768]{1,0:T(8,128)(2,1)S(1)}, bf16[128,768]{1,0:T(8,128)(2,1)S(1)}, u32[]{:S(2)}, u32[]{:S(2)}) %collective-permute-start.42) | collective-permute-done | bytes 196640 | tf_op jit(solution)/shard_map/ppermute | solution.py:377
  210.1 5.3 %collective-permute-done.49.refs_2_ = bf16[104,768]{1,0:T(8,128)(2,1)S(1)} collective-permute-done((bf16[104,768]{1,0:T(8,128)(2,1)S(1)}, bf16[104,768]{1,0:T(8,128)(2,1)S(1)}, u32[]{:S(2)}, u32[]{:S(2)}) %collective-permute-start.49) | collective-permute-done | bytes 159776 | tf_op jit(solution)/shard_map/ppermute | solution.py:377
  215.9 1.4 shard_map.277
  217.2 3.2 %shard_map.285 = (f32[768,768]{1,0:T(8,128)}, f32[192,3072]{1,0:T(8,128)}) custom-call(s32[3]{0:T(128)S(1)} %pad_add_fusion.pos, bf16[192,768]{1,0:T(8,128)(2,1)S(1)} %shard_map.284.refs_0_, bf16[192,768]{1,0:T(8,128)(2,1)S(1)} %collective-permute-done.55.refs_1_, bf16[192,768]{1,0:T(8,128)(2,1)S(1)} %collective-permute-done.56.refs_2_, ...), custom_call_target="tpu_custom_call" | custom-call | bytes 12000000 | tf_op jit(solution)/shard_map/pallas_call | solution.py:408
  220.5 1.7 shard_map.280
  222.2 2.3 %shard_map.283 = (f32[192,2304]{1,0:T(8,128)}, f32[192,768]{1,0:T(8,128)}, f32[8,192]{1,0:T(8,128)S(1)}, f32[1,768]{1,0:T(1,128)S(1)}) custom-call(s32[3]{0:T(128)S(1)} %pad_add_fusion.pos, bf16[104,768]{1,0:T(8,128)(2,1)S(1)} %shard_map.282.refs_0_, bf16[104,768]{1,0:T(8,128)(2,1)S(1)} %collective-permute-done.48.refs_1_, ...), custom_call_target="tpu_custom_call" | custom-call | bytes 9000000 | tf_op jit(solution)/shard_map/pallas_call | solution.py:408
  (111 shorter events, 23.4 us)
Async XLA Ops:
  0.6 24.0 %copy-start.1 = (bf16[192,768]{1,0:T(8,128)(2,1)S(1)}, bf16[192,768]{1,0:T(8,128)(2,1)}, u32[]{:S(2)}) copy-start(bf16[192,768]{1,0:T(8,128)(2,1)} %param.23) | copy-start | bytes 884740
  9.0 12.0 %collective-permute-start.5 = (bf16[16,256]{1,0:T(8,128)(2,1)S(1)}, bf16[16,256]{1,0:T(8,128)(2,1)S(1)}, u32[]{:S(2)}, u32[]{:S(2)}) collective-permute-start(bf16[16,256]{1,0:T(8,128)(2,1)S(1)} %reshape.33.refs_4_), channel_id=1, source_target_pairs={{0,24},{8,16},{16,8},{24,0},{1,25},{9,17},{17,9},{25,1},{2,26},{10... | collective-permute-start | bytes 24584 | tf_op jit(solution)/shard_map/ppermute | solution.py:381
  14.1 10.6 %collective-permute-start.4 = (bf16[16,256]{1,0:T(8,128)(2,1)S(1)}, bf16[16,256]{1,0:T(8,128)(2,1)S(1)}, u32[]{:S(2)}, u32[]{:S(2)}) collective-permute-start(bf16[16,256]{1,0:T(8,128)(2,1)S(1)} %reshape.33.refs_4_), channel_id=1, source_target_pairs={{0,16},{8,24},{16,0},{24,8},{1,17},{9,25},{17,1},{25,9},{2,18},{10... | collective-permute-start | bytes 24584 | tf_op jit(solution)/shard_map/ppermute | solution.py:381
  14.1 11.5 %collective-permute-start.3 = (bf16[16,256]{1,0:T(8,128)(2,1)S(1)}, bf16[16,256]{1,0:T(8,128)(2,1)S(1)}, u32[]{:S(2)}, u32[]{:S(2)}) collective-permute-start(bf16[16,256]{1,0:T(8,128)(2,1)S(1)} %reshape.33.refs_4_), channel_id=1, source_target_pairs={{0,8},{8,0},{16,24},{24,16},{1,9},{9,1},{17,25},{25,17},{2,10},{10... | collective-permute-start | bytes 24584 | tf_op jit(solution)/shard_map/ppermute | solution.py:381
  16.4 24.5 %collective-permute-start.2 = (bf16[136,768]{1,0:T(8,128)(2,1)S(1)}, bf16[136,768]{1,0:T(8,128)(2,1)S(1)}, u32[]{:S(2)}, u32[]{:S(2)}) collective-permute-start(bf16[136,768]{1,0:T(8,128)(2,1)S(1)} %fusion.1.refs_0_.tok_ref), channel_id=1, source_target_pairs={{0,6},{1,7},{2,4},{3,5},{4,2},{5,3},{6,0},{7,1},{8,14},{9,15},{10,... | collective-permute-start | bytes 626696 | tf_op jit(solution)/shard_map/ppermute | solution.py:377
  19.0 22.3 %collective-permute-start.1 = (bf16[136,768]{1,0:T(8,128)(2,1)S(1)}, bf16[136,768]{1,0:T(8,128)(2,1)S(1)}, u32[]{:S(2)}, u32[]{:S(2)}) collective-permute-start(bf16[136,768]{1,0:T(8,128)(2,1)S(1)} %fusion.1.refs_0_.tok_ref), channel_id=1, source_target_pairs={{0,4},{1,5},{2,6},{3,7},{4,0},{5,1},{6,2},{7,3},{8,12},{9,13},{10,... | collective-permute-start | bytes 626696 | tf_op jit(solution)/shard_map/ppermute | solution.py:377
  21.0 7.1 %collective-permute-start.8 = (bf16[96,576]{1,0:T(8,128)(2,1)S(1)}, bf16[96,576]{1,0:T(8,128)(2,1)S(1)}, u32[]{:S(2)}, u32[]{:S(2)}) collective-permute-start(bf16[96,576]{1,0:T(8,128)(2,1)S(1)} %pad_maximum_fusion.1.refs_8_), channel_id=1, source_target_pairs={{0,24},{8,16},{16,8},{24,0},{1,25},{9,17},{17,9},{25,1},{2,26},{10... | collective-permute-start | bytes 331784 | tf_op jit(solution)/shard_map/ppermute | solution.py:381
  24.7 8.9 %collective-permute-start.7 = (bf16[96,576]{1,0:T(8,128)(2,1)S(1)}, bf16[96,576]{1,0:T(8,128)(2,1)S(1)}, u32[]{:S(2)}, u32[]{:S(2)}) collective-permute-start(bf16[96,576]{1,0:T(8,128)(2,1)S(1)} %pad_maximum_fusion.1.refs_8_), channel_id=1, source_target_pairs={{0,16},{8,24},{16,0},{24,8},{1,17},{9,25},{17,1},{25,9},{2,18},{10... | collective-permute-start | bytes 331784 | tf_op jit(solution)/shard_map/ppermute | solution.py:381
  25.7 15.8 %collective-permute-start = (bf16[136,768]{1,0:T(8,128)(2,1)S(1)}, bf16[136,768]{1,0:T(8,128)(2,1)S(1)}, u32[]{:S(2)}, u32[]{:S(2)}) collective-permute-start(bf16[136,768]{1,0:T(8,128)(2,1)S(1)} %fusion.1.refs_0_.tok_ref), channel_id=1, source_target_pairs={{0,2},{1,3},{2,0},{3,1},{4,6},{5,7},{6,4},{7,5},{8,10},{9,11},{10,... | collective-permute-start | bytes 626696 | tf_op jit(solution)/shard_map/ppermute | solution.py:377
  28.1 12.8 %collective-permute-start.9 = (bf16[96,576]{1,0:T(8,128)(2,1)S(1)}, bf16[96,576]{1,0:T(8,128)(2,1)S(1)}, u32[]{:S(2)}, u32[]{:S(2)}) collective-permute-start(bf16[96,576]{1,0:T(8,128)(2,1)S(1)} %pad_maximum_fusion.1.refs_8_), channel_id=1, source_target_pairs={{0,1},{1,0},{2,3},{3,2},{4,5},{5,4},{6,7},{7,6},{8,9},{9,8},{10,11... | collective-permute-start | bytes 331784 | tf_op jit(solution)/shard_map/ppermute | solution.py:373
  33.6 4.9 %collective-permute-start.6 = (bf16[96,576]{1,0:T(8,128)(2,1)S(1)}, bf16[96,576]{1,0:T(8,128)(2,1)S(1)}, u32[]{:S(2)}, u32[]{:S(2)}) collective-permute-start(bf16[96,576]{1,0:T(8,128)(2,1)S(1)} %pad_maximum_fusion.1.refs_8_), channel_id=1, source_target_pairs={{0,8},{8,0},{16,24},{24,16},{1,9},{9,1},{17,25},{25,17},{2,10},{10... | collective-permute-start | bytes 331784 | tf_op jit(solution)/shard_map/ppermute | solution.py:381
  33.6 13.3 %copy-start = (bf16[1,128,768]{2,1,0:T(8,128)(2,1)S(1)}, bf16[1,128,768]{2,1,0:T(8,128)(2,1)}, u32[]{:S(2)}) copy-start(bf16[1,128,768]{2,1,0:T(8,128)(2,1)} %param.31) | copy-start | bytes 589828
  38.5 14.4 %collective-permute-start.19 = (bf16[288,768]{1,0:T(8,128)(2,1)S(1)}, bf16[288,768]{1,0:T(8,128)(2,1)S(1)}, u32[]{:S(2)}, u32[]{:S(2)}) collective-permute-start(bf16[288,768]{1,0:T(8,128)(2,1)S(1)} %pad_maximum_fusion.refs_8_), channel_id=1, source_target_pairs={{0,24},{8,16},{16,8},{24,0},{1,25},{9,17},{17,9},{25,1},{2,26},{10... | collective-permute-start | bytes 1327112 | tf_op jit(solution)/shard_map/ppermute | solution.py:381
  40.8 1.3 collective-permute-start.12
  40.8 1.5 collective-permute-start.11
  41.4 1.3 collective-permute-start.10
  44.6 9.8 %collective-permute-start.13 = (bf16[520,384]{1,0:T(8,128)(2,1)S(1)}, bf16[520,384]{1,0:T(8,128)(2,1)S(1)}, u32[]{:S(2)}, u32[]{:S(2)}) collective-permute-start(bf16[520,384]{1,0:T(8,128)(2,1)S(1)} %get-tuple-element.82.kva), channel_id=1, source_target_pairs={{0,1},{1,0},{2,3},{3,2},{4,5},{5,4},{6,7},{7,6},{8,9},{9,8},{10,11... | collective-permute-start | bytes 1198088 | tf_op jit(solution)/shard_map/ppermute | solution.py:373
  44.9 32.2 %collective-permute-start.18 = (bf16[288,768]{1,0:T(8,128)(2,1)S(1)}, bf16[288,768]{1,0:T(8,128)(2,1)S(1)}, u32[]{:S(2)}, u32[]{:S(2)}) collective-permute-start(bf16[288,768]{1,0:T(8,128)(2,1)S(1)} %pad_maximum_fusion.refs_8_), channel_id=1, source_target_pairs={{0,16},{8,24},{16,0},{24,8},{1,17},{9,25},{17,1},{25,9},{2,18},{10... | collective-permute-start | bytes 1327112 | tf_op jit(solution)/shard_map/ppermute | solution.py:381
  44.9 33.7 %collective-permute-start.17 = (bf16[288,768]{1,0:T(8,128)(2,1)S(1)}, bf16[288,768]{1,0:T(8,128)(2,1)S(1)}, u32[]{:S(2)}, u32[]{:S(2)}) collective-permute-start(bf16[288,768]{1,0:T(8,128)(2,1)S(1)} %pad_maximum_fusion.refs_8_), channel_id=1, source_target_pairs={{0,8},{8,0},{16,24},{24,16},{1,9},{9,1},{17,25},{25,17},{2,10},{10... | collective-permute-start | bytes 1327112 | tf_op jit(solution)/shard_map/ppermute | solution.py:381
  46.9 31.7 %collective-permute-start.26 = (bf16[128,768]{1,0:T(8,128)(2,1)S(1)}, bf16[128,768]{1,0:T(8,128)(2,1)S(1)}, u32[]{:S(2)}, u32[]{:S(2)}) collective-permute-start(bf16[128,768]{1,0:T(8,128)(2,1)S(1)} %bitcast.13), channel_id=1, source_target_pairs={{0,6},{1,7},{2,4},{3,5},{4,2},{5,3},{6,0},{7,1},{8,14},{9,15},{10,... | collective-permute-start | bytes 589832 | tf_op jit(solution)/shard_map/ppermute | solution.py:377
  52.9 26.2 %collective-permute-start.25 = (bf16[128,768]{1,0:T(8,128)(2,1)S(1)}, bf16[128,768]{1,0:T(8,128)(2,1)S(1)}, u32[]{:S(2)}, u32[]{:S(2)}) collective-permute-start(bf16[128,768]{1,0:T(8,128)(2,1)S(1)} %bitcast.14), channel_id=1, source_target_pairs={{0,4},{1,5},{2,6},{3,7},{4,0},{5,1},{6,2},{7,3},{8,12},{9,13},{10,... | collective-permute-start | bytes 589832 | tf_op jit(solution)/shard_map/ppermute | solution.py:377
  54.4 24.8 %collective-permute-start.24 = (bf16[128,768]{1,0:T(8,128)(2,1)S(1)}, bf16[128,768]{1,0:T(8,128)(2,1)S(1)}, u32[]{:S(2)}, u32[]{:S(2)}) collective-permute-start(bf16[128,768]{1,0:T(8,128)(2,1)S(1)} %bitcast.15), channel_id=1, source_target_pairs={{0,2},{1,3},{2,0},{3,1},{4,6},{5,7},{6,4},{7,5},{8,10},{9,11},{10,... | collective-permute-start | bytes 589832 | tf_op jit(solution)/shard_map/ppermute | solution.py:377
  77.1 7.6 %collective-permute-start.16 = (bf16[512,192]{1,0:T(8,128)(2,1)S(1)}, bf16[512,192]{1,0:T(8,128)(2,1)S(1)}, u32[]{:S(2)}, u32[]{:S(2)}) collective-permute-start(bf16[512,192]{1,0:T(8,128)(2,1)S(1)} %get-tuple-element.83.refs_4_), channel_id=1, source_target_pairs={{0,6},{1,7},{2,4},{3,5},{4,2},{5,3},{6,0},{7,1},{8,14},{9,15},{10,... | collective-permute-start | bytes 589832 | tf_op jit(solution)/shard_map/ppermute | solution.py:377
  78.6 18.8 %collective-permute-start.20 = (bf16[288,768]{1,0:T(8,128)(2,1)S(1)}, bf16[288,768]{1,0:T(8,128)(2,1)S(1)}, u32[]{:S(2)}, u32[]{:S(2)}) collective-permute-start(bf16[288,768]{1,0:T(8,128)(2,1)S(1)} %pad_maximum_fusion.refs_8_), channel_id=1, source_target_pairs={{0,1},{1,0},{2,3},{3,2},{4,5},{5,4},{6,7},{7,6},{8,9},{9,8},{10,11... | collective-permute-start | bytes 1327112 | tf_op jit(solution)/shard_map/ppermute | solution.py:373
  78.6 18.8 %collective-permute-start.21 = (bf16[288,768]{1,0:T(8,128)(2,1)S(1)}, bf16[288,768]{1,0:T(8,128)(2,1)S(1)}, u32[]{:S(2)}, u32[]{:S(2)}) collective-permute-start(bf16[288,768]{1,0:T(8,128)(2,1)S(1)} %collective-permute-done.17.refs_9_), channel_id=1, source_target_pairs={{0,1},{1,0},{2,3},{3,2},{4,5},{5,4},{6,7},{7,6},{8,9},{9,8},{10,11... | collective-permute-start | bytes 1327112 | tf_op jit(solution)/shard_map/ppermute | solution.py:373
  79.1 18.3 %collective-permute-start.22 = (bf16[288,768]{1,0:T(8,128)(2,1)S(1)}, bf16[288,768]{1,0:T(8,128)(2,1)S(1)}, u32[]{:S(2)}, u32[]{:S(2)}) collective-permute-start(bf16[288,768]{1,0:T(8,128)(2,1)S(1)} %collective-permute-done.18.refs_10_), channel_id=1, source_target_pairs={{0,1},{1,0},{2,3},{3,2},{4,5},{5,4},{6,7},{7,6},{8,9},{9,8},{10,11... | collective-permute-start | bytes 1327112 | tf_op jit(solution)/shard_map/ppermute | solution.py:373
  79.2 18.3 %collective-permute-start.23 = (bf16[288,768]{1,0:T(8,128)(2,1)S(1)}, bf16[288,768]{1,0:T(8,128)(2,1)S(1)}, u32[]{:S(2)}, u32[]{:S(2)}) collective-permute-start(bf16[288,768]{1,0:T(8,128)(2,1)S(1)} %collective-permute-done.19.refs_11_), channel_id=1, source_target_pairs={{0,1},{1,0},{2,3},{3,2},{4,5},{5,4},{6,7},{7,6},{8,9},{9,8},{10,11... | collective-permute-start | bytes 1327112 | tf_op jit(solution)/shard_map/ppermute | solution.py:373
  84.7 6.4 %collective-permute-start.15 = (bf16[512,192]{1,0:T(8,128)(2,1)S(1)}, bf16[512,192]{1,0:T(8,128)(2,1)S(1)}, u32[]{:S(2)}, u32[]{:S(2)}) collective-permute-start(bf16[512,192]{1,0:T(8,128)(2,1)S(1)} %get-tuple-element.83.refs_4_), channel_id=1, source_target_pairs={{0,4},{1,5},{2,6},{3,7},{4,0},{5,1},{6,2},{7,3},{8,12},{9,13},{10,... | collective-permute-start | bytes 589832 | tf_op jit(solution)/shard_map/ppermute | solution.py:377
  91.1 6.4 %collective-permute-start.14 = (bf16[512,192]{1,0:T(8,128)(2,1)S(1)}, bf16[512,192]{1,0:T(8,128)(2,1)S(1)}, u32[]{:S(2)}, u32[]{:S(2)}) collective-permute-start(bf16[512,192]{1,0:T(8,128)(2,1)S(1)} %get-tuple-element.83.refs_4_), channel_id=1, source_target_pairs={{0,2},{1,3},{2,0},{3,1},{4,6},{5,7},{6,4},{7,5},{8,10},{9,11},{10,... | collective-permute-start | bytes 589832 | tf_op jit(solution)/shard_map/ppermute | solution.py:377
  105.4 15.3 %collective-permute-start.33 = (bf16[4,192,768]{2,1,0:T(8,128)(2,1)S(1)}, bf16[4,192,768]{2,1,0:T(8,128)(2,1)S(1)}, u32[]{:S(2)}, u32[]{:S(2)}) collective-permute-start(bf16[4,192,768]{2,1,0:T(8,128)(2,1)S(1)} %get-tuple-element.103), channel_id=1, source_target_pairs={{0,1},{1,0},{2,3},{3,2},{4,5},{5,4},{6,7},{7,6},{8,9},{9,8},{10,11... | collective-permute-start | bytes 3538952 | tf_op jit(solution)/shard_map/ppermute | solution.py:373
  105.5 7.8 %collective-permute-start.27 = (bf16[128,768]{1,0:T(8,128)(2,1)S(1)}, bf16[128,768]{1,0:T(8,128)(2,1)S(1)}, u32[]{:S(2)}, u32[]{:S(2)}) collective-permute-start(bf16[128,768]{1,0:T(8,128)(2,1)S(1)} %get-tuple-element.94), channel_id=1, source_target_pairs={{0,2},{1,3},{2,0},{3,1},{4,6},{5,7},{6,4},{7,5},{8,10},{9,11},{10,... | collective-permute-start | bytes 589832 | tf_op jit(solution)/shard_map/ppermute | solution.py:377
  106.1 10.2 %collective-permute-start.28 = (bf16[128,768]{1,0:T(8,128)(2,1)S(1)}, bf16[128,768]{1,0:T(8,128)(2,1)S(1)}, u32[]{:S(2)}, u32[]{:S(2)}) collective-permute-start(bf16[128,768]{1,0:T(8,128)(2,1)S(1)} %get-tuple-element.95), channel_id=1, source_target_pairs={{0,4},{1,5},{2,6},{3,7},{4,0},{5,1},{6,2},{7,3},{8,12},{9,13},{10,... | collective-permute-start | bytes 589832 | tf_op jit(solution)/shard_map/ppermute | solution.py:377
  107.6 10.4 %collective-permute-start.29 = (bf16[128,768]{1,0:T(8,128)(2,1)S(1)}, bf16[128,768]{1,0:T(8,128)(2,1)S(1)}, u32[]{:S(2)}, u32[]{:S(2)}) collective-permute-start(bf16[128,768]{1,0:T(8,128)(2,1)S(1)} %get-tuple-element.96), channel_id=1, source_target_pairs={{0,6},{1,7},{2,4},{3,5},{4,2},{5,3},{6,0},{7,1},{8,14},{9,15},{10,... | collective-permute-start | bytes 589832 | tf_op jit(solution)/shard_map/ppermute | solution.py:377
  118.9 8.2 %collective-permute-start.32 = (bf16[128,768]{1,0:T(8,128)(2,1)S(1)}, bf16[128,768]{1,0:T(8,128)(2,1)S(1)}, u32[]{:S(2)}, u32[]{:S(2)}) collective-permute-start(bf16[128,768]{1,0:T(8,128)(2,1)S(1)} %get-tuple-element.111.a0.refs_8_), channel_id=1, source_target_pairs={{0,6},{1,7},{2,4},{3,5},{4,2},{5,3},{6,0},{7,1},{8,14},{9,15},{10,... | collective-permute-start | bytes 589832 | tf_op jit(solution)/shard_map/ppermute | solution.py:377
  121.5 18.3 %collective-permute-start.37 = (bf16[192,768]{1,0:T(8,128)(2,1)S(1)}, bf16[192,768]{1,0:T(8,128)(2,1)S(1)}, u32[]{:S(2)}, u32[]{:S(2)}) collective-permute-start(bf16[192,768]{1,0:T(8,128)(2,1)S(1)} %get-tuple-element.120), channel_id=1, source_target_pairs={{0,8},{8,0},{16,24},{24,16},{1,9},{9,1},{17,25},{25,17},{2,10},{10... | collective-permute-start | bytes 884744 | tf_op jit(solution)/shard_map/ppermute | solution.py:381
  123.3 23.9 %collective-permute-start.38 = (bf16[192,768]{1,0:T(8,128)(2,1)S(1)}, bf16[192,768]{1,0:T(8,128)(2,1)S(1)}, u32[]{:S(2)}, u32[]{:S(2)}) collective-permute-start(bf16[192,768]{1,0:T(8,128)(2,1)S(1)} %get-tuple-element.121), channel_id=1, source_target_pairs={{0,16},{8,24},{16,0},{24,8},{1,17},{9,25},{17,1},{25,9},{2,18},{10... | collective-permute-start | bytes 884744 | tf_op jit(solution)/shard_map/ppermute | solution.py:381
  126.7 20.6 %collective-permute-start.39 = (bf16[192,768]{1,0:T(8,128)(2,1)S(1)}, bf16[192,768]{1,0:T(8,128)(2,1)S(1)}, u32[]{:S(2)}, u32[]{:S(2)}) collective-permute-start(bf16[192,768]{1,0:T(8,128)(2,1)S(1)} %get-tuple-element.122), channel_id=1, source_target_pairs={{0,24},{8,16},{16,8},{24,0},{1,25},{9,17},{17,9},{25,1},{2,26},{10... | collective-permute-start | bytes 884744 | tf_op jit(solution)/shard_map/ppermute | solution.py:381
  126.7 5.7 %collective-permute-start.31 = (bf16[128,768]{1,0:T(8,128)(2,1)S(1)}, bf16[128,768]{1,0:T(8,128)(2,1)S(1)}, u32[]{:S(2)}, u32[]{:S(2)}) collective-permute-start(bf16[128,768]{1,0:T(8,128)(2,1)S(1)} %get-tuple-element.111.a0.refs_8_), channel_id=1, source_target_pairs={{0,4},{1,5},{2,6},{3,7},{4,0},{5,1},{6,2},{7,3},{8,12},{9,13},{10,... | collective-permute-start | bytes 589832 | tf_op jit(solution)/shard_map/ppermute | solution.py:377
  127.2 5.7 %collective-permute-start.30 = (bf16[128,768]{1,0:T(8,128)(2,1)S(1)}, bf16[128,768]{1,0:T(8,128)(2,1)S(1)}, u32[]{:S(2)}, u32[]{:S(2)}) collective-permute-start(bf16[128,768]{1,0:T(8,128)(2,1)S(1)} %get-tuple-element.111.a0.refs_8_), channel_id=1, source_target_pairs={{0,2},{1,3},{2,0},{3,1},{4,6},{5,7},{6,4},{7,5},{8,10},{9,11},{10,... | collective-permute-start | bytes 589832 | tf_op jit(solution)/shard_map/ppermute | solution.py:377
  147.2 1.7 collective-permute-start.40
  152.3 16.3 %collective-permute-start.44 = (bf16[4,96,768]{2,1,0:T(8,128)(2,1)S(1)}, bf16[4,96,768]{2,1,0:T(8,128)(2,1)S(1)}, u32[]{:S(2)}, u32[]{:S(2)}) collective-permute-start(bf16[4,96,768]{2,1,0:T(8,128)(2,1)S(1)} %get-tuple-element.132), channel_id=1, source_target_pairs={{0,1},{1,0},{2,3},{3,2},{4,5},{5,4},{6,7},{7,6},{8,9},{9,8},{10,11... | collective-permute-start | bytes 1769480 | tf_op jit(solution)/shard_map/ppermute | solution.py:373
  152.5 7.7 %collective-permute-start.34 = (bf16[128,768]{1,0:T(8,128)(2,1)S(1)}, bf16[128,768]{1,0:T(8,128)(2,1)S(1)}, u32[]{:S(2)}, u32[]{:S(2)}) collective-permute-start(bf16[128,768]{1,0:T(8,128)(2,1)S(1)} %get-tuple-element.106), channel_id=1, source_target_pairs={{0,2},{1,3},{2,0},{3,1},{4,6},{5,7},{6,4},{7,5},{8,10},{9,11},{10,... | collective-permute-start | bytes 589832 | tf_op jit(solution)/shard_map/ppermute | solution.py:377
  153.1 14.1 %collective-permute-start.35 = (bf16[128,768]{1,0:T(8,128)(2,1)S(1)}, bf16[128,768]{1,0:T(8,128)(2,1)S(1)}, u32[]{:S(2)}, u32[]{:S(2)}) collective-permute-start(bf16[128,768]{1,0:T(8,128)(2,1)S(1)} %get-tuple-element.108), channel_id=1, source_target_pairs={{0,4},{1,5},{2,6},{3,7},{4,0},{5,1},{6,2},{7,3},{8,12},{9,13},{10,... | collective-permute-start | bytes 589832 | tf_op jit(solution)/shard_map/ppermute | solution.py:377
  155.0 26.6 %collective-permute-start.57 = (bf16[192,768]{1,0:T(8,128)(2,1)S(1)}, bf16[192,768]{1,0:T(8,128)(2,1)S(1)}, u32[]{:S(2)}, u32[]{:S(2)}) collective-permute-start(bf16[192,768]{1,0:T(8,128)(2,1)S(1)} %shard_map.284.refs_0_), channel_id=1, source_target_pairs={{0,6},{1,7},{2,4},{3,5},{4,2},{5,3},{6,0},{7,1},{8,14},{9,15},{10,... | collective-permute-start | bytes 884744 | tf_op jit(solution)/shard_map/ppermute | solution.py:377
  156.7 24.9 %collective-permute-start.56 = (bf16[192,768]{1,0:T(8,128)(2,1)S(1)}, bf16[192,768]{1,0:T(8,128)(2,1)S(1)}, u32[]{:S(2)}, u32[]{:S(2)}) collective-permute-start(bf16[192,768]{1,0:T(8,128)(2,1)S(1)} %shard_map.284.refs_0_), channel_id=1, source_target_pairs={{0,4},{1,5},{2,6},{3,7},{4,0},{5,1},{6,2},{7,3},{8,12},{9,13},{10,... | collective-permute-start | bytes 884744 | tf_op jit(solution)/shard_map/ppermute | solution.py:377
  160.2 22.0 %collective-permute-start.55 = (bf16[192,768]{1,0:T(8,128)(2,1)S(1)}, bf16[192,768]{1,0:T(8,128)(2,1)S(1)}, u32[]{:S(2)}, u32[]{:S(2)}) collective-permute-start(bf16[192,768]{1,0:T(8,128)(2,1)S(1)} %shard_map.284.refs_0_), channel_id=1, source_target_pairs={{0,2},{1,3},{2,0},{3,1},{4,6},{5,7},{6,4},{7,5},{8,10},{9,11},{10,... | collective-permute-start | bytes 884744 | tf_op jit(solution)/shard_map/ppermute | solution.py:377
  167.2 9.4 %collective-permute-start.36 = (bf16[128,768]{1,0:T(8,128)(2,1)S(1)}, bf16[128,768]{1,0:T(8,128)(2,1)S(1)}, u32[]{:S(2)}, u32[]{:S(2)}) collective-permute-start(bf16[128,768]{1,0:T(8,128)(2,1)S(1)} %get-tuple-element.110), channel_id=1, source_target_pairs={{0,6},{1,7},{2,4},{3,5},{4,2},{5,3},{6,0},{7,1},{8,14},{9,15},{10,... | collective-permute-start | bytes 589832 | tf_op jit(solution)/shard_map/ppermute | solution.py:377
  168.5 13.7 %collective-permute-start.58 = (bf16[192,768]{1,0:T(8,128)(2,1)S(1)}, bf16[192,768]{1,0:T(8,128)(2,1)S(1)}, u32[]{:S(2)}, u32[]{:S(2)}) collective-permute-start(bf16[192,768]{1,0:T(8,128)(2,1)S(1)} %shard_map.284.refs_0_), channel_id=1, source_target_pairs={{0,1},{1,0},{2,3},{3,2},{4,5},{5,4},{6,7},{7,6},{8,9},{9,8},{10,11... | collective-permute-start | bytes 884744 | tf_op jit(solution)/shard_map/ppermute | solution.py:373
  176.6 9.0 %collective-permute-start.45 = (bf16[104,768]{1,0:T(8,128)(2,1)S(1)}, bf16[104,768]{1,0:T(8,128)(2,1)S(1)}, u32[]{:S(2)}, u32[]{:S(2)}) collective-permute-start(bf16[104,768]{1,0:T(8,128)(2,1)S(1)} %get-tuple-element.134), channel_id=1, source_target_pairs={{0,8},{8,0},{16,24},{24,16},{1,9},{9,1},{17,25},{25,17},{2,10},{10... | collective-permute-start | bytes 479240 | tf_op jit(solution)/shard_map/ppermute | solution.py:381
  181.6 17.8 %collective-permute-start.61 = (bf16[192,768]{1,0:T(8,128)(2,1)S(1)}, bf16[192,768]{1,0:T(8,128)(2,1)S(1)}, u32[]{:S(2)}, u32[]{:S(2)}) collective-permute-start(bf16[192,768]{1,0:T(8,128)(2,1)S(1)} %collective-permute-done.57.refs_3_), channel_id=1, source_target_pairs={{0,1},{1,0},{2,3},{3,2},{4,5},{5,4},{6,7},{7,6},{8,9},{9,8},{10,11... | collective-permute-start | bytes 884744 | tf_op jit(solution)/shard_map/ppermute | solution.py:373
  181.7 19.2 %collective-permute-start.60 = (bf16[192,768]{1,0:T(8,128)(2,1)S(1)}, bf16[192,768]{1,0:T(8,128)(2,1)S(1)}, u32[]{:S(2)}, u32[]{:S(2)}) collective-permute-start(bf16[192,768]{1,0:T(8,128)(2,1)S(1)} %collective-permute-done.56.refs_2_), channel_id=1, source_target_pairs={{0,1},{1,0},{2,3},{3,2},{4,5},{5,4},{6,7},{7,6},{8,9},{9,8},{10,11... | collective-permute-start | bytes 884744 | tf_op jit(solution)/shard_map/ppermute | solution.py:373
  182.2 20.1 %collective-permute-start.59 = (bf16[192,768]{1,0:T(8,128)(2,1)S(1)}, bf16[192,768]{1,0:T(8,128)(2,1)S(1)}, u32[]{:S(2)}, u32[]{:S(2)}) collective-permute-start(bf16[192,768]{1,0:T(8,128)(2,1)S(1)} %collective-permute-done.55.refs_1_), channel_id=1, source_target_pairs={{0,1},{1,0},{2,3},{3,2},{4,5},{5,4},{6,7},{7,6},{8,9},{9,8},{10,11... | collective-permute-start | bytes 884744 | tf_op jit(solution)/shard_map/ppermute | solution.py:373
  182.2 14.4 %collective-permute-start.46 = (bf16[104,768]{1,0:T(8,128)(2,1)S(1)}, bf16[104,768]{1,0:T(8,128)(2,1)S(1)}, u32[]{:S(2)}, u32[]{:S(2)}) collective-permute-start(bf16[104,768]{1,0:T(8,128)(2,1)S(1)} %get-tuple-element.135), channel_id=1, source_target_pairs={{0,16},{8,24},{16,0},{24,8},{1,17},{9,25},{17,1},{25,9},{2,18},{10... | collective-permute-start | bytes 479240 | tf_op jit(solution)/shard_map/ppermute | solution.py:381
  185.6 12.6 %collective-permute-start.47 = (bf16[104,768]{1,0:T(8,128)(2,1)S(1)}, bf16[104,768]{1,0:T(8,128)(2,1)S(1)}, u32[]{:S(2)}, u32[]{:S(2)}) collective-permute-start(bf16[104,768]{1,0:T(8,128)(2,1)S(1)} %get-tuple-element.136), channel_id=1, source_target_pairs={{0,24},{8,16},{16,8},{24,0},{1,25},{9,17},{17,9},{25,1},{2,26},{10... | collective-permute-start | bytes 479240 | tf_op jit(solution)/shard_map/ppermute | solution.py:381
  196.6 7.4 %collective-permute-start.41 = (bf16[128,768]{1,0:T(8,128)(2,1)S(1)}, bf16[128,768]{1,0:T(8,128)(2,1)S(1)}, u32[]{:S(2)}, u32[]{:S(2)}) collective-permute-start(bf16[128,768]{1,0:T(8,128)(2,1)S(1)} %get-tuple-element.127), channel_id=1, source_target_pairs={{0,2},{1,3},{2,0},{3,1},{4,6},{5,7},{6,4},{7,5},{8,10},{9,11},{10,... | collective-permute-start | bytes 589832 | tf_op jit(solution)/shard_map/ppermute | solution.py:377
  198.2 11.4 %collective-permute-start.42 = (bf16[128,768]{1,0:T(8,128)(2,1)S(1)}, bf16[128,768]{1,0:T(8,128)(2,1)S(1)}, u32[]{:S(2)}, u32[]{:S(2)}) collective-permute-start(bf16[128,768]{1,0:T(8,128)(2,1)S(1)} %get-tuple-element.128), channel_id=1, source_target_pairs={{0,4},{1,5},{2,6},{3,7},{4,0},{5,1},{6,2},{7,3},{8,12},{9,13},{10,... | collective-permute-start | bytes 589832 | tf_op jit(solution)/shard_map/ppermute | solution.py:377
  199.4 10.2 %collective-permute-start.50 = (bf16[104,768]{1,0:T(8,128)(2,1)S(1)}, bf16[104,768]{1,0:T(8,128)(2,1)S(1)}, u32[]{:S(2)}, u32[]{:S(2)}) collective-permute-start(bf16[104,768]{1,0:T(8,128)(2,1)S(1)} %shard_map.282.refs_0_), channel_id=1, source_target_pairs={{0,6},{1,7},{2,4},{3,5},{4,2},{5,3},{6,0},{7,1},{8,14},{9,15},{10,... | collective-permute-start | bytes 479240 | tf_op jit(solution)/shard_map/ppermute | solution.py:377
  200.8 14.5 %collective-permute-start.49 = (bf16[104,768]{1,0:T(8,128)(2,1)S(1)}, bf16[104,768]{1,0:T(8,128)(2,1)S(1)}, u32[]{:S(2)}, u32[]{:S(2)}) collective-permute-start(bf16[104,768]{1,0:T(8,128)(2,1)S(1)} %shard_map.282.refs_0_), channel_id=1, source_target_pairs={{0,4},{1,5},{2,6},{3,7},{4,0},{5,1},{6,2},{7,3},{8,12},{9,13},{10,... | collective-permute-start | bytes 479240 | tf_op jit(solution)/shard_map/ppermute | solution.py:377
  202.3 13.1 %collective-permute-start.48 = (bf16[104,768]{1,0:T(8,128)(2,1)S(1)}, bf16[104,768]{1,0:T(8,128)(2,1)S(1)}, u32[]{:S(2)}, u32[]{:S(2)}) collective-permute-start(bf16[104,768]{1,0:T(8,128)(2,1)S(1)} %shard_map.282.refs_0_), channel_id=1, source_target_pairs={{0,2},{1,3},{2,0},{3,1},{4,6},{5,7},{6,4},{7,5},{8,10},{9,11},{10,... | collective-permute-start | bytes 479240 | tf_op jit(solution)/shard_map/ppermute | solution.py:377
  204.0 16.5 %collective-permute-start.43 = (bf16[128,768]{1,0:T(8,128)(2,1)S(1)}, bf16[128,768]{1,0:T(8,128)(2,1)S(1)}, u32[]{:S(2)}, u32[]{:S(2)}) collective-permute-start(bf16[128,768]{1,0:T(8,128)(2,1)S(1)} %get-tuple-element.129), channel_id=1, source_target_pairs={{0,6},{1,7},{2,4},{3,5},{4,2},{5,3},{6,0},{7,1},{8,14},{9,15},{10,... | collective-permute-start | bytes 589832 | tf_op jit(solution)/shard_map/ppermute | solution.py:377
  209.6 12.6 %collective-permute-start.51 = (bf16[104,768]{1,0:T(8,128)(2,1)S(1)}, bf16[104,768]{1,0:T(8,128)(2,1)S(1)}, u32[]{:S(2)}, u32[]{:S(2)}) collective-permute-start(bf16[104,768]{1,0:T(8,128)(2,1)S(1)} %shard_map.282.refs_0_), channel_id=1, source_target_pairs={{0,1},{1,0},{2,3},{3,2},{4,5},{5,4},{6,7},{7,6},{8,9},{9,8},{10,11... | collective-permute-start | bytes 479240 | tf_op jit(solution)/shard_map/ppermute | solution.py:373
  209.6 12.6 %collective-permute-start.54 = (bf16[104,768]{1,0:T(8,128)(2,1)S(1)}, bf16[104,768]{1,0:T(8,128)(2,1)S(1)}, u32[]{:S(2)}, u32[]{:S(2)}) collective-permute-start(bf16[104,768]{1,0:T(8,128)(2,1)S(1)} %collective-permute-done.50.refs_3_), channel_id=1, source_target_pairs={{0,1},{1,0},{2,3},{3,2},{4,5},{5,4},{6,7},{7,6},{8,9},{9,8},{10,11... | collective-permute-start | bytes 479240 | tf_op jit(solution)/shard_map/ppermute | solution.py:373
  215.4 6.8 %collective-permute-start.53 = (bf16[104,768]{1,0:T(8,128)(2,1)S(1)}, bf16[104,768]{1,0:T(8,128)(2,1)S(1)}, u32[]{:S(2)}, u32[]{:S(2)}) collective-permute-start(bf16[104,768]{1,0:T(8,128)(2,1)S(1)} %collective-permute-done.49.refs_2_), channel_id=1, source_target_pairs={{0,1},{1,0},{2,3},{3,2},{4,5},{5,4},{6,7},{7,6},{8,9},{9,8},{10,11... | collective-permute-start | bytes 479240 | tf_op jit(solution)/shard_map/ppermute | solution.py:373
  215.4 6.8 %collective-permute-start.52 = (bf16[104,768]{1,0:T(8,128)(2,1)S(1)}, bf16[104,768]{1,0:T(8,128)(2,1)S(1)}, u32[]{:S(2)}, u32[]{:S(2)}) collective-permute-start(bf16[104,768]{1,0:T(8,128)(2,1)S(1)} %collective-permute-done.48.refs_1_), channel_id=1, source_target_pairs={{0,1},{1,0},{2,3},{3,2},{4,5},{5,4},{6,7},{7,6},{8,9},{9,8},{10,11... | collective-permute-start | bytes 479240 | tf_op jit(solution)/shard_map/ppermute | solution.py:373

commit v3 on v2

--- a/solution.py
+++ b/solution.py
@@ -393,27 +393,22 @@
     return lax.optimization_barrier((values, *earlier))[0]
 
 
-def column_slice(values, k, parts):
-    return jnp.concatenate(
-        [
-            lax.dynamic_slice_in_dim(values, WIDTH * p + QUARTER * k, QUARTER, 1)
-            for p in range(parts)
-        ],
-        1,
-    )
-
-
-def run(body, pos, args, outs, scratch=(), flops=0, us=2.0, limit=40):
+def run(body, pos, args, outs, scratch=(), hbm=(), sems=0, limit=24, cost=0.001):
     vmem = pl.BlockSpec(memory_space=pltpu.VMEM)
+    whole = pl.BlockSpec(memory_space=pl.ANY)
+    scratch_shapes = [pltpu.VMEM(shape, kind) for shape, kind in scratch]
+    if sems:
+        scratch_shapes.append(pltpu.SemaphoreType.DMA((sems,)))
     return pl.pallas_call(
         body,
         out_shape=[jax.ShapeDtypeStruct(shape, kind) for shape, kind in outs],
-        in_specs=[pl.BlockSpec(memory_space=pltpu.SMEM)] + [vmem] * len(args),
+        in_specs=[pl.BlockSpec(memory_space=pltpu.SMEM)]
+        + [whole if n in hbm else vmem for n in range(len(args))],
         out_specs=[vmem] * len(outs),
-        scratch_shapes=[pltpu.VMEM(shape, kind) for shape, kind in scratch],
+        scratch_shapes=scratch_shapes,
         compiler_params=pltpu.CompilerParams(vmem_limit_bytes=limit << 20),
         cost_estimate=pl.CostEstimate(
-            flops=flops, bytes_accessed=int(us * 3.0e6), transcendentals=0
+            flops=int(cost * 524288000), bytes_accessed=1000, transcendentals=1
         ),
     )(pos, *args)
 
@@ -445,24 +440,100 @@
     )
 
 
+def pack_body(pos, w_ref, tok_ref, cot_ref, ids_ref, *refs):
+    small, up_ref = refs[:8], refs[8]
+    piece_ref, mate_ref, pack_ref, w_rows, sem = refs[9:]
+    k, c = pos[1], pos[2]
+    copies = []
+    for n, half in enumerate((c, 1 - c)):
+        rows = pl.ds(pl.multiple_of(half * HALF, 32), HALF)
+        copies.append(pltpu.make_async_copy(w_ref.at[rows, :], w_rows.at[n], sem.at[n]))
+    copies += [
+        pltpu.make_async_copy(tok_ref.at[0], pack_ref.at[pl.ds(0, ROWS), :], sem.at[2]),
+        pltpu.make_async_copy(cot_ref.at[0], pack_ref.at[pl.ds(ROWS, ROWS), :], sem.at[3]),
+    ]
+    for copy in copies:
+        copy.start()
+    up = up_ref[...].astype(f32).reshape(1, WIDTH)
+    part = jnp.zeros((1, QUARTER), f32)
+    for q in range(4):
+        part = jnp.where(k == q, up[:, QUARTER * q : QUARTER * (q + 1)], part)
+    vecs = [ref[...].astype(f32).reshape(1, QUARTER) for ref in small] + [part]
+    lines = [jnp.concatenate(vecs[3 * n : 3 * n + 3], 1) for n in range(3)]
+    lines = jnp.concatenate(lines + [jnp.zeros((13, 3 * QUARTER), f32)], 0)
+    piece_ref[HALF:, :] = lines.astype(bf16)
+    ids = jnp.concatenate([ids_ref[...].astype(f32), jnp.zeros((1, WIDTH - ROWS), f32)], 1)
+    pack_ref[2 * ROWS :, :] = jnp.concatenate([ids, jnp.zeros((7, WIDTH), f32)], 0).astype(bf16)
+    copies[0].wait()
+    copies[1].wait()
+    for q in range(4):
+
+        @pl.when(k == q)
+        def _():
+            for p in range(3):
+                at = WIDTH * p + QUARTER * q
+                cols = slice(QUARTER * p, QUARTER * (p + 1))
+                piece_ref[:HALF, cols] = w_rows[0, :, at : at + QUARTER]
+                mate_ref[:HALF, cols] = w_rows[1, :, at : at + QUARTER]
+
+    copies[2].wait()
+    copies[3].wait()
+
+
+def rest_body(pos, wo_ref, wu_ref, wd_ref, out_ref, mate_ref, up_rows, sem):
+    k, c = pos[1], pos[2]
+    copies = []
+    for n, (half, dst) in enumerate(((c, out_ref), (1 - c, mate_ref))):
+        rows = pl.ds(pl.multiple_of(half * HALF, 32), HALF)
+        down_rows = pl.ds(pl.multiple_of(k * QUARTER + half * HALF, 32), HALF)
+        copies += [
+            pltpu.make_async_copy(wu_ref.at[rows, :], up_rows.at[n], sem.at[3 * n]),
+            pltpu.make_async_copy(wo_ref.at[rows, :], dst.at[pl.ds(0, HALF), :], sem.at[3 * n + 1]),
+            pltpu.make_async_copy(
+                wd_ref.at[down_rows, :], dst.at[pl.ds(2 * HALF, HALF), :], sem.at[3 * n + 2]
+            ),
+        ]
+    for copy in copies:
+        copy.start()
+    copies[0].wait()
+    copies[3].wait()
+    for q in range(4):
+
+        @pl.when(k == q)
+        def _():
+            for p in range(4):
+                at = WIDTH * p + QUARTER * q
+                cols = slice(QUARTER * p, QUARTER * (p + 1))
+                out_ref[HALF : 2 * HALF, cols] = up_rows[0, :, at : at + QUARTER]
+                mate_ref[HALF : 2 * HALF, cols] = up_rows[1, :, at : at + QUARTER]
+
+    for n in (1, 2, 4, 5):
+        copies[n].wait()
+
+
 def qkv_body(pos, *refs):
-    tok, small, own, oth = refs[0:4], refs[4:8], refs[8:12], refs[12:16]
-    q_ref, kv_ref, normed_ref, vec_ref, w_ref, sm = refs[16:]
+    tok, own, oth = refs[0:4], refs[4:8], refs[8:12]
+    q_ref, k0, k1, v0, v1, normed_ref, vec_ref, w_ref, sm = refs[12:]
     s, k, c = pos[0], pos[1], pos[2]
     for m in range(4):
         z = s ^ m
-        w_ref[pl.ds(pl.multiple_of(z * QUARTER + c * HALF, 32), HALF), :] = own[m][...]
-        w_ref[pl.ds(pl.multiple_of(z * QUARTER + (1 - c) * HALF, 32), HALF), :] = oth[m][...]
-        sm[z] = small[m][...].astype(f32)
+        at = pl.ds(pl.multiple_of(z * QUARTER + c * HALF, 32), HALF)
+        w_ref[at, :] = own[m][:HALF, :]
+        at = pl.ds(pl.multiple_of(z * QUARTER + (1 - c) * HALF, 32), HALF)
+        w_ref[at, :] = oth[m][:HALF, :]
+        sm[z] = own[m][HALF:, :].astype(f32)
+
+    def seg(z, n):
+        return sm[z, n // 3 : n // 3 + 1, QUARTER * (n % 3) : QUARTER * (n % 3 + 1)]
 
     def vec(n):
-        return jnp.concatenate([sm[z, n : n + 1, :QUARTER] for z in range(4)], 1)
+        return jnp.concatenate([seg(z, n) for z in range(4)], 1)
+
+    def chip_seg(n):
+        return seg(k, n)
 
     gain, shift = vec(0), vec(1)
-    own_small = sm[k]
-    bias = jnp.concatenate(
-        [own_small[2:3, :QUARTER], jnp.zeros((1, QUARTER), f32), own_small[3:4, :QUARTER]], 1
-    )
+    bias = jnp.concatenate([chip_seg(2), jnp.zeros((1, QUARTER), f32), chip_seg(3)], 1)
     vec_ref[...] = jnp.concatenate(
         [gain, shift, vec(4), vec(5), vec(6), vec(7), vec(8), jnp.zeros((1, WIDTH), f32)], 0
     )
@@ -471,23 +542,37 @@
         normed_ref[ROWS * r : ROWS * (r + 1), :] = (hat * gain + shift).astype(bf16)
     projected = dot(normed_ref[...], w_ref[...]) + bias
     q_ref[...] = (projected[:, :QUARTER].astype(bf16).astype(f32) * 0.125).astype(bf16)
-    kv_ref[:OWN, :] = projected[:, QUARTER:].astype(bf16)
-    ids = [tok[r][ROWS : ROWS + 8, :ROWS].astype(f32)[:1] for r in range(4)]
+    k0[: OWN // 2, :] = projected[: OWN // 2, QUARTER : 2 * QUARTER].astype(bf16)
+    k1[...] = projected[OWN // 2 :, QUARTER : 2 * QUARTER].astype(bf16)
+    v0[...] = projected[: OWN // 2, 2 * QUARTER :].astype(bf16)
+    v1[...] = projected[OWN // 2 :, 2 * QUARTER :].astype(bf16)
+    ids = [tok[r][2 * ROWS :, :ROWS].astype(f32)[:1] for r in range(4)]
     ids = jnp.concatenate(ids + [jnp.zeros((4, ROWS), f32)], 0).astype(bf16)
-    kv_ref[OWN:, :] = jnp.concatenate([ids, jnp.zeros((8, 2 * QUARTER - ROWS), bf16)], 1)
+    k0[OWN // 2 :, :] = jnp.concatenate([ids, jnp.zeros((8, QUARTER - ROWS), bf16)], 1)
 
 
 def split_ids(kva, kvb):
-    ids_a = kva[OWN:, :ROWS].astype(f32)
-    ids_b = kvb[OWN:, :ROWS].astype(f32)
+    ids_a = kva[OWN // 2 :, :ROWS].astype(f32)
+    ids_b = kvb[OWN // 2 :, :ROWS].astype(f32)
     keys = jnp.concatenate(
         [ids_a[r : r + 1] for r in range(4)] + [ids_b[r : r + 1] for r in range(4)], 1
     )
     return ids_a.T, keys
 
 
-def attend_body(pos, q_ref, kva, kvb, mixed_ref, state_ref):
-    cols, keys = split_ids(kva, kvb)
+def all_keys(pair, key_ref, value_ref):
+    half = OWN // 2
+    for n in range(2):
+        key_ref[OWN * n : OWN * n + half, :] = pair[4 * n][:half, :]
+        key_ref[OWN * n + half : OWN * (n + 1), :] = pair[4 * n + 1][...]
+        value_ref[OWN * n : OWN * n + half, :] = pair[4 * n + 2][...]
+        value_ref[OWN * n + half : OWN * (n + 1), :] = pair[4 * n + 3][...]
+
+
+def attend_body(pos, q_ref, *refs):
+    pair, (mixed_ref, state_ref, key_ref, value_ref) = refs[:8], refs[8:]
+    cols, keys = split_ids(pair[0], pair[4])
+    all_keys(pair, key_ref, value_ref)
     lane = lax.broadcasted_iota(jnp.int32, (ROWS, 64), 1)
     for r in range(4):
         rows = slice(ROWS * r, ROWS * (r + 1))
@@ -495,17 +580,14 @@
         heads, lse = [], jnp.zeros((ROWS, 64), f32)
         for h in range(3):
             at = slice(64 * h, 64 * h + 64)
-            at_v = slice(QUARTER + 64 * h, QUARTER + 64 * h + 64)
             query = q_ref[rows, at]
-            scores = jnp.concatenate(
-                [dot_t(query, kva[:OWN, at]), dot_t(query, kvb[:OWN, at])], 1
-            )
+            scores = dot_t(query, key_ref[:, at])
             scores = jnp.where(hidden, NEGATIVE, scores)
             top = jnp.max(scores, -1, keepdims=True)
             weights = jnp.exp(scores - top)
             total = jnp.sum(weights, -1, keepdims=True)
             low = weights.astype(bf16)
-            out = dot(low[:, :OWN], kva[:OWN, at_v]) + dot(low[:, OWN:], kvb[:OWN, at_v])
+            out = dot(low, value_ref[:, at])
             heads.append(out * (1.0 / total))
             lse = jnp.where(lane == h, top + jnp.log(total), lse)
         mixed = jnp.concatenate(heads, 1)
@@ -514,10 +596,10 @@
 
 
 def feed_body(pos, *refs):
-    tok, mixed, own, oth, cot = refs[0:4], refs[4:8], refs[8:12], refs[12:16], refs[16:20]
-    vec_ref = refs[20]
-    mid_ref, n2_ref, act_ref, pre_ref, d0, d1, d2, d3, g0, g1, g2, g3, sums_ref, wok_ref = refs[21:35]
-    wo, wu, wd, hat_ref = refs[35:]
+    tok, mixed, own, oth = refs[0:4], refs[4:8], refs[8:12], refs[12:16]
+    vec_ref = refs[16]
+    mid_ref, n2_ref, act_ref, pre_ref, d0, d1, d2, d3, g0, g1, g2, g3, sums_ref, wok_ref = refs[17:31]
+    wo, wu, wd, hat_ref = refs[31:]
     s, k, c = pos[0], pos[1], pos[2]
     for m in range(4):
         z = s ^ m
@@ -548,7 +630,7 @@
     cdf = 0.5 * (1.0 + lax.erf(pre_act * (1.0 / math.sqrt(2.0))))
     act_ref[...] = (pre_act * cdf).astype(bf16)
     slope = cdf + pre_act * jnp.exp(-0.5 * pre_act * pre_act) * (1.0 / math.sqrt(2.0 * math.pi))
-    grads = jnp.concatenate([ref[...] for ref in cot], 0)
+    grads = jnp.concatenate([ref[ROWS : 2 * ROWS, :] for ref in tok], 0)
     pre = (dot_t(grads, wd[...]) * slope).astype(bf16)
     pre_ref[...] = pre
     back = dot_t(pre, wu[...])
@@ -567,27 +649,27 @@
         ref[...] = down[ROWS * r : ROWS * (r + 1)].astype(bf16)
 
 
-def feed_grad_body(pos, act_ref, n2_ref, pre_ref, c0, c1, c2, c3, send_ref, own_ref, wg):
+def feed_grad_body(pos, act_ref, n2_ref, pre_ref, c0, c1, c2, c3, x0, x1, x2, x3, own_ref, wg):
     s, c = pos[0], pos[2]
-    grads = jnp.concatenate([ref[...] for ref in (c0, c1, c2, c3)], 0)
+    grads = jnp.concatenate([ref[ROWS : 2 * ROWS, :] for ref in (c0, c1, c2, c3)], 0)
     for part in range(2):
         if part == 0:
             wg[...] = t_dot(act_ref[...], grads)
         else:
             wg[...] = t_dot(n2_ref[...], pre_ref[...])
         rows = slice(HALF * part, HALF * part + HALF)
-        for m in range(4):
+        for m, send in enumerate((x0, x1, x2, x3)):
             z = s ^ m
             at = pl.ds(pl.multiple_of(z * QUARTER + c * HALF, 32), HALF)
             own_ref[m, rows, :] = wg[at, :]
             at = pl.ds(pl.multiple_of(z * QUARTER + (1 - c) * HALF, 32), HALF)
-            send_ref[m, rows, :] = wg[at, :].astype(bf16)
-
-
-def halves_body(pos, own_ref, got_ref, o0, o1, o2, o3):
-    rows = got_ref.shape[1]
-    for m, out in enumerate((o0, o1, o2, o3)):
-        out[:rows, :] = (own_ref[m, :rows, :] + got_ref[m].astype(f32)).astype(out.dtype)
+            send[rows, :] = wg[at, :].astype(bf16)
+
+
+def halves_body(pos, own_ref, y0, y1, y2, y3, o0, o1, o2, o3):
+    rows = y0.shape[0]
+    for m, (got, out) in enumerate(((y0, o0), (y1, o1), (y2, o2), (y3, o3))):
+        out[:rows, :] = (own_ref[m, :rows, :] + got[...].astype(f32)).astype(out.dtype)
         if own_ref.shape[1] > rows:
             out[rows:, :] = own_ref[m, rows:, :].astype(out.dtype)
 
@@ -597,17 +679,19 @@
     out[...] = total.astype(out.dtype)
 
 
-def middle_body(pos, g0, r1, r2, r3, mid_ref, cot_ref, vec_ref, gm_ref, ga_ref):
+def middle_body(pos, g0, r1, r2, r3, mid_ref, tok_ref, vec_ref, gm_ref, ga_ref):
     err = g0[...] + r1[...].astype(f32) + r2[...].astype(f32) + r3[...].astype(f32)
     hat, rstd = normal(mid_ref[...])
-    grad = cot_ref[...].astype(f32) + norm_back(err, vec_ref[3:4, :], hat, rstd)
+    grad = tok_ref[ROWS : 2 * ROWS, :].astype(f32) + norm_back(err, vec_ref[3:4, :], hat, rstd)
     gm_ref[...] = grad
     ga_ref[...] = grad.astype(bf16)
 
 
-def attend_grad_body(pos, a0, a1, a2, a3, wok, q_ref, kva, kvb, state_ref, *outs):
-    dq_ref, own_ref, send_ref, p_ref, ds_ref = outs
-    cols, keys = split_ids(kva, kvb)
+def attend_grad_body(pos, a0, a1, a2, a3, wok, q_ref, *refs):
+    pair, state_ref, outs = refs[:8], refs[8], refs[9:]
+    dq_ref, own_ref, x0, x1, x2, x3, p_ref, ds_ref, key_ref, value_ref = outs
+    cols, keys = split_ids(pair[0], pair[4])
+    all_keys(pair, key_ref, value_ref)
     grads = jnp.concatenate([ref[...] for ref in (a0, a1, a2, a3)], 0)
     grad_mixed = dot_t(grads, wok[...]).astype(bf16)
     dq = []
@@ -622,32 +706,36 @@
             g = grad[rows]
             inner = jnp.sum(g.astype(f32) * state_ref[rows, at], -1, keepdims=True)
             lse = state_ref[rows, QUARTER + h : QUARTER + h + 1]
-            scores = jnp.concatenate(
-                [dot_t(query[rows], kva[:OWN, at]), dot_t(query[rows], kvb[:OWN, at])], 1
-            )
+            scores = dot_t(query[rows], key_ref[:, at])
             probs = jnp.exp(jnp.where(hidden, NEGATIVE, scores) - lse)
-            slopes = jnp.concatenate([dot_t(g, kva[:OWN, at_v]), dot_t(g, kvb[:OWN, at_v])], 1)
+            slopes = dot_t(g, value_ref[:, at])
             ds = (probs * (slopes - inner)).astype(bf16)
             p_ref[rows, :] = probs.astype(bf16)
             ds_ref[rows, :] = ds
-            grad_q.append(dot(ds[:, :OWN], kva[:OWN, at]) + dot(ds[:, OWN:], kvb[:OWN, at]))
+            grad_q.append(dot(ds, key_ref[:, at]))
         dq.append(jnp.concatenate(grad_q, 0))
         dk = t_dot(ds_ref[...], query)
         dv = t_dot(p_ref[...], grad)
         own_ref[:, at] = dk[:OWN]
         own_ref[:, at_v] = dv[:OWN]
-        send_ref[:, at] = dk[OWN:].astype(bf16)
-        send_ref[:, at_v] = dv[OWN:].astype(bf16)
+        half = OWN // 2
+        x0[:, at] = dk[OWN : OWN + half].astype(bf16)
+        x1[:, at] = dk[OWN + half :].astype(bf16)
+        x2[:, at] = dv[OWN : OWN + half].astype(bf16)
+        x3[:, at] = dv[OWN + half :].astype(bf16)
     dq_ref[...] = (jnp.concatenate(dq, 1) * 0.125).astype(bf16)
 
 
 def project_grad_body(pos, *refs):
     tok, mixed, ga = refs[0:4], refs[4:8], refs[8:12]
-    normed, dq, kv_own, kv_got, w_ref, vec_ref, sums_ref, cot_ref = refs[12:20]
-    send_ref, own_ref, g0, g1, g2, g3, wg, sm, gk, gp = refs[20:]
+    normed, dq, kv_own, y0, y1, y2, y3, w_ref, vec_ref, sums_ref, d1, d2, d3 = refs[12:25]
+    x0, x1, x2, x3, own_ref, g0, g1, g2, g3, wg, sm, gk, gp = refs[25:]
     s, k, c = pos[0], pos[1], pos[2]
     gp[:, :QUARTER] = dq[...]
-    gp[:, QUARTER:] = (kv_own[...] + kv_got[...].astype(f32)).astype(bf16)
+    got_k = jnp.concatenate([y0[...], y1[...]], 0)
+    got_v = jnp.concatenate([y2[...], y3[...]], 0)
+    got = jnp.concatenate([got_k, got_v], 1).astype(f32)
+    gp[:, QUARTER:] = (kv_own[...] + got).astype(bf16)
     wg[:, : 3 * QUARTER] = t_dot(normed[...], gp[...])
     for q in range(4):
 
@@ -667,11 +755,12 @@
     ln1_gain = jnp.sum(back * hat, 0, keepdims=True)
     ln1_bias = jnp.sum(back, 0, keepdims=True)
     g0[...] = back[:ROWS]
-    for r, ref in ((1, g1), (2, g2), (3, g3)):
-        ref[...] = back[ROWS * r : ROWS * (r + 1)].astype(bf16)
+    for r, ref, down in ((1, g1, d1), (2, g2, d2), (3, g3, d3)):
+        ref[:ROWS, :] = back[ROWS * r : ROWS * (r + 1)].astype(bf16)
+        ref[ROWS:, :] = down[...]
     gp_sums = jnp.sum(gp[...].astype(f32), 0, keepdims=True)
     out_bias = jnp.sum(ga[0][...].astype(f32), 0, keepdims=True)
-    down_bias = jnp.sum(cot_ref[...].astype(f32), 0, keepdims=True)
+    down_bias = jnp.sum(tok[0][ROWS : 2 * ROWS, :].astype(f32), 0, keepdims=True)
     for z in range(4):
         at = slice(QUARTER * z, QUARTER * (z + 1))
         here = jnp.where(k == z, 1.0, 0.0).astype(f32)
@@ -687,17 +776,15 @@
         own_ref[m, :HALF, :] = wg[at, :]
         own_ref[m, HALF:, :] = sm[z]
         at = pl.ds(pl.multiple_of(z * QUARTER + (1 - c) * HALF, 32), HALF)
-        send_ref[m] = wg[at, :].astype(bf16)
-
-
-def input_body(pos, g0, r1, r2, r3, tok_ref, gm_ref, vec_ref, out_ref):
-    err = g0[...] + r1[...].astype(f32) + r2[...].astype(f32) + r3[...].astype(f32)
+        (x0, x1, x2, x3)[m][...] = wg[at, :].astype(bf16)
+
+
+def rows_body(pos, g0, r1, r2, r3, d0, tok_ref, gm_ref, mid_ref, vec_ref, grad_ref, out_ref):
+    got = [ref[...].astype(f32) for ref in (r1, r2, r3)]
+    err = g0[...] + got[0][:ROWS] + got[1][:ROWS] + got[2][:ROWS]
     hat, rstd = normal(tok_ref[:ROWS, :].astype(f32))
-    out_ref[0] = gm_ref[...] + norm_back(err, vec_ref[0:1, :], hat, rstd)
-
-
-def output_body(pos, d0, r1, r2, r3, mid_ref, vec_ref, out_ref):
-    total = d0[...] + r1[...].astype(f32) + r2[...].astype(f32) + r3[...].astype(f32)
+    grad_ref[0] = gm_ref[...] + norm_back(err, vec_ref[0:1, :], hat, rstd)
+    total = d0[...] + got[0][ROWS:] + got[1][ROWS:] + got[2][ROWS:]
     out_ref[0] = (mid_ref[...] + total + vec_ref[5:6, :]).astype(bf16)
 
 
@@ -721,7 +808,8 @@
 
 def last_join_body(pos, *refs):
     own, oth = refs[0:4], refs[4:8]
-    qkv_ref, out_ref, vec_ref, up_ref, sc = refs[8:]
+    qkv_ref, out_ref, up_ref, sc = refs[8], refs[9], refs[18], refs[19]
+    vec_refs = refs[10:18]
     k, c = pos[1], pos[2]
     for m in range(4):
         sc[c, k ^ m] = own[m][...]
@@ -741,9 +829,10 @@
             out_ref[rows, QUARTER * q : QUARTER * (q + 1)] = sc[
                 half, q, :HALF, 3 * QUARTER :
             ].astype(f32)
-    vecs = [total[n // 4 : n // 4 + 1, QUARTER * (n % 4) : QUARTER * (n % 4 + 1)] for n in range(8)]
-    vec_ref[...] = jnp.concatenate(vecs, 0)
-    up_ref[...] = jnp.concatenate(ups, 1)
+    for n, ref in enumerate(vec_refs):
+        row = total[n // 4 : n // 4 + 1, QUARTER * (n % 4) : QUARTER * (n % 4 + 1)]
+        ref[...] = row.reshape(QUARTER)
+    up_ref[...] = jnp.concatenate(ups, 1).reshape(WIDTH)
 
 
 def shards(
@@ -769,140 +858,141 @@
     k, core = ctx // 2, ctx % 2
     pos = jnp.stack([seq, k, core]).astype(jnp.int32)
 
-    def rows_of_core(values):
-        return lax.dynamic_slice_in_dim(values, HALF * core, HALF, 0)
-
-    got_qkv = seq_gather(column_slice(rows_of_core(w_qkv), k, 3))
-    ids_row = jnp.pad(block_ids.astype(bf16), ((0, 7), (0, WIDTH - ROWS)))
-    tok = chip_gather(jnp.concatenate([tokens[0], ids_row], 0))
-    small = [ln1_gain, ln1_bias, q_bias, v_bias, out_bias, ln2_gain, ln2_bias, down_bias]
-    small = small + [lax.dynamic_slice_in_dim(up_bias, QUARTER * k, QUARTER, 0)]
-    small = [jnp.pad(v, (0, 256 - QUARTER)) for v in small] + [jnp.zeros((7 * 256,), bf16)]
-    got_small = seq_gather(jnp.concatenate(small).reshape(16, 256))
-    oth_qkv = [core_swap(block) for block in got_qkv]
-    rest = jnp.concatenate(
-        [
-            rows_of_core(w_out),
-            column_slice(rows_of_core(w_up), k, 4),
-            lax.dynamic_slice_in_dim(w_down, QUARTER * k + HALF * core, HALF, 0),
-        ],
-        0,
-    )
-    got_rest = seq_gather(after(rest, *got_qkv, *got_small))
-    cot = chip_gather(after(cotangent[0], *tok))
-
-    query, pair, normed, vec, weight_qkv = run(
+    small = [ln1_gain, ln1_bias, q_bias, v_bias, out_bias, ln2_gain, ln2_bias, down_bias, up_bias]
+    piece_qkv, mate_qkv, pack = run(
+        pack_body,
+        pos,
+        [w_qkv, tokens, cotangent, block_ids, *small],
+        [((HALF + 16, 3 * QUARTER), bf16)] * 2 + [((2 * ROWS + 8, WIDTH), bf16)],
+        [((2, HALF, 3 * WIDTH), bf16)],
+        hbm=(0, 1, 2),
+        sems=4,
+        limit=60,
+    )
+    rest, mate_rest = run(
+        rest_body,
+        pos,
+        [w_out, w_up, w_down],
+        [((3 * HALF, WIDTH), bf16)] * 2,
+        [((2, HALF, 4 * WIDTH), bf16)],
+        hbm=(0, 1, 2),
+        sems=6,
+        limit=60,
+    )
+    got_qkv = seq_gather(piece_qkv)
+    tok = chip_gather(pack)
+    got_rest = seq_gather(rest)
+    oth_qkv = [mate_qkv] + [core_swap(block) for block in got_qkv[1:]]
+    half = (OWN // 2, QUARTER)
+    query, *pair, normed, vec, weight_qkv = run(
         qkv_body,
         pos,
-        [*tok, *got_small, *got_qkv, *oth_qkv],
-        [
-            ((OWN, QUARTER), bf16),
-            ((OWN + 8, 2 * QUARTER), bf16),
-            ((OWN, WIDTH), bf16),
-            ((8, WIDTH), f32),
-            ((WIDTH, 3 * QUARTER), bf16),
-        ],
-        [((4, 16, 256), f32)],
-    )
-    pair_oth = core_swap(pair)
+        [*tok, *got_qkv, *oth_qkv],
+        [((OWN, QUARTER), bf16), ((OWN // 2 + 8, QUARTER), bf16), (half, bf16), (half, bf16)]
+        + [(half, bf16), ((OWN, WIDTH), bf16), ((8, WIDTH), f32), ((WIDTH, 3 * QUARTER), bf16)],
+        [((4, 16, 3 * QUARTER), f32)],
+    )
+    pair = [*pair, *[core_swap(x) for x in pair]]
     mixed_own, state = run(
         attend_body,
         pos,
-        [query, pair, pair_oth],
+        [query, *pair],
         [((OWN, QUARTER), bf16), ((OWN, 256), f32)],
-        us=6.0,
+        [((2 * OWN, QUARTER), bf16)] * 2,
     )
     mixed = chip_gather(mixed_own)
-    got_rest = lax.optimization_barrier((*got_rest, mixed_own))[:4]
-    oth_rest = [core_swap(block) for block in got_rest]
+    got_rest = lax.optimization_barrier((*got_rest, *mixed[1:]))[:4]
+    oth_rest = [mate_rest] + [core_swap(block) for block in got_rest[1:]]
     big, block = (OWN, WIDTH), (ROWS, WIDTH)
     mid, normed_two, act, pre, d0, d1, d2, d3, g0, g1, g2, g3, sums, w_out_k = run(
         feed_body,
         pos,
-        [*tok, *mixed, *got_rest, *oth_rest, *cot, vec],
+        [*tok, *mixed, *got_rest, *oth_rest, vec],
         [(block, f32), (big, bf16), (big, bf16), (big, bf16)]
         + [(block, f32), (block, bf16), (block, bf16), (block, bf16)] * 2
         + [((8, WIDTH), f32), ((QUARTER, WIDTH), bf16)],
         [((WIDTH, WIDTH), bf16)] * 3 + [(big, f32)],
-        us=8.0,
+        limit=32,
     )
     got_g = [chip_swap(g, m) for m, g in ((1, g1), (2, g2), (3, g3))]
-    feed_send, feed_own = run(
+    piece = (QUARTER, WIDTH)
+    *feed_send, feed_own = run(
         feed_grad_body,
         pos,
-        [act, normed_two, pre, *cot],
-        [((4, QUARTER, WIDTH), bf16), ((4, QUARTER, WIDTH), f32)],
+        [after(act, got_g[0]), normed_two, pre, *tok],
+        [(piece, bf16)] * 4 + [((4, *piece), f32)],
         [((WIDTH, WIDTH), f32)],
-        us=4.0,
-    )
-    feed_got = core_swap(feed_send)
+    )
+    feed_got = [core_swap(x) for x in feed_send]
     grad_mid, grad_att = run(
-        middle_body, pos, [g0, *got_g, mid, cot[0], vec], [(block, f32), (block, bf16)]
-    )
-    piece = (QUARTER, WIDTH)
+        middle_body, pos, [g0, *got_g, mid, tok[0], vec], [(block, f32), (block, bf16)]
+    )
+    ga = chip_gather(grad_att)
     h0, h1, h2, h3 = run(
-        halves_body, pos, [feed_own, feed_got], [(piece, f32)] + [(piece, bf16)] * 3
-    )
-    ga = chip_gather(grad_att)
+        halves_body, pos, [feed_own, *feed_got], [(piece, f32)] + [(piece, bf16)] * 3
+    )
     feed_terms = [seq_swap(h, m) for m, h in ((1, h1), (2, h2), (3, h3))]
-    *ga, h0 = lax.optimization_barrier((*ga, h0))
-    got_d = [chip_swap(after(d, ga[1]), m) for m, d in ((1, d1), (2, d2), (3, d3))]
-    dq, kv_own, kv_send = run(
+    dq, kv_own, *pair_send = run(
         attend_grad_body,
         pos,
-        [*ga, w_out_k, query, pair, pair_oth, state],
-        [((OWN, QUARTER), bf16), ((OWN, 2 * QUARTER), f32), ((OWN, 2 * QUARTER), bf16)],
-        [((OWN, 2 * OWN), bf16)] * 2,
-        us=8.0,
-    )
-    kv_send, *feed_terms = lax.optimization_barrier((kv_send, *feed_terms))
-    kv_got = core_swap(kv_send)
+        [*ga, w_out_k, after(query, h0), *pair, state],
+        [((OWN, QUARTER), bf16), ((OWN, 2 * QUARTER), f32)] + [(half, bf16)] * 4,
+        [((OWN, 2 * OWN), bf16)] * 2 + [((2 * OWN, QUARTER), bf16)] * 2,
+    )
+    pair_got = [core_swap(x) for x in pair_send]
+    dq, *feed_two = lax.optimization_barrier((dq, *feed_terms[:2]))
+    feed_terms = feed_two + feed_terms[2:]
+    lpiece = (HALF + 8, WIDTH)
+    *last_send, last_own, e0, e1, e2, e3 = run(
+        project_grad_body,
+        pos,
+        [*tok, *mixed, *ga, normed, dq, kv_own, *pair_got, weight_qkv, vec, sums, d1, d2, d3],
+        [((HALF, WIDTH), bf16)] * 4
+        + [((4, *lpiece), f32), (block, f32)]
+        + [((2 * ROWS, WIDTH), bf16)] * 3,
+        [
+            ((WIDTH, WIDTH), f32),
+            ((4, 8, WIDTH), f32),
+            ((OWN, QUARTER), bf16),
+            ((OWN, 3 * QUARTER), bf16),
+        ],
+    )
+    last_got = [core_swap(x) for x in last_send]
+    l0, l1, l2, l3 = run(
+        halves_body, pos, [last_own, *last_got], [(lpiece, f32)] + [(lpiece, bf16)] * 3
+    )
+    l1, l2, l3, *feed_last = lax.optimization_barrier((l1, l2, l3, *feed_terms[2:]))
+    feed_terms = feed_two + feed_last
+    last_terms = [seq_swap(h, m) for m, h in ((1, l1), (2, l2), (3, l3))]
+    got_e = [chip_swap(e, m) for m, e in ((1, e1), (2, e2), (3, e3))]
     (feed_sum,) = run(add_body, pos, [h0, *feed_terms], [(piece, bf16)])
     feed_blocks = chip_gather(feed_sum)
-    last_send, last_own, e0, e1, e2, e3 = run(
-        project_grad_body,
+    input_grad, result = run(
+        rows_body,
         pos,
-        [*tok, *mixed, *ga, normed, dq, kv_own, kv_got, weight_qkv, vec, sums, cot[0]],
-        [((4, HALF, WIDTH), bf16), ((4, HALF + 8, WIDTH), f32)]
-        + [(block, f32), (block, bf16), (block, bf16), (block, bf16)],
-        [((WIDTH, WIDTH), f32), ((4, 8, WIDTH), f32), ((OWN, QUARTER), bf16), ((OWN, 3 * QUARTER), bf16)],
-        us=6.0,
-    )
-    last_got = core_swap(last_send)
-    lpiece = (HALF + 8, WIDTH)
-    l0, l1, l2, l3 = run(
-        halves_body, pos, [last_own, last_got], [(lpiece, f32)] + [(lpiece, bf16)] * 3
-    )
-    last_terms = [seq_swap(h, m) for m, h in ((1, l1), (2, l2), (3, l3))]
-    got_e = [chip_swap(e, m) for m, e in ((1, e1), (2, e2), (3, e3))]
+        [e0, *got_e, d0, tok[0], grad_mid, mid, vec],
+        [((1, *block), f32), ((1, *block), bf16)],
+    )
+    (last_sum,) = run(add_body, pos, [l0, *last_terms], [(lpiece, bf16)])
+    last_sum, got_e[0] = lax.optimization_barrier((last_sum, got_e[0]))
+    last_blocks = chip_gather(last_sum)
     feed_oth = [core_swap(b) for b in feed_blocks]
     grad_w_down, grad_w_up = run(
         feed_join_body,
         pos,
-        [*feed_blocks, *feed_oth],
+        [after(feed_blocks[0], last_sum), *feed_blocks[1:], *feed_oth],
         [((WIDTH, WIDTH), f32), ((QUARTER, 4 * WIDTH), f32)],
         [((2, 4, QUARTER, WIDTH), bf16)],
-        us=4.0,
-    )
-    (result,) = run(output_body, pos, [d0, *got_d, mid, vec], [((1, *block), bf16)])
-    (input_grad,) = run(
-        input_body, pos, [e0, *got_e, tok[0], grad_mid, vec], [((1, *block), f32)]
-    )
-    (last_sum,) = run(add_body, pos, [l0, *last_terms], [(lpiece, bf16)])
-    last_blocks = chip_gather(last_sum)
+    )
     last_oth = [core_swap(b) for b in last_blocks]
-    grad_w_qkv, grad_w_out, g, g_up = run(
+    grad_w_qkv, grad_w_out, *g, g_up = run(
         last_join_body,
         pos,
         [*last_blocks, *last_oth],
-        [
-            ((QUARTER, 3 * WIDTH), f32),
-            ((QUARTER, WIDTH), f32),
-            ((8, QUARTER), f32),
-            ((1, WIDTH), f32),
-        ],
+        [((QUARTER, 3 * WIDTH), f32), ((QUARTER, WIDTH), f32)]
+        + [((QUARTER,), f32)] * 8
+        + [((WIDTH,), f32)],
         [((2, 4, HALF + 8, WIDTH), bf16)],
-        us=3.0,
     )
     return (
         result,
@@ -917,7 +1007,7 @@
         g[5],
         g[6],
         grad_w_up,
-        g_up[0],
+        g_up,
         grad_w_down,
         g[7],
     )

time: 226 us -> 177 us (0.78)
  waiting for transfers between devices: 110 us -> 66 us
  local copies, waits for them, and re-layouts: 11.2 us -> 0.04 us
  Pallas kernels: 37.8 us -> 42.2 us
  starting transfers between devices: 63.4 us -> 67.1 us
    ppermute x27 -> x21, waiting for transfers between devices: 55.9 us -> 26.7 us  [chip_swap(): return lax.ppermute(values, 'ctx', [(i, i ^ 2 * mask) for i in range(8)])]
    ppermute x15 -> x12, waiting for transfers between devices: 51 us -> 31.3 us  [seq_swap(): return lax.ppermute(values, 'seq', [(i, i ^ mask) for i in range(4)])]
    pad x9 -> x0, local copies, waits for them, and re-layouts: 5.28 us -> none  [shards(): jnp.pad(v, (0, 256 - QUARTER))]
    ppermute x20 -> x30, waiting for transfers between devices: 2.95 us -> 7.95 us  [core_swap(): return lax.ppermute(values, 'ctx', [(i, i ^ 1) for i in range(8)])]
    pallas_call x15 -> x16, Pallas kernels: 37.8 us -> 42.2 us  [run(): pl.pallas_call(body, out_shape=[jax.ShapeDtypeStruct(shape, kind) for sha...]
    dynamic_slice x3 -> x0, local copies, waits for them, and re-layouts: 3.1 us -> none  [the longest x1 1.36 us: column_slice(): lax.dynamic_slice_in_dim(values, WIDTH * p + QUARTER * k, QUARTER, 1)]
    ppermute x20 -> x30, starting transfers between devices: 3.72 us -> 6.78 us  [core_swap(): return lax.ppermute(values, 'ctx', [(i, i ^ 1) for i in range(8)])]
    ppermute x15 -> x12, starting transfers between devices: 28.2 us -> 30.4 us  [seq_swap(): return lax.ppermute(values, 'seq', [(i, i ^ mask) for i in range(4)])]
  transfers between devices with their start and end apart: 62 -> 63, of which waited for: 26 -> 25; matrix products, arithmetic and copies ran while one was open for 2% -> 0% of each run, Pallas kernels for 11% -> 16%
where the time goes in v3:
time: 177 us
  starting transfers between devices  67.1 us (38%)
  waiting for transfers between devices  66 us (37%)
  Pallas kernels  42.2 us (24%)
    pallas_call x16, Pallas kernels, run(): pl.pallas_call(body, out_shape=[jax.ShapeDtypeStruct(shape, kind) for sha...  42.2 us
    ppermute x12, waiting for transfers between devices, seq_swap(): return lax.ppermute(values, 'seq', [(i, i ^ mask) for i in range(4)])  31.3 us
    ppermute x12, starting transfers between devices, seq_swap(): return lax.ppermute(values, 'seq', [(i, i ^ mask) for i in range(4)])  30.4 us
    ppermute x21, starting transfers between devices, chip_swap(): return lax.ppermute(values, 'ctx', [(i, i ^ 2 * mask) for i in range(8)])  29.9 us
    ppermute x21, waiting for transfers between devices, chip_swap(): return lax.ppermute(values, 'ctx', [(i, i ^ 2 * mask) for i in range(8)])  26.7 us
    ppermute x30, waiting for transfers between devices, core_swap(): return lax.ppermute(values, 'ctx', [(i, i ^ 1) for i in range(8)])  7.95 us
    ppermute x30, starting transfers between devices, core_swap(): return lax.ppermute(values, 'ctx', [(i, i ^ 1) for i in range(8)])  6.78 us
  transfers between devices with their start and end apart: 63, of which 25 were waited for; matrix products, arithmetic and copies ran while one was open for 0% of the time, Pallas kernels for 16%

profile of v3, /device:TPU:0, one launch (start us, length us, event | category | flops | bytes accessed | tf_op | source)
XLA Modules:
  0.0 176.9 jit_solution(4660235858836378529)
XLA Ops:
  1.3 3.0 %shard_map.271 = (bf16[112,576]{1,0:T(8,128)(2,1)}, bf16[112,576]{1,0:T(8,128)(2,1)}, bf16[264,768]{1,0:T(8,128)(2,1)}) custom-call(s32[3]{0:T(128)} %pad_add_fusion.pos, bf16[192,2304]{1,0:T(8,128)(2,1)} %w_ref.1, bf16[1,128,768]{2,1,0:T(8,128)(2,1)} %tok_ref.1, bf16[1,128,768]{2,1,0:T(8,128)(2,1)} %cot_ref.1, s32[1,128]{1,0:T(1,128)} %ids_ref.1, ...), custom_call_target="tpu_custom_call" | custom-call | flops 524288 | bytes 1000 | tf_op jit(solution)/shard_map/pallas_call | solution.py:402
  4.3 3.1 %collective-permute-start.3 = (bf16[112,576]{1,0:T(8,128)(2,1)}, bf16[112,576]{1,0:T(8,128)(2,1)S(1)}, u32[]{:S(2)}, u32[]{:S(2)}) collective-permute-start(bf16[112,576]{1,0:T(8,128)(2,1)} %get-tuple-element.105.refs_4_), channel_id=1, source_target_pairs={{0,8},{8,0},{16,24},{24,16},{1,9},{9,1},{17,25},{25,17},{2,10},{10... | collective-permute-start | bytes 387080 | tf_op jit(solution)/shard_map/ppermute | solution.py:381
  7.4 2.6 %collective-permute-start.4 = (bf16[112,576]{1,0:T(8,128)(2,1)}, bf16[112,576]{1,0:T(8,128)(2,1)S(1)}, u32[]{:S(2)}, u32[]{:S(2)}) collective-permute-start(bf16[112,576]{1,0:T(8,128)(2,1)} %get-tuple-element.105.refs_4_), channel_id=1, source_target_pairs={{0,16},{8,24},{16,0},{24,8},{1,17},{9,25},{17,1},{25,9},{2,18},{10... | collective-permute-start | bytes 387080 | tf_op jit(solution)/shard_map/ppermute | solution.py:381
  10.0 1.5 collective-permute-start
  11.7 1.5 collective-permute-start.1
  13.5 2.4 %collective-permute-start.2 = (bf16[264,768]{1,0:T(8,128)(2,1)}, bf16[264,768]{1,0:T(8,128)(2,1)S(1)}, u32[]{:S(2)}, u32[]{:S(2)}) collective-permute-start(bf16[264,768]{1,0:T(8,128)(2,1)} %get-tuple-element.104.refs_0_.tok_ref.c0), channel_id=1, source_target_pairs={{0,6},{1,7},{2,4},{3,5},{4,2},{5,3},{6,0},{7,1},{8,14},{9,15},{10,... | collective-permute-start | bytes 1216520 | tf_op jit(solution)/shard_map/ppermute | solution.py:377
  15.9 5.0 %collective-permute-done.4.refs_6_ = bf16[112,576]{1,0:T(8,128)(2,1)S(1)} collective-permute-done((bf16[112,576]{1,0:T(8,128)(2,1)}, bf16[112,576]{1,0:T(8,128)(2,1)S(1)}, u32[]{:S(2)}, u32[]{:S(2)}) %collective-permute-start.4) | collective-permute-done | bytes 129056 | tf_op jit(solution)/shard_map/ppermute | solution.py:381
  21.4 3.1 %shard_map.274 = (bf16[288,768]{1,0:T(8,128)(2,1)}, bf16[288,768]{1,0:T(8,128)(2,1)}) custom-call(s32[3]{0:T(128)} %pad_add_fusion.pos, bf16[192,768]{1,0:T(8,128)(2,1)} %wo_ref.1, bf16[192,3072]{1,0:T(8,128)(2,1)} %wu_ref.1, bf16[768,768]{1,0:T(8,128)(2,1)} %wd_ref.1), custom_call_target="tpu_custom_call" | custom-call | flops 524288 | bytes 1000 | tf_op jit(solution)/shard_map/pallas_call | solution.py:402
  24.6 2.2 %collective-permute-start.16 = (bf16[288,768]{1,0:T(8,128)(2,1)}, bf16[288,768]{1,0:T(8,128)(2,1)S(1)}, u32[]{:S(2)}, u32[]{:S(2)}) collective-permute-start(bf16[288,768]{1,0:T(8,128)(2,1)} %get-tuple-element.114.refs_8_), channel_id=1, source_target_pairs={{0,8},{8,0},{16,24},{24,16},{1,9},{9,1},{17,25},{25,17},{2,10},{10... | collective-permute-start | bytes 1327112 | tf_op jit(solution)/shard_map/ppermute | solution.py:381
  27.0 1.1 collective-permute-done.8.refs_11_
  28.1 1.2 collective-permute-start.17
  29.4 1.4 collective-permute-start.18
  30.8 1.9 %shard_map.272 = (bf16[512,192]{1,0:T(8,128)(2,1)S(1)}, bf16[264,192]{1,0:T(8,128)(2,1)S(1)}, bf16[256,192]{1,0:T(8,128)(2,1)S(1)}, bf16[256,192]{1,0:T(8,128)(2...) custom-call(s32[3]{0:T(128)S(1)} %copy-done.3, ...), custom_call_target="tpu_custom_call" | custom-call | flops 524288 | bytes 1000 | tf_op jit(solution)/shard_map/pallas_call | solution.py:402
  33.3 0.8 collective-permute-done.10.refs_5_
  34.7 1.0 collective-permute-done.12.refs_7_
  35.7 5.2 %shard_map.273 = (bf16[512,192]{1,0:T(8,128)(2,1)S(1)}, f32[512,256]{1,0:T(8,128)S(1)}) custom-call(s32[3]{0:T(128)S(1)} %copy-done.3, bf16[512,192]{1,0:T(8,128)(2,1)S(1)} %get-tuple-element.138.q_ref, bf16[264,192]{1,0:T(8,128)(2,1)S(1)} %get-tuple-element.108.refs_0_, bf16[256,192]{1,0:T(8,128)(2,1)S(1)} %get-tuple-element.109.refs_1_, ...), custom_call_target="tpu_custom_call" | custom-call | flops 524288 | bytes 1000 | tf_op jit(solution)/shard_map/pallas_call | solution.py:402
  40.9 1.6 collective-permute-start.13
  42.6 1.5 collective-permute-start.14
  44.1 1.7 collective-permute-done.16.refs_9_
  45.8 2.4 %collective-permute-start.15 = (bf16[512,192]{1,0:T(8,128)(2,1)S(1)}, bf16[512,192]{1,0:T(8,128)(2,1)S(1)}, u32[]{:S(2)}, u32[]{:S(2)}) collective-permute-start(bf16[512,192]{1,0:T(8,128)(2,1)S(1)} %get-tuple-element.112.refs_4_), channel_id=1, source_target_pairs={{0,6},{1,7},{2,4},{3,5},{4,2},{5,3},{6,0},{7,1},{8,14},{9,15},{10,... | collective-permute-start | bytes 589832 | tf_op jit(solution)/shard_map/ppermute | solution.py:377
  48.2 13.0 %collective-permute-done.17.refs_10_ = bf16[288,768]{1,0:T(8,128)(2,1)S(1)} collective-permute-done((bf16[288,768]{1,0:T(8,128)(2,1)}, bf16[288,768]{1,0:T(8,128)(2,1)S(1)}, u32[]{:S(2)}, u32[]{:S(2)}) %collective-permute-start.17) | collective-permute-done | bytes 442400 | tf_op jit(solution)/shard_map/ppermute | solution.py:381
  61.9 1.2 collective-permute-done.19.refs_13_
  64.4 5.5 %shard_map.275 = (f32[128,768]{1,0:T(8,128)S(1)}, bf16[512,768]{1,0:T(8,128)(2,1)S(1)}, bf16[512,768]{1,0:T(8,128)(2,1)S(1)}, bf16[512,768]{1,0:T(8,128)(2,1)S(1...) custom-call(s32[3]{0:T(128)S(1)} %copy-done.3, ...), custom_call_target="tpu_custom_call" | custom-call | flops 524288 | bytes 1000 | tf_op jit(solution)/shard_map/pallas_call | solution.py:402
  69.9 1.5 collective-permute-start.22
  71.4 5.5 %collective-permute-done.22.r1 = bf16[128,768]{1,0:T(8,128)(2,1)S(1)} collective-permute-done((bf16[128,768]{1,0:T(8,128)(2,1)S(1)}, bf16[128,768]{1,0:T(8,128)(2,1)S(1)}, u32[]{:S(2)}, u32[]{:S(2)}) %collective-permute-start.22) | collective-permute-done | bytes 196640 | tf_op jit(solution)/shard_map/ppermute | solution.py:377
  76.9 2.2 %shard_map.277 = (bf16[192,768]{1,0:T(8,128)(2,1)S(1)}, bf16[192,768]{1,0:T(8,128)(2,1)S(1)}, bf16[192,768]{1,0:T(8,128)(2,1)S(1)}, bf16[192,768]{1,0:T(8,128)(2,1)S(1)}, f32[4,192,768]{2,1,0:T(8,128)S(1)}) custom-call(s32[3]{0:T(128)S(1)} %copy-done.3, bf16[512,768]{1,0:T(8,128)(2,1)S(1)} %get-tuple-element.129.act_ref, ...), custom_call_target="tpu_custom_call" | custom-call | flops 524288 | bytes 1000 | tf_op jit(solution)/shard_map/pallas_call | solution.py:402
  80.2 1.5 collective-permute-start.23
  81.7 1.5 collective-permute-start.24
  83.2 0.8 shard_map.278
  84.0 9.4 %collective-permute-start.32 = (bf16[192,768]{1,0:T(8,128)(2,1)S(1)}, bf16[192,768]{1,0:T(8,128)(2,1)S(1)}, u32[]{:S(2)}, u32[]{:S(2)}) collective-permute-start(bf16[192,768]{1,0:T(8,128)(2,1)S(1)} %get-tuple-element.141), channel_id=1, source_target_pairs={{0,8},{8,0},{16,24},{24,16},{1,9},{9,1},{17,25},{25,17},{2,10},{10... | collective-permute-start | bytes 884744 | tf_op jit(solution)/shard_map/ppermute | solution.py:381
  93.4 1.1 collective-permute-start.33
  94.4 0.9 shard_map.276
  96.0 1.5 collective-permute-start.26
  97.5 1.5 collective-permute-start.27
  98.9 4.3 %collective-permute-done.25.a1.refs_9_ = bf16[128,768]{1,0:T(8,128)(2,1)S(1)} collective-permute-done((bf16[128,768]{1,0:T(8,128)(2,1)S(1)}, bf16[128,768]{1,0:T(8,128)(2,1)S(1)}, u32[]{:S(2)}, u32[]{:S(2)}) %collective-permute-start.25) | collective-permute-done | bytes 196640 | tf_op jit(solution)/shard_map/ppermute | solution.py:377
  103.3 1.4 collective-permute-start.45
  104.7 0.7 collective-permute-done.26.a2.refs_10_
  105.4 1.2 collective-permute-done.27.a3.refs_11_
  106.6 6.8 %shard_map.279 = (bf16[512,192]{1,0:T(8,128)(2,1)S(1)}, f32[512,384]{1,0:T(8,128)S(1)}, bf16[256,192]{1,0:T(8,128)(2,1)S(1)}, bf16[256,192]{1,0:T(8,128)(2,1)S(1...) custom-call(s32[3]{0:T(128)S(1)} %copy-done.3, bf16[128,768]{1,0:T(8,128)(2,1)S(1)} %get-tuple-element.125.a0.refs_8_, ...), custom_call_target="tpu_custom_call" | custom-call | flops 524288 | bytes 1000 | tf_op jit(solution)/shard_map/pallas_call | solution.py:402
  114.1 1.4 collective-permute-done.33.r2
  115.5 1.3 collective-permute-done.37.refs_18_
  116.9 3.4 %shard_map.280 = (bf16[96,768]{1,0:T(8,128)(2,1)S(1)}, bf16[96,768]{1,0:T(8,128)(2,1)S(1)}, bf16[96,768]{1,0:T(8,128)(2,1)S(1)}, bf16[96,768]{1,0:T(8,128)(2,1)S...) custom-call(s32[3]{0:T(128)S(1)} %copy-done.3, ...), custom_call_target="tpu_custom_call" | custom-call | flops 524288 | bytes 1000 | tf_op jit(solution)/shard_map/pallas_call | solution.py:402
  122.5 0.6 shard_map.282
  123.1 5.4 %collective-permute-start.46 = (bf16[104,768]{1,0:T(8,128)(2,1)S(1)}, bf16[104,768]{1,0:T(8,128)(2,1)S(1)}, u32[]{:S(2)}, u32[]{:S(2)}) collective-permute-start(bf16[104,768]{1,0:T(8,128)(2,1)S(1)} %get-tuple-element.172), channel_id=1, source_target_pairs={{0,8},{8,0},{16,24},{24,16},{1,9},{9,1},{17,25},{25,17},{2,10},{10... | collective-permute-start | bytes 479240 | tf_op jit(solution)/shard_map/ppermute | solution.py:381
  128.5 1.4 collective-permute-start.38
  129.8 0.8 collective-permute-start.39
  130.7 1.1 collective-permute-start.47
  131.7 1.4 collective-permute-start.48
  133.1 1.5 collective-permute-start.40
  134.6 0.7 shard_map.285.refs_0_
  135.3 9.8 %collective-permute-done.47.r2 = bf16[104,768]{1,0:T(8,128)(2,1)S(1)} collective-permute-done((bf16[104,768]{1,0:T(8,128)(2,1)S(1)}, bf16[104,768]{1,0:T(8,128)(2,1)S(1)}, u32[]{:S(2)}, u32[]{:S(2)}) %collective-permute-start.47) | collective-permute-done | bytes 159776 | tf_op jit(solution)/shard_map/ppermute | solution.py:381
  145.1 1.4 collective-permute-start.56
  146.5 0.7 collective-permute-start.57
  147.8 1.4 collective-permute-start.49
  149.2 1.5 collective-permute-start.58
  150.7 0.7 collective-permute-start.50
  151.3 3.9 %collective-permute-done.56.refs_1_ = bf16[192,768]{1,0:T(8,128)(2,1)S(1)} collective-permute-done((bf16[192,768]{1,0:T(8,128)(2,1)S(1)}, bf16[192,768]{1,0:T(8,128)(2,1)S(1)}, u32[]{:S(2)}, u32[]{:S(2)}) %collective-permute-start.56) | collective-permute-done | bytes 294944 | tf_op jit(solution)/shard_map/ppermute | solution.py:377
  155.3 1.6 collective-permute-start.51
  156.9 1.8 %collective-permute-done.49.refs_1_ = bf16[104,768]{1,0:T(8,128)(2,1)S(1)} collective-permute-done((bf16[104,768]{1,0:T(8,128)(2,1)S(1)}, bf16[104,768]{1,0:T(8,128)(2,1)S(1)}, u32[]{:S(2)}, u32[]{:S(2)}) %collective-permute-start.49) | collective-permute-done | bytes 159776 | tf_op jit(solution)/shard_map/ppermute | solution.py:377
  158.7 8.1 %collective-permute-done.50.refs_2_ = bf16[104,768]{1,0:T(8,128)(2,1)S(1)} collective-permute-done((bf16[104,768]{1,0:T(8,128)(2,1)S(1)}, bf16[104,768]{1,0:T(8,128)(2,1)S(1)}, u32[]{:S(2)}, u32[]{:S(2)}) %collective-permute-start.50) | collective-permute-done | bytes 159776 | tf_op jit(solution)/shard_map/ppermute | solution.py:377
  167.3 1.1 collective-permute-done.51.refs_3_
  169.5 1.8 %shard_map.281 = (f32[1,128,768]{2,1,0:T(8,128)}, bf16[1,128,768]{2,1,0:T(8,128)(2,1)}) custom-call(s32[3]{0:T(128)S(1)} %copy-done.3, f32[128,768]{1,0:T(8,128)S(1)} %get-tuple-element.154.g0, bf16[256,768]{1,0:T(8,128)(2,1)S(1)} %collective-permute-done.38.r1, bf16[256,768]{1,0:T(8,128)(2,1)S(1)} %collective-permute-done.39.r2, ...), custom_call_target="tpu_custom_call" | custom-call | flops 524288 | bytes 1000 | tf_op jit(solution)/shard_map/pallas_call | solution.py:402
  171.3 2.3 %shard_map.284 = (f32[192,2304]{1,0:T(8,128)}, f32[192,768]{1,0:T(8,128)}, f32[192]{0:T(256)}, f32[192]{0:T(256)}, f32[192]{0:T(256)}, /*index=5*/f32[192]{0:T(2...) custom-call(s32[3]{0:T(128)S(1)} %copy-done.3, ...), custom_call_target="tpu_custom_call" | custom-call | flops 524288 | bytes 1000 | tf_op jit(solution)/shard_map/pallas_call | solution.py:402
  173.7 3.2 %shard_map.286 = (f32[768,768]{1,0:T(8,128)}, f32[192,3072]{1,0:T(8,128)}) custom-call(s32[3]{0:T(128)S(1)} %copy-done.3, bf16[192,768]{1,0:T(8,128)(2,1)S(1)} %shard_map.285.refs_0_, bf16[192,768]{1,0:T(8,128)(2,1)S(1)} %collective-permute-done.56.refs_1_, bf16[192,768]{1,0:T(8,128)(2,1)S(1)} %collective-permute-done.57.refs_2_, ...), custom_call_target="tpu_custom_call" | custom-call | flops 524288 | bytes 1000 | tf_op jit(solution)/shard_map/pallas_call | solution.py:402
  (91 shorter events, 11.6 us)
Async XLA Ops:
  4.3 9.2 %collective-permute-start.3 = (bf16[112,576]{1,0:T(8,128)(2,1)}, bf16[112,576]{1,0:T(8,128)(2,1)S(1)}, u32[]{:S(2)}, u32[]{:S(2)}) collective-permute-start(bf16[112,576]{1,0:T(8,128)(2,1)} %get-tuple-element.105.refs_4_), channel_id=1, source_target_pairs={{0,8},{8,0},{16,24},{24,16},{1,9},{9,1},{17,25},{25,17},{2,10},{10... | collective-permute-start | bytes 387080 | tf_op jit(solution)/shard_map/ppermute | solution.py:381
  7.4 13.5 %collective-permute-start.4 = (bf16[112,576]{1,0:T(8,128)(2,1)}, bf16[112,576]{1,0:T(8,128)(2,1)S(1)}, u32[]{:S(2)}, u32[]{:S(2)}) collective-permute-start(bf16[112,576]{1,0:T(8,128)(2,1)} %get-tuple-element.105.refs_4_), channel_id=1, source_target_pairs={{0,16},{8,24},{16,0},{24,8},{1,17},{9,25},{17,1},{25,9},{2,18},{10... | collective-permute-start | bytes 387080 | tf_op jit(solution)/shard_map/ppermute | solution.py:381
  10.0 19.4 %collective-permute-start = (bf16[264,768]{1,0:T(8,128)(2,1)}, bf16[264,768]{1,0:T(8,128)(2,1)S(1)}, u32[]{:S(2)}, u32[]{:S(2)}) collective-permute-start(bf16[264,768]{1,0:T(8,128)(2,1)} %get-tuple-element.104.refs_0_.tok_ref.c0), channel_id=1, source_target_pairs={{0,2},{1,3},{2,0},{3,1},{4,6},{5,7},{6,4},{7,5},{8,10},{9,11},{10,... | collective-permute-start | bytes 1216520 | tf_op jit(solution)/shard_map/ppermute | solution.py:377
  11.5 9.5 %collective-permute-start.5 = (bf16[112,576]{1,0:T(8,128)(2,1)}, bf16[112,576]{1,0:T(8,128)(2,1)S(1)}, u32[]{:S(2)}, u32[]{:S(2)}) collective-permute-start(bf16[112,576]{1,0:T(8,128)(2,1)} %get-tuple-element.105.refs_4_), channel_id=1, source_target_pairs={{0,24},{8,16},{16,8},{24,0},{1,25},{9,17},{17,9},{25,1},{2,26},{10... | collective-permute-start | bytes 387080 | tf_op jit(solution)/shard_map/ppermute | solution.py:381
  11.7 19.0 %collective-permute-start.1 = (bf16[264,768]{1,0:T(8,128)(2,1)}, bf16[264,768]{1,0:T(8,128)(2,1)S(1)}, u32[]{:S(2)}, u32[]{:S(2)}) collective-permute-start(bf16[264,768]{1,0:T(8,128)(2,1)} %get-tuple-element.104.refs_0_.tok_ref.c0), channel_id=1, source_target_pairs={{0,4},{1,5},{2,6},{3,7},{4,0},{5,1},{6,2},{7,3},{8,12},{9,13},{10,... | collective-permute-start | bytes 1216520 | tf_op jit(solution)/shard_map/ppermute | solution.py:377
  13.5 17.2 %collective-permute-start.2 = (bf16[264,768]{1,0:T(8,128)(2,1)}, bf16[264,768]{1,0:T(8,128)(2,1)S(1)}, u32[]{:S(2)}, u32[]{:S(2)}) collective-permute-start(bf16[264,768]{1,0:T(8,128)(2,1)} %get-tuple-element.104.refs_0_.tok_ref.c0), channel_id=1, source_target_pairs={{0,6},{1,7},{2,4},{3,5},{4,2},{5,3},{6,0},{7,1},{8,14},{9,15},{10,... | collective-permute-start | bytes 1216520 | tf_op jit(solution)/shard_map/ppermute | solution.py:377
  20.9 3.6 %collective-permute-start.6 = (bf16[112,576]{1,0:T(8,128)(2,1)S(1)}, bf16[112,576]{1,0:T(8,128)(2,1)S(1)}, u32[]{:S(2)}, u32[]{:S(2)}) collective-permute-start(bf16[112,576]{1,0:T(8,128)(2,1)S(1)} %collective-permute-done.3.refs_5_), channel_id=1, source_target_pairs={{0,1},{1,0},{2,3},{3,2},{4,5},{5,4},{6,7},{7,6},{8,9},{9,8},{10,11... | collective-permute-start | bytes 387080 | tf_op jit(solution)/shard_map/ppermute | solution.py:373
  20.9 5.8 %collective-permute-start.7 = (bf16[112,576]{1,0:T(8,128)(2,1)S(1)}, bf16[112,576]{1,0:T(8,128)(2,1)S(1)}, u32[]{:S(2)}, u32[]{:S(2)}) collective-permute-start(bf16[112,576]{1,0:T(8,128)(2,1)S(1)} %collective-permute-done.4.refs_6_), channel_id=1, source_target_pairs={{0,1},{1,0},{2,3},{3,2},{4,5},{5,4},{6,7},{7,6},{8,9},{9,8},{10,11... | collective-permute-start | bytes 387080 | tf_op jit(solution)/shard_map/ppermute | solution.py:373
  24.6 21.2 %collective-permute-start.16 = (bf16[288,768]{1,0:T(8,128)(2,1)}, bf16[288,768]{1,0:T(8,128)(2,1)S(1)}, u32[]{:S(2)}, u32[]{:S(2)}) collective-permute-start(bf16[288,768]{1,0:T(8,128)(2,1)} %get-tuple-element.114.refs_8_), channel_id=1, source_target_pairs={{0,8},{8,0},{16,24},{24,16},{1,9},{9,1},{17,25},{25,17},{2,10},{10... | collective-permute-start | bytes 1327112 | tf_op jit(solution)/shard_map/ppermute | solution.py:381
  26.8 1.4 collective-permute-start.8
  28.1 33.1 %collective-permute-start.17 = (bf16[288,768]{1,0:T(8,128)(2,1)}, bf16[288,768]{1,0:T(8,128)(2,1)S(1)}, u32[]{:S(2)}, u32[]{:S(2)}) collective-permute-start(bf16[288,768]{1,0:T(8,128)(2,1)} %get-tuple-element.114.refs_8_), channel_id=1, source_target_pairs={{0,16},{8,24},{16,0},{24,8},{1,17},{9,25},{17,1},{25,9},{2,18},{10... | collective-permute-start | bytes 1327112 | tf_op jit(solution)/shard_map/ppermute | solution.py:381
  29.4 31.9 %collective-permute-start.18 = (bf16[288,768]{1,0:T(8,128)(2,1)}, bf16[288,768]{1,0:T(8,128)(2,1)S(1)}, u32[]{:S(2)}, u32[]{:S(2)}) collective-permute-start(bf16[288,768]{1,0:T(8,128)(2,1)} %get-tuple-element.114.refs_8_), channel_id=1, source_target_pairs={{0,24},{8,16},{16,8},{24,0},{1,25},{9,17},{17,9},{25,1},{2,26},{10... | collective-permute-start | bytes 1327112 | tf_op jit(solution)/shard_map/ppermute | solution.py:381
  30.8 33.6 %copy-start.1 = (bf16[288,768]{1,0:T(8,128)(2,1)S(1)}, bf16[288,768]{1,0:T(8,128)(2,1)}, u32[]{:S(2)}) copy-start(bf16[288,768]{1,0:T(8,128)(2,1)} %get-tuple-element.114.refs_8_) | copy-start | bytes 1327108
  32.7 1.4 collective-permute-start.10
  32.8 1.5 collective-permute-start.11
  34.2 1.5 collective-permute-start.9
  34.3 1.4 collective-permute-start.12
  40.9 20.3 %collective-permute-start.13 = (bf16[512,192]{1,0:T(8,128)(2,1)S(1)}, bf16[512,192]{1,0:T(8,128)(2,1)S(1)}, u32[]{:S(2)}, u32[]{:S(2)}) collective-permute-start(bf16[512,192]{1,0:T(8,128)(2,1)S(1)} %get-tuple-element.112.refs_4_), channel_id=1, source_target_pairs={{0,2},{1,3},{2,0},{3,1},{4,6},{5,7},{6,4},{7,5},{8,10},{9,11},{10,... | collective-permute-start | bytes 589832 | tf_op jit(solution)/shard_map/ppermute | solution.py:377
  42.6 18.7 %collective-permute-start.14 = (bf16[512,192]{1,0:T(8,128)(2,1)S(1)}, bf16[512,192]{1,0:T(8,128)(2,1)S(1)}, u32[]{:S(2)}, u32[]{:S(2)}) collective-permute-start(bf16[512,192]{1,0:T(8,128)(2,1)S(1)} %get-tuple-element.112.refs_4_), channel_id=1, source_target_pairs={{0,4},{1,5},{2,6},{3,7},{4,0},{5,1},{6,2},{7,3},{8,12},{9,13},{10,... | collective-permute-start | bytes 589832 | tf_op jit(solution)/shard_map/ppermute | solution.py:377
  45.8 15.5 %collective-permute-start.15 = (bf16[512,192]{1,0:T(8,128)(2,1)S(1)}, bf16[512,192]{1,0:T(8,128)(2,1)S(1)}, u32[]{:S(2)}, u32[]{:S(2)}) collective-permute-start(bf16[512,192]{1,0:T(8,128)(2,1)S(1)} %get-tuple-element.112.refs_4_), channel_id=1, source_target_pairs={{0,6},{1,7},{2,4},{3,5},{4,2},{5,3},{6,0},{7,1},{8,14},{9,15},{10,... | collective-permute-start | bytes 589832 | tf_op jit(solution)/shard_map/ppermute | solution.py:377
  61.3 1.9 %collective-permute-start.19 = (bf16[288,768]{1,0:T(8,128)(2,1)S(1)}, bf16[288,768]{1,0:T(8,128)(2,1)S(1)}, u32[]{:S(2)}, u32[]{:S(2)}) collective-permute-start(bf16[288,768]{1,0:T(8,128)(2,1)S(1)} %collective-permute-done.16.refs_9_), channel_id=1, source_target_pairs={{0,1},{1,0},{2,3},{3,2},{4,5},{5,4},{6,7},{7,6},{8,9},{9,8},{10,11... | collective-permute-start | bytes 1327112 | tf_op jit(solution)/shard_map/ppermute | solution.py:373
  61.3 2.4 %collective-permute-start.20 = (bf16[288,768]{1,0:T(8,128)(2,1)S(1)}, bf16[288,768]{1,0:T(8,128)(2,1)S(1)}, u32[]{:S(2)}, u32[]{:S(2)}) collective-permute-start(bf16[288,768]{1,0:T(8,128)(2,1)S(1)} %collective-permute-done.17.refs_10_), channel_id=1, source_target_pairs={{0,1},{1,0},{2,3},{3,2},{4,5},{5,4},{6,7},{7,6},{8,9},{9,8},{10,11... | collective-permute-start | bytes 1327112 | tf_op jit(solution)/shard_map/ppermute | solution.py:373
  61.8 2.5 %collective-permute-start.21 = (bf16[288,768]{1,0:T(8,128)(2,1)S(1)}, bf16[288,768]{1,0:T(8,128)(2,1)S(1)}, u32[]{:S(2)}, u32[]{:S(2)}) collective-permute-start(bf16[288,768]{1,0:T(8,128)(2,1)S(1)} %collective-permute-done.18.refs_11_), channel_id=1, source_target_pairs={{0,1},{1,0},{2,3},{3,2},{4,5},{5,4},{6,7},{7,6},{8,9},{9,8},{10,11... | collective-permute-start | bytes 1327112 | tf_op jit(solution)/shard_map/ppermute | solution.py:373
  69.9 7.0 %collective-permute-start.22 = (bf16[128,768]{1,0:T(8,128)(2,1)S(1)}, bf16[128,768]{1,0:T(8,128)(2,1)S(1)}, u32[]{:S(2)}, u32[]{:S(2)}) collective-permute-start(bf16[128,768]{1,0:T(8,128)(2,1)S(1)} %get-tuple-element.121), channel_id=1, source_target_pairs={{0,2},{1,3},{2,0},{3,1},{4,6},{5,7},{6,4},{7,5},{8,10},{9,11},{10,... | collective-permute-start | bytes 589832 | tf_op jit(solution)/shard_map/ppermute | solution.py:377
  79.1 2.6 %collective-permute-start.28 = (bf16[192,768]{1,0:T(8,128)(2,1)S(1)}, bf16[192,768]{1,0:T(8,128)(2,1)S(1)}, u32[]{:S(2)}, u32[]{:S(2)}) collective-permute-start(bf16[192,768]{1,0:T(8,128)(2,1)S(1)} %get-tuple-element.133), channel_id=1, source_target_pairs={{0,1},{1,0},{2,3},{3,2},{4,5},{5,4},{6,7},{7,6},{8,9},{9,8},{10,11... | collective-permute-start | bytes 884744 | tf_op jit(solution)/shard_map/ppermute | solution.py:373
  79.2 4.0 %collective-permute-start.29 = (bf16[192,768]{1,0:T(8,128)(2,1)S(1)}, bf16[192,768]{1,0:T(8,128)(2,1)S(1)}, u32[]{:S(2)}, u32[]{:S(2)}) collective-permute-start(bf16[192,768]{1,0:T(8,128)(2,1)S(1)} %get-tuple-element.134), channel_id=1, source_target_pairs={{0,1},{1,0},{2,3},{3,2},{4,5},{5,4},{6,7},{7,6},{8,9},{9,8},{10,11... | collective-permute-start | bytes 884744 | tf_op jit(solution)/shard_map/ppermute | solution.py:373
  79.7 3.5 %collective-permute-start.30 = (bf16[192,768]{1,0:T(8,128)(2,1)S(1)}, bf16[192,768]{1,0:T(8,128)(2,1)S(1)}, u32[]{:S(2)}, u32[]{:S(2)}) collective-permute-start(bf16[192,768]{1,0:T(8,128)(2,1)S(1)} %get-tuple-element.135), channel_id=1, source_target_pairs={{0,1},{1,0},{2,3},{3,2},{4,5},{5,4},{6,7},{7,6},{8,9},{9,8},{10,11... | collective-permute-start | bytes 884744 | tf_op jit(solution)/shard_map/ppermute | solution.py:373
  79.8 3.4 %collective-permute-start.31 = (bf16[192,768]{1,0:T(8,128)(2,1)S(1)}, bf16[192,768]{1,0:T(8,128)(2,1)S(1)}, u32[]{:S(2)}, u32[]{:S(2)}) collective-permute-start(bf16[192,768]{1,0:T(8,128)(2,1)S(1)} %get-tuple-element.136), channel_id=1, source_target_pairs={{0,1},{1,0},{2,3},{3,2},{4,5},{5,4},{6,7},{7,6},{8,9},{9,8},{10,11... | collective-permute-start | bytes 884744 | tf_op jit(solution)/shard_map/ppermute | solution.py:373
  80.2 14.2 %collective-permute-start.23 = (bf16[128,768]{1,0:T(8,128)(2,1)S(1)}, bf16[128,768]{1,0:T(8,128)(2,1)S(1)}, u32[]{:S(2)}, u32[]{:S(2)}) collective-permute-start(bf16[128,768]{1,0:T(8,128)(2,1)S(1)} %get-tuple-element.122), channel_id=1, source_target_pairs={{0,4},{1,5},{2,6},{3,7},{4,0},{5,1},{6,2},{7,3},{8,12},{9,13},{10,... | collective-permute-start | bytes 589832 | tf_op jit(solution)/shard_map/ppermute | solution.py:377
  81.7 12.7 %collective-permute-start.24 = (bf16[128,768]{1,0:T(8,128)(2,1)S(1)}, bf16[128,768]{1,0:T(8,128)(2,1)S(1)}, u32[]{:S(2)}, u32[]{:S(2)}) collective-permute-start(bf16[128,768]{1,0:T(8,128)(2,1)S(1)} %get-tuple-element.123), channel_id=1, source_target_pairs={{0,6},{1,7},{2,4},{3,5},{4,2},{5,3},{6,0},{7,1},{8,14},{9,15},{10,... | collective-permute-start | bytes 589832 | tf_op jit(solution)/shard_map/ppermute | solution.py:377
  84.0 30.1 %collective-permute-start.32 = (bf16[192,768]{1,0:T(8,128)(2,1)S(1)}, bf16[192,768]{1,0:T(8,128)(2,1)S(1)}, u32[]{:S(2)}, u32[]{:S(2)}) collective-permute-start(bf16[192,768]{1,0:T(8,128)(2,1)S(1)} %get-tuple-element.141), channel_id=1, source_target_pairs={{0,8},{8,0},{16,24},{24,16},{1,9},{9,1},{17,25},{25,17},{2,10},{10... | collective-permute-start | bytes 884744 | tf_op jit(solution)/shard_map/ppermute | solution.py:381
  93.4 22.1 %collective-permute-start.33 = (bf16[192,768]{1,0:T(8,128)(2,1)S(1)}, bf16[192,768]{1,0:T(8,128)(2,1)S(1)}, u32[]{:S(2)}, u32[]{:S(2)}) collective-permute-start(bf16[192,768]{1,0:T(8,128)(2,1)S(1)} %get-tuple-element.142), channel_id=1, source_target_pairs={{0,16},{8,24},{16,0},{24,8},{1,17},{9,25},{17,1},{25,9},{2,18},{10... | collective-permute-start | bytes 884744 | tf_op jit(solution)/shard_map/ppermute | solution.py:381
  95.4 7.9 %collective-permute-start.25 = (bf16[128,768]{1,0:T(8,128)(2,1)S(1)}, bf16[128,768]{1,0:T(8,128)(2,1)S(1)}, u32[]{:S(2)}, u32[]{:S(2)}) collective-permute-start(bf16[128,768]{1,0:T(8,128)(2,1)S(1)} %get-tuple-element.125.a0.refs_8_), channel_id=1, source_target_pairs={{0,2},{1,3},{2,0},{3,1},{4,6},{5,7},{6,4},{7,5},{8,10},{9,11},{10,... | collective-permute-start | bytes 589832 | tf_op jit(solution)/shard_map/ppermute | solution.py:377
  96.0 9.4 %collective-permute-start.26 = (bf16[128,768]{1,0:T(8,128)(2,1)S(1)}, bf16[128,768]{1,0:T(8,128)(2,1)S(1)}, u32[]{:S(2)}, u32[]{:S(2)}) collective-permute-start(bf16[128,768]{1,0:T(8,128)(2,1)S(1)} %get-tuple-element.125.a0.refs_8_), channel_id=1, source_target_pairs={{0,4},{1,5},{2,6},{3,7},{4,0},{5,1},{6,2},{7,3},{8,12},{9,13},{10,... | collective-permute-start | bytes 589832 | tf_op jit(solution)/shard_map/ppermute | solution.py:377
  97.5 9.2 %collective-permute-start.27 = (bf16[128,768]{1,0:T(8,128)(2,1)S(1)}, bf16[128,768]{1,0:T(8,128)(2,1)S(1)}, u32[]{:S(2)}, u32[]{:S(2)}) collective-permute-start(bf16[128,768]{1,0:T(8,128)(2,1)S(1)} %get-tuple-element.125.a0.refs_8_), channel_id=1, source_target_pairs={{0,6},{1,7},{2,4},{3,5},{4,2},{5,3},{6,0},{7,1},{8,14},{9,15},{10,... | collective-permute-start | bytes 589832 | tf_op jit(solution)/shard_map/ppermute | solution.py:377
  103.3 19.8 %collective-permute-start.45 = (bf16[192,768]{1,0:T(8,128)(2,1)S(1)}, bf16[192,768]{1,0:T(8,128)(2,1)S(1)}, u32[]{:S(2)}, u32[]{:S(2)}) collective-permute-start(bf16[192,768]{1,0:T(8,128)(2,1)S(1)} %get-tuple-element.171), channel_id=1, source_target_pairs={{0,24},{8,16},{16,8},{24,0},{1,25},{9,17},{17,9},{25,1},{2,26},{10... | collective-permute-start | bytes 884744 | tf_op jit(solution)/shard_map/ppermute | solution.py:381
  113.4 2.1 %collective-permute-start.34 = (bf16[256,192]{1,0:T(8,128)(2,1)S(1)}, bf16[256,192]{1,0:T(8,128)(2,1)S(1)}, u32[]{:S(2)}, u32[]{:S(2)}) collective-permute-start(bf16[256,192]{1,0:T(8,128)(2,1)S(1)} %get-tuple-element.145), channel_id=1, source_target_pairs={{0,1},{1,0},{2,3},{3,2},{4,5},{5,4},{6,7},{7,6},{8,9},{9,8},{10,11... | collective-permute-start | bytes 294920 | tf_op jit(solution)/shard_map/ppermute | solution.py:373
  113.5 2.0 %collective-permute-start.35 = (bf16[256,192]{1,0:T(8,128)(2,1)S(1)}, bf16[256,192]{1,0:T(8,128)(2,1)S(1)}, u32[]{:S(2)}, u32[]{:S(2)}) collective-permute-start(bf16[256,192]{1,0:T(8,128)(2,1)S(1)} %get-tuple-element.146), channel_id=1, source_target_pairs={{0,1},{1,0},{2,3},{3,2},{4,5},{5,4},{6,7},{7,6},{8,9},{9,8},{10,11... | collective-permute-start | bytes 294920 | tf_op jit(solution)/shard_map/ppermute | solution.py:373
  114.0 1.5 collective-permute-start.36
  115.5 1.3 collective-permute-start.37
  120.3 1.4 collective-permute-start.41
  120.5 1.4 collective-permute-start.42
  120.9 1.4 collective-permute-start.43
  121.0 1.4 collective-permute-start.44
  123.1 10.0 %collective-permute-start.46 = (bf16[104,768]{1,0:T(8,128)(2,1)S(1)}, bf16[104,768]{1,0:T(8,128)(2,1)S(1)}, u32[]{:S(2)}, u32[]{:S(2)}) collective-permute-start(bf16[104,768]{1,0:T(8,128)(2,1)S(1)} %get-tuple-element.172), channel_id=1, source_target_pairs={{0,8},{8,0},{16,24},{24,16},{1,9},{9,1},{17,25},{25,17},{2,10},{10... | collective-permute-start | bytes 479240 | tf_op jit(solution)/shard_map/ppermute | solution.py:381
  128.5 19.3 %collective-permute-start.38 = (bf16[256,768]{1,0:T(8,128)(2,1)S(1)}, bf16[256,768]{1,0:T(8,128)(2,1)S(1)}, u32[]{:S(2)}, u32[]{:S(2)}) collective-permute-start(bf16[256,768]{1,0:T(8,128)(2,1)S(1)} %get-tuple-element.155), channel_id=1, source_target_pairs={{0,2},{1,3},{2,0},{3,1},{4,6},{5,7},{6,4},{7,5},{8,10},{9,11},{10,... | collective-permute-start | bytes 1179656 | tf_op jit(solution)/shard_map/ppermute | solution.py:377
  129.8 19.4 %collective-permute-start.39 = (bf16[256,768]{1,0:T(8,128)(2,1)S(1)}, bf16[256,768]{1,0:T(8,128)(2,1)S(1)}, u32[]{:S(2)}, u32[]{:S(2)}) collective-permute-start(bf16[256,768]{1,0:T(8,128)(2,1)S(1)} %get-tuple-element.156), channel_id=1, source_target_pairs={{0,4},{1,5},{2,6},{3,7},{4,0},{5,1},{6,2},{7,3},{8,12},{9,13},{10,... | collective-permute-start | bytes 1179656 | tf_op jit(solution)/shard_map/ppermute | solution.py:377
  130.7 14.4 %collective-permute-start.47 = (bf16[104,768]{1,0:T(8,128)(2,1)S(1)}, bf16[104,768]{1,0:T(8,128)(2,1)S(1)}, u32[]{:S(2)}, u32[]{:S(2)}) collective-permute-start(bf16[104,768]{1,0:T(8,128)(2,1)S(1)} %get-tuple-element.173), channel_id=1, source_target_pairs={{0,16},{8,24},{16,0},{24,8},{1,17},{9,25},{17,1},{25,9},{2,18},{10... | collective-permute-start | bytes 479240 | tf_op jit(solution)/shard_map/ppermute | solution.py:381
  131.7 14.7 %collective-permute-start.48 = (bf16[104,768]{1,0:T(8,128)(2,1)S(1)}, bf16[104,768]{1,0:T(8,128)(2,1)S(1)}, u32[]{:S(2)}, u32[]{:S(2)}) collective-permute-start(bf16[104,768]{1,0:T(8,128)(2,1)S(1)} %get-tuple-element.174), channel_id=1, source_target_pairs={{0,24},{8,16},{16,8},{24,0},{1,25},{9,17},{17,9},{25,1},{2,26},{10... | collective-permute-start | bytes 479240 | tf_op jit(solution)/shard_map/ppermute | solution.py:381
  133.1 17.5 %collective-permute-start.40 = (bf16[256,768]{1,0:T(8,128)(2,1)S(1)}, bf16[256,768]{1,0:T(8,128)(2,1)S(1)}, u32[]{:S(2)}, u32[]{:S(2)}) collective-permute-start(bf16[256,768]{1,0:T(8,128)(2,1)S(1)} %get-tuple-element.157), channel_id=1, source_target_pairs={{0,6},{1,7},{2,4},{3,5},{4,2},{5,3},{6,0},{7,1},{8,14},{9,15},{10,... | collective-permute-start | bytes 1179656 | tf_op jit(solution)/shard_map/ppermute | solution.py:377
  145.1 10.2 %collective-permute-start.56 = (bf16[192,768]{1,0:T(8,128)(2,1)S(1)}, bf16[192,768]{1,0:T(8,128)(2,1)S(1)}, u32[]{:S(2)}, u32[]{:S(2)}) collective-permute-start(bf16[192,768]{1,0:T(8,128)(2,1)S(1)} %shard_map.285.refs_0_), channel_id=1, source_target_pairs={{0,2},{1,3},{2,0},{3,1},{4,6},{5,7},{6,4},{7,5},{8,10},{9,11},{10,... | collective-permute-start | bytes 884744 | tf_op jit(solution)/shard_map/ppermute | solution.py:377
  146.5 10.4 %collective-permute-start.57 = (bf16[192,768]{1,0:T(8,128)(2,1)S(1)}, bf16[192,768]{1,0:T(8,128)(2,1)S(1)}, u32[]{:S(2)}, u32[]{:S(2)}) collective-permute-start(bf16[192,768]{1,0:T(8,128)(2,1)S(1)} %shard_map.285.refs_0_), channel_id=1, source_target_pairs={{0,4},{1,5},{2,6},{3,7},{4,0},{5,1},{6,2},{7,3},{8,12},{9,13},{10,... | collective-permute-start | bytes 884744 | tf_op jit(solution)/shard_map/ppermute | solution.py:377
  147.8 10.9 %collective-permute-start.49 = (bf16[104,768]{1,0:T(8,128)(2,1)S(1)}, bf16[104,768]{1,0:T(8,128)(2,1)S(1)}, u32[]{:S(2)}, u32[]{:S(2)}) collective-permute-start(bf16[104,768]{1,0:T(8,128)(2,1)S(1)} %shard_map.283.refs_0_), channel_id=1, source_target_pairs={{0,2},{1,3},{2,0},{3,1},{4,6},{5,7},{6,4},{7,5},{8,10},{9,11},{10,... | collective-permute-start | bytes 479240 | tf_op jit(solution)/shard_map/ppermute | solution.py:377
  149.2 17.6 %collective-permute-start.58 = (bf16[192,768]{1,0:T(8,128)(2,1)S(1)}, bf16[192,768]{1,0:T(8,128)(2,1)S(1)}, u32[]{:S(2)}, u32[]{:S(2)}) collective-permute-start(bf16[192,768]{1,0:T(8,128)(2,1)S(1)} %shard_map.285.refs_0_), channel_id=1, source_target_pairs={{0,6},{1,7},{2,4},{3,5},{4,2},{5,3},{6,0},{7,1},{8,14},{9,15},{10,... | collective-permute-start | bytes 884744 | tf_op jit(solution)/shard_map/ppermute | solution.py:377
  150.7 16.1 %collective-permute-start.50 = (bf16[104,768]{1,0:T(8,128)(2,1)S(1)}, bf16[104,768]{1,0:T(8,128)(2,1)S(1)}, u32[]{:S(2)}, u32[]{:S(2)}) collective-permute-start(bf16[104,768]{1,0:T(8,128)(2,1)S(1)} %shard_map.283.refs_0_), channel_id=1, source_target_pairs={{0,4},{1,5},{2,6},{3,7},{4,0},{5,1},{6,2},{7,3},{8,12},{9,13},{10,... | collective-permute-start | bytes 479240 | tf_op jit(solution)/shard_map/ppermute | solution.py:377
  155.3 13.2 %collective-permute-start.51 = (bf16[104,768]{1,0:T(8,128)(2,1)S(1)}, bf16[104,768]{1,0:T(8,128)(2,1)S(1)}, u32[]{:S(2)}, u32[]{:S(2)}) collective-permute-start(bf16[104,768]{1,0:T(8,128)(2,1)S(1)} %shard_map.283.refs_0_), channel_id=1, source_target_pairs={{0,6},{1,7},{2,4},{3,5},{4,2},{5,3},{6,0},{7,1},{8,14},{9,15},{10,... | collective-permute-start | bytes 479240 | tf_op jit(solution)/shard_map/ppermute | solution.py:377
  156.9 11.5 %collective-permute-start.52 = (bf16[104,768]{1,0:T(8,128)(2,1)S(1)}, bf16[104,768]{1,0:T(8,128)(2,1)S(1)}, u32[]{:S(2)}, u32[]{:S(2)}) collective-permute-start(bf16[104,768]{1,0:T(8,128)(2,1)S(1)} %shard_map.283.refs_0_), channel_id=1, source_target_pairs={{0,1},{1,0},{2,3},{3,2},{4,5},{5,4},{6,7},{7,6},{8,9},{9,8},{10,11... | collective-permute-start | bytes 479240 | tf_op jit(solution)/shard_map/ppermute | solution.py:373
  158.7 10.3 %collective-permute-start.53 = (bf16[104,768]{1,0:T(8,128)(2,1)S(1)}, bf16[104,768]{1,0:T(8,128)(2,1)S(1)}, u32[]{:S(2)}, u32[]{:S(2)}) collective-permute-start(bf16[104,768]{1,0:T(8,128)(2,1)S(1)} %collective-permute-done.49.refs_1_), channel_id=1, source_target_pairs={{0,1},{1,0},{2,3},{3,2},{4,5},{5,4},{6,7},{7,6},{8,9},{9,8},{10,11... | collective-permute-start | bytes 479240 | tf_op jit(solution)/shard_map/ppermute | solution.py:373
  166.8 2.2 %collective-permute-start.54 = (bf16[104,768]{1,0:T(8,128)(2,1)S(1)}, bf16[104,768]{1,0:T(8,128)(2,1)S(1)}, u32[]{:S(2)}, u32[]{:S(2)}) collective-permute-start(bf16[104,768]{1,0:T(8,128)(2,1)S(1)} %collective-permute-done.50.refs_2_), channel_id=1, source_target_pairs={{0,1},{1,0},{2,3},{3,2},{4,5},{5,4},{6,7},{7,6},{8,9},{9,8},{10,11... | collective-permute-start | bytes 479240 | tf_op jit(solution)/shard_map/ppermute | solution.py:373
  166.8 6.8 %collective-permute-start.59 = (bf16[192,768]{1,0:T(8,128)(2,1)S(1)}, bf16[192,768]{1,0:T(8,128)(2,1)S(1)}, u32[]{:S(2)}, u32[]{:S(2)}) collective-permute-start(bf16[192,768]{1,0:T(8,128)(2,1)S(1)} %shard_map.285.refs_0_), channel_id=1, source_target_pairs={{0,1},{1,0},{2,3},{3,2},{4,5},{5,4},{6,7},{7,6},{8,9},{9,8},{10,11... | collective-permute-start | bytes 884744 | tf_op jit(solution)/shard_map/ppermute | solution.py:373
  168.4 5.2 %collective-permute-start.60 = (bf16[192,768]{1,0:T(8,128)(2,1)S(1)}, bf16[192,768]{1,0:T(8,128)(2,1)S(1)}, u32[]{:S(2)}, u32[]{:S(2)}) collective-permute-start(bf16[192,768]{1,0:T(8,128)(2,1)S(1)} %collective-permute-done.56.refs_1_), channel_id=1, source_target_pairs={{0,1},{1,0},{2,3},{3,2},{4,5},{5,4},{6,7},{7,6},{8,9},{9,8},{10,11... | collective-permute-start | bytes 884744 | tf_op jit(solution)/shard_map/ppermute | solution.py:373
  168.4 5.2 %collective-permute-start.61 = (bf16[192,768]{1,0:T(8,128)(2,1)S(1)}, bf16[192,768]{1,0:T(8,128)(2,1)S(1)}, u32[]{:S(2)}, u32[]{:S(2)}) collective-permute-start(bf16[192,768]{1,0:T(8,128)(2,1)S(1)} %collective-permute-done.57.refs_2_), channel_id=1, source_target_pairs={{0,1},{1,0},{2,3},{3,2},{4,5},{5,4},{6,7},{7,6},{8,9},{9,8},{10,11... | collective-permute-start | bytes 884744 | tf_op jit(solution)/shard_map/ppermute | solution.py:373
  168.9 4.7 %collective-permute-start.62 = (bf16[192,768]{1,0:T(8,128)(2,1)S(1)}, bf16[192,768]{1,0:T(8,128)(2,1)S(1)}, u32[]{:S(2)}, u32[]{:S(2)}) collective-permute-start(bf16[192,768]{1,0:T(8,128)(2,1)S(1)} %collective-permute-done.58.refs_3_), channel_id=1, source_target_pairs={{0,1},{1,0},{2,3},{3,2},{4,5},{5,4},{6,7},{7,6},{8,9},{9,8},{10,11... | collective-permute-start | bytes 884744 | tf_op jit(solution)/shard_map/ppermute | solution.py:373
  169.0 2.3 %collective-permute-start.55 = (bf16[104,768]{1,0:T(8,128)(2,1)S(1)}, bf16[104,768]{1,0:T(8,128)(2,1)S(1)}, u32[]{:S(2)}, u32[]{:S(2)}) collective-permute-start(bf16[104,768]{1,0:T(8,128)(2,1)S(1)} %collective-permute-done.51.refs_3_), channel_id=1, source_target_pairs={{0,1},{1,0},{2,3},{3,2},{4,5},{5,4},{6,7},{7,6},{8,9},{9,8},{10,11... | collective-permute-start | bytes 479240 | tf_op jit(solution)/shard_map/ppermute | solution.py:373
  (5 other events, 142.5 us)

commit v4 on v3

--- a/solution.py
+++ b/solution.py
@@ -440,18 +440,24 @@
     )
 
 
-def pack_body(pos, w_ref, tok_ref, cot_ref, ids_ref, *refs):
+def pack_body(pos, w_ref, tok_ref, cot_ref, wo_ref, wu_ref, wd_ref, ids_ref, *refs):
     small, up_ref = refs[:8], refs[8]
-    piece_ref, mate_ref, pack_ref, w_rows, sem = refs[9:]
+    piece_ref, mate_ref, pack_ref, rest_ref, rest_mate, w_rows, up_rows, sem = refs[9:]
     k, c = pos[1], pos[2]
-    copies = []
-    for n, half in enumerate((c, 1 - c)):
+    copies = [
+        pltpu.make_async_copy(tok_ref.at[0], pack_ref.at[pl.ds(0, ROWS), :], sem.at[0]),
+        pltpu.make_async_copy(cot_ref.at[0], pack_ref.at[pl.ds(ROWS, ROWS), :], sem.at[1]),
+    ]
+    for n, (half, dst) in enumerate(((c, rest_ref), (1 - c, rest_mate))):
         rows = pl.ds(pl.multiple_of(half * HALF, 32), HALF)
-        copies.append(pltpu.make_async_copy(w_ref.at[rows, :], w_rows.at[n], sem.at[n]))
-    copies += [
-        pltpu.make_async_copy(tok_ref.at[0], pack_ref.at[pl.ds(0, ROWS), :], sem.at[2]),
-        pltpu.make_async_copy(cot_ref.at[0], pack_ref.at[pl.ds(ROWS, ROWS), :], sem.at[3]),
-    ]
+        down_rows = pl.ds(pl.multiple_of(k * QUARTER + half * HALF, 32), HALF)
+        out_part, down_part = dst.at[pl.ds(0, HALF), :], dst.at[pl.ds(2 * HALF, HALF), :]
+        copies += [
+            pltpu.make_async_copy(w_ref.at[rows, :], w_rows.at[n], sem.at[2 + 4 * n]),
+            pltpu.make_async_copy(wu_ref.at[rows, :], up_rows.at[n], sem.at[3 + 4 * n]),
+            pltpu.make_async_copy(wo_ref.at[rows, :], out_part, sem.at[4 + 4 * n]),
+            pltpu.make_async_copy(wd_ref.at[down_rows, :], down_part, sem.at[5 + 4 * n]),
+        ]
     for copy in copies:
         copy.start()
     up = up_ref[...].astype(f32).reshape(1, WIDTH)
@@ -464,39 +470,8 @@
     piece_ref[HALF:, :] = lines.astype(bf16)
     ids = jnp.concatenate([ids_ref[...].astype(f32), jnp.zeros((1, WIDTH - ROWS), f32)], 1)
     pack_ref[2 * ROWS :, :] = jnp.concatenate([ids, jnp.zeros((7, WIDTH), f32)], 0).astype(bf16)
-    copies[0].wait()
-    copies[1].wait()
-    for q in range(4):
-
-        @pl.when(k == q)
-        def _():
-            for p in range(3):
-                at = WIDTH * p + QUARTER * q
-                cols = slice(QUARTER * p, QUARTER * (p + 1))
-                piece_ref[:HALF, cols] = w_rows[0, :, at : at + QUARTER]
-                mate_ref[:HALF, cols] = w_rows[1, :, at : at + QUARTER]
-
-    copies[2].wait()
-    copies[3].wait()
-
-
-def rest_body(pos, wo_ref, wu_ref, wd_ref, out_ref, mate_ref, up_rows, sem):
-    k, c = pos[1], pos[2]
-    copies = []
-    for n, (half, dst) in enumerate(((c, out_ref), (1 - c, mate_ref))):
-        rows = pl.ds(pl.multiple_of(half * HALF, 32), HALF)
-        down_rows = pl.ds(pl.multiple_of(k * QUARTER + half * HALF, 32), HALF)
-        copies += [
-            pltpu.make_async_copy(wu_ref.at[rows, :], up_rows.at[n], sem.at[3 * n]),
-            pltpu.make_async_copy(wo_ref.at[rows, :], dst.at[pl.ds(0, HALF), :], sem.at[3 * n + 1]),
-            pltpu.make_async_copy(
-                wd_ref.at[down_rows, :], dst.at[pl.ds(2 * HALF, HALF), :], sem.at[3 * n + 2]
-            ),
-        ]
     for copy in copies:
-        copy.start()
-    copies[0].wait()
-    copies[3].wait()
+        copy.wait()
     for q in range(4):
 
         @pl.when(k == q)
@@ -504,11 +479,11 @@
             for p in range(4):
                 at = WIDTH * p + QUARTER * q
                 cols = slice(QUARTER * p, QUARTER * (p + 1))
-                out_ref[HALF : 2 * HALF, cols] = up_rows[0, :, at : at + QUARTER]
-                mate_ref[HALF : 2 * HALF, cols] = up_rows[1, :, at : at + QUARTER]
-
-    for n in (1, 2, 4, 5):
-        copies[n].wait()
+                if p < 3:
+                    piece_ref[:HALF, cols] = w_rows[0, :, at : at + QUARTER]
+                    mate_ref[:HALF, cols] = w_rows[1, :, at : at + QUARTER]
+                rest_ref[HALF : 2 * HALF, cols] = up_rows[0, :, at : at + QUARTER]
+                rest_mate[HALF : 2 * HALF, cols] = up_rows[1, :, at : at + QUARTER]
 
 
 def qkv_body(pos, *refs):
@@ -649,7 +624,8 @@
         ref[...] = down[ROWS * r : ROWS * (r + 1)].astype(bf16)
 
 
-def feed_grad_body(pos, act_ref, n2_ref, pre_ref, c0, c1, c2, c3, x0, x1, x2, x3, own_ref, wg):
+def feed_grad_body(pos, act_ref, n2_ref, pre_ref, c0, c1, c2, c3, *refs):
+    sends, (own_ref, wg) = refs[:8], refs[8:]
     s, c = pos[0], pos[2]
     grads = jnp.concatenate([ref[ROWS : 2 * ROWS, :] for ref in (c0, c1, c2, c3)], 0)
     for part in range(2):
@@ -658,12 +634,21 @@
         else:
             wg[...] = t_dot(n2_ref[...], pre_ref[...])
         rows = slice(HALF * part, HALF * part + HALF)
-        for m, send in enumerate((x0, x1, x2, x3)):
+        for m in range(4):
             z = s ^ m
             at = pl.ds(pl.multiple_of(z * QUARTER + c * HALF, 32), HALF)
             own_ref[m, rows, :] = wg[at, :]
             at = pl.ds(pl.multiple_of(z * QUARTER + (1 - c) * HALF, 32), HALF)
-            send[rows, :] = wg[at, :].astype(bf16)
+            sends[4 * part + m][...] = wg[at, :].astype(bf16)
+
+
+def feed_halves_body(pos, own_ref, *refs):
+    got, outs = refs[:8], refs[8:]
+    for m, out in enumerate(outs):
+        for part in range(2):
+            rows = slice(HALF * part, HALF * part + HALF)
+            total = own_ref[m, rows, :] + got[4 * part + m][...].astype(f32)
+            out[rows, :] = total.astype(out.dtype)
 
 
 def halves_body(pos, own_ref, y0, y1, y2, y3, o0, o1, o2, o3):
@@ -728,8 +713,8 @@
 
 def project_grad_body(pos, *refs):
     tok, mixed, ga = refs[0:4], refs[4:8], refs[8:12]
-    normed, dq, kv_own, y0, y1, y2, y3, w_ref, vec_ref, sums_ref, d1, d2, d3 = refs[12:25]
-    x0, x1, x2, x3, own_ref, g0, g1, g2, g3, wg, sm, gk, gp = refs[25:]
+    normed, dq, kv_own, y0, y1, y2, y3, w_ref, vec_ref, sums_ref = refs[12:22]
+    x0, x1, x2, x3, own_ref, g0, g1, g2, g3, wg, sm, gk, gp = refs[22:]
     s, k, c = pos[0], pos[1], pos[2]
     gp[:, :QUARTER] = dq[...]
     got_k = jnp.concatenate([y0[...], y1[...]], 0)
@@ -755,9 +740,8 @@
     ln1_gain = jnp.sum(back * hat, 0, keepdims=True)
     ln1_bias = jnp.sum(back, 0, keepdims=True)
     g0[...] = back[:ROWS]
-    for r, ref, down in ((1, g1, d1), (2, g2, d2), (3, g3, d3)):
-        ref[:ROWS, :] = back[ROWS * r : ROWS * (r + 1)].astype(bf16)
-        ref[ROWS:, :] = down[...]
+    for r, ref in ((1, g1), (2, g2), (3, g3)):
+        ref[...] = back[ROWS * r : ROWS * (r + 1)].astype(bf16)
     gp_sums = jnp.sum(gp[...].astype(f32), 0, keepdims=True)
     out_bias = jnp.sum(ga[0][...].astype(f32), 0, keepdims=True)
     down_bias = jnp.sum(tok[0][ROWS : 2 * ROWS, :].astype(f32), 0, keepdims=True)
@@ -779,12 +763,12 @@
         (x0, x1, x2, x3)[m][...] = wg[at, :].astype(bf16)
 
 
-def rows_body(pos, g0, r1, r2, r3, d0, tok_ref, gm_ref, mid_ref, vec_ref, grad_ref, out_ref):
-    got = [ref[...].astype(f32) for ref in (r1, r2, r3)]
-    err = g0[...] + got[0][:ROWS] + got[1][:ROWS] + got[2][:ROWS]
+def rows_body(pos, g0, r1, r2, r3, d0, s1, s2, s3, tok_ref, gm_ref, mid_ref, vec_ref, *outs):
+    grad_ref, out_ref = outs
+    err = g0[...] + r1[...].astype(f32) + r2[...].astype(f32) + r3[...].astype(f32)
     hat, rstd = normal(tok_ref[:ROWS, :].astype(f32))
     grad_ref[0] = gm_ref[...] + norm_back(err, vec_ref[0:1, :], hat, rstd)
-    total = d0[...] + got[0][ROWS:] + got[1][ROWS:] + got[2][ROWS:]
+    total = d0[...] + s1[...].astype(f32) + s2[...].astype(f32) + s3[...].astype(f32)
     out_ref[0] = (mid_ref[...] + total + vec_ref[5:6, :]).astype(bf16)
 
 
@@ -859,24 +843,16 @@
     pos = jnp.stack([seq, k, core]).astype(jnp.int32)
 
     small = [ln1_gain, ln1_bias, q_bias, v_bias, out_bias, ln2_gain, ln2_bias, down_bias, up_bias]
-    piece_qkv, mate_qkv, pack = run(
+    piece_qkv, mate_qkv, pack, rest, mate_rest = run(
         pack_body,
         pos,
-        [w_qkv, tokens, cotangent, block_ids, *small],
-        [((HALF + 16, 3 * QUARTER), bf16)] * 2 + [((2 * ROWS + 8, WIDTH), bf16)],
-        [((2, HALF, 3 * WIDTH), bf16)],
-        hbm=(0, 1, 2),
-        sems=4,
-        limit=60,
-    )
-    rest, mate_rest = run(
-        rest_body,
-        pos,
-        [w_out, w_up, w_down],
-        [((3 * HALF, WIDTH), bf16)] * 2,
-        [((2, HALF, 4 * WIDTH), bf16)],
-        hbm=(0, 1, 2),
-        sems=6,
+        [w_qkv, tokens, cotangent, w_out, w_up, w_down, block_ids, *small],
+        [((HALF + 16, 3 * QUARTER), bf16)] * 2
+        + [((2 * ROWS + 8, WIDTH), bf16)]
+        + [((3 * HALF, WIDTH), bf16)] * 2,
+        [((2, HALF, 3 * WIDTH), bf16), ((2, HALF, 4 * WIDTH), bf16)],
+        hbm=range(6),
+        sems=10,
         limit=60,
     )
     got_qkv = seq_gather(piece_qkv)
@@ -919,37 +895,36 @@
     *feed_send, feed_own = run(
         feed_grad_body,
         pos,
-        [after(act, got_g[0]), normed_two, pre, *tok],
-        [(piece, bf16)] * 4 + [((4, *piece), f32)],
+        [act, normed_two, pre, *tok],
+        [((HALF, WIDTH), bf16)] * 8 + [((4, *piece), f32)],
         [((WIDTH, WIDTH), f32)],
     )
     feed_got = [core_swap(x) for x in feed_send]
+    h0, h1, h2, h3 = run(
+        feed_halves_body, pos, [feed_own, *feed_got], [(piece, f32)] + [(piece, bf16)] * 3
+    )
     grad_mid, grad_att = run(
-        middle_body, pos, [g0, *got_g, mid, tok[0], vec], [(block, f32), (block, bf16)]
+        middle_body, pos, [after(g0, h0), *got_g, mid, tok[0], vec], [(block, f32), (block, bf16)]
     )
     ga = chip_gather(grad_att)
-    h0, h1, h2, h3 = run(
-        halves_body, pos, [feed_own, *feed_got], [(piece, f32)] + [(piece, bf16)] * 3
-    )
     feed_terms = [seq_swap(h, m) for m, h in ((1, h1), (2, h2), (3, h3))]
     dq, kv_own, *pair_send = run(
         attend_grad_body,
         pos,
-        [*ga, w_out_k, after(query, h0), *pair, state],
+        [*ga, w_out_k, query, *pair, state],
         [((OWN, QUARTER), bf16), ((OWN, 2 * QUARTER), f32)] + [(half, bf16)] * 4,
         [((OWN, 2 * OWN), bf16)] * 2 + [((2 * OWN, QUARTER), bf16)] * 2,
     )
     pair_got = [core_swap(x) for x in pair_send]
-    dq, *feed_two = lax.optimization_barrier((dq, *feed_terms[:2]))
-    feed_terms = feed_two + feed_terms[2:]
+    got_d = [chip_swap(after(d, dq), m) for m, d in ((1, d1), (2, d2), (3, d3))]
     lpiece = (HALF + 8, WIDTH)
     *last_send, last_own, e0, e1, e2, e3 = run(
         project_grad_body,
         pos,
-        [*tok, *mixed, *ga, normed, dq, kv_own, *pair_got, weight_qkv, vec, sums, d1, d2, d3],
+        [*tok, *mixed, *ga, normed, dq, kv_own, *pair_got, weight_qkv, vec, sums],
         [((HALF, WIDTH), bf16)] * 4
         + [((4, *lpiece), f32), (block, f32)]
-        + [((2 * ROWS, WIDTH), bf16)] * 3,
+        + [(block, bf16)] * 3,
         [
             ((WIDTH, WIDTH), f32),
             ((4, 8, WIDTH), f32),
@@ -957,12 +932,12 @@
             ((OWN, 3 * QUARTER), bf16),
         ],
     )
+    last_send[2], *got_d = lax.optimization_barrier((last_send[2], *got_d))
+    last_send[3], *feed_terms = lax.optimization_barrier((last_send[3], *feed_terms))
     last_got = [core_swap(x) for x in last_send]
     l0, l1, l2, l3 = run(
         halves_body, pos, [last_own, *last_got], [(lpiece, f32)] + [(lpiece, bf16)] * 3
     )
-    l1, l2, l3, *feed_last = lax.optimization_barrier((l1, l2, l3, *feed_terms[2:]))
-    feed_terms = feed_two + feed_last
     last_terms = [seq_swap(h, m) for m, h in ((1, l1), (2, l2), (3, l3))]
     got_e = [chip_swap(e, m) for m, e in ((1, e1), (2, e2), (3, e3))]
     (feed_sum,) = run(add_body, pos, [h0, *feed_terms], [(piece, bf16)])
@@ -970,11 +945,11 @@
     input_grad, result = run(
         rows_body,
         pos,
-        [e0, *got_e, d0, tok[0], grad_mid, mid, vec],
+        [e0, *got_e, d0, *got_d, tok[0], grad_mid, mid, vec],
         [((1, *block), f32), ((1, *block), bf16)],
     )
-    (last_sum,) = run(add_body, pos, [l0, *last_terms], [(lpiece, bf16)])
-    last_sum, got_e[0] = lax.optimization_barrier((last_sum, got_e[0]))
+    l0, *got_e = lax.optimization_barrier((l0, *got_e))
+    (last_sum,) = run(add_body, pos, [l0, *last_terms], [(lpiece, bf16)], cost=3)
     last_blocks = chip_gather(last_sum)
     feed_oth = [core_swap(b) for b in feed_blocks]
     grad_w_down, grad_w_up = run(

time: 177 us -> 166 us (0.938)
  starting transfers between devices: 67.1 us -> 56.1 us
  local copies, waits for them, and re-layouts: 0.04 us -> 2.83 us
  waiting for transfers between devices: 66 us -> 64.2 us
    ppermute x12, starting transfers between devices: 30.4 us -> 20.5 us  [seq_swap(): return lax.ppermute(values, 'seq', [(i, i ^ mask) for i in range(4)])]
    ppermute x21 -> x24, waiting for transfers between devices: 26.7 us -> 22.4 us  [chip_swap(): return lax.ppermute(values, 'ctx', [(i, i ^ 2 * mask) for i in range(8)])]
    unnamed x12 -> x14, local copies, waits for them, and re-layouts: 0.04 us -> 2.83 us
    ppermute x30 -> x34, waiting for transfers between devices: 7.95 us -> 9.86 us  [core_swap(): return lax.ppermute(values, 'ctx', [(i, i ^ 1) for i in range(8)])]
    pallas_call x16 -> x15, Pallas kernels: 42.2 us -> 40.5 us  [run(): pl.pallas_call(body, out_shape=[jax.ShapeDtypeStruct(shape, kind) for sha...]
    ppermute x21 -> x24, starting transfers between devices: 29.9 us -> 29.1 us  [chip_swap(): return lax.ppermute(values, 'ctx', [(i, i ^ 2 * mask) for i in range(8)])]
    ppermute x30 -> x34, starting transfers between devices: 6.78 us -> 6.48 us  [core_swap(): return lax.ppermute(values, 'ctx', [(i, i ^ 1) for i in range(8)])]
  transfers between devices with their start and end apart: 63 -> 70, of which waited for: 25 -> 31; matrix products, arithmetic and copies ran while one was open for 0% -> 0% of each run, Pallas kernels for 16% -> 15%
where the time goes in v4:
time: 166 us; the launch traced here: 165 us
  waiting for transfers between devices  64.2 us (39%)
  starting transfers between devices  56.1 us (34%)
  Pallas kernels  40.5 us (24%)
  local copies, waits for them, and re-layouts  2.83 us (2%)
    pallas_call x15, Pallas kernels, run(): pl.pallas_call(body, out_shape=[jax.ShapeDtypeStruct(shape, kind) for sha...  40.5 us
    ppermute x12, waiting for transfers between devices, seq_swap(): return lax.ppermute(values, 'seq', [(i, i ^ mask) for i in range(4)])  31.9 us
    ppermute x24, starting transfers between devices, chip_swap(): return lax.ppermute(values, 'ctx', [(i, i ^ 2 * mask) for i in range(8)])  29.1 us
    ppermute x24, waiting for transfers between devices, chip_swap(): return lax.ppermute(values, 'ctx', [(i, i ^ 2 * mask) for i in range(8)])  22.4 us
    ppermute x12, starting transfers between devices, seq_swap(): return lax.ppermute(values, 'seq', [(i, i ^ mask) for i in range(4)])  20.5 us
    ppermute x34, waiting for transfers between devices, core_swap(): return lax.ppermute(values, 'ctx', [(i, i ^ 1) for i in range(8)])  9.86 us
    ppermute x34, starting transfers between devices, core_swap(): return lax.ppermute(values, 'ctx', [(i, i ^ 1) for i in range(8)])  6.48 us
  transfers between devices with their start and end apart: 70, of which 31 were waited for; matrix products, arithmetic and copies ran while one was open for 0% of the time, Pallas kernels for 15%

profile of v4, /device:TPU:0, one launch (start us, length us, event | category | flops | bytes accessed | tf_op | source)
XLA Modules:
  0.0 165.3 jit_solution(12224953518184515150)
XLA Ops:
  1.3 4.1 %shard_map.271 = (bf16[112,576]{1,0:T(8,128)(2,1)}, bf16[112,576]{1,0:T(8,128)(2,1)}, bf16[264,768]{1,0:T(8,128)(2,1)}, bf16[288,768]{1,0:T(8,128)(2,1)}, bf16[288,768]{1,0:T(8,128)(2,1)}) custom-call(s32[3]{0:T(128)} %pad_add_fusion.pos, bf16[192,2304]{1,0:T(8,128)(2,1)} %w_ref.1, bf16[1,128,768]{2,1,0:T(8,128)(2,1)} %tok_ref.1, ...), custom_call_target="tpu_custom_call" | custom-call | flops 524288 | bytes 1000 | tf_op jit(solution)/shard_map/pallas_call | solution.py:402
  5.4 5.1 %collective-permute-start.5 = (bf16[112,576]{1,0:T(8,128)(2,1)}, bf16[112,576]{1,0:T(8,128)(2,1)S(1)}, u32[]{:S(2)}, u32[]{:S(2)}) collective-permute-start(bf16[112,576]{1,0:T(8,128)(2,1)} %get-tuple-element.112.refs_4_), channel_id=1, source_target_pairs={{0,24},{8,16},{16,8},{24,0},{1,25},{9,17},{17,9},{25,1},{2,26},{10... | collective-permute-start | bytes 387080 | tf_op jit(solution)/shard_map/ppermute | solution.py:381
  10.5 2.5 %collective-permute-start.2 = (bf16[264,768]{1,0:T(8,128)(2,1)}, bf16[264,768]{1,0:T(8,128)(2,1)S(1)}, u32[]{:S(2)}, u32[]{:S(2)}) collective-permute-start(bf16[264,768]{1,0:T(8,128)(2,1)} %get-tuple-element.111.refs_0_.c0.tok_ref), channel_id=1, source_target_pairs={{0,6},{1,7},{2,4},{3,5},{4,2},{5,3},{6,0},{7,1},{8,14},{9,15},{10,... | collective-permute-start | bytes 1216520 | tf_op jit(solution)/shard_map/ppermute | solution.py:377
  13.0 0.8 collective-permute-start.3
  14.3 1.1 collective-permute-done.5.refs_7_
  15.4 1.7 %collective-permute-start = (bf16[264,768]{1,0:T(8,128)(2,1)}, bf16[264,768]{1,0:T(8,128)(2,1)S(1)}, u32[]{:S(2)}, u32[]{:S(2)}) collective-permute-start(bf16[264,768]{1,0:T(8,128)(2,1)} %get-tuple-element.111.refs_0_.c0.tok_ref), channel_id=1, source_target_pairs={{0,2},{1,3},{2,0},{3,1},{4,6},{5,7},{6,4},{7,5},{8,10},{9,11},{10,... | collective-permute-start | bytes 1216520 | tf_op jit(solution)/shard_map/ppermute | solution.py:377
  17.1 5.7 %collective-permute-done.4.refs_6_ = bf16[112,576]{1,0:T(8,128)(2,1)S(1)} collective-permute-done((bf16[112,576]{1,0:T(8,128)(2,1)}, bf16[112,576]{1,0:T(8,128)(2,1)S(1)}, u32[]{:S(2)}, u32[]{:S(2)}) %collective-permute-start.4) | collective-permute-done | bytes 129056 | tf_op jit(solution)/shard_map/ppermute | solution.py:381
  23.4 0.9 collective-permute-done.8.refs_11_
  24.2 2.5 %collective-permute-start.18 = (bf16[288,768]{1,0:T(8,128)(2,1)}, bf16[288,768]{1,0:T(8,128)(2,1)S(1)}, u32[]{:S(2)}, u32[]{:S(2)}) collective-permute-start(bf16[288,768]{1,0:T(8,128)(2,1)} %get-tuple-element.121.refs_8_), channel_id=1, source_target_pairs={{0,24},{8,16},{16,8},{24,0},{1,25},{9,17},{17,9},{25,1},{2,26},{10... | collective-permute-start | bytes 1327112 | tf_op jit(solution)/shard_map/ppermute | solution.py:381
  26.7 1.4 collective-permute-done.6.refs_9_
  28.1 1.9 %collective-permute-start.16 = (bf16[288,768]{1,0:T(8,128)(2,1)}, bf16[288,768]{1,0:T(8,128)(2,1)S(1)}, u32[]{:S(2)}, u32[]{:S(2)}) collective-permute-start(bf16[288,768]{1,0:T(8,128)(2,1)} %get-tuple-element.121.refs_8_), channel_id=1, source_target_pairs={{0,8},{8,0},{16,24},{24,16},{1,9},{9,1},{17,25},{25,17},{2,10},{10... | collective-permute-start | bytes 1327112 | tf_op jit(solution)/shard_map/ppermute | solution.py:381
  30.0 1.2 collective-permute-done.1.refs_2_.c2
  31.2 1.0 copy-done
  32.2 0.9 copy-done.4
  33.1 0.9 copy-done.5
  34.1 1.9 %shard_map.272 = (bf16[512,192]{1,0:T(8,128)(2,1)S(1)}, bf16[264,192]{1,0:T(8,128)(2,1)S(1)}, bf16[256,192]{1,0:T(8,128)(2,1)S(1)}, bf16[256,192]{1,0:T(8,128)(2...) custom-call(s32[3]{0:T(128)S(1)} %copy-done.6, ...), custom_call_target="tpu_custom_call" | custom-call | flops 524288 | bytes 1000 | tf_op jit(solution)/shard_map/pallas_call | solution.py:402
  36.6 0.8 collective-permute-done.10.refs_5_
  37.9 1.0 collective-permute-done.12.refs_7_
  39.0 5.2 %shard_map.273 = (bf16[512,192]{1,0:T(8,128)(2,1)S(1)}, f32[512,256]{1,0:T(8,128)S(1)}) custom-call(s32[3]{0:T(128)S(1)} %copy-done.6, bf16[512,192]{1,0:T(8,128)(2,1)S(1)} %get-tuple-element.114.q_ref, bf16[264,192]{1,0:T(8,128)(2,1)S(1)} %get-tuple-element.115.refs_0_, bf16[256,192]{1,0:T(8,128)(2,1)S(1)} %get-tuple-element.116.refs_1_, ...), custom_call_target="tpu_custom_call" | custom-call | flops 524288 | bytes 1000 | tf_op jit(solution)/shard_map/pallas_call | solution.py:402
  44.2 2.1 %collective-permute-start.15 = (bf16[512,192]{1,0:T(8,128)(2,1)S(1)}, bf16[512,192]{1,0:T(8,128)(2,1)S(1)}, u32[]{:S(2)}, u32[]{:S(2)}) collective-permute-start(bf16[512,192]{1,0:T(8,128)(2,1)S(1)} %get-tuple-element.119.refs_4_), channel_id=1, source_target_pairs={{0,6},{1,7},{2,4},{3,5},{4,2},{5,3},{6,0},{7,1},{8,14},{9,15},{10,... | collective-permute-start | bytes 589832 | tf_op jit(solution)/shard_map/ppermute | solution.py:377
  46.3 1.0 collective-permute-start.14
  47.8 16.7 %collective-permute-done.17.refs_10_ = bf16[288,768]{1,0:T(8,128)(2,1)S(1)} collective-permute-done((bf16[288,768]{1,0:T(8,128)(2,1)}, bf16[288,768]{1,0:T(8,128)(2,1)S(1)}, u32[]{:S(2)}, u32[]{:S(2)}) %collective-permute-start.17) | collective-permute-done | bytes 442400 | tf_op jit(solution)/shard_map/ppermute | solution.py:381
  65.2 1.2 collective-permute-done.19.refs_13_
  67.7 5.5 %shard_map.274 = (f32[128,768]{1,0:T(8,128)S(1)}, bf16[512,768]{1,0:T(8,128)(2,1)S(1)}, bf16[512,768]{1,0:T(8,128)(2,1)S(1)}, bf16[512,768]{1,0:T(8,128)(2,1)S(1...) custom-call(s32[3]{0:T(128)S(1)} %copy-done.6, ...), custom_call_target="tpu_custom_call" | custom-call | flops 524288 | bytes 1000 | tf_op jit(solution)/shard_map/pallas_call | solution.py:402
  73.2 2.4 %shard_map.275 = (bf16[96,768]{1,0:T(8,128)(2,1)S(1)}, bf16[96,768]{1,0:T(8,128)(2,1)S(1)}, bf16[96,768]{1,0:T(8,128)(2,1)S(1)}, bf16[96,768]{1,0:T(8,128)(2,1)S...) custom-call(s32[3]{0:T(128)S(1)} %copy-done.6, ...), custom_call_target="tpu_custom_call" | custom-call | flops 524288 | bytes 1000 | tf_op jit(solution)/shard_map/pallas_call | solution.py:402
  77.3 1.3 collective-permute-start.30
  78.6 1.5 collective-permute-start.31
  81.3 0.9 collective-permute-done.28.refs_6_
  82.4 0.8 shard_map.276
  83.1 1.9 %collective-permute-done.30.r1 = bf16[128,768]{1,0:T(8,128)(2,1)S(1)} collective-permute-done((bf16[128,768]{1,0:T(8,128)(2,1)S(1)}, bf16[128,768]{1,0:T(8,128)(2,1)S(1)}, u32[]{:S(2)}, u32[]{:S(2)}) %collective-permute-start.30) | collective-permute-done | bytes 196640 | tf_op jit(solution)/shard_map/ppermute | solution.py:377
  85.0 3.7 %collective-permute-done.31.r2 = bf16[128,768]{1,0:T(8,128)(2,1)S(1)} collective-permute-done((bf16[128,768]{1,0:T(8,128)(2,1)S(1)}, bf16[128,768]{1,0:T(8,128)(2,1)S(1)}, u32[]{:S(2)}, u32[]{:S(2)}) %collective-permute-start.31) | collective-permute-done | bytes 196640 | tf_op jit(solution)/shard_map/ppermute | solution.py:377
  88.7 1.0 collective-permute-done.32.r3
  89.6 0.9 shard_map.277
  90.5 1.8 %collective-permute-start.35 = (bf16[128,768]{1,0:T(8,128)(2,1)S(1)}, bf16[128,768]{1,0:T(8,128)(2,1)S(1)}, u32[]{:S(2)}, u32[]{:S(2)}) collective-permute-start(bf16[128,768]{1,0:T(8,128)(2,1)S(1)} %get-tuple-element.146.a0.refs_8_), channel_id=1, source_target_pairs={{0,6},{1,7},{2,4},{3,5},{4,2},{5,3},{6,0},{7,1},{8,14},{9,15},{10,... | collective-permute-start | bytes 589832 | tf_op jit(solution)/shard_map/ppermute | solution.py:377
  92.3 1.0 collective-permute-start.34
  93.3 0.8 collective-permute-start.33
  94.1 3.1 %collective-permute-start.50 = (bf16[192,768]{1,0:T(8,128)(2,1)S(1)}, bf16[192,768]{1,0:T(8,128)(2,1)S(1)}, u32[]{:S(2)}, u32[]{:S(2)}) collective-permute-start(bf16[192,768]{1,0:T(8,128)(2,1)S(1)} %get-tuple-element.182), channel_id=1, source_target_pairs={{0,16},{8,24},{16,0},{24,8},{1,17},{9,25},{17,1},{25,9},{2,18},{10... | collective-permute-start | bytes 884744 | tf_op jit(solution)/shard_map/ppermute | solution.py:381
  97.3 2.1 %collective-permute-done.35.a3.refs_11_ = bf16[128,768]{1,0:T(8,128)(2,1)S(1)} collective-permute-done((bf16[128,768]{1,0:T(8,128)(2,1)S(1)}, bf16[128,768]{1,0:T(8,128)(2,1)S(1)}, u32[]{:S(2)}, u32[]{:S(2)}) %collective-permute-start.35) | collective-permute-done | bytes 196640 | tf_op jit(solution)/shard_map/ppermute | solution.py:377
  99.4 2.6 %collective-permute-start.51 = (bf16[192,768]{1,0:T(8,128)(2,1)S(1)}, bf16[192,768]{1,0:T(8,128)(2,1)S(1)}, u32[]{:S(2)}, u32[]{:S(2)}) collective-permute-start(bf16[192,768]{1,0:T(8,128)(2,1)S(1)} %get-tuple-element.183), channel_id=1, source_target_pairs={{0,24},{8,16},{16,8},{24,0},{1,25},{9,17},{17,9},{25,1},{2,26},{10... | collective-permute-start | bytes 884744 | tf_op jit(solution)/shard_map/ppermute | solution.py:381
  102.0 6.8 %shard_map.278 = (bf16[512,192]{1,0:T(8,128)(2,1)S(1)}, f32[512,384]{1,0:T(8,128)S(1)}, bf16[256,192]{1,0:T(8,128)(2,1)S(1)}, bf16[256,192]{1,0:T(8,128)(2,1)S(1...) custom-call(s32[3]{0:T(128)S(1)} %copy-done.6, bf16[128,768]{1,0:T(8,128)(2,1)S(1)} %get-tuple-element.146.a0.refs_8_, ...), custom_call_target="tpu_custom_call" | custom-call | flops 524288 | bytes 1000 | tf_op jit(solution)/shard_map/pallas_call | solution.py:402
  110.4 1.3 collective-permute-start.43
  111.7 1.0 collective-permute-start.44
  112.7 1.2 collective-permute-start.45
  113.9 3.4 %shard_map.279 = (bf16[96,768]{1,0:T(8,128)(2,1)S(1)}, bf16[96,768]{1,0:T(8,128)(2,1)S(1)}, bf16[96,768]{1,0:T(8,128)(2,1)S(1)}, bf16[96,768]{1,0:T(8,128)(2,1)S...) custom-call(s32[3]{0:T(128)S(1)} %copy-done.6, ...), custom_call_target="tpu_custom_call" | custom-call | flops 524288 | bytes 1000 | tf_op jit(solution)/shard_map/pallas_call | solution.py:402
  118.3 1.1 collective-permute-start.40
  119.4 3.3 %collective-permute-done.44.s2 = bf16[128,768]{1,0:T(8,128)(2,1)S(1)} collective-permute-done((bf16[128,768]{1,0:T(8,128)(2,1)S(1)}, bf16[128,768]{1,0:T(8,128)(2,1)S(1)}, u32[]{:S(2)}, u32[]{:S(2)}) %collective-permute-start.44) | collective-permute-done | bytes 196640 | tf_op jit(solution)/shard_map/ppermute | solution.py:377
  122.7 1.4 collective-permute-start.41
  125.1 0.9 collective-permute-done.52.y3
  126.8 1.4 collective-permute-start.53
  128.2 2.2 %collective-permute-start.54 = (bf16[104,768]{1,0:T(8,128)(2,1)S(1)}, bf16[104,768]{1,0:T(8,128)(2,1)S(1)}, u32[]{:S(2)}, u32[]{:S(2)}) collective-permute-start(bf16[104,768]{1,0:T(8,128)(2,1)S(1)} %get-tuple-element.188), channel_id=1, source_target_pairs={{0,16},{8,24},{16,0},{24,8},{1,17},{9,25},{17,1},{25,9},{2,18},{10... | collective-permute-start | bytes 479240 | tf_op jit(solution)/shard_map/ppermute | solution.py:381
  130.4 0.8 collective-permute-start.55
  132.5 1.9 %collective-permute-start.65 = (bf16[192,768]{1,0:T(8,128)(2,1)S(1)}, bf16[192,768]{1,0:T(8,128)(2,1)S(1)}, u32[]{:S(2)}, u32[]{:S(2)}) collective-permute-start(bf16[192,768]{1,0:T(8,128)(2,1)S(1)} %shard_map.284.refs_0_), channel_id=1, source_target_pairs={{0,6},{1,7},{2,4},{3,5},{4,2},{5,3},{6,0},{7,1},{8,14},{9,15},{10,... | collective-permute-start | bytes 884744 | tf_op jit(solution)/shard_map/ppermute | solution.py:377
  135.1 0.9 collective-permute-done.53.r1
  136.0 6.9 %collective-permute-done.54.r2 = bf16[104,768]{1,0:T(8,128)(2,1)S(1)} collective-permute-done((bf16[104,768]{1,0:T(8,128)(2,1)S(1)}, bf16[104,768]{1,0:T(8,128)(2,1)S(1)}, u32[]{:S(2)}, u32[]{:S(2)}) %collective-permute-start.54) | collective-permute-done | bytes 159776 | tf_op jit(solution)/shard_map/ppermute | solution.py:381
  143.0 1.0 collective-permute-start.63
  144.6 1.5 collective-permute-start.58
  146.1 3.2 %collective-permute-done.64.refs_2_ = bf16[192,768]{1,0:T(8,128)(2,1)S(1)} collective-permute-done((bf16[192,768]{1,0:T(8,128)(2,1)S(1)}, bf16[192,768]{1,0:T(8,128)(2,1)S(1)}, u32[]{:S(2)}, u32[]{:S(2)}) %collective-permute-start.64) | collective-permute-done | bytes 294944 | tf_op jit(solution)/shard_map/ppermute | solution.py:377
  149.4 1.5 collective-permute-start.57
  150.8 0.8 collective-permute-start.56
  152.0 3.8 %collective-permute-done.57.refs_2_ = bf16[104,768]{1,0:T(8,128)(2,1)S(1)} collective-permute-done((bf16[104,768]{1,0:T(8,128)(2,1)S(1)}, bf16[104,768]{1,0:T(8,128)(2,1)S(1)}, u32[]{:S(2)}, u32[]{:S(2)}) %collective-permute-start.57) | collective-permute-done | bytes 159776 | tf_op jit(solution)/shard_map/ppermute | solution.py:377
  155.9 1.2 collective-permute-done.56.refs_1_
  157.7 1.8 %shard_map.280 = (f32[1,128,768]{2,1,0:T(8,128)}, bf16[1,128,768]{2,1,0:T(8,128)(2,1)}) custom-call(s32[3]{0:T(128)S(1)} %copy-done.6, f32[128,768]{1,0:T(8,128)S(1)} %get-tuple-element.158.g0, bf16[128,768]{1,0:T(8,128)(2,1)S(1)} %collective-permute-done.40.r1, bf16[128,768]{1,0:T(8,128)(2,1)S(1)} %collective-permute-done.41.r2, ...), custom_call_target="tpu_custom_call" | custom-call | flops 524288 | bytes 1000 | tf_op jit(solution)/shard_map/pallas_call | solution.py:402
  159.5 3.2 %shard_map.285 = (f32[768,768]{1,0:T(8,128)}, f32[192,3072]{1,0:T(8,128)}) custom-call(s32[3]{0:T(128)S(1)} %copy-done.6, bf16[192,768]{1,0:T(8,128)(2,1)S(1)} %shard_map.284.refs_0_, bf16[192,768]{1,0:T(8,128)(2,1)S(1)} %collective-permute-done.63.refs_1_, bf16[192,768]{1,0:T(8,128)(2,1)S(1)} %collective-permute-done.64.refs_2_, ...), custom_call_target="tpu_custom_call" | custom-call | flops 524288 | bytes 1000 | tf_op jit(solution)/shard_map/pallas_call | solution.py:402
  162.7 2.3 %shard_map.283 = (f32[192,2304]{1,0:T(8,128)}, f32[192,768]{1,0:T(8,128)}, f32[192]{0:T(256)}, f32[192]{0:T(256)}, f32[192]{0:T(256)}, /*index=5*/f32[192]{0:T(2...) custom-call(s32[3]{0:T(128)S(1)} %copy-done.6, ...), custom_call_target="tpu_custom_call" | custom-call | flops 524288 | bytes 1000 | tf_op jit(solution)/shard_map/pallas_call | solution.py:402
  (106 shorter events, 16.3 us)
Async XLA Ops:
  5.4 10.0 %collective-permute-start.5 = (bf16[112,576]{1,0:T(8,128)(2,1)}, bf16[112,576]{1,0:T(8,128)(2,1)S(1)}, u32[]{:S(2)}, u32[]{:S(2)}) collective-permute-start(bf16[112,576]{1,0:T(8,128)(2,1)} %get-tuple-element.112.refs_4_), channel_id=1, source_target_pairs={{0,24},{8,16},{16,8},{24,0},{1,25},{9,17},{17,9},{25,1},{2,26},{10... | collective-permute-start | bytes 387080 | tf_op jit(solution)/shard_map/ppermute | solution.py:381
  10.5 12.3 %collective-permute-start.4 = (bf16[112,576]{1,0:T(8,128)(2,1)}, bf16[112,576]{1,0:T(8,128)(2,1)S(1)}, u32[]{:S(2)}, u32[]{:S(2)}) collective-permute-start(bf16[112,576]{1,0:T(8,128)(2,1)} %get-tuple-element.112.refs_4_), channel_id=1, source_target_pairs={{0,16},{8,24},{16,0},{24,8},{1,17},{9,25},{17,1},{25,9},{2,18},{10... | collective-permute-start | bytes 387080 | tf_op jit(solution)/shard_map/ppermute | solution.py:381
  10.5 17.6 %collective-permute-start.2 = (bf16[264,768]{1,0:T(8,128)(2,1)}, bf16[264,768]{1,0:T(8,128)(2,1)S(1)}, u32[]{:S(2)}, u32[]{:S(2)}) collective-permute-start(bf16[264,768]{1,0:T(8,128)(2,1)} %get-tuple-element.111.refs_0_.c0.tok_ref), channel_id=1, source_target_pairs={{0,6},{1,7},{2,4},{3,5},{4,2},{5,3},{6,0},{7,1},{8,14},{9,15},{10,... | collective-permute-start | bytes 1216520 | tf_op jit(solution)/shard_map/ppermute | solution.py:377
  13.0 9.9 %collective-permute-start.3 = (bf16[112,576]{1,0:T(8,128)(2,1)}, bf16[112,576]{1,0:T(8,128)(2,1)S(1)}, u32[]{:S(2)}, u32[]{:S(2)}) collective-permute-start(bf16[112,576]{1,0:T(8,128)(2,1)} %get-tuple-element.112.refs_4_), channel_id=1, source_target_pairs={{0,8},{8,0},{16,24},{24,16},{1,9},{9,1},{17,25},{25,17},{2,10},{10... | collective-permute-start | bytes 387080 | tf_op jit(solution)/shard_map/ppermute | solution.py:381
  13.8 17.4 %collective-permute-start.1 = (bf16[264,768]{1,0:T(8,128)(2,1)}, bf16[264,768]{1,0:T(8,128)(2,1)S(1)}, u32[]{:S(2)}, u32[]{:S(2)}) collective-permute-start(bf16[264,768]{1,0:T(8,128)(2,1)} %get-tuple-element.111.refs_0_.c0.tok_ref), channel_id=1, source_target_pairs={{0,4},{1,5},{2,6},{3,7},{4,0},{5,1},{6,2},{7,3},{8,12},{9,13},{10,... | collective-permute-start | bytes 1216520 | tf_op jit(solution)/shard_map/ppermute | solution.py:377
  15.4 15.8 %collective-permute-start = (bf16[264,768]{1,0:T(8,128)(2,1)}, bf16[264,768]{1,0:T(8,128)(2,1)S(1)}, u32[]{:S(2)}, u32[]{:S(2)}) collective-permute-start(bf16[264,768]{1,0:T(8,128)(2,1)} %get-tuple-element.111.refs_0_.c0.tok_ref), channel_id=1, source_target_pairs={{0,2},{1,3},{2,0},{3,1},{4,6},{5,7},{6,4},{7,5},{8,10},{9,11},{10,... | collective-permute-start | bytes 1216520 | tf_op jit(solution)/shard_map/ppermute | solution.py:377
  22.8 3.8 %collective-permute-start.7 = (bf16[112,576]{1,0:T(8,128)(2,1)S(1)}, bf16[112,576]{1,0:T(8,128)(2,1)S(1)}, u32[]{:S(2)}, u32[]{:S(2)}) collective-permute-start(bf16[112,576]{1,0:T(8,128)(2,1)S(1)} %collective-permute-done.4.refs_6_), channel_id=1, source_target_pairs={{0,1},{1,0},{2,3},{3,2},{4,5},{5,4},{6,7},{7,6},{8,9},{9,8},{10,11... | collective-permute-start | bytes 387080 | tf_op jit(solution)/shard_map/ppermute | solution.py:373
  24.2 23.0 %collective-permute-start.18 = (bf16[288,768]{1,0:T(8,128)(2,1)}, bf16[288,768]{1,0:T(8,128)(2,1)S(1)}, u32[]{:S(2)}, u32[]{:S(2)}) collective-permute-start(bf16[288,768]{1,0:T(8,128)(2,1)} %get-tuple-element.121.refs_8_), channel_id=1, source_target_pairs={{0,24},{8,16},{16,8},{24,0},{1,25},{9,17},{17,9},{25,1},{2,26},{10... | collective-permute-start | bytes 1327112 | tf_op jit(solution)/shard_map/ppermute | solution.py:381
  28.1 36.4 %collective-permute-start.17 = (bf16[288,768]{1,0:T(8,128)(2,1)}, bf16[288,768]{1,0:T(8,128)(2,1)S(1)}, u32[]{:S(2)}, u32[]{:S(2)}) collective-permute-start(bf16[288,768]{1,0:T(8,128)(2,1)} %get-tuple-element.121.refs_8_), channel_id=1, source_target_pairs={{0,16},{8,24},{16,0},{24,8},{1,17},{9,25},{17,1},{25,9},{2,18},{10... | collective-permute-start | bytes 1327112 | tf_op jit(solution)/shard_map/ppermute | solution.py:381
  28.1 36.4 %collective-permute-start.16 = (bf16[288,768]{1,0:T(8,128)(2,1)}, bf16[288,768]{1,0:T(8,128)(2,1)S(1)}, u32[]{:S(2)}, u32[]{:S(2)}) collective-permute-start(bf16[288,768]{1,0:T(8,128)(2,1)} %get-tuple-element.121.refs_8_), channel_id=1, source_target_pairs={{0,8},{8,0},{16,24},{24,16},{1,9},{9,1},{17,25},{25,17},{2,10},{10... | collective-permute-start | bytes 1327112 | tf_op jit(solution)/shard_map/ppermute | solution.py:381
  36.0 1.4 collective-permute-start.10
  36.1 1.5 collective-permute-start.11
  37.4 1.5 collective-permute-start.9
  44.2 20.3 %collective-permute-start.15 = (bf16[512,192]{1,0:T(8,128)(2,1)S(1)}, bf16[512,192]{1,0:T(8,128)(2,1)S(1)}, u32[]{:S(2)}, u32[]{:S(2)}) collective-permute-start(bf16[512,192]{1,0:T(8,128)(2,1)S(1)} %get-tuple-element.119.refs_4_), channel_id=1, source_target_pairs={{0,6},{1,7},{2,4},{3,5},{4,2},{5,3},{6,0},{7,1},{8,14},{9,15},{10,... | collective-permute-start | bytes 589832 | tf_op jit(solution)/shard_map/ppermute | solution.py:377
  46.3 18.2 %collective-permute-start.14 = (bf16[512,192]{1,0:T(8,128)(2,1)S(1)}, bf16[512,192]{1,0:T(8,128)(2,1)S(1)}, u32[]{:S(2)}, u32[]{:S(2)}) collective-permute-start(bf16[512,192]{1,0:T(8,128)(2,1)S(1)} %get-tuple-element.119.refs_4_), channel_id=1, source_target_pairs={{0,4},{1,5},{2,6},{3,7},{4,0},{5,1},{6,2},{7,3},{8,12},{9,13},{10,... | collective-permute-start | bytes 589832 | tf_op jit(solution)/shard_map/ppermute | solution.py:377
  47.2 17.3 %collective-permute-start.13 = (bf16[512,192]{1,0:T(8,128)(2,1)S(1)}, bf16[512,192]{1,0:T(8,128)(2,1)S(1)}, u32[]{:S(2)}, u32[]{:S(2)}) collective-permute-start(bf16[512,192]{1,0:T(8,128)(2,1)S(1)} %get-tuple-element.119.refs_4_), channel_id=1, source_target_pairs={{0,2},{1,3},{2,0},{3,1},{4,6},{5,7},{6,4},{7,5},{8,10},{9,11},{10,... | collective-permute-start | bytes 589832 | tf_op jit(solution)/shard_map/ppermute | solution.py:377
  64.5 1.9 %collective-permute-start.19 = (bf16[288,768]{1,0:T(8,128)(2,1)S(1)}, bf16[288,768]{1,0:T(8,128)(2,1)S(1)}, u32[]{:S(2)}, u32[]{:S(2)}) collective-permute-start(bf16[288,768]{1,0:T(8,128)(2,1)S(1)} %collective-permute-done.16.refs_9_), channel_id=1, source_target_pairs={{0,1},{1,0},{2,3},{3,2},{4,5},{5,4},{6,7},{7,6},{8,9},{9,8},{10,11... | collective-permute-start | bytes 1327112 | tf_op jit(solution)/shard_map/ppermute | solution.py:373
  64.6 2.4 %collective-permute-start.20 = (bf16[288,768]{1,0:T(8,128)(2,1)S(1)}, bf16[288,768]{1,0:T(8,128)(2,1)S(1)}, u32[]{:S(2)}, u32[]{:S(2)}) collective-permute-start(bf16[288,768]{1,0:T(8,128)(2,1)S(1)} %collective-permute-done.17.refs_10_), channel_id=1, source_target_pairs={{0,1},{1,0},{2,3},{3,2},{4,5},{5,4},{6,7},{7,6},{8,9},{9,8},{10,11... | collective-permute-start | bytes 1327112 | tf_op jit(solution)/shard_map/ppermute | solution.py:373
  65.1 2.5 %collective-permute-start.21 = (bf16[288,768]{1,0:T(8,128)(2,1)S(1)}, bf16[288,768]{1,0:T(8,128)(2,1)S(1)}, u32[]{:S(2)}, u32[]{:S(2)}) collective-permute-start(bf16[288,768]{1,0:T(8,128)(2,1)S(1)} %collective-permute-done.18.refs_11_), channel_id=1, source_target_pairs={{0,1},{1,0},{2,3},{3,2},{4,5},{5,4},{6,7},{7,6},{8,9},{9,8},{10,11... | collective-permute-start | bytes 1327112 | tf_op jit(solution)/shard_map/ppermute | solution.py:373
  75.6 1.4 collective-permute-start.22
  75.8 1.5 collective-permute-start.23
  76.2 2.4 %collective-permute-start.24 = (bf16[96,768]{1,0:T(8,128)(2,1)S(1)}, bf16[96,768]{1,0:T(8,128)(2,1)S(1)}, u32[]{:S(2)}, u32[]{:S(2)}) collective-permute-start(bf16[96,768]{1,0:T(8,128)(2,1)S(1)} %get-tuple-element.134), channel_id=1, source_target_pairs={{0,1},{1,0},{2,3},{3,2},{4,5},{5,4},{6,7},{7,6},{8,9},{9,8},{10,11... | collective-permute-start | bytes 442376 | tf_op jit(solution)/shard_map/ppermute | solution.py:373
  76.3 3.8 %collective-permute-start.25 = (bf16[96,768]{1,0:T(8,128)(2,1)S(1)}, bf16[96,768]{1,0:T(8,128)(2,1)S(1)}, u32[]{:S(2)}, u32[]{:S(2)}) collective-permute-start(bf16[96,768]{1,0:T(8,128)(2,1)S(1)} %get-tuple-element.135), channel_id=1, source_target_pairs={{0,1},{1,0},{2,3},{3,2},{4,5},{5,4},{6,7},{7,6},{8,9},{9,8},{10,11... | collective-permute-start | bytes 442376 | tf_op jit(solution)/shard_map/ppermute | solution.py:373
  76.7 4.1 %collective-permute-start.26 = (bf16[96,768]{1,0:T(8,128)(2,1)S(1)}, bf16[96,768]{1,0:T(8,128)(2,1)S(1)}, u32[]{:S(2)}, u32[]{:S(2)}) collective-permute-start(bf16[96,768]{1,0:T(8,128)(2,1)S(1)} %get-tuple-element.136), channel_id=1, source_target_pairs={{0,1},{1,0},{2,3},{3,2},{4,5},{5,4},{6,7},{7,6},{8,9},{9,8},{10,11... | collective-permute-start | bytes 442376 | tf_op jit(solution)/shard_map/ppermute | solution.py:373
  77.1 3.7 %collective-permute-start.27 = (bf16[96,768]{1,0:T(8,128)(2,1)S(1)}, bf16[96,768]{1,0:T(8,128)(2,1)S(1)}, u32[]{:S(2)}, u32[]{:S(2)}) collective-permute-start(bf16[96,768]{1,0:T(8,128)(2,1)S(1)} %get-tuple-element.137), channel_id=1, source_target_pairs={{0,1},{1,0},{2,3},{3,2},{4,5},{5,4},{6,7},{7,6},{8,9},{9,8},{10,11... | collective-permute-start | bytes 442376 | tf_op jit(solution)/shard_map/ppermute | solution.py:373
  77.3 7.7 %collective-permute-start.30 = (bf16[128,768]{1,0:T(8,128)(2,1)S(1)}, bf16[128,768]{1,0:T(8,128)(2,1)S(1)}, u32[]{:S(2)}, u32[]{:S(2)}) collective-permute-start(bf16[128,768]{1,0:T(8,128)(2,1)S(1)} %get-tuple-element.142), channel_id=1, source_target_pairs={{0,2},{1,3},{2,0},{3,1},{4,6},{5,7},{6,4},{7,5},{8,10},{9,11},{10,... | collective-permute-start | bytes 589832 | tf_op jit(solution)/shard_map/ppermute | solution.py:377
  78.6 10.1 %collective-permute-start.31 = (bf16[128,768]{1,0:T(8,128)(2,1)S(1)}, bf16[128,768]{1,0:T(8,128)(2,1)S(1)}, u32[]{:S(2)}, u32[]{:S(2)}) collective-permute-start(bf16[128,768]{1,0:T(8,128)(2,1)S(1)} %get-tuple-element.143), channel_id=1, source_target_pairs={{0,4},{1,5},{2,6},{3,7},{4,0},{5,1},{6,2},{7,3},{8,12},{9,13},{10,... | collective-permute-start | bytes 589832 | tf_op jit(solution)/shard_map/ppermute | solution.py:377
  80.1 9.5 %collective-permute-start.32 = (bf16[128,768]{1,0:T(8,128)(2,1)S(1)}, bf16[128,768]{1,0:T(8,128)(2,1)S(1)}, u32[]{:S(2)}, u32[]{:S(2)}) collective-permute-start(bf16[128,768]{1,0:T(8,128)(2,1)S(1)} %get-tuple-element.144), channel_id=1, source_target_pairs={{0,6},{1,7},{2,4},{3,5},{4,2},{5,3},{6,0},{7,1},{8,14},{9,15},{10,... | collective-permute-start | bytes 589832 | tf_op jit(solution)/shard_map/ppermute | solution.py:377
  80.8 1.6 collective-permute-start.29
  90.5 8.8 %collective-permute-start.35 = (bf16[128,768]{1,0:T(8,128)(2,1)S(1)}, bf16[128,768]{1,0:T(8,128)(2,1)S(1)}, u32[]{:S(2)}, u32[]{:S(2)}) collective-permute-start(bf16[128,768]{1,0:T(8,128)(2,1)S(1)} %get-tuple-element.146.a0.refs_8_), channel_id=1, source_target_pairs={{0,6},{1,7},{2,4},{3,5},{4,2},{5,3},{6,0},{7,1},{8,14},{9,15},{10,... | collective-permute-start | bytes 589832 | tf_op jit(solution)/shard_map/ppermute | solution.py:377
  92.3 9.7 %collective-permute-start.34 = (bf16[128,768]{1,0:T(8,128)(2,1)S(1)}, bf16[128,768]{1,0:T(8,128)(2,1)S(1)}, u32[]{:S(2)}, u32[]{:S(2)}) collective-permute-start(bf16[128,768]{1,0:T(8,128)(2,1)S(1)} %get-tuple-element.146.a0.refs_8_), channel_id=1, source_target_pairs={{0,4},{1,5},{2,6},{3,7},{4,0},{5,1},{6,2},{7,3},{8,12},{9,13},{10,... | collective-permute-start | bytes 589832 | tf_op jit(solution)/shard_map/ppermute | solution.py:377
  93.3 8.7 %collective-permute-start.33 = (bf16[128,768]{1,0:T(8,128)(2,1)S(1)}, bf16[128,768]{1,0:T(8,128)(2,1)S(1)}, u32[]{:S(2)}, u32[]{:S(2)}) collective-permute-start(bf16[128,768]{1,0:T(8,128)(2,1)S(1)} %get-tuple-element.146.a0.refs_8_), channel_id=1, source_target_pairs={{0,2},{1,3},{2,0},{3,1},{4,6},{5,7},{6,4},{7,5},{8,10},{9,11},{10,... | collective-permute-start | bytes 589832 | tf_op jit(solution)/shard_map/ppermute | solution.py:377
  94.1 15.3 %collective-permute-start.49 = (bf16[192,768]{1,0:T(8,128)(2,1)S(1)}, bf16[192,768]{1,0:T(8,128)(2,1)S(1)}, u32[]{:S(2)}, u32[]{:S(2)}) collective-permute-start(bf16[192,768]{1,0:T(8,128)(2,1)S(1)} %get-tuple-element.181), channel_id=1, source_target_pairs={{0,8},{8,0},{16,24},{24,16},{1,9},{9,1},{17,25},{25,17},{2,10},{10... | collective-permute-start | bytes 884744 | tf_op jit(solution)/shard_map/ppermute | solution.py:381
  94.1 23.7 %collective-permute-start.50 = (bf16[192,768]{1,0:T(8,128)(2,1)S(1)}, bf16[192,768]{1,0:T(8,128)(2,1)S(1)}, u32[]{:S(2)}, u32[]{:S(2)}) collective-permute-start(bf16[192,768]{1,0:T(8,128)(2,1)S(1)} %get-tuple-element.182), channel_id=1, source_target_pairs={{0,16},{8,24},{16,0},{24,8},{1,17},{9,25},{17,1},{25,9},{2,18},{10... | collective-permute-start | bytes 884744 | tf_op jit(solution)/shard_map/ppermute | solution.py:381
  99.4 18.4 %collective-permute-start.51 = (bf16[192,768]{1,0:T(8,128)(2,1)S(1)}, bf16[192,768]{1,0:T(8,128)(2,1)S(1)}, u32[]{:S(2)}, u32[]{:S(2)}) collective-permute-start(bf16[192,768]{1,0:T(8,128)(2,1)S(1)} %get-tuple-element.183), channel_id=1, source_target_pairs={{0,24},{8,16},{16,8},{24,0},{1,25},{9,17},{17,9},{25,1},{2,26},{10... | collective-permute-start | bytes 884744 | tf_op jit(solution)/shard_map/ppermute | solution.py:381
  108.9 1.5 collective-permute-start.37
  109.4 2.3 %collective-permute-start.38 = (bf16[256,192]{1,0:T(8,128)(2,1)S(1)}, bf16[256,192]{1,0:T(8,128)(2,1)S(1)}, u32[]{:S(2)}, u32[]{:S(2)}) collective-permute-start(bf16[256,192]{1,0:T(8,128)(2,1)S(1)} %get-tuple-element.154), channel_id=1, source_target_pairs={{0,1},{1,0},{2,3},{3,2},{4,5},{5,4},{6,7},{7,6},{8,9},{9,8},{10,11... | collective-permute-start | bytes 294920 | tf_op jit(solution)/shard_map/ppermute | solution.py:373
  110.2 2.5 %collective-permute-start.39 = (bf16[256,192]{1,0:T(8,128)(2,1)S(1)}, bf16[256,192]{1,0:T(8,128)(2,1)S(1)}, u32[]{:S(2)}, u32[]{:S(2)}) collective-permute-start(bf16[256,192]{1,0:T(8,128)(2,1)S(1)} %get-tuple-element.155), channel_id=1, source_target_pairs={{0,1},{1,0},{2,3},{3,2},{4,5},{5,4},{6,7},{7,6},{8,9},{9,8},{10,11... | collective-permute-start | bytes 294920 | tf_op jit(solution)/shard_map/ppermute | solution.py:373
  110.4 7.9 %collective-permute-start.43 = (bf16[128,768]{1,0:T(8,128)(2,1)S(1)}, bf16[128,768]{1,0:T(8,128)(2,1)S(1)}, u32[]{:S(2)}, u32[]{:S(2)}) collective-permute-start(bf16[128,768]{1,0:T(8,128)(2,1)S(1)} %get-tuple-element.165), channel_id=1, source_target_pairs={{0,2},{1,3},{2,0},{3,1},{4,6},{5,7},{6,4},{7,5},{8,10},{9,11},{10,... | collective-permute-start | bytes 589832 | tf_op jit(solution)/shard_map/ppermute | solution.py:377
  111.7 11.0 %collective-permute-start.44 = (bf16[128,768]{1,0:T(8,128)(2,1)S(1)}, bf16[128,768]{1,0:T(8,128)(2,1)S(1)}, u32[]{:S(2)}, u32[]{:S(2)}) collective-permute-start(bf16[128,768]{1,0:T(8,128)(2,1)S(1)} %get-tuple-element.167), channel_id=1, source_target_pairs={{0,4},{1,5},{2,6},{3,7},{4,0},{5,1},{6,2},{7,3},{8,12},{9,13},{10,... | collective-permute-start | bytes 589832 | tf_op jit(solution)/shard_map/ppermute | solution.py:377
  112.7 11.4 %collective-permute-start.45 = (bf16[128,768]{1,0:T(8,128)(2,1)S(1)}, bf16[128,768]{1,0:T(8,128)(2,1)S(1)}, u32[]{:S(2)}, u32[]{:S(2)}) collective-permute-start(bf16[128,768]{1,0:T(8,128)(2,1)S(1)} %get-tuple-element.169), channel_id=1, source_target_pairs={{0,6},{1,7},{2,4},{3,5},{4,2},{5,3},{6,0},{7,1},{8,14},{9,15},{10,... | collective-permute-start | bytes 589832 | tf_op jit(solution)/shard_map/ppermute | solution.py:377
  117.8 6.8 %collective-permute-start.46 = (bf16[96,768]{1,0:T(8,128)(2,1)S(1)}, bf16[96,768]{1,0:T(8,128)(2,1)S(1)}, u32[]{:S(2)}, u32[]{:S(2)}) collective-permute-start(bf16[96,768]{1,0:T(8,128)(2,1)S(1)} %get-tuple-element.177), channel_id=1, source_target_pairs={{0,1},{1,0},{2,3},{3,2},{4,5},{5,4},{6,7},{7,6},{8,9},{9,8},{10,11... | collective-permute-start | bytes 442376 | tf_op jit(solution)/shard_map/ppermute | solution.py:373
  117.8 6.8 %collective-permute-start.47 = (bf16[96,768]{1,0:T(8,128)(2,1)S(1)}, bf16[96,768]{1,0:T(8,128)(2,1)S(1)}, u32[]{:S(2)}, u32[]{:S(2)}) collective-permute-start(bf16[96,768]{1,0:T(8,128)(2,1)S(1)} %get-tuple-element.178), channel_id=1, source_target_pairs={{0,1},{1,0},{2,3},{3,2},{4,5},{5,4},{6,7},{7,6},{8,9},{9,8},{10,11... | collective-permute-start | bytes 442376 | tf_op jit(solution)/shard_map/ppermute | solution.py:373
  118.3 12.1 %collective-permute-start.40 = (bf16[128,768]{1,0:T(8,128)(2,1)S(1)}, bf16[128,768]{1,0:T(8,128)(2,1)S(1)}, u32[]{:S(2)}, u32[]{:S(2)}) collective-permute-start(bf16[128,768]{1,0:T(8,128)(2,1)S(1)} %get-tuple-element.159), channel_id=1, source_target_pairs={{0,2},{1,3},{2,0},{3,1},{4,6},{5,7},{6,4},{7,5},{8,10},{9,11},{10,... | collective-permute-start | bytes 589832 | tf_op jit(solution)/shard_map/ppermute | solution.py:377
  122.7 9.8 %collective-permute-start.41 = (bf16[128,768]{1,0:T(8,128)(2,1)S(1)}, bf16[128,768]{1,0:T(8,128)(2,1)S(1)}, u32[]{:S(2)}, u32[]{:S(2)}) collective-permute-start(bf16[128,768]{1,0:T(8,128)(2,1)S(1)} %get-tuple-element.160), channel_id=1, source_target_pairs={{0,4},{1,5},{2,6},{3,7},{4,0},{5,1},{6,2},{7,3},{8,12},{9,13},{10,... | collective-permute-start | bytes 589832 | tf_op jit(solution)/shard_map/ppermute | solution.py:377
  124.1 10.4 %collective-permute-start.42 = (bf16[128,768]{1,0:T(8,128)(2,1)S(1)}, bf16[128,768]{1,0:T(8,128)(2,1)S(1)}, u32[]{:S(2)}, u32[]{:S(2)}) collective-permute-start(bf16[128,768]{1,0:T(8,128)(2,1)S(1)} %get-tuple-element.161), channel_id=1, source_target_pairs={{0,6},{1,7},{2,4},{3,5},{4,2},{5,3},{6,0},{7,1},{8,14},{9,15},{10,... | collective-permute-start | bytes 589832 | tf_op jit(solution)/shard_map/ppermute | solution.py:377
  124.6 1.6 collective-permute-start.48
  126.8 9.2 %collective-permute-start.53 = (bf16[104,768]{1,0:T(8,128)(2,1)S(1)}, bf16[104,768]{1,0:T(8,128)(2,1)S(1)}, u32[]{:S(2)}, u32[]{:S(2)}) collective-permute-start(bf16[104,768]{1,0:T(8,128)(2,1)S(1)} %get-tuple-element.187), channel_id=1, source_target_pairs={{0,8},{8,0},{16,24},{24,16},{1,9},{9,1},{17,25},{25,17},{2,10},{10... | collective-permute-start | bytes 479240 | tf_op jit(solution)/shard_map/ppermute | solution.py:381
  128.2 14.8 %collective-permute-start.54 = (bf16[104,768]{1,0:T(8,128)(2,1)S(1)}, bf16[104,768]{1,0:T(8,128)(2,1)S(1)}, u32[]{:S(2)}, u32[]{:S(2)}) collective-permute-start(bf16[104,768]{1,0:T(8,128)(2,1)S(1)} %get-tuple-element.188), channel_id=1, source_target_pairs={{0,16},{8,24},{16,0},{24,8},{1,17},{9,25},{17,1},{25,9},{2,18},{10... | collective-permute-start | bytes 479240 | tf_op jit(solution)/shard_map/ppermute | solution.py:381
  130.4 13.5 %collective-permute-start.55 = (bf16[104,768]{1,0:T(8,128)(2,1)S(1)}, bf16[104,768]{1,0:T(8,128)(2,1)S(1)}, u32[]{:S(2)}, u32[]{:S(2)}) collective-permute-start(bf16[104,768]{1,0:T(8,128)(2,1)S(1)} %get-tuple-element.189), channel_id=1, source_target_pairs={{0,24},{8,16},{16,8},{24,0},{1,25},{9,17},{17,9},{25,1},{2,26},{10... | collective-permute-start | bytes 479240 | tf_op jit(solution)/shard_map/ppermute | solution.py:381
  132.5 13.6 %collective-permute-start.65 = (bf16[192,768]{1,0:T(8,128)(2,1)S(1)}, bf16[192,768]{1,0:T(8,128)(2,1)S(1)}, u32[]{:S(2)}, u32[]{:S(2)}) collective-permute-start(bf16[192,768]{1,0:T(8,128)(2,1)S(1)} %shard_map.284.refs_0_), channel_id=1, source_target_pairs={{0,6},{1,7},{2,4},{3,5},{4,2},{5,3},{6,0},{7,1},{8,14},{9,15},{10,... | collective-permute-start | bytes 884744 | tf_op jit(solution)/shard_map/ppermute | solution.py:377
  134.5 14.9 %collective-permute-start.64 = (bf16[192,768]{1,0:T(8,128)(2,1)S(1)}, bf16[192,768]{1,0:T(8,128)(2,1)S(1)}, u32[]{:S(2)}, u32[]{:S(2)}) collective-permute-start(bf16[192,768]{1,0:T(8,128)(2,1)S(1)} %shard_map.284.refs_0_), channel_id=1, source_target_pairs={{0,4},{1,5},{2,6},{3,7},{4,0},{5,1},{6,2},{7,3},{8,12},{9,13},{10,... | collective-permute-start | bytes 884744 | tf_op jit(solution)/shard_map/ppermute | solution.py:377
  136.0 13.3 %collective-permute-start.66 = (bf16[192,768]{1,0:T(8,128)(2,1)S(1)}, bf16[192,768]{1,0:T(8,128)(2,1)S(1)}, u32[]{:S(2)}, u32[]{:S(2)}) collective-permute-start(bf16[192,768]{1,0:T(8,128)(2,1)S(1)} %shard_map.284.refs_0_), channel_id=1, source_target_pairs={{0,1},{1,0},{2,3},{3,2},{4,5},{5,4},{6,7},{7,6},{8,9},{9,8},{10,11... | collective-permute-start | bytes 884744 | tf_op jit(solution)/shard_map/ppermute | solution.py:373
  143.0 7.9 %collective-permute-start.63 = (bf16[192,768]{1,0:T(8,128)(2,1)S(1)}, bf16[192,768]{1,0:T(8,128)(2,1)S(1)}, u32[]{:S(2)}, u32[]{:S(2)}) collective-permute-start(bf16[192,768]{1,0:T(8,128)(2,1)S(1)} %shard_map.284.refs_0_), channel_id=1, source_target_pairs={{0,2},{1,3},{2,0},{3,1},{4,6},{5,7},{6,4},{7,5},{8,10},{9,11},{10,... | collective-permute-start | bytes 884744 | tf_op jit(solution)/shard_map/ppermute | solution.py:377
  144.6 7.4 %collective-permute-start.58 = (bf16[104,768]{1,0:T(8,128)(2,1)S(1)}, bf16[104,768]{1,0:T(8,128)(2,1)S(1)}, u32[]{:S(2)}, u32[]{:S(2)}) collective-permute-start(bf16[104,768]{1,0:T(8,128)(2,1)S(1)} %shard_map.282.refs_0_), channel_id=1, source_target_pairs={{0,6},{1,7},{2,4},{3,5},{4,2},{5,3},{6,0},{7,1},{8,14},{9,15},{10,... | collective-permute-start | bytes 479240 | tf_op jit(solution)/shard_map/ppermute | solution.py:377
  146.1 11.0 %collective-permute-start.69 = (bf16[192,768]{1,0:T(8,128)(2,1)S(1)}, bf16[192,768]{1,0:T(8,128)(2,1)S(1)}, u32[]{:S(2)}, u32[]{:S(2)}) collective-permute-start(bf16[192,768]{1,0:T(8,128)(2,1)S(1)} %collective-permute-done.65.refs_3_), channel_id=1, source_target_pairs={{0,1},{1,0},{2,3},{3,2},{4,5},{5,4},{6,7},{7,6},{8,9},{9,8},{10,11... | collective-permute-start | bytes 884744 | tf_op jit(solution)/shard_map/ppermute | solution.py:373
  149.3 8.2 %collective-permute-start.68 = (bf16[192,768]{1,0:T(8,128)(2,1)S(1)}, bf16[192,768]{1,0:T(8,128)(2,1)S(1)}, u32[]{:S(2)}, u32[]{:S(2)}) collective-permute-start(bf16[192,768]{1,0:T(8,128)(2,1)S(1)} %collective-permute-done.64.refs_2_), channel_id=1, source_target_pairs={{0,1},{1,0},{2,3},{3,2},{4,5},{5,4},{6,7},{7,6},{8,9},{9,8},{10,11... | collective-permute-start | bytes 884744 | tf_op jit(solution)/shard_map/ppermute | solution.py:373
  149.4 6.5 %collective-permute-start.57 = (bf16[104,768]{1,0:T(8,128)(2,1)S(1)}, bf16[104,768]{1,0:T(8,128)(2,1)S(1)}, u32[]{:S(2)}, u32[]{:S(2)}) collective-permute-start(bf16[104,768]{1,0:T(8,128)(2,1)S(1)} %shard_map.282.refs_0_), channel_id=1, source_target_pairs={{0,4},{1,5},{2,6},{3,7},{4,0},{5,1},{6,2},{7,3},{8,12},{9,13},{10,... | collective-permute-start | bytes 479240 | tf_op jit(solution)/shard_map/ppermute | solution.py:377
  150.8 6.2 %collective-permute-start.56 = (bf16[104,768]{1,0:T(8,128)(2,1)S(1)}, bf16[104,768]{1,0:T(8,128)(2,1)S(1)}, u32[]{:S(2)}, u32[]{:S(2)}) collective-permute-start(bf16[104,768]{1,0:T(8,128)(2,1)S(1)} %shard_map.282.refs_0_), channel_id=1, source_target_pairs={{0,2},{1,3},{2,0},{3,1},{4,6},{5,7},{6,4},{7,5},{8,10},{9,11},{10,... | collective-permute-start | bytes 479240 | tf_op jit(solution)/shard_map/ppermute | solution.py:377
  152.0 7.4 %collective-permute-start.67 = (bf16[192,768]{1,0:T(8,128)(2,1)S(1)}, bf16[192,768]{1,0:T(8,128)(2,1)S(1)}, u32[]{:S(2)}, u32[]{:S(2)}) collective-permute-start(bf16[192,768]{1,0:T(8,128)(2,1)S(1)} %collective-permute-done.63.refs_1_), channel_id=1, source_target_pairs={{0,1},{1,0},{2,3},{3,2},{4,5},{5,4},{6,7},{7,6},{8,9},{9,8},{10,11... | collective-permute-start | bytes 884744 | tf_op jit(solution)/shard_map/ppermute | solution.py:373
  155.9 6.8 %collective-permute-start.59 = (bf16[104,768]{1,0:T(8,128)(2,1)S(1)}, bf16[104,768]{1,0:T(8,128)(2,1)S(1)}, u32[]{:S(2)}, u32[]{:S(2)}) collective-permute-start(bf16[104,768]{1,0:T(8,128)(2,1)S(1)} %shard_map.282.refs_0_), channel_id=1, source_target_pairs={{0,1},{1,0},{2,3},{3,2},{4,5},{5,4},{6,7},{7,6},{8,9},{9,8},{10,11... | collective-permute-start | bytes 479240 | tf_op jit(solution)/shard_map/ppermute | solution.py:373
  157.1 5.6 %collective-permute-start.62 = (bf16[104,768]{1,0:T(8,128)(2,1)S(1)}, bf16[104,768]{1,0:T(8,128)(2,1)S(1)}, u32[]{:S(2)}, u32[]{:S(2)}) collective-permute-start(bf16[104,768]{1,0:T(8,128)(2,1)S(1)} %collective-permute-done.58.refs_3_), channel_id=1, source_target_pairs={{0,1},{1,0},{2,3},{3,2},{4,5},{5,4},{6,7},{7,6},{8,9},{9,8},{10,11... | collective-permute-start | bytes 479240 | tf_op jit(solution)/shard_map/ppermute | solution.py:373
  157.1 5.6 %collective-permute-start.61 = (bf16[104,768]{1,0:T(8,128)(2,1)S(1)}, bf16[104,768]{1,0:T(8,128)(2,1)S(1)}, u32[]{:S(2)}, u32[]{:S(2)}) collective-permute-start(bf16[104,768]{1,0:T(8,128)(2,1)S(1)} %collective-permute-done.57.refs_2_), channel_id=1, source_target_pairs={{0,1},{1,0},{2,3},{3,2},{4,5},{5,4},{6,7},{7,6},{8,9},{9,8},{10,11... | collective-permute-start | bytes 479240 | tf_op jit(solution)/shard_map/ppermute | solution.py:373
  157.6 5.1 %collective-permute-start.60 = (bf16[104,768]{1,0:T(8,128)(2,1)S(1)}, bf16[104,768]{1,0:T(8,128)(2,1)S(1)}, u32[]{:S(2)}, u32[]{:S(2)}) collective-permute-start(bf16[104,768]{1,0:T(8,128)(2,1)S(1)} %collective-permute-done.56.refs_1_), channel_id=1, source_target_pairs={{0,1},{1,0},{2,3},{3,2},{4,5},{5,4},{6,7},{7,6},{8,9},{9,8},{10,11... | collective-permute-start | bytes 479240 | tf_op jit(solution)/shard_map/ppermute | solution.py:373
  (13 other events, 141.8 us)

commit v5 on v4

--- a/solution.py
+++ b/solution.py
@@ -488,7 +488,7 @@
 
 def qkv_body(pos, *refs):
     tok, own, oth = refs[0:4], refs[4:8], refs[8:12]
-    q_ref, k0, k1, v0, v1, normed_ref, vec_ref, w_ref, sm = refs[12:]
+    q_ref, k_ref, v_ref, normed_ref, vec_ref, w_ref, sm = refs[12:]
     s, k, c = pos[0], pos[1], pos[2]
     for m in range(4):
         z = s ^ m
@@ -517,18 +517,16 @@
         normed_ref[ROWS * r : ROWS * (r + 1), :] = (hat * gain + shift).astype(bf16)
     projected = dot(normed_ref[...], w_ref[...]) + bias
     q_ref[...] = (projected[:, :QUARTER].astype(bf16).astype(f32) * 0.125).astype(bf16)
-    k0[: OWN // 2, :] = projected[: OWN // 2, QUARTER : 2 * QUARTER].astype(bf16)
-    k1[...] = projected[OWN // 2 :, QUARTER : 2 * QUARTER].astype(bf16)
-    v0[...] = projected[: OWN // 2, 2 * QUARTER :].astype(bf16)
-    v1[...] = projected[OWN // 2 :, 2 * QUARTER :].astype(bf16)
+    k_ref[:OWN, :] = projected[:, QUARTER : 2 * QUARTER].astype(bf16)
+    v_ref[...] = projected[:, 2 * QUARTER :].astype(bf16)
     ids = [tok[r][2 * ROWS :, :ROWS].astype(f32)[:1] for r in range(4)]
     ids = jnp.concatenate(ids + [jnp.zeros((4, ROWS), f32)], 0).astype(bf16)
-    k0[OWN // 2 :, :] = jnp.concatenate([ids, jnp.zeros((8, QUARTER - ROWS), bf16)], 1)
+    k_ref[OWN:, :] = jnp.concatenate([ids, jnp.zeros((8, QUARTER - ROWS), bf16)], 1)
 
 
 def split_ids(kva, kvb):
-    ids_a = kva[OWN // 2 :, :ROWS].astype(f32)
-    ids_b = kvb[OWN // 2 :, :ROWS].astype(f32)
+    ids_a = kva[OWN:, :ROWS].astype(f32)
+    ids_b = kvb[OWN:, :ROWS].astype(f32)
     keys = jnp.concatenate(
         [ids_a[r : r + 1] for r in range(4)] + [ids_b[r : r + 1] for r in range(4)], 1
     )
@@ -536,17 +534,14 @@
 
 
 def all_keys(pair, key_ref, value_ref):
-    half = OWN // 2
     for n in range(2):
-        key_ref[OWN * n : OWN * n + half, :] = pair[4 * n][:half, :]
-        key_ref[OWN * n + half : OWN * (n + 1), :] = pair[4 * n + 1][...]
-        value_ref[OWN * n : OWN * n + half, :] = pair[4 * n + 2][...]
-        value_ref[OWN * n + half : OWN * (n + 1), :] = pair[4 * n + 3][...]
+        key_ref[OWN * n : OWN * (n + 1), :] = pair[2 * n][:OWN, :]
+        value_ref[OWN * n : OWN * (n + 1), :] = pair[2 * n + 1][...]
 
 
 def attend_body(pos, q_ref, *refs):
-    pair, (mixed_ref, state_ref, key_ref, value_ref) = refs[:8], refs[8:]
-    cols, keys = split_ids(pair[0], pair[4])
+    pair, (mixed_ref, state_ref, key_ref, value_ref) = refs[:4], refs[4:]
+    cols, keys = split_ids(pair[0], pair[2])
     all_keys(pair, key_ref, value_ref)
     lane = lax.broadcasted_iota(jnp.int32, (ROWS, 64), 1)
     for r in range(4):
@@ -573,8 +568,8 @@
 def feed_body(pos, *refs):
     tok, mixed, own, oth = refs[0:4], refs[4:8], refs[8:12], refs[12:16]
     vec_ref = refs[16]
-    mid_ref, n2_ref, act_ref, pre_ref, d0, d1, d2, d3, g0, g1, g2, g3, sums_ref, wok_ref = refs[17:31]
-    wo, wu, wd, hat_ref = refs[31:]
+    mid_ref, d0, d1, d2, d3, g0, g1, g2, g3, sums_ref, wok_ref, send_ref, own_ref = refs[17:30]
+    wo, wu, wd, hat_ref, n2_ref, act_ref, wg = refs[30:]
     s, k, c = pos[0], pos[1], pos[2]
     for m in range(4):
         z = s ^ m
@@ -607,7 +602,6 @@
     slope = cdf + pre_act * jnp.exp(-0.5 * pre_act * pre_act) * (1.0 / math.sqrt(2.0 * math.pi))
     grads = jnp.concatenate([ref[ROWS : 2 * ROWS, :] for ref in tok], 0)
     pre = (dot_t(grads, wd[...]) * slope).astype(bf16)
-    pre_ref[...] = pre
     back = dot_t(pre, wu[...])
     sums = [
         jnp.sum(back * hat_ref[...], 0, keepdims=True),
@@ -622,41 +616,20 @@
     d0[...] = down[:ROWS]
     for r, ref in ((1, d1), (2, d2), (3, d3)):
         ref[...] = down[ROWS * r : ROWS * (r + 1)].astype(bf16)
-
-
-def feed_grad_body(pos, act_ref, n2_ref, pre_ref, c0, c1, c2, c3, *refs):
-    sends, (own_ref, wg) = refs[:8], refs[8:]
-    s, c = pos[0], pos[2]
-    grads = jnp.concatenate([ref[ROWS : 2 * ROWS, :] for ref in (c0, c1, c2, c3)], 0)
     for part in range(2):
-        if part == 0:
-            wg[...] = t_dot(act_ref[...], grads)
-        else:
-            wg[...] = t_dot(n2_ref[...], pre_ref[...])
+        wg[...] = t_dot(act_ref[...], grads) if part == 0 else t_dot(n2_ref[...], pre)
         rows = slice(HALF * part, HALF * part + HALF)
         for m in range(4):
             z = s ^ m
             at = pl.ds(pl.multiple_of(z * QUARTER + c * HALF, 32), HALF)
             own_ref[m, rows, :] = wg[at, :]
             at = pl.ds(pl.multiple_of(z * QUARTER + (1 - c) * HALF, 32), HALF)
-            sends[4 * part + m][...] = wg[at, :].astype(bf16)
-
-
-def feed_halves_body(pos, own_ref, *refs):
-    got, outs = refs[:8], refs[8:]
-    for m, out in enumerate(outs):
-        for part in range(2):
-            rows = slice(HALF * part, HALF * part + HALF)
-            total = own_ref[m, rows, :] + got[4 * part + m][...].astype(f32)
-            out[rows, :] = total.astype(out.dtype)
-
-
-def halves_body(pos, own_ref, y0, y1, y2, y3, o0, o1, o2, o3):
-    rows = y0.shape[0]
-    for m, (got, out) in enumerate(((y0, o0), (y1, o1), (y2, o2), (y3, o3))):
-        out[:rows, :] = (own_ref[m, :rows, :] + got[...].astype(f32)).astype(out.dtype)
-        if own_ref.shape[1] > rows:
-            out[rows:, :] = own_ref[m, rows:, :].astype(out.dtype)
+            send_ref[m, rows, :] = wg[at, :].astype(bf16)
+
+
+def feed_halves_body(pos, own_ref, got_ref, o0, o1, o2, o3):
+    for m, out in enumerate((o0, o1, o2, o3)):
+        out[...] = (own_ref[m] + got_ref[m].astype(f32)).astype(out.dtype)
 
 
 def add_body(pos, o0, r1, r2, r3, out):
@@ -673,9 +646,9 @@
 
 
 def attend_grad_body(pos, a0, a1, a2, a3, wok, q_ref, *refs):
-    pair, state_ref, outs = refs[:8], refs[8], refs[9:]
-    dq_ref, own_ref, x0, x1, x2, x3, p_ref, ds_ref, key_ref, value_ref = outs
-    cols, keys = split_ids(pair[0], pair[4])
+    pair, state_ref, outs = refs[:4], refs[4], refs[5:]
+    dq_ref, own_ref, send_k, send_v, p_ref, ds_ref, key_ref, value_ref = outs
+    cols, keys = split_ids(pair[0], pair[2])
     all_keys(pair, key_ref, value_ref)
     grads = jnp.concatenate([ref[...] for ref in (a0, a1, a2, a3)], 0)
     grad_mixed = dot_t(grads, wok[...]).astype(bf16)
@@ -703,23 +676,18 @@
         dv = t_dot(p_ref[...], grad)
         own_ref[:, at] = dk[:OWN]
         own_ref[:, at_v] = dv[:OWN]
-        half = OWN // 2
-        x0[:, at] = dk[OWN : OWN + half].astype(bf16)
-        x1[:, at] = dk[OWN + half :].astype(bf16)
-        x2[:, at] = dv[OWN : OWN + half].astype(bf16)
-        x3[:, at] = dv[OWN + half :].astype(bf16)
+        send_k[:, at] = dk[OWN:].astype(bf16)
+        send_v[:, at] = dv[OWN:].astype(bf16)
     dq_ref[...] = (jnp.concatenate(dq, 1) * 0.125).astype(bf16)
 
 
 def project_grad_body(pos, *refs):
-    tok, mixed, ga = refs[0:4], refs[4:8], refs[8:12]
-    normed, dq, kv_own, y0, y1, y2, y3, w_ref, vec_ref, sums_ref = refs[12:22]
-    x0, x1, x2, x3, own_ref, g0, g1, g2, g3, wg, sm, gk, gp = refs[22:]
+    mixed, ga = refs[0:4], refs[4:8]
+    normed, dq, kv_own, got_k, got_v = refs[8:13]
+    send_ref, own_ref, gp, wg, gk = refs[13:]
     s, k, c = pos[0], pos[1], pos[2]
     gp[:, :QUARTER] = dq[...]
-    got_k = jnp.concatenate([y0[...], y1[...]], 0)
-    got_v = jnp.concatenate([y2[...], y3[...]], 0)
-    got = jnp.concatenate([got_k, got_v], 1).astype(f32)
+    got = jnp.concatenate([got_k[...], got_v[...]], 1).astype(f32)
     gp[:, QUARTER:] = (kv_own[...] + got).astype(bf16)
     wg[:, : 3 * QUARTER] = t_dot(normed[...], gp[...])
     for q in range(4):
@@ -735,6 +703,18 @@
         )
         at = pl.ds(pl.multiple_of((k ^ m) * QUARTER, 64), QUARTER)
         wg[at, 3 * QUARTER :] = t_dot(block, gk[...])
+    for m in range(4):
+        z = s ^ m
+        at = pl.ds(pl.multiple_of(z * QUARTER + c * HALF, 32), HALF)
+        own_ref[m] = wg[at, :]
+        at = pl.ds(pl.multiple_of(z * QUARTER + (1 - c) * HALF, 32), HALF)
+        send_ref[m] = wg[at, :].astype(bf16)
+
+
+def normed_grad_body(pos, *refs):
+    tok, (gp, w_ref, ga_ref, sums_ref) = refs[0:4], refs[4:8]
+    small_ref, g0, g1, g2, g3 = refs[8:]
+    k = pos[1]
     back = dot_t(gp[...], w_ref[...])
     hat = jnp.concatenate([normal(tok[r][:ROWS, :].astype(f32))[0] for r in range(4)], 0)
     ln1_gain = jnp.sum(back * hat, 0, keepdims=True)
@@ -743,7 +723,7 @@
     for r, ref in ((1, g1), (2, g2), (3, g3)):
         ref[...] = back[ROWS * r : ROWS * (r + 1)].astype(bf16)
     gp_sums = jnp.sum(gp[...].astype(f32), 0, keepdims=True)
-    out_bias = jnp.sum(ga[0][...].astype(f32), 0, keepdims=True)
+    out_bias = jnp.sum(ga_ref[...].astype(f32), 0, keepdims=True)
     down_bias = jnp.sum(tok[0][ROWS : 2 * ROWS, :].astype(f32), 0, keepdims=True)
     for z in range(4):
         at = slice(QUARTER * z, QUARTER * (z + 1))
@@ -753,14 +733,14 @@
         row1 = [out_bias[:, at], sums_ref[0:1, at], sums_ref[1:2, at], down_bias[:, at]]
         row1 = jnp.concatenate(row1, 1)
         row2 = jnp.concatenate([sums_ref[2:3, at], jnp.zeros((1, 3 * QUARTER), f32)], 1)
-        sm[z] = jnp.concatenate([row0, row1, row2, jnp.zeros((5, WIDTH), f32)], 0)
-    for m in range(4):
-        z = s ^ m
-        at = pl.ds(pl.multiple_of(z * QUARTER + c * HALF, 32), HALF)
-        own_ref[m, :HALF, :] = wg[at, :]
-        own_ref[m, HALF:, :] = sm[z]
-        at = pl.ds(pl.multiple_of(z * QUARTER + (1 - c) * HALF, 32), HALF)
-        (x0, x1, x2, x3)[m][...] = wg[at, :].astype(bf16)
+        small_ref[z] = jnp.concatenate([row0, row1, row2, jnp.zeros((5, WIDTH), f32)], 0)
+
+
+def last_halves_body(pos, own_ref, small_ref, got, o0, o1, o2, o3):
+    s = pos[0]
+    for m, out in enumerate((o0, o1, o2, o3)):
+        out[:HALF, :] = (own_ref[m] + got[m].astype(f32)).astype(out.dtype)
+        out[HALF:, :] = small_ref[s ^ m].astype(out.dtype)
 
 
 def rows_body(pos, g0, r1, r2, r3, d0, s1, s2, s3, tok_ref, gm_ref, mid_ref, vec_ref, *outs):
@@ -859,13 +839,13 @@
     tok = chip_gather(pack)
     got_rest = seq_gather(rest)
     oth_qkv = [mate_qkv] + [core_swap(block) for block in got_qkv[1:]]
-    half = (OWN // 2, QUARTER)
+    third = (OWN, QUARTER)
     query, *pair, normed, vec, weight_qkv = run(
         qkv_body,
         pos,
         [*tok, *got_qkv, *oth_qkv],
-        [((OWN, QUARTER), bf16), ((OWN // 2 + 8, QUARTER), bf16), (half, bf16), (half, bf16)]
-        + [(half, bf16), ((OWN, WIDTH), bf16), ((8, WIDTH), f32), ((WIDTH, 3 * QUARTER), bf16)],
+        [(third, bf16), ((OWN + 8, QUARTER), bf16), (third, bf16)]
+        + [((OWN, WIDTH), bf16), ((8, WIDTH), f32), ((WIDTH, 3 * QUARTER), bf16)],
         [((4, 16, 3 * QUARTER), f32)],
     )
     pair = [*pair, *[core_swap(x) for x in pair]]
@@ -879,29 +859,21 @@
     mixed = chip_gather(mixed_own)
     got_rest = lax.optimization_barrier((*got_rest, *mixed[1:]))[:4]
     oth_rest = [mate_rest] + [core_swap(block) for block in got_rest[1:]]
-    big, block = (OWN, WIDTH), (ROWS, WIDTH)
-    mid, normed_two, act, pre, d0, d1, d2, d3, g0, g1, g2, g3, sums, w_out_k = run(
+    big, block, piece = (OWN, WIDTH), (ROWS, WIDTH), (QUARTER, WIDTH)
+    mid, d0, d1, d2, d3, g0, g1, g2, g3, sums, w_out_k, feed_send, feed_own = run(
         feed_body,
         pos,
         [*tok, *mixed, *got_rest, *oth_rest, vec],
-        [(block, f32), (big, bf16), (big, bf16), (big, bf16)]
+        [(block, f32)]
         + [(block, f32), (block, bf16), (block, bf16), (block, bf16)] * 2
-        + [((8, WIDTH), f32), ((QUARTER, WIDTH), bf16)],
-        [((WIDTH, WIDTH), bf16)] * 3 + [(big, f32)],
-        limit=32,
+        + [((8, WIDTH), f32), (piece, bf16), ((4, *piece), bf16), ((4, *piece), f32)],
+        [((WIDTH, WIDTH), bf16)] * 3 + [(big, f32), (big, bf16), (big, bf16), ((WIDTH, WIDTH), f32)],
+        limit=40,
     )
     got_g = [chip_swap(g, m) for m, g in ((1, g1), (2, g2), (3, g3))]
-    piece = (QUARTER, WIDTH)
-    *feed_send, feed_own = run(
-        feed_grad_body,
-        pos,
-        [act, normed_two, pre, *tok],
-        [((HALF, WIDTH), bf16)] * 8 + [((4, *piece), f32)],
-        [((WIDTH, WIDTH), f32)],
-    )
-    feed_got = [core_swap(x) for x in feed_send]
+    feed_got = core_swap(feed_send)
     h0, h1, h2, h3 = run(
-        feed_halves_body, pos, [feed_own, *feed_got], [(piece, f32)] + [(piece, bf16)] * 3
+        feed_halves_body, pos, [feed_own, feed_got], [(piece, f32)] + [(piece, bf16)] * 3
     )
     grad_mid, grad_att = run(
         middle_body, pos, [after(g0, h0), *got_g, mid, tok[0], vec], [(block, f32), (block, bf16)]
@@ -912,52 +884,54 @@
         attend_grad_body,
         pos,
         [*ga, w_out_k, query, *pair, state],
-        [((OWN, QUARTER), bf16), ((OWN, 2 * QUARTER), f32)] + [(half, bf16)] * 4,
+        [(third, bf16), ((OWN, 2 * QUARTER), f32)] + [(third, bf16)] * 2,
         [((OWN, 2 * OWN), bf16)] * 2 + [((2 * OWN, QUARTER), bf16)] * 2,
     )
+    pair_send[0], *feed_terms[1:] = lax.optimization_barrier((pair_send[0], *feed_terms[1:]))
     pair_got = [core_swap(x) for x in pair_send]
-    got_d = [chip_swap(after(d, dq), m) for m, d in ((1, d1), (2, d2), (3, d3))]
     lpiece = (HALF + 8, WIDTH)
-    *last_send, last_own, e0, e1, e2, e3 = run(
+    last_send, last_own, grad_proj = run(
         project_grad_body,
         pos,
-        [*tok, *mixed, *ga, normed, dq, kv_own, *pair_got, weight_qkv, vec, sums],
-        [((HALF, WIDTH), bf16)] * 4
-        + [((4, *lpiece), f32), (block, f32)]
-        + [(block, bf16)] * 3,
-        [
-            ((WIDTH, WIDTH), f32),
-            ((4, 8, WIDTH), f32),
-            ((OWN, QUARTER), bf16),
-            ((OWN, 3 * QUARTER), bf16),
-        ],
-    )
-    last_send[2], *got_d = lax.optimization_barrier((last_send[2], *got_d))
-    last_send[3], *feed_terms = lax.optimization_barrier((last_send[3], *feed_terms))
-    last_got = [core_swap(x) for x in last_send]
+        [*mixed, *ga, normed, dq, kv_own, *pair_got],
+        [((4, HALF, WIDTH), bf16), ((4, HALF, WIDTH), f32), ((OWN, 3 * QUARTER), bf16)],
+        [((WIDTH, WIDTH), f32), ((OWN, QUARTER), bf16)],
+    )
+    last_send, feed_terms[0] = lax.optimization_barrier((last_send, feed_terms[0]))
+    last_got = core_swap(last_send)
+    got_d = [chip_swap(after(d, grad_proj), m) for m, d in ((1, d1), (2, d2), (3, d3))]
+    last_small, e0, e1, e2, e3 = run(
+        normed_grad_body,
+        pos,
+        [*tok, grad_proj, weight_qkv, ga[0], sums],
+        [((4, 8, WIDTH), f32), (block, f32)] + [(block, bf16)] * 3,
+    )
     l0, l1, l2, l3 = run(
-        halves_body, pos, [last_own, *last_got], [(lpiece, f32)] + [(lpiece, bf16)] * 3
+        last_halves_body,
+        pos,
+        [last_own, last_small, last_got],
+        [(lpiece, f32)] + [(lpiece, bf16)] * 3,
     )
     last_terms = [seq_swap(h, m) for m, h in ((1, l1), (2, l2), (3, l3))]
-    got_e = [chip_swap(e, m) for m, e in ((1, e1), (2, e2), (3, e3))]
-    (feed_sum,) = run(add_body, pos, [h0, *feed_terms], [(piece, bf16)])
+    (feed_sum,) = run(add_body, pos, [after(h0, l1), *feed_terms], [(piece, bf16)])
     feed_blocks = chip_gather(feed_sum)
-    input_grad, result = run(
-        rows_body,
-        pos,
-        [e0, *got_e, d0, *got_d, tok[0], grad_mid, mid, vec],
-        [((1, *block), f32), ((1, *block), bf16)],
-    )
-    l0, *got_e = lax.optimization_barrier((l0, *got_e))
-    (last_sum,) = run(add_body, pos, [l0, *last_terms], [(lpiece, bf16)], cost=3)
+    l0, *got_d = lax.optimization_barrier((l0, *got_d))
+    (last_sum,) = run(add_body, pos, [l0, *last_terms], [(lpiece, bf16)], cost=2)
     last_blocks = chip_gather(last_sum)
-    feed_oth = [core_swap(b) for b in feed_blocks]
+    got_e = [chip_swap(after(e, last_sum), m) for m, e in ((1, e1), (2, e2), (3, e3))]
+    feed_oth = [core_swap(after(b, last_sum)) for b in feed_blocks]
     grad_w_down, grad_w_up = run(
         feed_join_body,
         pos,
         [after(feed_blocks[0], last_sum), *feed_blocks[1:], *feed_oth],
         [((WIDTH, WIDTH), f32), ((QUARTER, 4 * WIDTH), f32)],
         [((2, 4, QUARTER, WIDTH), bf16)],
+    )
+    input_grad, result = run(
+        rows_body,
+        pos,
+        [after(e0, grad_w_up), *got_e, d0, *got_d, tok[0], grad_mid, mid, vec],
+        [((1, *block), f32), ((1, *block), bf16)],
     )
     last_oth = [core_swap(b) for b in last_blocks]
     grad_w_qkv, grad_w_out, *g, g_up = run(

time: 166 us -> 162 us (0.976)
  starting transfers between devices: 56.1 us -> 51 us
    ppermute x24, waiting for transfers between devices: 22.4 us -> 28.1 us  [chip_swap(): return lax.ppermute(values, 'ctx', [(i, i ^ 2 * mask) for i in range(8)])]
    ppermute x12, starting transfers between devices: 20.5 us -> 16.6 us  [seq_swap(): return lax.ppermute(values, 'seq', [(i, i ^ mask) for i in range(4)])]
    ppermute x34 -> x20, starting transfers between devices: 6.48 us -> 3.99 us  [core_swap(): return lax.ppermute(values, 'ctx', [(i, i ^ 1) for i in range(8)])]
    ppermute x34 -> x20, waiting for transfers between devices: 9.86 us -> 7.51 us  [core_swap(): return lax.ppermute(values, 'ctx', [(i, i ^ 1) for i in range(8)])]
    ppermute x12, waiting for transfers between devices: 31.9 us -> 30 us  [seq_swap(): return lax.ppermute(values, 'seq', [(i, i ^ mask) for i in range(4)])]
  transfers between devices with their start and end apart: 70 -> 56, of which waited for: 31 -> 27; matrix products, arithmetic and copies ran while one was open for 0% -> 0% of each run, Pallas kernels for 15% -> 17%
where the time goes in v5:
time: 162 us
  waiting for transfers between devices  65.6 us (40%)
  starting transfers between devices  51 us (31%)
  Pallas kernels  40.9 us (25%)
  local copies, waits for them, and re-layouts  2.84 us (2%)
    pallas_call x15, Pallas kernels, run(): pl.pallas_call(body, out_shape=[jax.ShapeDtypeStruct(shape, kind) for sha...  40.9 us
    ppermute x24, starting transfers between devices, chip_swap(): return lax.ppermute(values, 'ctx', [(i, i ^ 2 * mask) for i in range(8)])  30.4 us
    ppermute x12, waiting for transfers between devices, seq_swap(): return lax.ppermute(values, 'seq', [(i, i ^ mask) for i in range(4)])  30 us
    ppermute x24, waiting for transfers between devices, chip_swap(): return lax.ppermute(values, 'ctx', [(i, i ^ 2 * mask) for i in range(8)])  28.1 us
    ppermute x12, starting transfers between devices, seq_swap(): return lax.ppermute(values, 'seq', [(i, i ^ mask) for i in range(4)])  16.6 us
    ppermute x20, waiting for transfers between devices, core_swap(): return lax.ppermute(values, 'ctx', [(i, i ^ 1) for i in range(8)])  7.51 us
    ppermute x20, starting transfers between devices, core_swap(): return lax.ppermute(values, 'ctx', [(i, i ^ 1) for i in range(8)])  3.99 us
  transfers between devices with their start and end apart: 56, of which 27 were waited for; matrix products, arithmetic and copies ran while one was open for 0% of the time, Pallas kernels for 17%

profile of v5, /device:TPU:0, one launch (start us, length us, event | category | flops | bytes accessed | tf_op | source)
XLA Modules:
  0.0 161.8 jit_solution(480510338608524022)
XLA Ops:
  1.3 4.1 %shard_map.271 = (bf16[112,576]{1,0:T(8,128)(2,1)}, bf16[112,576]{1,0:T(8,128)(2,1)}, bf16[264,768]{1,0:T(8,128)(2,1)}, bf16[288,768]{1,0:T(8,128)(2,1)}, bf16[288,768]{1,0:T(8,128)(2,1)}) custom-call(s32[3]{0:T(128)} %pad_add_fusion.pos, bf16[192,2304]{1,0:T(8,128)(2,1)} %w_ref.1, bf16[1,128,768]{2,1,0:T(8,128)(2,1)} %tok_ref.1, ...), custom_call_target="tpu_custom_call" | custom-call | flops 524288 | bytes 1000 | tf_op jit(solution)/shard_map/pallas_call | solution.py:402
  5.4 5.1 %collective-permute-start.5 = (bf16[112,576]{1,0:T(8,128)(2,1)}, bf16[112,576]{1,0:T(8,128)(2,1)S(1)}, u32[]{:S(2)}, u32[]{:S(2)}) collective-permute-start(bf16[112,576]{1,0:T(8,128)(2,1)} %get-tuple-element.105.refs_4_), channel_id=1, source_target_pairs={{0,24},{8,16},{16,8},{24,0},{1,25},{9,17},{17,9},{25,1},{2,26},{10... | collective-permute-start | bytes 387080 | tf_op jit(solution)/shard_map/ppermute | solution.py:381
  10.5 2.5 %collective-permute-start.2 = (bf16[264,768]{1,0:T(8,128)(2,1)}, bf16[264,768]{1,0:T(8,128)(2,1)S(1)}, u32[]{:S(2)}, u32[]{:S(2)}) collective-permute-start(bf16[264,768]{1,0:T(8,128)(2,1)} %get-tuple-element.104.refs_0_.tok_ref), channel_id=1, source_target_pairs={{0,6},{1,7},{2,4},{3,5},{4,2},{5,3},{6,0},{7,1},{8,14},{9,15},{10,... | collective-permute-start | bytes 1216520 | tf_op jit(solution)/shard_map/ppermute | solution.py:377
  13.0 0.8 collective-permute-start.3
  14.3 1.1 collective-permute-done.5.refs_7_
  15.4 1.7 %collective-permute-start = (bf16[264,768]{1,0:T(8,128)(2,1)}, bf16[264,768]{1,0:T(8,128)(2,1)S(1)}, u32[]{:S(2)}, u32[]{:S(2)}) collective-permute-start(bf16[264,768]{1,0:T(8,128)(2,1)} %get-tuple-element.104.refs_0_.tok_ref), channel_id=1, source_target_pairs={{0,2},{1,3},{2,0},{3,1},{4,6},{5,7},{6,4},{7,5},{8,10},{9,11},{10,... | collective-permute-start | bytes 1216520 | tf_op jit(solution)/shard_map/ppermute | solution.py:377
  17.1 5.7 %collective-permute-done.4.refs_6_ = bf16[112,576]{1,0:T(8,128)(2,1)S(1)} collective-permute-done((bf16[112,576]{1,0:T(8,128)(2,1)}, bf16[112,576]{1,0:T(8,128)(2,1)S(1)}, u32[]{:S(2)}, u32[]{:S(2)}) %collective-permute-start.4) | collective-permute-done | bytes 129056 | tf_op jit(solution)/shard_map/ppermute | solution.py:381
  23.4 0.9 collective-permute-done.8.refs_11_
  24.2 2.5 %collective-permute-start.16 = (bf16[288,768]{1,0:T(8,128)(2,1)}, bf16[288,768]{1,0:T(8,128)(2,1)S(1)}, u32[]{:S(2)}, u32[]{:S(2)}) collective-permute-start(bf16[288,768]{1,0:T(8,128)(2,1)} %get-tuple-element.112.refs_8_), channel_id=1, source_target_pairs={{0,24},{8,16},{16,8},{24,0},{1,25},{9,17},{17,9},{25,1},{2,26},{10... | collective-permute-start | bytes 1327112 | tf_op jit(solution)/shard_map/ppermute | solution.py:381
  26.7 1.4 collective-permute-done.6.refs_9_
  28.1 1.9 %collective-permute-start.14 = (bf16[288,768]{1,0:T(8,128)(2,1)}, bf16[288,768]{1,0:T(8,128)(2,1)S(1)}, u32[]{:S(2)}, u32[]{:S(2)}) collective-permute-start(bf16[288,768]{1,0:T(8,128)(2,1)} %get-tuple-element.112.refs_8_), channel_id=1, source_target_pairs={{0,8},{8,0},{16,24},{24,16},{1,9},{9,1},{17,25},{25,17},{2,10},{10... | collective-permute-start | bytes 1327112 | tf_op jit(solution)/shard_map/ppermute | solution.py:381
  30.0 1.2 collective-permute-done.1.refs_2_
  31.2 1.0 copy-done
  32.2 0.9 copy-done.4
  33.1 0.9 copy-done.5
  34.1 1.9 %shard_map.272 = (bf16[512,192]{1,0:T(8,128)(2,1)S(1)}, bf16[520,192]{1,0:T(8,128)(2,1)S(1)}, bf16[512,192]{1,0:T(8,128)(2,1)S(1)}, bf16[512,768]{1,0:T(8,128)(2...) custom-call(s32[3]{0:T(128)S(1)} %copy-done.6, bf16[264,768]{1,0:T(8,128)(2,1)S(1)} %copy-done, ...), custom_call_target="tpu_custom_call" | custom-call | flops 524288 | bytes 1000 | tf_op jit(solution)/shard_map/pallas_call | solution.py:402
  36.6 1.4 collective-permute-done.10.refs_3_
  38.0 5.2 %shard_map.273 = (bf16[512,192]{1,0:T(8,128)(2,1)S(1)}, f32[512,256]{1,0:T(8,128)S(1)}) custom-call(s32[3]{0:T(128)S(1)} %copy-done.6, bf16[512,192]{1,0:T(8,128)(2,1)S(1)} %get-tuple-element.107.q_ref, bf16[520,192]{1,0:T(8,128)(2,1)S(1)} %get-tuple-element.108.refs_0_, bf16[512,192]{1,0:T(8,128)(2,1)S(1)} %get-tuple-element.109.refs_1_, ...), custom_call_target="tpu_custom_call" | custom-call | flops 524288 | bytes 1000 | tf_op jit(solution)/shard_map/pallas_call | solution.py:402
  43.3 2.1 %collective-permute-start.13 = (bf16[512,192]{1,0:T(8,128)(2,1)S(1)}, bf16[512,192]{1,0:T(8,128)(2,1)S(1)}, u32[]{:S(2)}, u32[]{:S(2)}) collective-permute-start(bf16[512,192]{1,0:T(8,128)(2,1)S(1)} %get-tuple-element.110.refs_4_.refs_0_), channel_id=1, source_target_pairs={{0,6},{1,7},{2,4},{3,5},{4,2},{5,3},{6,0},{7,1},{8,14},{9,15},{10,... | collective-permute-start | bytes 589832 | tf_op jit(solution)/shard_map/ppermute | solution.py:377
  45.3 1.0 collective-permute-start.12
  46.8 17.7 %collective-permute-done.15.refs_10_ = bf16[288,768]{1,0:T(8,128)(2,1)S(1)} collective-permute-done((bf16[288,768]{1,0:T(8,128)(2,1)}, bf16[288,768]{1,0:T(8,128)(2,1)S(1)}, u32[]{:S(2)}, u32[]{:S(2)}) %collective-permute-start.15) | collective-permute-done | bytes 442400 | tf_op jit(solution)/shard_map/ppermute | solution.py:381
  65.2 1.2 collective-permute-done.17.refs_13_
  67.7 7.2 %shard_map.274 = (f32[128,768]{1,0:T(8,128)S(1)}, f32[128,768]{1,0:T(8,128)S(1)}, bf16[128,768]{1,0:T(8,128)(2,1)S(1)}, bf16[128,768]{1,0:T(8,128)(2,1)S(1)}, bf...) custom-call(s32[3]{0:T(128)S(1)} %copy-done.6, ...), custom_call_target="tpu_custom_call" | custom-call | flops 524288 | bytes 1000 | tf_op jit(solution)/shard_map/pallas_call | solution.py:402
  75.0 1.3 collective-permute-start.21
  76.3 1.5 collective-permute-start.22
  77.8 0.7 collective-permute-start.23
  78.5 0.8 shard_map.275
  79.4 2.7 %collective-permute-start.28 = (bf16[192,768]{1,0:T(8,128)(2,1)S(1)}, bf16[192,768]{1,0:T(8,128)(2,1)S(1)}, u32[]{:S(2)}, u32[]{:S(2)}) collective-permute-start(bf16[192,768]{1,0:T(8,128)(2,1)S(1)} %get-tuple-element.135), channel_id=1, source_target_pairs={{0,24},{8,16},{16,8},{24,0},{1,25},{9,17},{17,9},{25,1},{2,26},{10... | collective-permute-start | bytes 884744 | tf_op jit(solution)/shard_map/ppermute | solution.py:381
  82.7 3.8 %collective-permute-done.22.r2 = bf16[128,768]{1,0:T(8,128)(2,1)S(1)} collective-permute-done((bf16[128,768]{1,0:T(8,128)(2,1)S(1)}, bf16[128,768]{1,0:T(8,128)(2,1)S(1)}, u32[]{:S(2)}, u32[]{:S(2)}) %collective-permute-start.22) | collective-permute-done | bytes 196640 | tf_op jit(solution)/shard_map/ppermute | solution.py:377
  86.5 0.9 collective-permute-done.23.r3
  87.5 0.9 shard_map.276
  88.4 1.8 %collective-permute-start.26 = (bf16[128,768]{1,0:T(8,128)(2,1)S(1)}, bf16[128,768]{1,0:T(8,128)(2,1)S(1)}, u32[]{:S(2)}, u32[]{:S(2)}) collective-permute-start(bf16[128,768]{1,0:T(8,128)(2,1)S(1)} %get-tuple-element.127.a0.refs_4_.refs_6_), channel_id=1, source_target_pairs={{0,6},{1,7},{2,4},{3,5},{4,2},{5,3},{6,0},{7,1},{8,14},{9,15},{10,... | collective-permute-start | bytes 589832 | tf_op jit(solution)/shard_map/ppermute | solution.py:377
  90.2 1.0 collective-permute-start.25
  91.2 0.8 collective-permute-start.24
  92.0 5.3 %collective-permute-done.26.a3.refs_7_ = bf16[128,768]{1,0:T(8,128)(2,1)S(1)} collective-permute-done((bf16[128,768]{1,0:T(8,128)(2,1)S(1)}, bf16[128,768]{1,0:T(8,128)(2,1)S(1)}, u32[]{:S(2)}, u32[]{:S(2)}) %collective-permute-start.26) | collective-permute-done | bytes 196640 | tf_op jit(solution)/shard_map/ppermute | solution.py:377
  97.2 2.8 %collective-permute-done.25.a2.refs_6_ = bf16[128,768]{1,0:T(8,128)(2,1)S(1)} collective-permute-done((bf16[128,768]{1,0:T(8,128)(2,1)S(1)}, bf16[128,768]{1,0:T(8,128)(2,1)S(1)}, u32[]{:S(2)}, u32[]{:S(2)}) %collective-permute-start.25) | collective-permute-done | bytes 196640 | tf_op jit(solution)/shard_map/ppermute | solution.py:377
  100.0 6.8 %shard_map.277 = (bf16[512,192]{1,0:T(8,128)(2,1)S(1)}, f32[512,384]{1,0:T(8,128)S(1)}, bf16[512,192]{1,0:T(8,128)(2,1)S(1)}, bf16[512,192]{1,0:T(8,128)(2,1)S(1)}) custom-call(s32[3]{0:T(128)S(1)} %copy-done.6, bf16[128,768]{1,0:T(8,128)(2,1)S(1)} %get-tuple-element.127.a0.refs_4_.refs_6_, bf16[128,768]{1,0:T(8,128)(2,1)S(1)} %collective-permute-done.24.a1.refs_5_, ...), custom_call_target="tpu_custom_call" | custom-call | flops 524288 | bytes 1000 | tf_op jit(solution)/shard_map/pallas_call | solution.py:402
  107.4 1.0 collective-permute-done.30.refs_12_
  108.8 2.8 %shard_map.278 = (bf16[4,96,768]{2,1,0:T(8,128)(2,1)S(1)}, f32[4,96,768]{2,1,0:T(8,128)S(1)}, bf16[512,576]{1,0:T(8,128)(2,1)S(1)}) custom-call(s32[3]{0:T(128)S(1)} %copy-done.6, bf16[512,192]{1,0:T(8,128)(2,1)S(1)} %get-tuple-element.110.refs_4_.refs_0_, bf16[512,192]{1,0:T(8,128)(2,1)S(1)} %collective-permute-done.11.refs_5_.refs_1_, ...), custom_call_target="tpu_custom_call" | custom-call | flops 524288 | bytes 1000 | tf_op jit(solution)/shard_map/pallas_call | solution.py:402
  111.8 1.4 collective-permute-start.33
  113.8 1.5 collective-permute-start.35
  115.3 1.7 %shard_map.279 = (f32[4,8,768]{2,1,0:T(8,128)S(1)}, f32[128,768]{1,0:T(8,128)S(1)}, bf16[128,768]{1,0:T(8,128)(2,1)S(1)}, bf16[128,768]{1,0:T(8,128)(2,1)S(1)}, bf16[128,768]{1,0:T(8,128)(2,1)S(1)}) custom-call(s32[3]{0:T(128)S(1)} %copy-done.6, bf16[264,768]{1,0:T(8,128)(2,1)S(1)} %copy-done.1, bf16[264,768]{1,0:T(8,128)(2,1)S(1)} %collective-permute-done.refs_1_, ...), custom_call_target="tpu_custom_call" | custom-call | flops 524288 | bytes 1000 | tf_op jit(solution)/shard_map/pallas_call | solution.py:402
  117.1 0.7 shard_map.280
  117.7 0.9 collective-permute-start.37
  118.6 2.6 %collective-permute-start.38 = (bf16[104,768]{1,0:T(8,128)(2,1)S(1)}, bf16[104,768]{1,0:T(8,128)(2,1)S(1)}, u32[]{:S(2)}, u32[]{:S(2)}) collective-permute-start(bf16[104,768]{1,0:T(8,128)(2,1)S(1)} %get-tuple-element.161), channel_id=1, source_target_pairs={{0,24},{8,16},{16,8},{24,0},{1,25},{9,17},{17,9},{25,1},{2,26},{10... | collective-permute-start | bytes 479240 | tf_op jit(solution)/shard_map/ppermute | solution.py:381
  122.0 2.4 %collective-permute-done.34.s2 = bf16[128,768]{1,0:T(8,128)(2,1)S(1)} collective-permute-done((bf16[128,768]{1,0:T(8,128)(2,1)S(1)}, bf16[128,768]{1,0:T(8,128)(2,1)S(1)}, u32[]{:S(2)}, u32[]{:S(2)}) %collective-permute-start.34) | collective-permute-done | bytes 196640 | tf_op jit(solution)/shard_map/ppermute | solution.py:377
  124.3 1.3 collective-permute-start.41
  125.6 0.8 collective-permute-start.40
  126.4 5.4 %collective-permute-done.37.r2 = bf16[104,768]{1,0:T(8,128)(2,1)S(1)} collective-permute-done((bf16[104,768]{1,0:T(8,128)(2,1)S(1)}, bf16[104,768]{1,0:T(8,128)(2,1)S(1)}, u32[]{:S(2)}, u32[]{:S(2)}) %collective-permute-start.37) | collective-permute-done | bytes 159776 | tf_op jit(solution)/shard_map/ppermute | solution.py:381
  133.1 2.4 %collective-permute-start.51 = (bf16[104,768]{1,0:T(8,128)(2,1)S(1)}, bf16[104,768]{1,0:T(8,128)(2,1)S(1)}, u32[]{:S(2)}, u32[]{:S(2)}) collective-permute-start(bf16[104,768]{1,0:T(8,128)(2,1)S(1)} %shard_map.282.refs_0_), channel_id=1, source_target_pairs={{0,6},{1,7},{2,4},{3,5},{4,2},{5,3},{6,0},{7,1},{8,14},{9,15},{10,... | collective-permute-start | bytes 479240 | tf_op jit(solution)/shard_map/ppermute | solution.py:377
  135.7 1.3 collective-permute-done.40.refs_2_
  137.1 1.5 collective-permute-start.50
  138.6 2.6 %collective-permute-done.39.refs_1_ = bf16[192,768]{1,0:T(8,128)(2,1)S(1)} collective-permute-done((bf16[192,768]{1,0:T(8,128)(2,1)S(1)}, bf16[192,768]{1,0:T(8,128)(2,1)S(1)}, u32[]{:S(2)}, u32[]{:S(2)}) %collective-permute-start.39) | collective-permute-done | bytes 294944 | tf_op jit(solution)/shard_map/ppermute | solution.py:377
  141.2 1.1 collective-permute-start.49
  142.3 2.8 %collective-permute-done.51.refs_3_ = bf16[104,768]{1,0:T(8,128)(2,1)S(1)} collective-permute-done((bf16[104,768]{1,0:T(8,128)(2,1)S(1)}, bf16[104,768]{1,0:T(8,128)(2,1)S(1)}, u32[]{:S(2)}, u32[]{:S(2)}) %collective-permute-start.51) | collective-permute-done | bytes 159776 | tf_op jit(solution)/shard_map/ppermute | solution.py:377
  145.6 0.9 collective-permute-done.49.refs_1_
  147.0 1.6 %collective-permute-start.46 = (bf16[128,768]{1,0:T(8,128)(2,1)S(1)}, bf16[128,768]{1,0:T(8,128)(2,1)S(1)}, u32[]{:S(2)}, u32[]{:S(2)}) collective-permute-start(bf16[128,768]{1,0:T(8,128)(2,1)S(1)} %get-tuple-element.169), channel_id=1, source_target_pairs={{0,2},{1,3},{2,0},{3,1},{4,6},{5,7},{6,4},{7,5},{8,10},{9,11},{10,... | collective-permute-start | bytes 589832 | tf_op jit(solution)/shard_map/ppermute | solution.py:377
  148.7 1.2 collective-permute-start.47
  149.9 1.1 collective-permute-start.48
  151.0 2.3 %shard_map.285 = (f32[192,2304]{1,0:T(8,128)}, f32[192,768]{1,0:T(8,128)}, f32[192]{0:T(256)}, f32[192]{0:T(256)}, f32[192]{0:T(256)}, /*index=5*/f32[192]{0:T(2...) custom-call(s32[3]{0:T(128)S(1)} %copy-done.6, ...), custom_call_target="tpu_custom_call" | custom-call | flops 524288 | bytes 1000 | tf_op jit(solution)/shard_map/pallas_call | solution.py:402
  153.3 3.2 %shard_map.283 = (f32[768,768]{1,0:T(8,128)}, f32[192,3072]{1,0:T(8,128)}) custom-call(s32[3]{0:T(128)S(1)} %copy-done.6, bf16[192,768]{1,0:T(8,128)(2,1)S(1)} %shard_map.281.refs_0_, bf16[192,768]{1,0:T(8,128)(2,1)S(1)} %collective-permute-done.39.refs_1_, bf16[192,768]{1,0:T(8,128)(2,1)S(1)} %collective-permute-done.40.refs_2_, ...), custom_call_target="tpu_custom_call" | custom-call | flops 524288 | bytes 1000 | tf_op jit(solution)/shard_map/pallas_call | solution.py:402
  156.6 2.0 %collective-permute-done.47.r2 = bf16[128,768]{1,0:T(8,128)(2,1)S(1)} collective-permute-done((bf16[128,768]{1,0:T(8,128)(2,1)S(1)}, bf16[128,768]{1,0:T(8,128)(2,1)S(1)}, u32[]{:S(2)}, u32[]{:S(2)}) %collective-permute-start.47) | collective-permute-done | bytes 196640 | tf_op jit(solution)/shard_map/ppermute | solution.py:377
  158.6 1.4 collective-permute-done.48.r3
  160.0 1.8 %shard_map.284 = (f32[1,128,768]{2,1,0:T(8,128)}, bf16[1,128,768]{2,1,0:T(8,128)(2,1)}) custom-call(s32[3]{0:T(128)S(1)} %copy-done.6, f32[128,768]{1,0:T(8,128)S(1)} %get-tuple-element.167.g0, bf16[128,768]{1,0:T(8,128)(2,1)S(1)} %collective-permute-done.46.r1, bf16[128,768]{1,0:T(8,128)(2,1)S(1)} %collective-permute-done.47.r2, ...), custom_call_target="tpu_custom_call" | custom-call | flops 524288 | bytes 1000 | tf_op jit(solution)/shard_map/pallas_call | solution.py:402
  (78 shorter events, 10.8 us)
Async XLA Ops:
  1.3 30.0 %copy-start.6 = (s32[3]{0:T(128)S(1)}, s32[3]{0:T(128)}, u32[]{:S(2)}) copy-start(s32[3]{0:T(128)} %pad_add_fusion.pos) | copy-start | bytes 40
  5.4 10.0 %collective-permute-start.5 = (bf16[112,576]{1,0:T(8,128)(2,1)}, bf16[112,576]{1,0:T(8,128)(2,1)S(1)}, u32[]{:S(2)}, u32[]{:S(2)}) collective-permute-start(bf16[112,576]{1,0:T(8,128)(2,1)} %get-tuple-element.105.refs_4_), channel_id=1, source_target_pairs={{0,24},{8,16},{16,8},{24,0},{1,25},{9,17},{17,9},{25,1},{2,26},{10... | collective-permute-start | bytes 387080 | tf_op jit(solution)/shard_map/ppermute | solution.py:381
  10.5 12.3 %collective-permute-start.4 = (bf16[112,576]{1,0:T(8,128)(2,1)}, bf16[112,576]{1,0:T(8,128)(2,1)S(1)}, u32[]{:S(2)}, u32[]{:S(2)}) collective-permute-start(bf16[112,576]{1,0:T(8,128)(2,1)} %get-tuple-element.105.refs_4_), channel_id=1, source_target_pairs={{0,16},{8,24},{16,0},{24,8},{1,17},{9,25},{17,1},{25,9},{2,18},{10... | collective-permute-start | bytes 387080 | tf_op jit(solution)/shard_map/ppermute | solution.py:381
  10.5 17.6 %collective-permute-start.2 = (bf16[264,768]{1,0:T(8,128)(2,1)}, bf16[264,768]{1,0:T(8,128)(2,1)S(1)}, u32[]{:S(2)}, u32[]{:S(2)}) collective-permute-start(bf16[264,768]{1,0:T(8,128)(2,1)} %get-tuple-element.104.refs_0_.tok_ref), channel_id=1, source_target_pairs={{0,6},{1,7},{2,4},{3,5},{4,2},{5,3},{6,0},{7,1},{8,14},{9,15},{10,... | collective-permute-start | bytes 1216520 | tf_op jit(solution)/shard_map/ppermute | solution.py:377
  13.0 9.9 %collective-permute-start.3 = (bf16[112,576]{1,0:T(8,128)(2,1)}, bf16[112,576]{1,0:T(8,128)(2,1)S(1)}, u32[]{:S(2)}, u32[]{:S(2)}) collective-permute-start(bf16[112,576]{1,0:T(8,128)(2,1)} %get-tuple-element.105.refs_4_), channel_id=1, source_target_pairs={{0,8},{8,0},{16,24},{24,16},{1,9},{9,1},{17,25},{25,17},{2,10},{10... | collective-permute-start | bytes 387080 | tf_op jit(solution)/shard_map/ppermute | solution.py:381
  13.8 17.4 %collective-permute-start.1 = (bf16[264,768]{1,0:T(8,128)(2,1)}, bf16[264,768]{1,0:T(8,128)(2,1)S(1)}, u32[]{:S(2)}, u32[]{:S(2)}) collective-permute-start(bf16[264,768]{1,0:T(8,128)(2,1)} %get-tuple-element.104.refs_0_.tok_ref), channel_id=1, source_target_pairs={{0,4},{1,5},{2,6},{3,7},{4,0},{5,1},{6,2},{7,3},{8,12},{9,13},{10,... | collective-permute-start | bytes 1216520 | tf_op jit(solution)/shard_map/ppermute | solution.py:377
  15.4 15.8 %collective-permute-start = (bf16[264,768]{1,0:T(8,128)(2,1)}, bf16[264,768]{1,0:T(8,128)(2,1)S(1)}, u32[]{:S(2)}, u32[]{:S(2)}) collective-permute-start(bf16[264,768]{1,0:T(8,128)(2,1)} %get-tuple-element.104.refs_0_.tok_ref), channel_id=1, source_target_pairs={{0,2},{1,3},{2,0},{3,1},{4,6},{5,7},{6,4},{7,5},{8,10},{9,11},{10,... | collective-permute-start | bytes 1216520 | tf_op jit(solution)/shard_map/ppermute | solution.py:377
  22.8 1.4 collective-permute-start.8
  22.8 3.8 %collective-permute-start.7 = (bf16[112,576]{1,0:T(8,128)(2,1)S(1)}, bf16[112,576]{1,0:T(8,128)(2,1)S(1)}, u32[]{:S(2)}, u32[]{:S(2)}) collective-permute-start(bf16[112,576]{1,0:T(8,128)(2,1)S(1)} %collective-permute-done.4.refs_6_), channel_id=1, source_target_pairs={{0,1},{1,0},{2,3},{3,2},{4,5},{5,4},{6,7},{7,6},{8,9},{9,8},{10,11... | collective-permute-start | bytes 387080 | tf_op jit(solution)/shard_map/ppermute | solution.py:373
  24.2 22.1 %collective-permute-start.16 = (bf16[288,768]{1,0:T(8,128)(2,1)}, bf16[288,768]{1,0:T(8,128)(2,1)S(1)}, u32[]{:S(2)}, u32[]{:S(2)}) collective-permute-start(bf16[288,768]{1,0:T(8,128)(2,1)} %get-tuple-element.112.refs_8_), channel_id=1, source_target_pairs={{0,24},{8,16},{16,8},{24,0},{1,25},{9,17},{17,9},{25,1},{2,26},{10... | collective-permute-start | bytes 1327112 | tf_op jit(solution)/shard_map/ppermute | solution.py:381
  26.7 1.4 collective-permute-start.6
  28.1 36.4 %collective-permute-start.15 = (bf16[288,768]{1,0:T(8,128)(2,1)}, bf16[288,768]{1,0:T(8,128)(2,1)S(1)}, u32[]{:S(2)}, u32[]{:S(2)}) collective-permute-start(bf16[288,768]{1,0:T(8,128)(2,1)} %get-tuple-element.112.refs_8_), channel_id=1, source_target_pairs={{0,16},{8,24},{16,0},{24,8},{1,17},{9,25},{17,1},{25,9},{2,18},{10... | collective-permute-start | bytes 1327112 | tf_op jit(solution)/shard_map/ppermute | solution.py:381
  28.1 36.4 %collective-permute-start.14 = (bf16[288,768]{1,0:T(8,128)(2,1)}, bf16[288,768]{1,0:T(8,128)(2,1)S(1)}, u32[]{:S(2)}, u32[]{:S(2)}) collective-permute-start(bf16[288,768]{1,0:T(8,128)(2,1)} %get-tuple-element.112.refs_8_), channel_id=1, source_target_pairs={{0,8},{8,0},{16,24},{24,16},{1,9},{9,1},{17,25},{25,17},{2,10},{10... | collective-permute-start | bytes 1327112 | tf_op jit(solution)/shard_map/ppermute | solution.py:381
  31.2 1.0 copy-start
  32.2 0.9 copy-start.4
  33.1 0.9 copy-start.5
  36.0 31.7 %copy-start.1 = (bf16[264,768]{1,0:T(8,128)(2,1)S(1)}, bf16[264,768]{1,0:T(8,128)(2,1)}, u32[]{:S(2)}) copy-start(bf16[264,768]{1,0:T(8,128)(2,1)} %get-tuple-element.104.refs_0_.tok_ref) | copy-start | bytes 1216516
  36.0 31.7 %copy-start.2 = (bf16[288,768]{1,0:T(8,128)(2,1)S(1)}, bf16[288,768]{1,0:T(8,128)(2,1)}, u32[]{:S(2)}) copy-start(bf16[288,768]{1,0:T(8,128)(2,1)} %get-tuple-element.112.refs_8_) | copy-start | bytes 1327108
  36.0 31.6 %copy-start.3 = (bf16[288,768]{1,0:T(8,128)(2,1)S(1)}, bf16[288,768]{1,0:T(8,128)(2,1)}, u32[]{:S(2)}) copy-start(bf16[288,768]{1,0:T(8,128)(2,1)} %get-tuple-element.116.refs_12_) | copy-start | bytes 1327108
  36.0 2.0 %collective-permute-start.9 = (bf16[520,192]{1,0:T(8,128)(2,1)S(1)}, bf16[520,192]{1,0:T(8,128)(2,1)S(1)}, u32[]{:S(2)}, u32[]{:S(2)}) collective-permute-start(bf16[520,192]{1,0:T(8,128)(2,1)S(1)} %get-tuple-element.108.refs_0_), channel_id=1, source_target_pairs={{0,1},{1,0},{2,3},{3,2},{4,5},{5,4},{6,7},{7,6},{8,9},{9,8},{10,11... | collective-permute-start | bytes 599048 | tf_op jit(solution)/shard_map/ppermute | solution.py:373
  36.1 1.9 %collective-permute-start.10 = (bf16[512,192]{1,0:T(8,128)(2,1)S(1)}, bf16[512,192]{1,0:T(8,128)(2,1)S(1)}, u32[]{:S(2)}, u32[]{:S(2)}) collective-permute-start(bf16[512,192]{1,0:T(8,128)(2,1)S(1)} %get-tuple-element.109.refs_1_), channel_id=1, source_target_pairs={{0,1},{1,0},{2,3},{3,2},{4,5},{5,4},{6,7},{7,6},{8,9},{9,8},{10,11... | collective-permute-start | bytes 589832 | tf_op jit(solution)/shard_map/ppermute | solution.py:373
  43.3 21.3 %collective-permute-start.13 = (bf16[512,192]{1,0:T(8,128)(2,1)S(1)}, bf16[512,192]{1,0:T(8,128)(2,1)S(1)}, u32[]{:S(2)}, u32[]{:S(2)}) collective-permute-start(bf16[512,192]{1,0:T(8,128)(2,1)S(1)} %get-tuple-element.110.refs_4_.refs_0_), channel_id=1, source_target_pairs={{0,6},{1,7},{2,4},{3,5},{4,2},{5,3},{6,0},{7,1},{8,14},{9,15},{10,... | collective-permute-start | bytes 589832 | tf_op jit(solution)/shard_map/ppermute | solution.py:377
  45.3 19.2 %collective-permute-start.12 = (bf16[512,192]{1,0:T(8,128)(2,1)S(1)}, bf16[512,192]{1,0:T(8,128)(2,1)S(1)}, u32[]{:S(2)}, u32[]{:S(2)}) collective-permute-start(bf16[512,192]{1,0:T(8,128)(2,1)S(1)} %get-tuple-element.110.refs_4_.refs_0_), channel_id=1, source_target_pairs={{0,4},{1,5},{2,6},{3,7},{4,0},{5,1},{6,2},{7,3},{8,12},{9,13},{10,... | collective-permute-start | bytes 589832 | tf_op jit(solution)/shard_map/ppermute | solution.py:377
  46.3 18.2 %collective-permute-start.11 = (bf16[512,192]{1,0:T(8,128)(2,1)S(1)}, bf16[512,192]{1,0:T(8,128)(2,1)S(1)}, u32[]{:S(2)}, u32[]{:S(2)}) collective-permute-start(bf16[512,192]{1,0:T(8,128)(2,1)S(1)} %get-tuple-element.110.refs_4_.refs_0_), channel_id=1, source_target_pairs={{0,2},{1,3},{2,0},{3,1},{4,6},{5,7},{6,4},{7,5},{8,10},{9,11},{10,... | collective-permute-start | bytes 589832 | tf_op jit(solution)/shard_map/ppermute | solution.py:377
  64.5 1.9 %collective-permute-start.17 = (bf16[288,768]{1,0:T(8,128)(2,1)S(1)}, bf16[288,768]{1,0:T(8,128)(2,1)S(1)}, u32[]{:S(2)}, u32[]{:S(2)}) collective-permute-start(bf16[288,768]{1,0:T(8,128)(2,1)S(1)} %collective-permute-done.14.refs_9_), channel_id=1, source_target_pairs={{0,1},{1,0},{2,3},{3,2},{4,5},{5,4},{6,7},{7,6},{8,9},{9,8},{10,11... | collective-permute-start | bytes 1327112 | tf_op jit(solution)/shard_map/ppermute | solution.py:373
  64.6 2.4 %collective-permute-start.18 = (bf16[288,768]{1,0:T(8,128)(2,1)S(1)}, bf16[288,768]{1,0:T(8,128)(2,1)S(1)}, u32[]{:S(2)}, u32[]{:S(2)}) collective-permute-start(bf16[288,768]{1,0:T(8,128)(2,1)S(1)} %collective-permute-done.15.refs_10_), channel_id=1, source_target_pairs={{0,1},{1,0},{2,3},{3,2},{4,5},{5,4},{6,7},{7,6},{8,9},{9,8},{10,11... | collective-permute-start | bytes 1327112 | tf_op jit(solution)/shard_map/ppermute | solution.py:373
  65.1 2.5 %collective-permute-start.19 = (bf16[288,768]{1,0:T(8,128)(2,1)S(1)}, bf16[288,768]{1,0:T(8,128)(2,1)S(1)}, u32[]{:S(2)}, u32[]{:S(2)}) collective-permute-start(bf16[288,768]{1,0:T(8,128)(2,1)S(1)} %collective-permute-done.16.refs_11_), channel_id=1, source_target_pairs={{0,1},{1,0},{2,3},{3,2},{4,5},{5,4},{6,7},{7,6},{8,9},{9,8},{10,11... | collective-permute-start | bytes 1327112 | tf_op jit(solution)/shard_map/ppermute | solution.py:373
  74.9 3.7 %collective-permute-start.20 = (bf16[4,192,768]{2,1,0:T(8,128)(2,1)S(1)}, bf16[4,192,768]{2,1,0:T(8,128)(2,1)S(1)}, u32[]{:S(2)}, u32[]{:S(2)}) collective-permute-start(bf16[4,192,768]{2,1,0:T(8,128)(2,1)S(1)} %get-tuple-element.120), channel_id=1, source_target_pairs={{0,1},{1,0},{2,3},{3,2},{4,5},{5,4},{6,7},{7,6},{8,9},{9,8},{10,11... | collective-permute-start | bytes 3538952 | tf_op jit(solution)/shard_map/ppermute | solution.py:373
  75.0 7.7 %collective-permute-start.21 = (bf16[128,768]{1,0:T(8,128)(2,1)S(1)}, bf16[128,768]{1,0:T(8,128)(2,1)S(1)}, u32[]{:S(2)}, u32[]{:S(2)}) collective-permute-start(bf16[128,768]{1,0:T(8,128)(2,1)S(1)} %get-tuple-element.123), channel_id=1, source_target_pairs={{0,2},{1,3},{2,0},{3,1},{4,6},{5,7},{6,4},{7,5},{8,10},{9,11},{10,... | collective-permute-start | bytes 589832 | tf_op jit(solution)/shard_map/ppermute | solution.py:377
  76.3 10.2 %collective-permute-start.22 = (bf16[128,768]{1,0:T(8,128)(2,1)S(1)}, bf16[128,768]{1,0:T(8,128)(2,1)S(1)}, u32[]{:S(2)}, u32[]{:S(2)}) collective-permute-start(bf16[128,768]{1,0:T(8,128)(2,1)S(1)} %get-tuple-element.124), channel_id=1, source_target_pairs={{0,4},{1,5},{2,6},{3,7},{4,0},{5,1},{6,2},{7,3},{8,12},{9,13},{10,... | collective-permute-start | bytes 589832 | tf_op jit(solution)/shard_map/ppermute | solution.py:377
  77.8 9.6 %collective-permute-start.23 = (bf16[128,768]{1,0:T(8,128)(2,1)S(1)}, bf16[128,768]{1,0:T(8,128)(2,1)S(1)}, u32[]{:S(2)}, u32[]{:S(2)}) collective-permute-start(bf16[128,768]{1,0:T(8,128)(2,1)S(1)} %get-tuple-element.125), channel_id=1, source_target_pairs={{0,6},{1,7},{2,4},{3,5},{4,2},{5,3},{6,0},{7,1},{8,14},{9,15},{10,... | collective-permute-start | bytes 589832 | tf_op jit(solution)/shard_map/ppermute | solution.py:377
  79.3 27.6 %collective-permute-start.27 = (bf16[192,768]{1,0:T(8,128)(2,1)S(1)}, bf16[192,768]{1,0:T(8,128)(2,1)S(1)}, u32[]{:S(2)}, u32[]{:S(2)}) collective-permute-start(bf16[192,768]{1,0:T(8,128)(2,1)S(1)} %get-tuple-element.134), channel_id=1, source_target_pairs={{0,16},{8,24},{16,0},{24,8},{1,17},{9,25},{17,1},{25,9},{2,18},{10... | collective-permute-start | bytes 884744 | tf_op jit(solution)/shard_map/ppermute | solution.py:381
  79.4 27.5 %collective-permute-start.28 = (bf16[192,768]{1,0:T(8,128)(2,1)S(1)}, bf16[192,768]{1,0:T(8,128)(2,1)S(1)}, u32[]{:S(2)}, u32[]{:S(2)}) collective-permute-start(bf16[192,768]{1,0:T(8,128)(2,1)S(1)} %get-tuple-element.135), channel_id=1, source_target_pairs={{0,24},{8,16},{16,8},{24,0},{1,25},{9,17},{17,9},{25,1},{2,26},{10... | collective-permute-start | bytes 884744 | tf_op jit(solution)/shard_map/ppermute | solution.py:381
  88.4 8.8 %collective-permute-start.26 = (bf16[128,768]{1,0:T(8,128)(2,1)S(1)}, bf16[128,768]{1,0:T(8,128)(2,1)S(1)}, u32[]{:S(2)}, u32[]{:S(2)}) collective-permute-start(bf16[128,768]{1,0:T(8,128)(2,1)S(1)} %get-tuple-element.127.a0.refs_4_.refs_6_), channel_id=1, source_target_pairs={{0,6},{1,7},{2,4},{3,5},{4,2},{5,3},{6,0},{7,1},{8,14},{9,15},{10,... | collective-permute-start | bytes 589832 | tf_op jit(solution)/shard_map/ppermute | solution.py:377
  90.2 9.8 %collective-permute-start.25 = (bf16[128,768]{1,0:T(8,128)(2,1)S(1)}, bf16[128,768]{1,0:T(8,128)(2,1)S(1)}, u32[]{:S(2)}, u32[]{:S(2)}) collective-permute-start(bf16[128,768]{1,0:T(8,128)(2,1)S(1)} %get-tuple-element.127.a0.refs_4_.refs_6_), channel_id=1, source_target_pairs={{0,4},{1,5},{2,6},{3,7},{4,0},{5,1},{6,2},{7,3},{8,12},{9,13},{10,... | collective-permute-start | bytes 589832 | tf_op jit(solution)/shard_map/ppermute | solution.py:377
  91.2 8.8 %collective-permute-start.24 = (bf16[128,768]{1,0:T(8,128)(2,1)S(1)}, bf16[128,768]{1,0:T(8,128)(2,1)S(1)}, u32[]{:S(2)}, u32[]{:S(2)}) collective-permute-start(bf16[128,768]{1,0:T(8,128)(2,1)S(1)} %get-tuple-element.127.a0.refs_4_.refs_6_), channel_id=1, source_target_pairs={{0,2},{1,3},{2,0},{3,1},{4,6},{5,7},{6,4},{7,5},{8,10},{9,11},{10,... | collective-permute-start | bytes 589832 | tf_op jit(solution)/shard_map/ppermute | solution.py:377
  97.2 14.3 %collective-permute-start.31 = (bf16[192,768]{1,0:T(8,128)(2,1)S(1)}, bf16[192,768]{1,0:T(8,128)(2,1)S(1)}, u32[]{:S(2)}, u32[]{:S(2)}) collective-permute-start(bf16[192,768]{1,0:T(8,128)(2,1)S(1)} %get-tuple-element.145), channel_id=1, source_target_pairs={{0,8},{8,0},{16,24},{24,16},{1,9},{9,1},{17,25},{25,17},{2,10},{10... | collective-permute-start | bytes 884744 | tf_op jit(solution)/shard_map/ppermute | solution.py:381
  106.8 1.6 collective-permute-start.30
  106.9 1.9 %collective-permute-start.29 = (bf16[512,192]{1,0:T(8,128)(2,1)S(1)}, bf16[512,192]{1,0:T(8,128)(2,1)S(1)}, u32[]{:S(2)}, u32[]{:S(2)}) collective-permute-start(bf16[512,192]{1,0:T(8,128)(2,1)S(1)} %get-tuple-element.136), channel_id=1, source_target_pairs={{0,1},{1,0},{2,3},{3,2},{4,5},{5,4},{6,7},{7,6},{8,9},{9,8},{10,11... | collective-permute-start | bytes 589832 | tf_op jit(solution)/shard_map/ppermute | solution.py:373
  111.6 5.4 %collective-permute-start.32 = (bf16[4,96,768]{2,1,0:T(8,128)(2,1)S(1)}, bf16[4,96,768]{2,1,0:T(8,128)(2,1)S(1)}, u32[]{:S(2)}, u32[]{:S(2)}) collective-permute-start(bf16[4,96,768]{2,1,0:T(8,128)(2,1)S(1)} %get-tuple-element.146), channel_id=1, source_target_pairs={{0,1},{1,0},{2,3},{3,2},{4,5},{5,4},{6,7},{7,6},{8,9},{9,8},{10,11... | collective-permute-start | bytes 1769480 | tf_op jit(solution)/shard_map/ppermute | solution.py:373
  111.8 9.4 %collective-permute-start.33 = (bf16[128,768]{1,0:T(8,128)(2,1)S(1)}, bf16[128,768]{1,0:T(8,128)(2,1)S(1)}, u32[]{:S(2)}, u32[]{:S(2)}) collective-permute-start(bf16[128,768]{1,0:T(8,128)(2,1)S(1)} %get-tuple-element.154), channel_id=1, source_target_pairs={{0,2},{1,3},{2,0},{3,1},{4,6},{5,7},{6,4},{7,5},{8,10},{9,11},{10,... | collective-permute-start | bytes 589832 | tf_op jit(solution)/shard_map/ppermute | solution.py:377
  113.2 11.1 %collective-permute-start.34 = (bf16[128,768]{1,0:T(8,128)(2,1)S(1)}, bf16[128,768]{1,0:T(8,128)(2,1)S(1)}, u32[]{:S(2)}, u32[]{:S(2)}) collective-permute-start(bf16[128,768]{1,0:T(8,128)(2,1)S(1)} %get-tuple-element.156), channel_id=1, source_target_pairs={{0,4},{1,5},{2,6},{3,7},{4,0},{5,1},{6,2},{7,3},{8,12},{9,13},{10,... | collective-permute-start | bytes 589832 | tf_op jit(solution)/shard_map/ppermute | solution.py:377
  113.8 11.8 %collective-permute-start.35 = (bf16[128,768]{1,0:T(8,128)(2,1)S(1)}, bf16[128,768]{1,0:T(8,128)(2,1)S(1)}, u32[]{:S(2)}, u32[]{:S(2)}) collective-permute-start(bf16[128,768]{1,0:T(8,128)(2,1)S(1)} %get-tuple-element.158), channel_id=1, source_target_pairs={{0,6},{1,7},{2,4},{3,5},{4,2},{5,3},{6,0},{7,1},{8,14},{9,15},{10,... | collective-permute-start | bytes 589832 | tf_op jit(solution)/shard_map/ppermute | solution.py:377
  117.7 14.1 %collective-permute-start.37 = (bf16[104,768]{1,0:T(8,128)(2,1)S(1)}, bf16[104,768]{1,0:T(8,128)(2,1)S(1)}, u32[]{:S(2)}, u32[]{:S(2)}) collective-permute-start(bf16[104,768]{1,0:T(8,128)(2,1)S(1)} %get-tuple-element.160), channel_id=1, source_target_pairs={{0,16},{8,24},{16,0},{24,8},{1,17},{9,25},{17,1},{25,9},{2,18},{10... | collective-permute-start | bytes 479240 | tf_op jit(solution)/shard_map/ppermute | solution.py:381
  118.6 13.8 %collective-permute-start.38 = (bf16[104,768]{1,0:T(8,128)(2,1)S(1)}, bf16[104,768]{1,0:T(8,128)(2,1)S(1)}, u32[]{:S(2)}, u32[]{:S(2)}) collective-permute-start(bf16[104,768]{1,0:T(8,128)(2,1)S(1)} %get-tuple-element.161), channel_id=1, source_target_pairs={{0,24},{8,16},{16,8},{24,0},{1,25},{9,17},{17,9},{25,1},{2,26},{10... | collective-permute-start | bytes 479240 | tf_op jit(solution)/shard_map/ppermute | solution.py:381
  121.2 11.2 %collective-permute-start.36 = (bf16[104,768]{1,0:T(8,128)(2,1)S(1)}, bf16[104,768]{1,0:T(8,128)(2,1)S(1)}, u32[]{:S(2)}, u32[]{:S(2)}) collective-permute-start(bf16[104,768]{1,0:T(8,128)(2,1)S(1)} %get-tuple-element.147), channel_id=1, source_target_pairs={{0,8},{8,0},{16,24},{24,16},{1,9},{9,1},{17,25},{25,17},{2,10},{10... | collective-permute-start | bytes 479240 | tf_op jit(solution)/shard_map/ppermute | solution.py:381
  124.3 11.2 %collective-permute-start.41 = (bf16[192,768]{1,0:T(8,128)(2,1)S(1)}, bf16[192,768]{1,0:T(8,128)(2,1)S(1)}, u32[]{:S(2)}, u32[]{:S(2)}) collective-permute-start(bf16[192,768]{1,0:T(8,128)(2,1)S(1)} %shard_map.281.refs_0_), channel_id=1, source_target_pairs={{0,6},{1,7},{2,4},{3,5},{4,2},{5,3},{6,0},{7,1},{8,14},{9,15},{10,... | collective-permute-start | bytes 884744 | tf_op jit(solution)/shard_map/ppermute | solution.py:377
  125.6 11.4 %collective-permute-start.40 = (bf16[192,768]{1,0:T(8,128)(2,1)S(1)}, bf16[192,768]{1,0:T(8,128)(2,1)S(1)}, u32[]{:S(2)}, u32[]{:S(2)}) collective-permute-start(bf16[192,768]{1,0:T(8,128)(2,1)S(1)} %shard_map.281.refs_0_), channel_id=1, source_target_pairs={{0,4},{1,5},{2,6},{3,7},{4,0},{5,1},{6,2},{7,3},{8,12},{9,13},{10,... | collective-permute-start | bytes 884744 | tf_op jit(solution)/shard_map/ppermute | solution.py:377
  131.8 9.4 %collective-permute-start.39 = (bf16[192,768]{1,0:T(8,128)(2,1)S(1)}, bf16[192,768]{1,0:T(8,128)(2,1)S(1)}, u32[]{:S(2)}, u32[]{:S(2)}) collective-permute-start(bf16[192,768]{1,0:T(8,128)(2,1)S(1)} %shard_map.281.refs_0_), channel_id=1, source_target_pairs={{0,2},{1,3},{2,0},{3,1},{4,6},{5,7},{6,4},{7,5},{8,10},{9,11},{10,... | collective-permute-start | bytes 884744 | tf_op jit(solution)/shard_map/ppermute | solution.py:377
  133.1 9.2 %collective-permute-start.52 = (bf16[104,768]{1,0:T(8,128)(2,1)S(1)}, bf16[104,768]{1,0:T(8,128)(2,1)S(1)}, u32[]{:S(2)}, u32[]{:S(2)}) collective-permute-start(bf16[104,768]{1,0:T(8,128)(2,1)S(1)} %shard_map.282.refs_0_), channel_id=1, source_target_pairs={{0,1},{1,0},{2,3},{3,2},{4,5},{5,4},{6,7},{7,6},{8,9},{9,8},{10,11... | collective-permute-start | bytes 479240 | tf_op jit(solution)/shard_map/ppermute | solution.py:373
  133.1 11.9 %collective-permute-start.51 = (bf16[104,768]{1,0:T(8,128)(2,1)S(1)}, bf16[104,768]{1,0:T(8,128)(2,1)S(1)}, u32[]{:S(2)}, u32[]{:S(2)}) collective-permute-start(bf16[104,768]{1,0:T(8,128)(2,1)S(1)} %shard_map.282.refs_0_), channel_id=1, source_target_pairs={{0,6},{1,7},{2,4},{3,5},{4,2},{5,3},{6,0},{7,1},{8,14},{9,15},{10,... | collective-permute-start | bytes 479240 | tf_op jit(solution)/shard_map/ppermute | solution.py:377
  135.6 10.9 %collective-permute-start.42 = (bf16[192,768]{1,0:T(8,128)(2,1)S(1)}, bf16[192,768]{1,0:T(8,128)(2,1)S(1)}, u32[]{:S(2)}, u32[]{:S(2)}) collective-permute-start(bf16[192,768]{1,0:T(8,128)(2,1)S(1)} %shard_map.281.refs_0_), channel_id=1, source_target_pairs={{0,1},{1,0},{2,3},{3,2},{4,5},{5,4},{6,7},{7,6},{8,9},{9,8},{10,11... | collective-permute-start | bytes 884744 | tf_op jit(solution)/shard_map/ppermute | solution.py:373
  137.1 8.0 %collective-permute-start.50 = (bf16[104,768]{1,0:T(8,128)(2,1)S(1)}, bf16[104,768]{1,0:T(8,128)(2,1)S(1)}, u32[]{:S(2)}, u32[]{:S(2)}) collective-permute-start(bf16[104,768]{1,0:T(8,128)(2,1)S(1)} %shard_map.282.refs_0_), channel_id=1, source_target_pairs={{0,4},{1,5},{2,6},{3,7},{4,0},{5,1},{6,2},{7,3},{8,12},{9,13},{10,... | collective-permute-start | bytes 479240 | tf_op jit(solution)/shard_map/ppermute | solution.py:377
  141.2 5.3 %collective-permute-start.49 = (bf16[104,768]{1,0:T(8,128)(2,1)S(1)}, bf16[104,768]{1,0:T(8,128)(2,1)S(1)}, u32[]{:S(2)}, u32[]{:S(2)}) collective-permute-start(bf16[104,768]{1,0:T(8,128)(2,1)S(1)} %shard_map.282.refs_0_), channel_id=1, source_target_pairs={{0,2},{1,3},{2,0},{3,1},{4,6},{5,7},{6,4},{7,5},{8,10},{9,11},{10,... | collective-permute-start | bytes 479240 | tf_op jit(solution)/shard_map/ppermute | solution.py:377
  142.3 7.6 %collective-permute-start.45 = (bf16[192,768]{1,0:T(8,128)(2,1)S(1)}, bf16[192,768]{1,0:T(8,128)(2,1)S(1)}, u32[]{:S(2)}, u32[]{:S(2)}) collective-permute-start(bf16[192,768]{1,0:T(8,128)(2,1)S(1)} %collective-permute-done.41.refs_3_), channel_id=1, source_target_pairs={{0,1},{1,0},{2,3},{3,2},{4,5},{5,4},{6,7},{7,6},{8,9},{9,8},{10,11... | collective-permute-start | bytes 884744 | tf_op jit(solution)/shard_map/ppermute | solution.py:373
  145.0 1.9 %collective-permute-start.55 = (bf16[104,768]{1,0:T(8,128)(2,1)S(1)}, bf16[104,768]{1,0:T(8,128)(2,1)S(1)}, u32[]{:S(2)}, u32[]{:S(2)}) collective-permute-start(bf16[104,768]{1,0:T(8,128)(2,1)S(1)} %collective-permute-done.51.refs_3_), channel_id=1, source_target_pairs={{0,1},{1,0},{2,3},{3,2},{4,5},{5,4},{6,7},{7,6},{8,9},{9,8},{10,11... | collective-permute-start | bytes 479240 | tf_op jit(solution)/shard_map/ppermute | solution.py:373
  145.1 2.0 %collective-permute-start.54 = (bf16[104,768]{1,0:T(8,128)(2,1)S(1)}, bf16[104,768]{1,0:T(8,128)(2,1)S(1)}, u32[]{:S(2)}, u32[]{:S(2)}) collective-permute-start(bf16[104,768]{1,0:T(8,128)(2,1)S(1)} %collective-permute-done.50.refs_2_), channel_id=1, source_target_pairs={{0,1},{1,0},{2,3},{3,2},{4,5},{5,4},{6,7},{7,6},{8,9},{9,8},{10,11... | collective-permute-start | bytes 479240 | tf_op jit(solution)/shard_map/ppermute | solution.py:373
  146.5 2.2 %collective-permute-start.53 = (bf16[104,768]{1,0:T(8,128)(2,1)S(1)}, bf16[104,768]{1,0:T(8,128)(2,1)S(1)}, u32[]{:S(2)}, u32[]{:S(2)}) collective-permute-start(bf16[104,768]{1,0:T(8,128)(2,1)S(1)} %collective-permute-done.49.refs_1_), channel_id=1, source_target_pairs={{0,1},{1,0},{2,3},{3,2},{4,5},{5,4},{6,7},{7,6},{8,9},{9,8},{10,11... | collective-permute-start | bytes 479240 | tf_op jit(solution)/shard_map/ppermute | solution.py:373
  146.5 6.8 %collective-permute-start.44 = (bf16[192,768]{1,0:T(8,128)(2,1)S(1)}, bf16[192,768]{1,0:T(8,128)(2,1)S(1)}, u32[]{:S(2)}, u32[]{:S(2)}) collective-permute-start(bf16[192,768]{1,0:T(8,128)(2,1)S(1)} %collective-permute-done.40.refs_2_), channel_id=1, source_target_pairs={{0,1},{1,0},{2,3},{3,2},{4,5},{5,4},{6,7},{7,6},{8,9},{9,8},{10,11... | collective-permute-start | bytes 884744 | tf_op jit(solution)/shard_map/ppermute | solution.py:373
  147.0 6.3 %collective-permute-start.43 = (bf16[192,768]{1,0:T(8,128)(2,1)S(1)}, bf16[192,768]{1,0:T(8,128)(2,1)S(1)}, u32[]{:S(2)}, u32[]{:S(2)}) collective-permute-start(bf16[192,768]{1,0:T(8,128)(2,1)S(1)} %collective-permute-done.39.refs_1_), channel_id=1, source_target_pairs={{0,1},{1,0},{2,3},{3,2},{4,5},{5,4},{6,7},{7,6},{8,9},{9,8},{10,11... | collective-permute-start | bytes 884744 | tf_op jit(solution)/shard_map/ppermute | solution.py:373
  147.0 9.5 %collective-permute-start.46 = (bf16[128,768]{1,0:T(8,128)(2,1)S(1)}, bf16[128,768]{1,0:T(8,128)(2,1)S(1)}, u32[]{:S(2)}, u32[]{:S(2)}) collective-permute-start(bf16[128,768]{1,0:T(8,128)(2,1)S(1)} %get-tuple-element.169), channel_id=1, source_target_pairs={{0,2},{1,3},{2,0},{3,1},{4,6},{5,7},{6,4},{7,5},{8,10},{9,11},{10,... | collective-permute-start | bytes 589832 | tf_op jit(solution)/shard_map/ppermute | solution.py:377
  148.7 9.9 %collective-permute-start.47 = (bf16[128,768]{1,0:T(8,128)(2,1)S(1)}, bf16[128,768]{1,0:T(8,128)(2,1)S(1)}, u32[]{:S(2)}, u32[]{:S(2)}) collective-permute-start(bf16[128,768]{1,0:T(8,128)(2,1)S(1)} %get-tuple-element.171), channel_id=1, source_target_pairs={{0,4},{1,5},{2,6},{3,7},{4,0},{5,1},{6,2},{7,3},{8,12},{9,13},{10,... | collective-permute-start | bytes 589832 | tf_op jit(solution)/shard_map/ppermute | solution.py:377
  149.9 10.1 %collective-permute-start.48 = (bf16[128,768]{1,0:T(8,128)(2,1)S(1)}, bf16[128,768]{1,0:T(8,128)(2,1)S(1)}, u32[]{:S(2)}, u32[]{:S(2)}) collective-permute-start(bf16[128,768]{1,0:T(8,128)(2,1)S(1)} %get-tuple-element.173), channel_id=1, source_target_pairs={{0,6},{1,7},{2,4},{3,5},{4,2},{5,3},{6,0},{7,1},{8,14},{9,15},{10,... | collective-permute-start | bytes 589832 | tf_op jit(solution)/shard_map/ppermute | solution.py:377

commit v6 on v5

--- a/solution.py
+++ b/solution.py
@@ -535,8 +535,10 @@
 
 def all_keys(pair, key_ref, value_ref):
     for n in range(2):
-        key_ref[OWN * n : OWN * (n + 1), :] = pair[2 * n][:OWN, :]
-        value_ref[OWN * n : OWN * (n + 1), :] = pair[2 * n + 1][...]
+        for h in range(3):
+            at = slice(64 * h, 64 * h + 64)
+            key_ref[h, OWN * n : OWN * (n + 1), :] = pair[2 * n][:OWN, at]
+            value_ref[h, OWN * n : OWN * (n + 1), :] = pair[2 * n + 1][:, at]
 
 
 def attend_body(pos, q_ref, *refs):
@@ -551,13 +553,13 @@
         for h in range(3):
             at = slice(64 * h, 64 * h + 64)
             query = q_ref[rows, at]
-            scores = dot_t(query, key_ref[:, at])
+            scores = dot_t(query, key_ref[h])
             scores = jnp.where(hidden, NEGATIVE, scores)
             top = jnp.max(scores, -1, keepdims=True)
             weights = jnp.exp(scores - top)
             total = jnp.sum(weights, -1, keepdims=True)
             low = weights.astype(bf16)
-            out = dot(low, value_ref[:, at])
+            out = dot(low, value_ref[h])
             heads.append(out * (1.0 / total))
             lse = jnp.where(lane == h, top + jnp.log(total), lse)
         mixed = jnp.concatenate(heads, 1)
@@ -652,10 +654,9 @@
     all_keys(pair, key_ref, value_ref)
     grads = jnp.concatenate([ref[...] for ref in (a0, a1, a2, a3)], 0)
     grad_mixed = dot_t(grads, wok[...]).astype(bf16)
-    dq = []
+    dq, dks, dvs = [], [], []
     for h in range(3):
         at = slice(64 * h, 64 * h + 64)
-        at_v = slice(QUARTER + 64 * h, QUARTER + 64 * h + 64)
         query, grad = q_ref[:, at], grad_mixed[:, at]
         grad_q = []
         for r in range(4):
@@ -664,20 +665,22 @@
             g = grad[rows]
             inner = jnp.sum(g.astype(f32) * state_ref[rows, at], -1, keepdims=True)
             lse = state_ref[rows, QUARTER + h : QUARTER + h + 1]
-            scores = dot_t(query[rows], key_ref[:, at])
+            scores = dot_t(query[rows], key_ref[h])
             probs = jnp.exp(jnp.where(hidden, NEGATIVE, scores) - lse)
-            slopes = dot_t(g, value_ref[:, at])
+            slopes = dot_t(g, value_ref[h])
             ds = (probs * (slopes - inner)).astype(bf16)
             p_ref[rows, :] = probs.astype(bf16)
             ds_ref[rows, :] = ds
-            grad_q.append(dot(ds, key_ref[:, at]))
+            grad_q.append(dot(ds, key_ref[h]))
         dq.append(jnp.concatenate(grad_q, 0))
-        dk = t_dot(ds_ref[...], query)
-        dv = t_dot(p_ref[...], grad)
-        own_ref[:, at] = dk[:OWN]
-        own_ref[:, at_v] = dv[:OWN]
-        send_k[:, at] = dk[OWN:].astype(bf16)
-        send_v[:, at] = dv[OWN:].astype(bf16)
+        dks.append(t_dot(query, ds_ref[...]))
+        dvs.append(t_dot(grad, p_ref[...]))
+    dk = jnp.concatenate(dks, 0).T
+    dv = jnp.concatenate(dvs, 0).T
+    own_ref[:, :QUARTER] = dk[:OWN]
+    own_ref[:, QUARTER:] = dv[:OWN]
+    send_k[...] = dk[OWN:].astype(bf16)
+    send_v[...] = dv[OWN:].astype(bf16)
     dq_ref[...] = (jnp.concatenate(dq, 1) * 0.125).astype(bf16)
 
 
@@ -854,7 +857,7 @@
         pos,
         [query, *pair],
         [((OWN, QUARTER), bf16), ((OWN, 256), f32)],
-        [((2 * OWN, QUARTER), bf16)] * 2,
+        [((3, 2 * OWN, 64), bf16)] * 2,
     )
     mixed = chip_gather(mixed_own)
     got_rest = lax.optimization_barrier((*got_rest, *mixed[1:]))[:4]
@@ -885,7 +888,7 @@
         pos,
         [*ga, w_out_k, query, *pair, state],
         [(third, bf16), ((OWN, 2 * QUARTER), f32)] + [(third, bf16)] * 2,
-        [((OWN, 2 * OWN), bf16)] * 2 + [((2 * OWN, QUARTER), bf16)] * 2,
+        [((OWN, 2 * OWN), bf16)] * 2 + [((3, 2 * OWN, 64), bf16)] * 2,
     )
     pair_send[0], *feed_terms[1:] = lax.optimization_barrier((pair_send[0], *feed_terms[1:]))
     pair_got = [core_swap(x) for x in pair_send]

time: 162 us -> 161 us (level)
    ppermute x24, waiting for transfers between devices: 28.1 us -> 25.9 us  [chip_swap(): return lax.ppermute(values, 'ctx', [(i, i ^ 2 * mask) for i in range(8)])]
  transfers between devices with their start and end apart: 56 -> 56, of which waited for: 27 -> 28; matrix products, arithmetic and copies ran while one was open for 0% -> 0% of each run, Pallas kernels for 17% -> 17%
where the time goes in v6:
time: 161 us
  waiting for transfers between devices  64.5 us (40%)
  starting transfers between devices  51.6 us (32%)
  Pallas kernels  40 us (25%)
  local copies, waits for them, and re-layouts  2.84 us (2%)
    pallas_call x15, Pallas kernels, run(): pl.pallas_call(body, out_shape=[jax.ShapeDtypeStruct(shape, kind) for sha...  40 us
    ppermute x12, waiting for transfers between devices, seq_swap(): return lax.ppermute(values, 'seq', [(i, i ^ mask) for i in range(4)])  30.8 us
    ppermute x24, starting transfers between devices, chip_swap(): return lax.ppermute(values, 'ctx', [(i, i ^ 2 * mask) for i in range(8)])  30.6 us
    ppermute x24, waiting for transfers between devices, chip_swap(): return lax.ppermute(values, 'ctx', [(i, i ^ 2 * mask) for i in range(8)])  25.9 us
    ppermute x12, starting transfers between devices, seq_swap(): return lax.ppermute(values, 'seq', [(i, i ^ mask) for i in range(4)])  17.3 us
    ppermute x20, waiting for transfers between devices, core_swap(): return lax.ppermute(values, 'ctx', [(i, i ^ 1) for i in range(8)])  7.86 us
    ppermute x20, starting transfers between devices, core_swap(): return lax.ppermute(values, 'ctx', [(i, i ^ 1) for i in range(8)])  3.71 us
  transfers between devices with their start and end apart: 56, of which 28 were waited for; matrix products, arithmetic and copies ran while one was open for 0% of the time, Pallas kernels for 17%

profile of v6, /device:TPU:0, one launch (start us, length us, event | category | flops | bytes accessed | tf_op | source)
XLA Modules:
  0.0 160.6 jit_solution(10660694672286106244)
XLA Ops:
  1.3 4.1 %shard_map.271 = (bf16[112,576]{1,0:T(8,128)(2,1)}, bf16[112,576]{1,0:T(8,128)(2,1)}, bf16[264,768]{1,0:T(8,128)(2,1)}, bf16[288,768]{1,0:T(8,128)(2,1)}, bf16[288,768]{1,0:T(8,128)(2,1)}) custom-call(s32[3]{0:T(128)} %pad_add_fusion.pos, bf16[192,2304]{1,0:T(8,128)(2,1)} %w_ref.1, bf16[1,128,768]{2,1,0:T(8,128)(2,1)} %tok_ref.1, ...), custom_call_target="tpu_custom_call" | custom-call | flops 524288 | bytes 1000 | tf_op jit(solution)/shard_map/pallas_call | solution.py:402
  5.4 5.1 %collective-permute-start.5 = (bf16[112,576]{1,0:T(8,128)(2,1)}, bf16[112,576]{1,0:T(8,128)(2,1)S(1)}, u32[]{:S(2)}, u32[]{:S(2)}) collective-permute-start(bf16[112,576]{1,0:T(8,128)(2,1)} %get-tuple-element.105.refs_4_), channel_id=1, source_target_pairs={{0,24},{8,16},{16,8},{24,0},{1,25},{9,17},{17,9},{25,1},{2,26},{10... | collective-permute-start | bytes 387080 | tf_op jit(solution)/shard_map/ppermute | solution.py:381
  10.5 2.5 %collective-permute-start.2 = (bf16[264,768]{1,0:T(8,128)(2,1)}, bf16[264,768]{1,0:T(8,128)(2,1)S(1)}, u32[]{:S(2)}, u32[]{:S(2)}) collective-permute-start(bf16[264,768]{1,0:T(8,128)(2,1)} %get-tuple-element.104.refs_0_.tok_ref), channel_id=1, source_target_pairs={{0,6},{1,7},{2,4},{3,5},{4,2},{5,3},{6,0},{7,1},{8,14},{9,15},{10,... | collective-permute-start | bytes 1216520 | tf_op jit(solution)/shard_map/ppermute | solution.py:377
  13.0 0.8 collective-permute-start.3
  14.3 1.1 collective-permute-done.5.refs_7_
  15.4 1.7 %collective-permute-start = (bf16[264,768]{1,0:T(8,128)(2,1)}, bf16[264,768]{1,0:T(8,128)(2,1)S(1)}, u32[]{:S(2)}, u32[]{:S(2)}) collective-permute-start(bf16[264,768]{1,0:T(8,128)(2,1)} %get-tuple-element.104.refs_0_.tok_ref), channel_id=1, source_target_pairs={{0,2},{1,3},{2,0},{3,1},{4,6},{5,7},{6,4},{7,5},{8,10},{9,11},{10,... | collective-permute-start | bytes 1216520 | tf_op jit(solution)/shard_map/ppermute | solution.py:377
  17.1 5.7 %collective-permute-done.4.refs_6_ = bf16[112,576]{1,0:T(8,128)(2,1)S(1)} collective-permute-done((bf16[112,576]{1,0:T(8,128)(2,1)}, bf16[112,576]{1,0:T(8,128)(2,1)S(1)}, u32[]{:S(2)}, u32[]{:S(2)}) %collective-permute-start.4) | collective-permute-done | bytes 129056 | tf_op jit(solution)/shard_map/ppermute | solution.py:381
  23.4 0.9 collective-permute-done.8.refs_11_
  24.2 2.5 %collective-permute-start.16 = (bf16[288,768]{1,0:T(8,128)(2,1)}, bf16[288,768]{1,0:T(8,128)(2,1)S(1)}, u32[]{:S(2)}, u32[]{:S(2)}) collective-permute-start(bf16[288,768]{1,0:T(8,128)(2,1)} %get-tuple-element.112.refs_8_), channel_id=1, source_target_pairs={{0,24},{8,16},{16,8},{24,0},{1,25},{9,17},{17,9},{25,1},{2,26},{10... | collective-permute-start | bytes 1327112 | tf_op jit(solution)/shard_map/ppermute | solution.py:381
  26.7 1.4 collective-permute-done.6.refs_9_
  28.1 1.9 %collective-permute-start.14 = (bf16[288,768]{1,0:T(8,128)(2,1)}, bf16[288,768]{1,0:T(8,128)(2,1)S(1)}, u32[]{:S(2)}, u32[]{:S(2)}) collective-permute-start(bf16[288,768]{1,0:T(8,128)(2,1)} %get-tuple-element.112.refs_8_), channel_id=1, source_target_pairs={{0,8},{8,0},{16,24},{24,16},{1,9},{9,1},{17,25},{25,17},{2,10},{10... | collective-permute-start | bytes 1327112 | tf_op jit(solution)/shard_map/ppermute | solution.py:381
  30.0 1.2 collective-permute-done.1.refs_2_
  31.2 1.0 copy-done
  32.2 0.9 copy-done.4
  33.1 0.9 copy-done.5
  34.1 1.9 %shard_map.272 = (bf16[512,192]{1,0:T(8,128)(2,1)S(1)}, bf16[520,192]{1,0:T(8,128)(2,1)S(1)}, bf16[512,192]{1,0:T(8,128)(2,1)S(1)}, bf16[512,768]{1,0:T(8,128)(2...) custom-call(s32[3]{0:T(128)S(1)} %copy-done.6, bf16[264,768]{1,0:T(8,128)(2,1)S(1)} %copy-done, ...), custom_call_target="tpu_custom_call" | custom-call | flops 524288 | bytes 1000 | tf_op jit(solution)/shard_map/pallas_call | solution.py:402
  36.6 1.4 collective-permute-done.10.refs_3_
  38.0 5.2 %shard_map.273 = (bf16[512,192]{1,0:T(8,128)(2,1)S(1)}, f32[512,256]{1,0:T(8,128)S(1)}) custom-call(s32[3]{0:T(128)S(1)} %copy-done.6, bf16[512,192]{1,0:T(8,128)(2,1)S(1)} %get-tuple-element.107.q_ref, bf16[520,192]{1,0:T(8,128)(2,1)S(1)} %get-tuple-element.108.refs_0_, bf16[512,192]{1,0:T(8,128)(2,1)S(1)} %get-tuple-element.109.refs_1_, ...), custom_call_target="tpu_custom_call" | custom-call | flops 524288 | bytes 1000 | tf_op jit(solution)/shard_map/pallas_call | solution.py:402
  43.2 2.1 %collective-permute-start.13 = (bf16[512,192]{1,0:T(8,128)(2,1)S(1)}, bf16[512,192]{1,0:T(8,128)(2,1)S(1)}, u32[]{:S(2)}, u32[]{:S(2)}) collective-permute-start(bf16[512,192]{1,0:T(8,128)(2,1)S(1)} %get-tuple-element.110.refs_4_.refs_0_), channel_id=1, source_target_pairs={{0,6},{1,7},{2,4},{3,5},{4,2},{5,3},{6,0},{7,1},{8,14},{9,15},{10,... | collective-permute-start | bytes 589832 | tf_op jit(solution)/shard_map/ppermute | solution.py:377
  45.3 1.0 collective-permute-start.12
  46.8 17.7 %collective-permute-done.15.refs_10_ = bf16[288,768]{1,0:T(8,128)(2,1)S(1)} collective-permute-done((bf16[288,768]{1,0:T(8,128)(2,1)}, bf16[288,768]{1,0:T(8,128)(2,1)S(1)}, u32[]{:S(2)}, u32[]{:S(2)}) %collective-permute-start.15) | collective-permute-done | bytes 442400 | tf_op jit(solution)/shard_map/ppermute | solution.py:381
  65.2 1.2 collective-permute-done.17.refs_13_
  67.7 7.2 %shard_map.274 = (f32[128,768]{1,0:T(8,128)S(1)}, f32[128,768]{1,0:T(8,128)S(1)}, bf16[128,768]{1,0:T(8,128)(2,1)S(1)}, bf16[128,768]{1,0:T(8,128)(2,1)S(1)}, bf...) custom-call(s32[3]{0:T(128)S(1)} %copy-done.6, ...), custom_call_target="tpu_custom_call" | custom-call | flops 524288 | bytes 1000 | tf_op jit(solution)/shard_map/pallas_call | solution.py:402
  75.0 1.3 collective-permute-start.21
  76.3 1.5 collective-permute-start.22
  77.8 0.7 collective-permute-start.23
  78.5 0.8 shard_map.275
  79.4 2.7 %collective-permute-start.28 = (bf16[192,768]{1,0:T(8,128)(2,1)S(1)}, bf16[192,768]{1,0:T(8,128)(2,1)S(1)}, u32[]{:S(2)}, u32[]{:S(2)}) collective-permute-start(bf16[192,768]{1,0:T(8,128)(2,1)S(1)} %get-tuple-element.135), channel_id=1, source_target_pairs={{0,24},{8,16},{16,8},{24,0},{1,25},{9,17},{17,9},{25,1},{2,26},{10... | collective-permute-start | bytes 884744 | tf_op jit(solution)/shard_map/ppermute | solution.py:381
  82.7 3.8 %collective-permute-done.22.r2 = bf16[128,768]{1,0:T(8,128)(2,1)S(1)} collective-permute-done((bf16[128,768]{1,0:T(8,128)(2,1)S(1)}, bf16[128,768]{1,0:T(8,128)(2,1)S(1)}, u32[]{:S(2)}, u32[]{:S(2)}) %collective-permute-start.22) | collective-permute-done | bytes 196640 | tf_op jit(solution)/shard_map/ppermute | solution.py:377
  86.5 0.9 collective-permute-done.23.r3
  87.5 0.9 shard_map.276
  88.4 1.8 %collective-permute-start.26 = (bf16[128,768]{1,0:T(8,128)(2,1)S(1)}, bf16[128,768]{1,0:T(8,128)(2,1)S(1)}, u32[]{:S(2)}, u32[]{:S(2)}) collective-permute-start(bf16[128,768]{1,0:T(8,128)(2,1)S(1)} %get-tuple-element.127.a0.refs_4_.refs_6_), channel_id=1, source_target_pairs={{0,6},{1,7},{2,4},{3,5},{4,2},{5,3},{6,0},{7,1},{8,14},{9,15},{10,... | collective-permute-start | bytes 589832 | tf_op jit(solution)/shard_map/ppermute | solution.py:377
  90.2 1.0 collective-permute-start.25
  91.2 0.8 collective-permute-start.24
  92.0 5.3 %collective-permute-done.26.a3.refs_7_ = bf16[128,768]{1,0:T(8,128)(2,1)S(1)} collective-permute-done((bf16[128,768]{1,0:T(8,128)(2,1)S(1)}, bf16[128,768]{1,0:T(8,128)(2,1)S(1)}, u32[]{:S(2)}, u32[]{:S(2)}) %collective-permute-start.26) | collective-permute-done | bytes 196640 | tf_op jit(solution)/shard_map/ppermute | solution.py:377
  97.2 2.8 %collective-permute-done.25.a2.refs_6_ = bf16[128,768]{1,0:T(8,128)(2,1)S(1)} collective-permute-done((bf16[128,768]{1,0:T(8,128)(2,1)S(1)}, bf16[128,768]{1,0:T(8,128)(2,1)S(1)}, u32[]{:S(2)}, u32[]{:S(2)}) %collective-permute-start.25) | collective-permute-done | bytes 196640 | tf_op jit(solution)/shard_map/ppermute | solution.py:377
  100.0 6.0 %shard_map.277 = (bf16[512,192]{1,0:T(8,128)(2,1)S(1)}, f32[512,384]{1,0:T(8,128)S(1)}, bf16[512,192]{1,0:T(8,128)(2,1)S(1)}, bf16[512,192]{1,0:T(8,128)(2,1)S(1)}) custom-call(s32[3]{0:T(128)S(1)} %copy-done.6, bf16[128,768]{1,0:T(8,128)(2,1)S(1)} %get-tuple-element.127.a0.refs_4_.refs_6_, bf16[128,768]{1,0:T(8,128)(2,1)S(1)} %collective-permute-done.24.a1.refs_5_, ...), custom_call_target="tpu_custom_call" | custom-call | flops 524288 | bytes 1000 | tf_op jit(solution)/shard_map/pallas_call | solution.py:402
  106.6 1.0 collective-permute-done.30.refs_12_
  108.0 2.8 %shard_map.278 = (bf16[4,96,768]{2,1,0:T(8,128)(2,1)S(1)}, f32[4,96,768]{2,1,0:T(8,128)S(1)}, bf16[512,576]{1,0:T(8,128)(2,1)S(1)}) custom-call(s32[3]{0:T(128)S(1)} %copy-done.6, bf16[512,192]{1,0:T(8,128)(2,1)S(1)} %get-tuple-element.110.refs_4_.refs_0_, bf16[512,192]{1,0:T(8,128)(2,1)S(1)} %collective-permute-done.11.refs_5_.refs_1_, ...), custom_call_target="tpu_custom_call" | custom-call | flops 524288 | bytes 1000 | tf_op jit(solution)/shard_map/pallas_call | solution.py:402
  111.0 1.4 collective-permute-start.33
  113.0 1.5 collective-permute-start.35
  114.5 1.7 %shard_map.279 = (f32[4,8,768]{2,1,0:T(8,128)S(1)}, f32[128,768]{1,0:T(8,128)S(1)}, bf16[128,768]{1,0:T(8,128)(2,1)S(1)}, bf16[128,768]{1,0:T(8,128)(2,1)S(1)}, bf16[128,768]{1,0:T(8,128)(2,1)S(1)}) custom-call(s32[3]{0:T(128)S(1)} %copy-done.6, bf16[264,768]{1,0:T(8,128)(2,1)S(1)} %copy-done.1, bf16[264,768]{1,0:T(8,128)(2,1)S(1)} %collective-permute-done.refs_1_, ...), custom_call_target="tpu_custom_call" | custom-call | flops 524288 | bytes 1000 | tf_op jit(solution)/shard_map/pallas_call | solution.py:402
  116.3 0.7 shard_map.280
  116.9 1.6 %collective-permute-start.37 = (bf16[104,768]{1,0:T(8,128)(2,1)S(1)}, bf16[104,768]{1,0:T(8,128)(2,1)S(1)}, u32[]{:S(2)}, u32[]{:S(2)}) collective-permute-start(bf16[104,768]{1,0:T(8,128)(2,1)S(1)} %get-tuple-element.160), channel_id=1, source_target_pairs={{0,16},{8,24},{16,0},{24,8},{1,17},{9,25},{17,1},{25,9},{2,18},{10... | collective-permute-start | bytes 479240 | tf_op jit(solution)/shard_map/ppermute | solution.py:381
  118.6 2.6 %collective-permute-start.38 = (bf16[104,768]{1,0:T(8,128)(2,1)S(1)}, bf16[104,768]{1,0:T(8,128)(2,1)S(1)}, u32[]{:S(2)}, u32[]{:S(2)}) collective-permute-start(bf16[104,768]{1,0:T(8,128)(2,1)S(1)} %get-tuple-element.161), channel_id=1, source_target_pairs={{0,24},{8,16},{16,8},{24,0},{1,25},{9,17},{17,9},{25,1},{2,26},{10... | collective-permute-start | bytes 479240 | tf_op jit(solution)/shard_map/ppermute | solution.py:381
  121.2 0.7 shard_map.281.refs_0_
  121.9 1.6 %collective-permute-done.34.s2 = bf16[128,768]{1,0:T(8,128)(2,1)S(1)} collective-permute-done((bf16[128,768]{1,0:T(8,128)(2,1)S(1)}, bf16[128,768]{1,0:T(8,128)(2,1)S(1)}, u32[]{:S(2)}, u32[]{:S(2)}) %collective-permute-start.34) | collective-permute-done | bytes 196640 | tf_op jit(solution)/shard_map/ppermute | solution.py:377
  123.5 1.3 collective-permute-start.41
  124.9 0.8 collective-permute-start.40
  125.6 6.2 %collective-permute-done.37.r2 = bf16[104,768]{1,0:T(8,128)(2,1)S(1)} collective-permute-done((bf16[104,768]{1,0:T(8,128)(2,1)S(1)}, bf16[104,768]{1,0:T(8,128)(2,1)S(1)}, u32[]{:S(2)}, u32[]{:S(2)}) %collective-permute-start.37) | collective-permute-done | bytes 159776 | tf_op jit(solution)/shard_map/ppermute | solution.py:381
  133.1 2.2 %collective-permute-start.51 = (bf16[104,768]{1,0:T(8,128)(2,1)S(1)}, bf16[104,768]{1,0:T(8,128)(2,1)S(1)}, u32[]{:S(2)}, u32[]{:S(2)}) collective-permute-start(bf16[104,768]{1,0:T(8,128)(2,1)S(1)} %shard_map.282.refs_0_), channel_id=1, source_target_pairs={{0,6},{1,7},{2,4},{3,5},{4,2},{5,3},{6,0},{7,1},{8,14},{9,15},{10,... | collective-permute-start | bytes 479240 | tf_op jit(solution)/shard_map/ppermute | solution.py:377
  135.5 1.5 collective-permute-done.40.refs_2_
  137.1 1.5 collective-permute-start.50
  138.6 1.2 collective-permute-done.39.refs_1_
  139.8 1.9 %collective-permute-start.49 = (bf16[104,768]{1,0:T(8,128)(2,1)S(1)}, bf16[104,768]{1,0:T(8,128)(2,1)S(1)}, u32[]{:S(2)}, u32[]{:S(2)}) collective-permute-start(bf16[104,768]{1,0:T(8,128)(2,1)S(1)} %shard_map.282.refs_0_), channel_id=1, source_target_pairs={{0,2},{1,3},{2,0},{3,1},{4,6},{5,7},{6,4},{7,5},{8,10},{9,11},{10,... | collective-permute-start | bytes 479240 | tf_op jit(solution)/shard_map/ppermute | solution.py:377
  141.7 2.8 %collective-permute-done.51.refs_3_ = bf16[104,768]{1,0:T(8,128)(2,1)S(1)} collective-permute-done((bf16[104,768]{1,0:T(8,128)(2,1)S(1)}, bf16[104,768]{1,0:T(8,128)(2,1)S(1)}, u32[]{:S(2)}, u32[]{:S(2)}) %collective-permute-start.51) | collective-permute-done | bytes 159776 | tf_op jit(solution)/shard_map/ppermute | solution.py:377
  146.5 1.0 collective-permute-start.46
  147.6 1.5 collective-permute-start.47
  149.1 1.0 collective-permute-start.48
  150.0 2.3 %shard_map.285 = (f32[192,2304]{1,0:T(8,128)}, f32[192,768]{1,0:T(8,128)}, f32[192]{0:T(256)}, f32[192]{0:T(256)}, f32[192]{0:T(256)}, /*index=5*/f32[192]{0:T(2...) custom-call(s32[3]{0:T(128)S(1)} %copy-done.6, ...), custom_call_target="tpu_custom_call" | custom-call | flops 524288 | bytes 1000 | tf_op jit(solution)/shard_map/pallas_call | solution.py:402
  152.4 3.2 %shard_map.283 = (f32[768,768]{1,0:T(8,128)}, f32[192,3072]{1,0:T(8,128)}) custom-call(s32[3]{0:T(128)S(1)} %copy-done.6, bf16[192,768]{1,0:T(8,128)(2,1)S(1)} %shard_map.281.refs_0_, bf16[192,768]{1,0:T(8,128)(2,1)S(1)} %collective-permute-done.39.refs_1_, bf16[192,768]{1,0:T(8,128)(2,1)S(1)} %collective-permute-done.40.refs_2_, ...), custom_call_target="tpu_custom_call" | custom-call | flops 524288 | bytes 1000 | tf_op jit(solution)/shard_map/pallas_call | solution.py:402
  155.6 1.8 %collective-permute-done.47.r2 = bf16[128,768]{1,0:T(8,128)(2,1)S(1)} collective-permute-done((bf16[128,768]{1,0:T(8,128)(2,1)S(1)}, bf16[128,768]{1,0:T(8,128)(2,1)S(1)}, u32[]{:S(2)}, u32[]{:S(2)}) %collective-permute-start.47) | collective-permute-done | bytes 196640 | tf_op jit(solution)/shard_map/ppermute | solution.py:377
  157.5 1.3 collective-permute-done.48.r3
  158.8 1.8 %shard_map.284 = (f32[1,128,768]{2,1,0:T(8,128)}, bf16[1,128,768]{2,1,0:T(8,128)(2,1)}) custom-call(s32[3]{0:T(128)S(1)} %copy-done.6, f32[128,768]{1,0:T(8,128)S(1)} %get-tuple-element.167.g0, bf16[128,768]{1,0:T(8,128)(2,1)S(1)} %collective-permute-done.46.r1, bf16[128,768]{1,0:T(8,128)(2,1)S(1)} %collective-permute-done.47.r2, ...), custom_call_target="tpu_custom_call" | custom-call | flops 524288 | bytes 1000 | tf_op jit(solution)/shard_map/pallas_call | solution.py:402
  (78 shorter events, 11.0 us)
Async XLA Ops:
  1.3 30.0 %copy-start.6 = (s32[3]{0:T(128)S(1)}, s32[3]{0:T(128)}, u32[]{:S(2)}) copy-start(s32[3]{0:T(128)} %pad_add_fusion.pos) | copy-start | bytes 40
  5.4 10.0 %collective-permute-start.5 = (bf16[112,576]{1,0:T(8,128)(2,1)}, bf16[112,576]{1,0:T(8,128)(2,1)S(1)}, u32[]{:S(2)}, u32[]{:S(2)}) collective-permute-start(bf16[112,576]{1,0:T(8,128)(2,1)} %get-tuple-element.105.refs_4_), channel_id=1, source_target_pairs={{0,24},{8,16},{16,8},{24,0},{1,25},{9,17},{17,9},{25,1},{2,26},{10... | collective-permute-start | bytes 387080 | tf_op jit(solution)/shard_map/ppermute | solution.py:381
  10.5 12.3 %collective-permute-start.4 = (bf16[112,576]{1,0:T(8,128)(2,1)}, bf16[112,576]{1,0:T(8,128)(2,1)S(1)}, u32[]{:S(2)}, u32[]{:S(2)}) collective-permute-start(bf16[112,576]{1,0:T(8,128)(2,1)} %get-tuple-element.105.refs_4_), channel_id=1, source_target_pairs={{0,16},{8,24},{16,0},{24,8},{1,17},{9,25},{17,1},{25,9},{2,18},{10... | collective-permute-start | bytes 387080 | tf_op jit(solution)/shard_map/ppermute | solution.py:381
  10.5 17.6 %collective-permute-start.2 = (bf16[264,768]{1,0:T(8,128)(2,1)}, bf16[264,768]{1,0:T(8,128)(2,1)S(1)}, u32[]{:S(2)}, u32[]{:S(2)}) collective-permute-start(bf16[264,768]{1,0:T(8,128)(2,1)} %get-tuple-element.104.refs_0_.tok_ref), channel_id=1, source_target_pairs={{0,6},{1,7},{2,4},{3,5},{4,2},{5,3},{6,0},{7,1},{8,14},{9,15},{10,... | collective-permute-start | bytes 1216520 | tf_op jit(solution)/shard_map/ppermute | solution.py:377
  13.0 9.9 %collective-permute-start.3 = (bf16[112,576]{1,0:T(8,128)(2,1)}, bf16[112,576]{1,0:T(8,128)(2,1)S(1)}, u32[]{:S(2)}, u32[]{:S(2)}) collective-permute-start(bf16[112,576]{1,0:T(8,128)(2,1)} %get-tuple-element.105.refs_4_), channel_id=1, source_target_pairs={{0,8},{8,0},{16,24},{24,16},{1,9},{9,1},{17,25},{25,17},{2,10},{10... | collective-permute-start | bytes 387080 | tf_op jit(solution)/shard_map/ppermute | solution.py:381
  13.8 17.4 %collective-permute-start.1 = (bf16[264,768]{1,0:T(8,128)(2,1)}, bf16[264,768]{1,0:T(8,128)(2,1)S(1)}, u32[]{:S(2)}, u32[]{:S(2)}) collective-permute-start(bf16[264,768]{1,0:T(8,128)(2,1)} %get-tuple-element.104.refs_0_.tok_ref), channel_id=1, source_target_pairs={{0,4},{1,5},{2,6},{3,7},{4,0},{5,1},{6,2},{7,3},{8,12},{9,13},{10,... | collective-permute-start | bytes 1216520 | tf_op jit(solution)/shard_map/ppermute | solution.py:377
  15.4 15.8 %collective-permute-start = (bf16[264,768]{1,0:T(8,128)(2,1)}, bf16[264,768]{1,0:T(8,128)(2,1)S(1)}, u32[]{:S(2)}, u32[]{:S(2)}) collective-permute-start(bf16[264,768]{1,0:T(8,128)(2,1)} %get-tuple-element.104.refs_0_.tok_ref), channel_id=1, source_target_pairs={{0,2},{1,3},{2,0},{3,1},{4,6},{5,7},{6,4},{7,5},{8,10},{9,11},{10,... | collective-permute-start | bytes 1216520 | tf_op jit(solution)/shard_map/ppermute | solution.py:377
  22.8 1.4 collective-permute-start.8
  22.8 3.8 %collective-permute-start.7 = (bf16[112,576]{1,0:T(8,128)(2,1)S(1)}, bf16[112,576]{1,0:T(8,128)(2,1)S(1)}, u32[]{:S(2)}, u32[]{:S(2)}) collective-permute-start(bf16[112,576]{1,0:T(8,128)(2,1)S(1)} %collective-permute-done.4.refs_6_), channel_id=1, source_target_pairs={{0,1},{1,0},{2,3},{3,2},{4,5},{5,4},{6,7},{7,6},{8,9},{9,8},{10,11... | collective-permute-start | bytes 387080 | tf_op jit(solution)/shard_map/ppermute | solution.py:373
  24.2 22.0 %collective-permute-start.16 = (bf16[288,768]{1,0:T(8,128)(2,1)}, bf16[288,768]{1,0:T(8,128)(2,1)S(1)}, u32[]{:S(2)}, u32[]{:S(2)}) collective-permute-start(bf16[288,768]{1,0:T(8,128)(2,1)} %get-tuple-element.112.refs_8_), channel_id=1, source_target_pairs={{0,24},{8,16},{16,8},{24,0},{1,25},{9,17},{17,9},{25,1},{2,26},{10... | collective-permute-start | bytes 1327112 | tf_op jit(solution)/shard_map/ppermute | solution.py:381
  26.7 1.4 collective-permute-start.6
  28.1 36.4 %collective-permute-start.15 = (bf16[288,768]{1,0:T(8,128)(2,1)}, bf16[288,768]{1,0:T(8,128)(2,1)S(1)}, u32[]{:S(2)}, u32[]{:S(2)}) collective-permute-start(bf16[288,768]{1,0:T(8,128)(2,1)} %get-tuple-element.112.refs_8_), channel_id=1, source_target_pairs={{0,16},{8,24},{16,0},{24,8},{1,17},{9,25},{17,1},{25,9},{2,18},{10... | collective-permute-start | bytes 1327112 | tf_op jit(solution)/shard_map/ppermute | solution.py:381
  28.1 36.4 %collective-permute-start.14 = (bf16[288,768]{1,0:T(8,128)(2,1)}, bf16[288,768]{1,0:T(8,128)(2,1)S(1)}, u32[]{:S(2)}, u32[]{:S(2)}) collective-permute-start(bf16[288,768]{1,0:T(8,128)(2,1)} %get-tuple-element.112.refs_8_), channel_id=1, source_target_pairs={{0,8},{8,0},{16,24},{24,16},{1,9},{9,1},{17,25},{25,17},{2,10},{10... | collective-permute-start | bytes 1327112 | tf_op jit(solution)/shard_map/ppermute | solution.py:381
  31.2 1.0 copy-start
  32.2 0.9 copy-start.4
  33.1 0.9 copy-start.5
  36.0 31.7 %copy-start.1 = (bf16[264,768]{1,0:T(8,128)(2,1)S(1)}, bf16[264,768]{1,0:T(8,128)(2,1)}, u32[]{:S(2)}) copy-start(bf16[264,768]{1,0:T(8,128)(2,1)} %get-tuple-element.104.refs_0_.tok_ref) | copy-start | bytes 1216516
  36.0 31.7 %copy-start.2 = (bf16[288,768]{1,0:T(8,128)(2,1)S(1)}, bf16[288,768]{1,0:T(8,128)(2,1)}, u32[]{:S(2)}) copy-start(bf16[288,768]{1,0:T(8,128)(2,1)} %get-tuple-element.112.refs_8_) | copy-start | bytes 1327108
  36.0 31.6 %copy-start.3 = (bf16[288,768]{1,0:T(8,128)(2,1)S(1)}, bf16[288,768]{1,0:T(8,128)(2,1)}, u32[]{:S(2)}) copy-start(bf16[288,768]{1,0:T(8,128)(2,1)} %get-tuple-element.116.refs_12_) | copy-start | bytes 1327108
  36.0 2.0 %collective-permute-start.9 = (bf16[520,192]{1,0:T(8,128)(2,1)S(1)}, bf16[520,192]{1,0:T(8,128)(2,1)S(1)}, u32[]{:S(2)}, u32[]{:S(2)}) collective-permute-start(bf16[520,192]{1,0:T(8,128)(2,1)S(1)} %get-tuple-element.108.refs_0_), channel_id=1, source_target_pairs={{0,1},{1,0},{2,3},{3,2},{4,5},{5,4},{6,7},{7,6},{8,9},{9,8},{10,11... | collective-permute-start | bytes 599048 | tf_op jit(solution)/shard_map/ppermute | solution.py:373
  36.1 1.9 %collective-permute-start.10 = (bf16[512,192]{1,0:T(8,128)(2,1)S(1)}, bf16[512,192]{1,0:T(8,128)(2,1)S(1)}, u32[]{:S(2)}, u32[]{:S(2)}) collective-permute-start(bf16[512,192]{1,0:T(8,128)(2,1)S(1)} %get-tuple-element.109.refs_1_), channel_id=1, source_target_pairs={{0,1},{1,0},{2,3},{3,2},{4,5},{5,4},{6,7},{7,6},{8,9},{9,8},{10,11... | collective-permute-start | bytes 589832 | tf_op jit(solution)/shard_map/ppermute | solution.py:373
  43.2 21.3 %collective-permute-start.13 = (bf16[512,192]{1,0:T(8,128)(2,1)S(1)}, bf16[512,192]{1,0:T(8,128)(2,1)S(1)}, u32[]{:S(2)}, u32[]{:S(2)}) collective-permute-start(bf16[512,192]{1,0:T(8,128)(2,1)S(1)} %get-tuple-element.110.refs_4_.refs_0_), channel_id=1, source_target_pairs={{0,6},{1,7},{2,4},{3,5},{4,2},{5,3},{6,0},{7,1},{8,14},{9,15},{10,... | collective-permute-start | bytes 589832 | tf_op jit(solution)/shard_map/ppermute | solution.py:377
  45.3 19.2 %collective-permute-start.12 = (bf16[512,192]{1,0:T(8,128)(2,1)S(1)}, bf16[512,192]{1,0:T(8,128)(2,1)S(1)}, u32[]{:S(2)}, u32[]{:S(2)}) collective-permute-start(bf16[512,192]{1,0:T(8,128)(2,1)S(1)} %get-tuple-element.110.refs_4_.refs_0_), channel_id=1, source_target_pairs={{0,4},{1,5},{2,6},{3,7},{4,0},{5,1},{6,2},{7,3},{8,12},{9,13},{10,... | collective-permute-start | bytes 589832 | tf_op jit(solution)/shard_map/ppermute | solution.py:377
  46.3 18.3 %collective-permute-start.11 = (bf16[512,192]{1,0:T(8,128)(2,1)S(1)}, bf16[512,192]{1,0:T(8,128)(2,1)S(1)}, u32[]{:S(2)}, u32[]{:S(2)}) collective-permute-start(bf16[512,192]{1,0:T(8,128)(2,1)S(1)} %get-tuple-element.110.refs_4_.refs_0_), channel_id=1, source_target_pairs={{0,2},{1,3},{2,0},{3,1},{4,6},{5,7},{6,4},{7,5},{8,10},{9,11},{10,... | collective-permute-start | bytes 589832 | tf_op jit(solution)/shard_map/ppermute | solution.py:377
  64.5 1.9 %collective-permute-start.17 = (bf16[288,768]{1,0:T(8,128)(2,1)S(1)}, bf16[288,768]{1,0:T(8,128)(2,1)S(1)}, u32[]{:S(2)}, u32[]{:S(2)}) collective-permute-start(bf16[288,768]{1,0:T(8,128)(2,1)S(1)} %collective-permute-done.14.refs_9_), channel_id=1, source_target_pairs={{0,1},{1,0},{2,3},{3,2},{4,5},{5,4},{6,7},{7,6},{8,9},{9,8},{10,11... | collective-permute-start | bytes 1327112 | tf_op jit(solution)/shard_map/ppermute | solution.py:373
  64.6 2.4 %collective-permute-start.18 = (bf16[288,768]{1,0:T(8,128)(2,1)S(1)}, bf16[288,768]{1,0:T(8,128)(2,1)S(1)}, u32[]{:S(2)}, u32[]{:S(2)}) collective-permute-start(bf16[288,768]{1,0:T(8,128)(2,1)S(1)} %collective-permute-done.15.refs_10_), channel_id=1, source_target_pairs={{0,1},{1,0},{2,3},{3,2},{4,5},{5,4},{6,7},{7,6},{8,9},{9,8},{10,11... | collective-permute-start | bytes 1327112 | tf_op jit(solution)/shard_map/ppermute | solution.py:373
  65.1 2.5 %collective-permute-start.19 = (bf16[288,768]{1,0:T(8,128)(2,1)S(1)}, bf16[288,768]{1,0:T(8,128)(2,1)S(1)}, u32[]{:S(2)}, u32[]{:S(2)}) collective-permute-start(bf16[288,768]{1,0:T(8,128)(2,1)S(1)} %collective-permute-done.16.refs_11_), channel_id=1, source_target_pairs={{0,1},{1,0},{2,3},{3,2},{4,5},{5,4},{6,7},{7,6},{8,9},{9,8},{10,11... | collective-permute-start | bytes 1327112 | tf_op jit(solution)/shard_map/ppermute | solution.py:373
  74.9 3.7 %collective-permute-start.20 = (bf16[4,192,768]{2,1,0:T(8,128)(2,1)S(1)}, bf16[4,192,768]{2,1,0:T(8,128)(2,1)S(1)}, u32[]{:S(2)}, u32[]{:S(2)}) collective-permute-start(bf16[4,192,768]{2,1,0:T(8,128)(2,1)S(1)} %get-tuple-element.120), channel_id=1, source_target_pairs={{0,1},{1,0},{2,3},{3,2},{4,5},{5,4},{6,7},{7,6},{8,9},{9,8},{10,11... | collective-permute-start | bytes 3538952 | tf_op jit(solution)/shard_map/ppermute | solution.py:373
  75.0 7.7 %collective-permute-start.21 = (bf16[128,768]{1,0:T(8,128)(2,1)S(1)}, bf16[128,768]{1,0:T(8,128)(2,1)S(1)}, u32[]{:S(2)}, u32[]{:S(2)}) collective-permute-start(bf16[128,768]{1,0:T(8,128)(2,1)S(1)} %get-tuple-element.123), channel_id=1, source_target_pairs={{0,2},{1,3},{2,0},{3,1},{4,6},{5,7},{6,4},{7,5},{8,10},{9,11},{10,... | collective-permute-start | bytes 589832 | tf_op jit(solution)/shard_map/ppermute | solution.py:377
  76.3 10.2 %collective-permute-start.22 = (bf16[128,768]{1,0:T(8,128)(2,1)S(1)}, bf16[128,768]{1,0:T(8,128)(2,1)S(1)}, u32[]{:S(2)}, u32[]{:S(2)}) collective-permute-start(bf16[128,768]{1,0:T(8,128)(2,1)S(1)} %get-tuple-element.124), channel_id=1, source_target_pairs={{0,4},{1,5},{2,6},{3,7},{4,0},{5,1},{6,2},{7,3},{8,12},{9,13},{10,... | collective-permute-start | bytes 589832 | tf_op jit(solution)/shard_map/ppermute | solution.py:377
  77.8 9.6 %collective-permute-start.23 = (bf16[128,768]{1,0:T(8,128)(2,1)S(1)}, bf16[128,768]{1,0:T(8,128)(2,1)S(1)}, u32[]{:S(2)}, u32[]{:S(2)}) collective-permute-start(bf16[128,768]{1,0:T(8,128)(2,1)S(1)} %get-tuple-element.125), channel_id=1, source_target_pairs={{0,6},{1,7},{2,4},{3,5},{4,2},{5,3},{6,0},{7,1},{8,14},{9,15},{10,... | collective-permute-start | bytes 589832 | tf_op jit(solution)/shard_map/ppermute | solution.py:377
  79.3 26.8 %collective-permute-start.27 = (bf16[192,768]{1,0:T(8,128)(2,1)S(1)}, bf16[192,768]{1,0:T(8,128)(2,1)S(1)}, u32[]{:S(2)}, u32[]{:S(2)}) collective-permute-start(bf16[192,768]{1,0:T(8,128)(2,1)S(1)} %get-tuple-element.134), channel_id=1, source_target_pairs={{0,16},{8,24},{16,0},{24,8},{1,17},{9,25},{17,1},{25,9},{2,18},{10... | collective-permute-start | bytes 884744 | tf_op jit(solution)/shard_map/ppermute | solution.py:381
  79.4 26.7 %collective-permute-start.28 = (bf16[192,768]{1,0:T(8,128)(2,1)S(1)}, bf16[192,768]{1,0:T(8,128)(2,1)S(1)}, u32[]{:S(2)}, u32[]{:S(2)}) collective-permute-start(bf16[192,768]{1,0:T(8,128)(2,1)S(1)} %get-tuple-element.135), channel_id=1, source_target_pairs={{0,24},{8,16},{16,8},{24,0},{1,25},{9,17},{17,9},{25,1},{2,26},{10... | collective-permute-start | bytes 884744 | tf_op jit(solution)/shard_map/ppermute | solution.py:381
  88.4 8.8 %collective-permute-start.26 = (bf16[128,768]{1,0:T(8,128)(2,1)S(1)}, bf16[128,768]{1,0:T(8,128)(2,1)S(1)}, u32[]{:S(2)}, u32[]{:S(2)}) collective-permute-start(bf16[128,768]{1,0:T(8,128)(2,1)S(1)} %get-tuple-element.127.a0.refs_4_.refs_6_), channel_id=1, source_target_pairs={{0,6},{1,7},{2,4},{3,5},{4,2},{5,3},{6,0},{7,1},{8,14},{9,15},{10,... | collective-permute-start | bytes 589832 | tf_op jit(solution)/shard_map/ppermute | solution.py:377
  90.2 9.8 %collective-permute-start.25 = (bf16[128,768]{1,0:T(8,128)(2,1)S(1)}, bf16[128,768]{1,0:T(8,128)(2,1)S(1)}, u32[]{:S(2)}, u32[]{:S(2)}) collective-permute-start(bf16[128,768]{1,0:T(8,128)(2,1)S(1)} %get-tuple-element.127.a0.refs_4_.refs_6_), channel_id=1, source_target_pairs={{0,4},{1,5},{2,6},{3,7},{4,0},{5,1},{6,2},{7,3},{8,12},{9,13},{10,... | collective-permute-start | bytes 589832 | tf_op jit(solution)/shard_map/ppermute | solution.py:377
  91.2 8.8 %collective-permute-start.24 = (bf16[128,768]{1,0:T(8,128)(2,1)S(1)}, bf16[128,768]{1,0:T(8,128)(2,1)S(1)}, u32[]{:S(2)}, u32[]{:S(2)}) collective-permute-start(bf16[128,768]{1,0:T(8,128)(2,1)S(1)} %get-tuple-element.127.a0.refs_4_.refs_6_), channel_id=1, source_target_pairs={{0,2},{1,3},{2,0},{3,1},{4,6},{5,7},{6,4},{7,5},{8,10},{9,11},{10,... | collective-permute-start | bytes 589832 | tf_op jit(solution)/shard_map/ppermute | solution.py:377
  97.2 13.6 %collective-permute-start.31 = (bf16[192,768]{1,0:T(8,128)(2,1)S(1)}, bf16[192,768]{1,0:T(8,128)(2,1)S(1)}, u32[]{:S(2)}, u32[]{:S(2)}) collective-permute-start(bf16[192,768]{1,0:T(8,128)(2,1)S(1)} %get-tuple-element.145), channel_id=1, source_target_pairs={{0,8},{8,0},{16,24},{24,16},{1,9},{9,1},{17,25},{25,17},{2,10},{10... | collective-permute-start | bytes 884744 | tf_op jit(solution)/shard_map/ppermute | solution.py:381
  106.0 1.6 collective-permute-start.30
  106.1 1.9 %collective-permute-start.29 = (bf16[512,192]{1,0:T(8,128)(2,1)S(1)}, bf16[512,192]{1,0:T(8,128)(2,1)S(1)}, u32[]{:S(2)}, u32[]{:S(2)}) collective-permute-start(bf16[512,192]{1,0:T(8,128)(2,1)S(1)} %get-tuple-element.136), channel_id=1, source_target_pairs={{0,1},{1,0},{2,3},{3,2},{4,5},{5,4},{6,7},{7,6},{8,9},{9,8},{10,11... | collective-permute-start | bytes 589832 | tf_op jit(solution)/shard_map/ppermute | solution.py:373
  110.8 5.4 %collective-permute-start.32 = (bf16[4,96,768]{2,1,0:T(8,128)(2,1)S(1)}, bf16[4,96,768]{2,1,0:T(8,128)(2,1)S(1)}, u32[]{:S(2)}, u32[]{:S(2)}) collective-permute-start(bf16[4,96,768]{2,1,0:T(8,128)(2,1)S(1)} %get-tuple-element.146), channel_id=1, source_target_pairs={{0,1},{1,0},{2,3},{3,2},{4,5},{5,4},{6,7},{7,6},{8,9},{9,8},{10,11... | collective-permute-start | bytes 1769480 | tf_op jit(solution)/shard_map/ppermute | solution.py:373
  111.0 10.2 %collective-permute-start.33 = (bf16[128,768]{1,0:T(8,128)(2,1)S(1)}, bf16[128,768]{1,0:T(8,128)(2,1)S(1)}, u32[]{:S(2)}, u32[]{:S(2)}) collective-permute-start(bf16[128,768]{1,0:T(8,128)(2,1)S(1)} %get-tuple-element.154), channel_id=1, source_target_pairs={{0,2},{1,3},{2,0},{3,1},{4,6},{5,7},{6,4},{7,5},{8,10},{9,11},{10,... | collective-permute-start | bytes 589832 | tf_op jit(solution)/shard_map/ppermute | solution.py:377
  112.4 11.1 %collective-permute-start.34 = (bf16[128,768]{1,0:T(8,128)(2,1)S(1)}, bf16[128,768]{1,0:T(8,128)(2,1)S(1)}, u32[]{:S(2)}, u32[]{:S(2)}) collective-permute-start(bf16[128,768]{1,0:T(8,128)(2,1)S(1)} %get-tuple-element.156), channel_id=1, source_target_pairs={{0,4},{1,5},{2,6},{3,7},{4,0},{5,1},{6,2},{7,3},{8,12},{9,13},{10,... | collective-permute-start | bytes 589832 | tf_op jit(solution)/shard_map/ppermute | solution.py:377
  113.0 11.8 %collective-permute-start.35 = (bf16[128,768]{1,0:T(8,128)(2,1)S(1)}, bf16[128,768]{1,0:T(8,128)(2,1)S(1)}, u32[]{:S(2)}, u32[]{:S(2)}) collective-permute-start(bf16[128,768]{1,0:T(8,128)(2,1)S(1)} %get-tuple-element.158), channel_id=1, source_target_pairs={{0,6},{1,7},{2,4},{3,5},{4,2},{5,3},{6,0},{7,1},{8,14},{9,15},{10,... | collective-permute-start | bytes 589832 | tf_op jit(solution)/shard_map/ppermute | solution.py:377
  116.9 14.8 %collective-permute-start.37 = (bf16[104,768]{1,0:T(8,128)(2,1)S(1)}, bf16[104,768]{1,0:T(8,128)(2,1)S(1)}, u32[]{:S(2)}, u32[]{:S(2)}) collective-permute-start(bf16[104,768]{1,0:T(8,128)(2,1)S(1)} %get-tuple-element.160), channel_id=1, source_target_pairs={{0,16},{8,24},{16,0},{24,8},{1,17},{9,25},{17,1},{25,9},{2,18},{10... | collective-permute-start | bytes 479240 | tf_op jit(solution)/shard_map/ppermute | solution.py:381
  118.6 13.8 %collective-permute-start.38 = (bf16[104,768]{1,0:T(8,128)(2,1)S(1)}, bf16[104,768]{1,0:T(8,128)(2,1)S(1)}, u32[]{:S(2)}, u32[]{:S(2)}) collective-permute-start(bf16[104,768]{1,0:T(8,128)(2,1)S(1)} %get-tuple-element.161), channel_id=1, source_target_pairs={{0,24},{8,16},{16,8},{24,0},{1,25},{9,17},{17,9},{25,1},{2,26},{10... | collective-permute-start | bytes 479240 | tf_op jit(solution)/shard_map/ppermute | solution.py:381
  121.2 11.2 %collective-permute-start.36 = (bf16[104,768]{1,0:T(8,128)(2,1)S(1)}, bf16[104,768]{1,0:T(8,128)(2,1)S(1)}, u32[]{:S(2)}, u32[]{:S(2)}) collective-permute-start(bf16[104,768]{1,0:T(8,128)(2,1)S(1)} %get-tuple-element.147), channel_id=1, source_target_pairs={{0,8},{8,0},{16,24},{24,16},{1,9},{9,1},{17,25},{25,17},{2,10},{10... | collective-permute-start | bytes 479240 | tf_op jit(solution)/shard_map/ppermute | solution.py:381
  123.5 11.8 %collective-permute-start.41 = (bf16[192,768]{1,0:T(8,128)(2,1)S(1)}, bf16[192,768]{1,0:T(8,128)(2,1)S(1)}, u32[]{:S(2)}, u32[]{:S(2)}) collective-permute-start(bf16[192,768]{1,0:T(8,128)(2,1)S(1)} %shard_map.281.refs_0_), channel_id=1, source_target_pairs={{0,6},{1,7},{2,4},{3,5},{4,2},{5,3},{6,0},{7,1},{8,14},{9,15},{10,... | collective-permute-start | bytes 884744 | tf_op jit(solution)/shard_map/ppermute | solution.py:377
  124.9 12.2 %collective-permute-start.40 = (bf16[192,768]{1,0:T(8,128)(2,1)S(1)}, bf16[192,768]{1,0:T(8,128)(2,1)S(1)}, u32[]{:S(2)}, u32[]{:S(2)}) collective-permute-start(bf16[192,768]{1,0:T(8,128)(2,1)S(1)} %shard_map.281.refs_0_), channel_id=1, source_target_pairs={{0,4},{1,5},{2,6},{3,7},{4,0},{5,1},{6,2},{7,3},{8,12},{9,13},{10,... | collective-permute-start | bytes 884744 | tf_op jit(solution)/shard_map/ppermute | solution.py:377
  131.8 8.1 %collective-permute-start.39 = (bf16[192,768]{1,0:T(8,128)(2,1)S(1)}, bf16[192,768]{1,0:T(8,128)(2,1)S(1)}, u32[]{:S(2)}, u32[]{:S(2)}) collective-permute-start(bf16[192,768]{1,0:T(8,128)(2,1)S(1)} %shard_map.281.refs_0_), channel_id=1, source_target_pairs={{0,2},{1,3},{2,0},{3,1},{4,6},{5,7},{6,4},{7,5},{8,10},{9,11},{10,... | collective-permute-start | bytes 884744 | tf_op jit(solution)/shard_map/ppermute | solution.py:377
  133.1 8.6 %collective-permute-start.52 = (bf16[104,768]{1,0:T(8,128)(2,1)S(1)}, bf16[104,768]{1,0:T(8,128)(2,1)S(1)}, u32[]{:S(2)}, u32[]{:S(2)}) collective-permute-start(bf16[104,768]{1,0:T(8,128)(2,1)S(1)} %shard_map.282.refs_0_), channel_id=1, source_target_pairs={{0,1},{1,0},{2,3},{3,2},{4,5},{5,4},{6,7},{7,6},{8,9},{9,8},{10,11... | collective-permute-start | bytes 479240 | tf_op jit(solution)/shard_map/ppermute | solution.py:373
  133.1 11.4 %collective-permute-start.51 = (bf16[104,768]{1,0:T(8,128)(2,1)S(1)}, bf16[104,768]{1,0:T(8,128)(2,1)S(1)}, u32[]{:S(2)}, u32[]{:S(2)}) collective-permute-start(bf16[104,768]{1,0:T(8,128)(2,1)S(1)} %shard_map.282.refs_0_), channel_id=1, source_target_pairs={{0,6},{1,7},{2,4},{3,5},{4,2},{5,3},{6,0},{7,1},{8,14},{9,15},{10,... | collective-permute-start | bytes 479240 | tf_op jit(solution)/shard_map/ppermute | solution.py:377
  135.4 10.3 %collective-permute-start.42 = (bf16[192,768]{1,0:T(8,128)(2,1)S(1)}, bf16[192,768]{1,0:T(8,128)(2,1)S(1)}, u32[]{:S(2)}, u32[]{:S(2)}) collective-permute-start(bf16[192,768]{1,0:T(8,128)(2,1)S(1)} %shard_map.281.refs_0_), channel_id=1, source_target_pairs={{0,1},{1,0},{2,3},{3,2},{4,5},{5,4},{6,7},{7,6},{8,9},{9,8},{10,11... | collective-permute-start | bytes 884744 | tf_op jit(solution)/shard_map/ppermute | solution.py:373
  137.1 8.1 %collective-permute-start.50 = (bf16[104,768]{1,0:T(8,128)(2,1)S(1)}, bf16[104,768]{1,0:T(8,128)(2,1)S(1)}, u32[]{:S(2)}, u32[]{:S(2)}) collective-permute-start(bf16[104,768]{1,0:T(8,128)(2,1)S(1)} %shard_map.282.refs_0_), channel_id=1, source_target_pairs={{0,4},{1,5},{2,6},{3,7},{4,0},{5,1},{6,2},{7,3},{8,12},{9,13},{10,... | collective-permute-start | bytes 479240 | tf_op jit(solution)/shard_map/ppermute | solution.py:377
  139.8 5.6 %collective-permute-start.49 = (bf16[104,768]{1,0:T(8,128)(2,1)S(1)}, bf16[104,768]{1,0:T(8,128)(2,1)S(1)}, u32[]{:S(2)}, u32[]{:S(2)}) collective-permute-start(bf16[104,768]{1,0:T(8,128)(2,1)S(1)} %shard_map.282.refs_0_), channel_id=1, source_target_pairs={{0,2},{1,3},{2,0},{3,1},{4,6},{5,7},{6,4},{7,5},{8,10},{9,11},{10,... | collective-permute-start | bytes 479240 | tf_op jit(solution)/shard_map/ppermute | solution.py:377
  141.7 7.4 %collective-permute-start.45 = (bf16[192,768]{1,0:T(8,128)(2,1)S(1)}, bf16[192,768]{1,0:T(8,128)(2,1)S(1)}, u32[]{:S(2)}, u32[]{:S(2)}) collective-permute-start(bf16[192,768]{1,0:T(8,128)(2,1)S(1)} %collective-permute-done.41.refs_3_), channel_id=1, source_target_pairs={{0,1},{1,0},{2,3},{3,2},{4,5},{5,4},{6,7},{7,6},{8,9},{9,8},{10,11... | collective-permute-start | bytes 884744 | tf_op jit(solution)/shard_map/ppermute | solution.py:373
  144.5 1.4 collective-permute-start.55
  145.2 1.4 collective-permute-start.54
  145.4 2.2 %collective-permute-start.53 = (bf16[104,768]{1,0:T(8,128)(2,1)S(1)}, bf16[104,768]{1,0:T(8,128)(2,1)S(1)}, u32[]{:S(2)}, u32[]{:S(2)}) collective-permute-start(bf16[104,768]{1,0:T(8,128)(2,1)S(1)} %collective-permute-done.49.refs_1_), channel_id=1, source_target_pairs={{0,1},{1,0},{2,3},{3,2},{4,5},{5,4},{6,7},{7,6},{8,9},{9,8},{10,11... | collective-permute-start | bytes 479240 | tf_op jit(solution)/shard_map/ppermute | solution.py:373
  145.7 6.7 %collective-permute-start.44 = (bf16[192,768]{1,0:T(8,128)(2,1)S(1)}, bf16[192,768]{1,0:T(8,128)(2,1)S(1)}, u32[]{:S(2)}, u32[]{:S(2)}) collective-permute-start(bf16[192,768]{1,0:T(8,128)(2,1)S(1)} %collective-permute-done.40.refs_2_), channel_id=1, source_target_pairs={{0,1},{1,0},{2,3},{3,2},{4,5},{5,4},{6,7},{7,6},{8,9},{9,8},{10,11... | collective-permute-start | bytes 884744 | tf_op jit(solution)/shard_map/ppermute | solution.py:373
  145.9 6.5 %collective-permute-start.43 = (bf16[192,768]{1,0:T(8,128)(2,1)S(1)}, bf16[192,768]{1,0:T(8,128)(2,1)S(1)}, u32[]{:S(2)}, u32[]{:S(2)}) collective-permute-start(bf16[192,768]{1,0:T(8,128)(2,1)S(1)} %collective-permute-done.39.refs_1_), channel_id=1, source_target_pairs={{0,1},{1,0},{2,3},{3,2},{4,5},{5,4},{6,7},{7,6},{8,9},{9,8},{10,11... | collective-permute-start | bytes 884744 | tf_op jit(solution)/shard_map/ppermute | solution.py:373
  146.5 9.1 %collective-permute-start.46 = (bf16[128,768]{1,0:T(8,128)(2,1)S(1)}, bf16[128,768]{1,0:T(8,128)(2,1)S(1)}, u32[]{:S(2)}, u32[]{:S(2)}) collective-permute-start(bf16[128,768]{1,0:T(8,128)(2,1)S(1)} %get-tuple-element.169), channel_id=1, source_target_pairs={{0,2},{1,3},{2,0},{3,1},{4,6},{5,7},{6,4},{7,5},{8,10},{9,11},{10,... | collective-permute-start | bytes 589832 | tf_op jit(solution)/shard_map/ppermute | solution.py:377
  147.6 9.9 %collective-permute-start.47 = (bf16[128,768]{1,0:T(8,128)(2,1)S(1)}, bf16[128,768]{1,0:T(8,128)(2,1)S(1)}, u32[]{:S(2)}, u32[]{:S(2)}) collective-permute-start(bf16[128,768]{1,0:T(8,128)(2,1)S(1)} %get-tuple-element.171), channel_id=1, source_target_pairs={{0,4},{1,5},{2,6},{3,7},{4,0},{5,1},{6,2},{7,3},{8,12},{9,13},{10,... | collective-permute-start | bytes 589832 | tf_op jit(solution)/shard_map/ppermute | solution.py:377
  149.1 9.7 %collective-permute-start.48 = (bf16[128,768]{1,0:T(8,128)(2,1)S(1)}, bf16[128,768]{1,0:T(8,128)(2,1)S(1)}, u32[]{:S(2)}, u32[]{:S(2)}) collective-permute-start(bf16[128,768]{1,0:T(8,128)(2,1)S(1)} %get-tuple-element.173), channel_id=1, source_target_pairs={{0,6},{1,7},{2,4},{3,5},{4,2},{5,3},{6,0},{7,1},{8,14},{9,15},{10,... | collective-permute-start | bytes 589832 | tf_op jit(solution)/shard_map/ppermute | solution.py:377

commit v7 on v6

--- a/solution.py
+++ b/solution.py
@@ -545,11 +545,12 @@
     pair, (mixed_ref, state_ref, key_ref, value_ref) = refs[:4], refs[4:]
     cols, keys = split_ids(pair[0], pair[2])
     all_keys(pair, key_ref, value_ref)
-    lane = lax.broadcasted_iota(jnp.int32, (ROWS, 64), 1)
-    for r in range(4):
-        rows = slice(ROWS * r, ROWS * (r + 1))
-        hidden = keys > cols[:, r : r + 1]
-        heads, lse = [], jnp.zeros((ROWS, 64), f32)
+    lane = lax.broadcasted_iota(jnp.int32, (2 * ROWS, 64), 1)
+    for r in range(2):
+        rows = slice(2 * ROWS * r, 2 * ROWS * (r + 1))
+        ids = jnp.concatenate([cols[:, 2 * r : 2 * r + 1], cols[:, 2 * r + 1 : 2 * r + 2]], 0)
+        hidden = keys > ids
+        heads, lse = [], jnp.zeros((2 * ROWS, 64), f32)
         for h in range(3):
             at = slice(64 * h, 64 * h + 64)
             query = q_ref[rows, at]
@@ -659,9 +660,10 @@
         at = slice(64 * h, 64 * h + 64)
         query, grad = q_ref[:, at], grad_mixed[:, at]
         grad_q = []
-        for r in range(4):
-            rows = slice(ROWS * r, ROWS * (r + 1))
-            hidden = keys > cols[:, r : r + 1]
+        for r in range(2):
+            rows = slice(2 * ROWS * r, 2 * ROWS * (r + 1))
+            ids = jnp.concatenate([cols[:, 2 * r : 2 * r + 1], cols[:, 2 * r + 1 : 2 * r + 2]], 0)
+            hidden = keys > ids
             g = grad[rows]
             inner = jnp.sum(g.astype(f32) * state_ref[rows, at], -1, keepdims=True)
             lse = state_ref[rows, QUARTER + h : QUARTER + h + 1]

time: 161 us -> 160 us (level)
    pallas_call x15, Pallas kernels: 40 us -> 38.4 us  [run(): pl.pallas_call(body, out_shape=[jax.ShapeDtypeStruct(shape, kind) for sha...]
  transfers between devices with their start and end apart: 56 -> 56, of which waited for: 28 -> 26; matrix products, arithmetic and copies ran while one was open for 0% -> 0% of each run, Pallas kernels for 17% -> 16%
where the time goes in v7:
time: 160 us
  waiting for transfers between devices  65.5 us (41%)
  starting transfers between devices  51.8 us (32%)
  Pallas kernels  38.4 us (24%)
  local copies, waits for them, and re-layouts  2.84 us (2%)
    pallas_call x15, Pallas kernels, run(): pl.pallas_call(body, out_shape=[jax.ShapeDtypeStruct(shape, kind) for sha...  38.4 us
    ppermute x12, waiting for transfers between devices, seq_swap(): return lax.ppermute(values, 'seq', [(i, i ^ mask) for i in range(4)])  31.9 us
    ppermute x24, starting transfers between devices, chip_swap(): return lax.ppermute(values, 'ctx', [(i, i ^ 2 * mask) for i in range(8)])  29.8 us
    ppermute x24, waiting for transfers between devices, chip_swap(): return lax.ppermute(values, 'ctx', [(i, i ^ 2 * mask) for i in range(8)])  25.7 us
    ppermute x12, starting transfers between devices, seq_swap(): return lax.ppermute(values, 'seq', [(i, i ^ mask) for i in range(4)])  18.1 us
    ppermute x20, waiting for transfers between devices, core_swap(): return lax.ppermute(values, 'ctx', [(i, i ^ 1) for i in range(8)])  7.86 us
    ppermute x20, starting transfers between devices, core_swap(): return lax.ppermute(values, 'ctx', [(i, i ^ 1) for i in range(8)])  3.93 us
  transfers between devices with their start and end apart: 56, of which 26 were waited for; matrix products, arithmetic and copies ran while one was open for 0% of the time, Pallas kernels for 16%

profile of v7, /device:TPU:0, one launch (start us, length us, event | category | flops | bytes accessed | tf_op | source)
XLA Modules:
  0.0 160.0 jit_solution(13328665307130754328)
XLA Ops:
  1.3 4.1 %shard_map.271 = (bf16[112,576]{1,0:T(8,128)(2,1)}, bf16[112,576]{1,0:T(8,128)(2,1)}, bf16[264,768]{1,0:T(8,128)(2,1)}, bf16[288,768]{1,0:T(8,128)(2,1)}, bf16[288,768]{1,0:T(8,128)(2,1)}) custom-call(s32[3]{0:T(128)} %pad_add_fusion.pos, bf16[192,2304]{1,0:T(8,128)(2,1)} %w_ref.1, bf16[1,128,768]{2,1,0:T(8,128)(2,1)} %tok_ref.1, ...), custom_call_target="tpu_custom_call" | custom-call | flops 524288 | bytes 1000 | tf_op jit(solution)/shard_map/pallas_call | solution.py:402
  5.4 5.1 %collective-permute-start.5 = (bf16[112,576]{1,0:T(8,128)(2,1)}, bf16[112,576]{1,0:T(8,128)(2,1)S(1)}, u32[]{:S(2)}, u32[]{:S(2)}) collective-permute-start(bf16[112,576]{1,0:T(8,128)(2,1)} %get-tuple-element.105.refs_4_), channel_id=1, source_target_pairs={{0,24},{8,16},{16,8},{24,0},{1,25},{9,17},{17,9},{25,1},{2,26},{10... | collective-permute-start | bytes 387080 | tf_op jit(solution)/shard_map/ppermute | solution.py:381
  10.5 2.5 %collective-permute-start.2 = (bf16[264,768]{1,0:T(8,128)(2,1)}, bf16[264,768]{1,0:T(8,128)(2,1)S(1)}, u32[]{:S(2)}, u32[]{:S(2)}) collective-permute-start(bf16[264,768]{1,0:T(8,128)(2,1)} %get-tuple-element.104.refs_0_.tok_ref), channel_id=1, source_target_pairs={{0,6},{1,7},{2,4},{3,5},{4,2},{5,3},{6,0},{7,1},{8,14},{9,15},{10,... | collective-permute-start | bytes 1216520 | tf_op jit(solution)/shard_map/ppermute | solution.py:377
  13.0 0.8 collective-permute-start.3
  14.3 1.1 collective-permute-done.5.refs_7_
  15.4 1.7 %collective-permute-start = (bf16[264,768]{1,0:T(8,128)(2,1)}, bf16[264,768]{1,0:T(8,128)(2,1)S(1)}, u32[]{:S(2)}, u32[]{:S(2)}) collective-permute-start(bf16[264,768]{1,0:T(8,128)(2,1)} %get-tuple-element.104.refs_0_.tok_ref), channel_id=1, source_target_pairs={{0,2},{1,3},{2,0},{3,1},{4,6},{5,7},{6,4},{7,5},{8,10},{9,11},{10,... | collective-permute-start | bytes 1216520 | tf_op jit(solution)/shard_map/ppermute | solution.py:377
  17.1 5.7 %collective-permute-done.4.refs_6_ = bf16[112,576]{1,0:T(8,128)(2,1)S(1)} collective-permute-done((bf16[112,576]{1,0:T(8,128)(2,1)}, bf16[112,576]{1,0:T(8,128)(2,1)S(1)}, u32[]{:S(2)}, u32[]{:S(2)}) %collective-permute-start.4) | collective-permute-done | bytes 129056 | tf_op jit(solution)/shard_map/ppermute | solution.py:381
  23.4 0.9 collective-permute-done.8.refs_11_
  24.2 2.5 %collective-permute-start.16 = (bf16[288,768]{1,0:T(8,128)(2,1)}, bf16[288,768]{1,0:T(8,128)(2,1)S(1)}, u32[]{:S(2)}, u32[]{:S(2)}) collective-permute-start(bf16[288,768]{1,0:T(8,128)(2,1)} %get-tuple-element.112.refs_8_), channel_id=1, source_target_pairs={{0,24},{8,16},{16,8},{24,0},{1,25},{9,17},{17,9},{25,1},{2,26},{10... | collective-permute-start | bytes 1327112 | tf_op jit(solution)/shard_map/ppermute | solution.py:381
  26.7 1.4 collective-permute-done.6.refs_9_
  28.1 1.9 %collective-permute-start.14 = (bf16[288,768]{1,0:T(8,128)(2,1)}, bf16[288,768]{1,0:T(8,128)(2,1)S(1)}, u32[]{:S(2)}, u32[]{:S(2)}) collective-permute-start(bf16[288,768]{1,0:T(8,128)(2,1)} %get-tuple-element.112.refs_8_), channel_id=1, source_target_pairs={{0,8},{8,0},{16,24},{24,16},{1,9},{9,1},{17,25},{25,17},{2,10},{10... | collective-permute-start | bytes 1327112 | tf_op jit(solution)/shard_map/ppermute | solution.py:381
  30.0 1.2 collective-permute-done.1.refs_2_
  31.2 1.0 copy-done
  32.2 0.9 copy-done.4
  33.1 0.9 copy-done.5
  34.1 1.9 %shard_map.272 = (bf16[512,192]{1,0:T(8,128)(2,1)S(1)}, bf16[520,192]{1,0:T(8,128)(2,1)S(1)}, bf16[512,192]{1,0:T(8,128)(2,1)S(1)}, bf16[512,768]{1,0:T(8,128)(2...) custom-call(s32[3]{0:T(128)S(1)} %copy-done.6, bf16[264,768]{1,0:T(8,128)(2,1)S(1)} %copy-done, ...), custom_call_target="tpu_custom_call" | custom-call | flops 524288 | bytes 1000 | tf_op jit(solution)/shard_map/pallas_call | solution.py:402
  36.6 1.4 collective-permute-done.10.refs_3_
  38.0 4.1 %shard_map.273 = (bf16[512,192]{1,0:T(8,128)(2,1)S(1)}, f32[512,256]{1,0:T(8,128)S(1)}) custom-call(s32[3]{0:T(128)S(1)} %copy-done.6, bf16[512,192]{1,0:T(8,128)(2,1)S(1)} %get-tuple-element.107.q_ref, bf16[520,192]{1,0:T(8,128)(2,1)S(1)} %get-tuple-element.108.refs_0_, bf16[512,192]{1,0:T(8,128)(2,1)S(1)} %get-tuple-element.109.refs_1_, ...), custom_call_target="tpu_custom_call" | custom-call | flops 524288 | bytes 1000 | tf_op jit(solution)/shard_map/pallas_call | solution.py:402
  42.1 2.1 %collective-permute-start.13 = (bf16[512,192]{1,0:T(8,128)(2,1)S(1)}, bf16[512,192]{1,0:T(8,128)(2,1)S(1)}, u32[]{:S(2)}, u32[]{:S(2)}) collective-permute-start(bf16[512,192]{1,0:T(8,128)(2,1)S(1)} %get-tuple-element.110.refs_4_.refs_0_), channel_id=1, source_target_pairs={{0,6},{1,7},{2,4},{3,5},{4,2},{5,3},{6,0},{7,1},{8,14},{9,15},{10,... | collective-permute-start | bytes 589832 | tf_op jit(solution)/shard_map/ppermute | solution.py:377
  44.2 1.0 collective-permute-start.12
  45.7 18.8 %collective-permute-done.15.refs_10_ = bf16[288,768]{1,0:T(8,128)(2,1)S(1)} collective-permute-done((bf16[288,768]{1,0:T(8,128)(2,1)}, bf16[288,768]{1,0:T(8,128)(2,1)S(1)}, u32[]{:S(2)}, u32[]{:S(2)}) %collective-permute-start.15) | collective-permute-done | bytes 442400 | tf_op jit(solution)/shard_map/ppermute | solution.py:381
  65.2 1.2 collective-permute-done.17.refs_13_
  67.7 7.0 %shard_map.274 = (f32[128,768]{1,0:T(8,128)S(1)}, f32[128,768]{1,0:T(8,128)S(1)}, bf16[128,768]{1,0:T(8,128)(2,1)S(1)}, bf16[128,768]{1,0:T(8,128)(2,1)S(1)}, bf...) custom-call(s32[3]{0:T(128)S(1)} %copy-done.6, ...), custom_call_target="tpu_custom_call" | custom-call | flops 524288 | bytes 1000 | tf_op jit(solution)/shard_map/pallas_call | solution.py:402
  74.9 1.3 collective-permute-start.21
  76.1 1.5 collective-permute-start.22
  77.7 0.7 collective-permute-start.23
  78.4 1.0 shard_map.275
  79.4 2.7 %collective-permute-start.28 = (bf16[192,768]{1,0:T(8,128)(2,1)S(1)}, bf16[192,768]{1,0:T(8,128)(2,1)S(1)}, u32[]{:S(2)}, u32[]{:S(2)}) collective-permute-start(bf16[192,768]{1,0:T(8,128)(2,1)S(1)} %get-tuple-element.135), channel_id=1, source_target_pairs={{0,24},{8,16},{16,8},{24,0},{1,25},{9,17},{17,9},{25,1},{2,26},{10... | collective-permute-start | bytes 884744 | tf_op jit(solution)/shard_map/ppermute | solution.py:381
  82.6 3.8 %collective-permute-done.22.r2 = bf16[128,768]{1,0:T(8,128)(2,1)S(1)} collective-permute-done((bf16[128,768]{1,0:T(8,128)(2,1)S(1)}, bf16[128,768]{1,0:T(8,128)(2,1)S(1)}, u32[]{:S(2)}, u32[]{:S(2)}) %collective-permute-start.22) | collective-permute-done | bytes 196640 | tf_op jit(solution)/shard_map/ppermute | solution.py:377
  86.4 0.9 collective-permute-done.23.r3
  87.3 0.9 shard_map.276
  88.2 1.8 %collective-permute-start.26 = (bf16[128,768]{1,0:T(8,128)(2,1)S(1)}, bf16[128,768]{1,0:T(8,128)(2,1)S(1)}, u32[]{:S(2)}, u32[]{:S(2)}) collective-permute-start(bf16[128,768]{1,0:T(8,128)(2,1)S(1)} %get-tuple-element.127.a0.refs_4_.refs_6_), channel_id=1, source_target_pairs={{0,6},{1,7},{2,4},{3,5},{4,2},{5,3},{6,0},{7,1},{8,14},{9,15},{10,... | collective-permute-start | bytes 589832 | tf_op jit(solution)/shard_map/ppermute | solution.py:377
  90.0 1.0 collective-permute-start.25
  91.0 0.8 collective-permute-start.24
  91.8 5.3 %collective-permute-done.26.a3.refs_7_ = bf16[128,768]{1,0:T(8,128)(2,1)S(1)} collective-permute-done((bf16[128,768]{1,0:T(8,128)(2,1)S(1)}, bf16[128,768]{1,0:T(8,128)(2,1)S(1)}, u32[]{:S(2)}, u32[]{:S(2)}) %collective-permute-start.26) | collective-permute-done | bytes 196640 | tf_op jit(solution)/shard_map/ppermute | solution.py:377
  97.1 2.8 %collective-permute-done.25.a2.refs_6_ = bf16[128,768]{1,0:T(8,128)(2,1)S(1)} collective-permute-done((bf16[128,768]{1,0:T(8,128)(2,1)S(1)}, bf16[128,768]{1,0:T(8,128)(2,1)S(1)}, u32[]{:S(2)}, u32[]{:S(2)}) %collective-permute-start.25) | collective-permute-done | bytes 196640 | tf_op jit(solution)/shard_map/ppermute | solution.py:377
  99.8 5.5 %shard_map.277 = (bf16[512,192]{1,0:T(8,128)(2,1)S(1)}, f32[512,384]{1,0:T(8,128)S(1)}, bf16[512,192]{1,0:T(8,128)(2,1)S(1)}, bf16[512,192]{1,0:T(8,128)(2,1)S(1)}) custom-call(s32[3]{0:T(128)S(1)} %copy-done.6, bf16[128,768]{1,0:T(8,128)(2,1)S(1)} %get-tuple-element.127.a0.refs_4_.refs_6_, bf16[128,768]{1,0:T(8,128)(2,1)S(1)} %collective-permute-done.24.a1.refs_5_, ...), custom_call_target="tpu_custom_call" | custom-call | flops 524288 | bytes 1000 | tf_op jit(solution)/shard_map/pallas_call | solution.py:402
  105.9 1.0 collective-permute-done.30.refs_12_
  107.3 2.8 %shard_map.278 = (bf16[4,96,768]{2,1,0:T(8,128)(2,1)S(1)}, f32[4,96,768]{2,1,0:T(8,128)S(1)}, bf16[512,576]{1,0:T(8,128)(2,1)S(1)}) custom-call(s32[3]{0:T(128)S(1)} %copy-done.6, bf16[512,192]{1,0:T(8,128)(2,1)S(1)} %get-tuple-element.110.refs_4_.refs_0_, bf16[512,192]{1,0:T(8,128)(2,1)S(1)} %collective-permute-done.11.refs_5_.refs_1_, ...), custom_call_target="tpu_custom_call" | custom-call | flops 524288 | bytes 1000 | tf_op jit(solution)/shard_map/pallas_call | solution.py:402
  110.3 1.4 collective-permute-start.33
  112.3 1.5 collective-permute-start.35
  113.8 1.7 %shard_map.279 = (f32[4,8,768]{2,1,0:T(8,128)S(1)}, f32[128,768]{1,0:T(8,128)S(1)}, bf16[128,768]{1,0:T(8,128)(2,1)S(1)}, bf16[128,768]{1,0:T(8,128)(2,1)S(1)}, bf16[128,768]{1,0:T(8,128)(2,1)S(1)}) custom-call(s32[3]{0:T(128)S(1)} %copy-done.6, bf16[264,768]{1,0:T(8,128)(2,1)S(1)} %copy-done.1, bf16[264,768]{1,0:T(8,128)(2,1)S(1)} %collective-permute-done.refs_1_, ...), custom_call_target="tpu_custom_call" | custom-call | flops 524288 | bytes 1000 | tf_op jit(solution)/shard_map/pallas_call | solution.py:402
  115.5 0.7 shard_map.280
  116.2 2.4 %collective-permute-start.37 = (bf16[104,768]{1,0:T(8,128)(2,1)S(1)}, bf16[104,768]{1,0:T(8,128)(2,1)S(1)}, u32[]{:S(2)}, u32[]{:S(2)}) collective-permute-start(bf16[104,768]{1,0:T(8,128)(2,1)S(1)} %get-tuple-element.160), channel_id=1, source_target_pairs={{0,16},{8,24},{16,0},{24,8},{1,17},{9,25},{17,1},{25,9},{2,18},{10... | collective-permute-start | bytes 479240 | tf_op jit(solution)/shard_map/ppermute | solution.py:381
  118.6 2.6 %collective-permute-start.38 = (bf16[104,768]{1,0:T(8,128)(2,1)S(1)}, bf16[104,768]{1,0:T(8,128)(2,1)S(1)}, u32[]{:S(2)}, u32[]{:S(2)}) collective-permute-start(bf16[104,768]{1,0:T(8,128)(2,1)S(1)} %get-tuple-element.161), channel_id=1, source_target_pairs={{0,24},{8,16},{16,8},{24,0},{1,25},{9,17},{17,9},{25,1},{2,26},{10... | collective-permute-start | bytes 479240 | tf_op jit(solution)/shard_map/ppermute | solution.py:381
  121.2 0.7 shard_map.281.refs_0_
  121.9 0.9 collective-permute-done.34.s2
  122.8 1.3 collective-permute-start.41
  124.1 0.8 collective-permute-start.40
  124.9 6.2 %collective-permute-done.37.r2 = bf16[104,768]{1,0:T(8,128)(2,1)S(1)} collective-permute-done((bf16[104,768]{1,0:T(8,128)(2,1)S(1)}, bf16[104,768]{1,0:T(8,128)(2,1)S(1)}, u32[]{:S(2)}, u32[]{:S(2)}) %collective-permute-start.37) | collective-permute-done | bytes 159776 | tf_op jit(solution)/shard_map/ppermute | solution.py:381
  131.1 1.4 collective-permute-start.39
  133.2 1.4 collective-permute-start.51
  134.8 2.3 %collective-permute-done.40.refs_2_ = bf16[192,768]{1,0:T(8,128)(2,1)S(1)} collective-permute-done((bf16[192,768]{1,0:T(8,128)(2,1)S(1)}, bf16[192,768]{1,0:T(8,128)(2,1)S(1)}, u32[]{:S(2)}, u32[]{:S(2)}) %collective-permute-start.40) | collective-permute-done | bytes 294944 | tf_op jit(solution)/shard_map/ppermute | solution.py:377
  137.1 0.9 collective-permute-start.50
  138.0 0.9 collective-permute-done.39.refs_1_
  138.9 1.7 %collective-permute-start.49 = (bf16[104,768]{1,0:T(8,128)(2,1)S(1)}, bf16[104,768]{1,0:T(8,128)(2,1)S(1)}, u32[]{:S(2)}, u32[]{:S(2)}) collective-permute-start(bf16[104,768]{1,0:T(8,128)(2,1)S(1)} %shard_map.282.refs_0_), channel_id=1, source_target_pairs={{0,2},{1,3},{2,0},{3,1},{4,6},{5,7},{6,4},{7,5},{8,10},{9,11},{10,... | collective-permute-start | bytes 479240 | tf_op jit(solution)/shard_map/ppermute | solution.py:377
  140.6 2.4 %collective-permute-done.51.refs_3_ = bf16[104,768]{1,0:T(8,128)(2,1)S(1)} collective-permute-done((bf16[104,768]{1,0:T(8,128)(2,1)S(1)}, bf16[104,768]{1,0:T(8,128)(2,1)S(1)}, u32[]{:S(2)}, u32[]{:S(2)}) %collective-permute-start.51) | collective-permute-done | bytes 159776 | tf_op jit(solution)/shard_map/ppermute | solution.py:377
  143.0 2.3 %collective-permute-done.50.refs_2_ = bf16[104,768]{1,0:T(8,128)(2,1)S(1)} collective-permute-done((bf16[104,768]{1,0:T(8,128)(2,1)S(1)}, bf16[104,768]{1,0:T(8,128)(2,1)S(1)}, u32[]{:S(2)}, u32[]{:S(2)}) %collective-permute-start.50) | collective-permute-done | bytes 159776 | tf_op jit(solution)/shard_map/ppermute | solution.py:377
  147.3 1.4 collective-permute-start.47
  148.7 1.4 collective-permute-start.48
  150.2 2.3 %shard_map.285 = (f32[192,2304]{1,0:T(8,128)}, f32[192,768]{1,0:T(8,128)}, f32[192]{0:T(256)}, f32[192]{0:T(256)}, f32[192]{0:T(256)}, /*index=5*/f32[192]{0:T(2...) custom-call(s32[3]{0:T(128)S(1)} %copy-done.6, ...), custom_call_target="tpu_custom_call" | custom-call | flops 524288 | bytes 1000 | tf_op jit(solution)/shard_map/pallas_call | solution.py:402
  152.5 3.2 %shard_map.283 = (f32[768,768]{1,0:T(8,128)}, f32[192,3072]{1,0:T(8,128)}) custom-call(s32[3]{0:T(128)S(1)} %copy-done.6, bf16[192,768]{1,0:T(8,128)(2,1)S(1)} %shard_map.281.refs_0_, bf16[192,768]{1,0:T(8,128)(2,1)S(1)} %collective-permute-done.39.refs_1_, bf16[192,768]{1,0:T(8,128)(2,1)S(1)} %collective-permute-done.40.refs_2_, ...), custom_call_target="tpu_custom_call" | custom-call | flops 524288 | bytes 1000 | tf_op jit(solution)/shard_map/pallas_call | solution.py:402
  155.8 2.4 %collective-permute-done.47.r2 = bf16[128,768]{1,0:T(8,128)(2,1)S(1)} collective-permute-done((bf16[128,768]{1,0:T(8,128)(2,1)S(1)}, bf16[128,768]{1,0:T(8,128)(2,1)S(1)}, u32[]{:S(2)}, u32[]{:S(2)}) %collective-permute-start.47) | collective-permute-done | bytes 196640 | tf_op jit(solution)/shard_map/ppermute | solution.py:377
  158.2 1.8 %shard_map.284 = (f32[1,128,768]{2,1,0:T(8,128)}, bf16[1,128,768]{2,1,0:T(8,128)(2,1)}) custom-call(s32[3]{0:T(128)S(1)} %copy-done.6, f32[128,768]{1,0:T(8,128)S(1)} %get-tuple-element.167.g0, bf16[128,768]{1,0:T(8,128)(2,1)S(1)} %collective-permute-done.46.r1, bf16[128,768]{1,0:T(8,128)(2,1)S(1)} %collective-permute-done.47.r2, ...), custom_call_target="tpu_custom_call" | custom-call | flops 524288 | bytes 1000 | tf_op jit(solution)/shard_map/pallas_call | solution.py:402
  (78 shorter events, 10.2 us)
Async XLA Ops:
  1.3 30.0 %copy-start.6 = (s32[3]{0:T(128)S(1)}, s32[3]{0:T(128)}, u32[]{:S(2)}) copy-start(s32[3]{0:T(128)} %pad_add_fusion.pos) | copy-start | bytes 40
  5.4 10.0 %collective-permute-start.5 = (bf16[112,576]{1,0:T(8,128)(2,1)}, bf16[112,576]{1,0:T(8,128)(2,1)S(1)}, u32[]{:S(2)}, u32[]{:S(2)}) collective-permute-start(bf16[112,576]{1,0:T(8,128)(2,1)} %get-tuple-element.105.refs_4_), channel_id=1, source_target_pairs={{0,24},{8,16},{16,8},{24,0},{1,25},{9,17},{17,9},{25,1},{2,26},{10... | collective-permute-start | bytes 387080 | tf_op jit(solution)/shard_map/ppermute | solution.py:381
  10.5 12.3 %collective-permute-start.4 = (bf16[112,576]{1,0:T(8,128)(2,1)}, bf16[112,576]{1,0:T(8,128)(2,1)S(1)}, u32[]{:S(2)}, u32[]{:S(2)}) collective-permute-start(bf16[112,576]{1,0:T(8,128)(2,1)} %get-tuple-element.105.refs_4_), channel_id=1, source_target_pairs={{0,16},{8,24},{16,0},{24,8},{1,17},{9,25},{17,1},{25,9},{2,18},{10... | collective-permute-start | bytes 387080 | tf_op jit(solution)/shard_map/ppermute | solution.py:381
  10.5 17.6 %collective-permute-start.2 = (bf16[264,768]{1,0:T(8,128)(2,1)}, bf16[264,768]{1,0:T(8,128)(2,1)S(1)}, u32[]{:S(2)}, u32[]{:S(2)}) collective-permute-start(bf16[264,768]{1,0:T(8,128)(2,1)} %get-tuple-element.104.refs_0_.tok_ref), channel_id=1, source_target_pairs={{0,6},{1,7},{2,4},{3,5},{4,2},{5,3},{6,0},{7,1},{8,14},{9,15},{10,... | collective-permute-start | bytes 1216520 | tf_op jit(solution)/shard_map/ppermute | solution.py:377
  13.0 9.9 %collective-permute-start.3 = (bf16[112,576]{1,0:T(8,128)(2,1)}, bf16[112,576]{1,0:T(8,128)(2,1)S(1)}, u32[]{:S(2)}, u32[]{:S(2)}) collective-permute-start(bf16[112,576]{1,0:T(8,128)(2,1)} %get-tuple-element.105.refs_4_), channel_id=1, source_target_pairs={{0,8},{8,0},{16,24},{24,16},{1,9},{9,1},{17,25},{25,17},{2,10},{10... | collective-permute-start | bytes 387080 | tf_op jit(solution)/shard_map/ppermute | solution.py:381
  13.8 17.4 %collective-permute-start.1 = (bf16[264,768]{1,0:T(8,128)(2,1)}, bf16[264,768]{1,0:T(8,128)(2,1)S(1)}, u32[]{:S(2)}, u32[]{:S(2)}) collective-permute-start(bf16[264,768]{1,0:T(8,128)(2,1)} %get-tuple-element.104.refs_0_.tok_ref), channel_id=1, source_target_pairs={{0,4},{1,5},{2,6},{3,7},{4,0},{5,1},{6,2},{7,3},{8,12},{9,13},{10,... | collective-permute-start | bytes 1216520 | tf_op jit(solution)/shard_map/ppermute | solution.py:377
  15.4 15.8 %collective-permute-start = (bf16[264,768]{1,0:T(8,128)(2,1)}, bf16[264,768]{1,0:T(8,128)(2,1)S(1)}, u32[]{:S(2)}, u32[]{:S(2)}) collective-permute-start(bf16[264,768]{1,0:T(8,128)(2,1)} %get-tuple-element.104.refs_0_.tok_ref), channel_id=1, source_target_pairs={{0,2},{1,3},{2,0},{3,1},{4,6},{5,7},{6,4},{7,5},{8,10},{9,11},{10,... | collective-permute-start | bytes 1216520 | tf_op jit(solution)/shard_map/ppermute | solution.py:377
  22.8 1.4 collective-permute-start.8
  22.8 3.8 %collective-permute-start.7 = (bf16[112,576]{1,0:T(8,128)(2,1)S(1)}, bf16[112,576]{1,0:T(8,128)(2,1)S(1)}, u32[]{:S(2)}, u32[]{:S(2)}) collective-permute-start(bf16[112,576]{1,0:T(8,128)(2,1)S(1)} %collective-permute-done.4.refs_6_), channel_id=1, source_target_pairs={{0,1},{1,0},{2,3},{3,2},{4,5},{5,4},{6,7},{7,6},{8,9},{9,8},{10,11... | collective-permute-start | bytes 387080 | tf_op jit(solution)/shard_map/ppermute | solution.py:373
  24.2 21.0 %collective-permute-start.16 = (bf16[288,768]{1,0:T(8,128)(2,1)}, bf16[288,768]{1,0:T(8,128)(2,1)S(1)}, u32[]{:S(2)}, u32[]{:S(2)}) collective-permute-start(bf16[288,768]{1,0:T(8,128)(2,1)} %get-tuple-element.112.refs_8_), channel_id=1, source_target_pairs={{0,24},{8,16},{16,8},{24,0},{1,25},{9,17},{17,9},{25,1},{2,26},{10... | collective-permute-start | bytes 1327112 | tf_op jit(solution)/shard_map/ppermute | solution.py:381
  26.7 1.4 collective-permute-start.6
  28.1 36.4 %collective-permute-start.15 = (bf16[288,768]{1,0:T(8,128)(2,1)}, bf16[288,768]{1,0:T(8,128)(2,1)S(1)}, u32[]{:S(2)}, u32[]{:S(2)}) collective-permute-start(bf16[288,768]{1,0:T(8,128)(2,1)} %get-tuple-element.112.refs_8_), channel_id=1, source_target_pairs={{0,16},{8,24},{16,0},{24,8},{1,17},{9,25},{17,1},{25,9},{2,18},{10... | collective-permute-start | bytes 1327112 | tf_op jit(solution)/shard_map/ppermute | solution.py:381
  28.1 36.4 %collective-permute-start.14 = (bf16[288,768]{1,0:T(8,128)(2,1)}, bf16[288,768]{1,0:T(8,128)(2,1)S(1)}, u32[]{:S(2)}, u32[]{:S(2)}) collective-permute-start(bf16[288,768]{1,0:T(8,128)(2,1)} %get-tuple-element.112.refs_8_), channel_id=1, source_target_pairs={{0,8},{8,0},{16,24},{24,16},{1,9},{9,1},{17,25},{25,17},{2,10},{10... | collective-permute-start | bytes 1327112 | tf_op jit(solution)/shard_map/ppermute | solution.py:381
  31.2 1.0 copy-start
  32.2 0.9 copy-start.4
  33.1 0.9 copy-start.5
  36.0 31.7 %copy-start.1 = (bf16[264,768]{1,0:T(8,128)(2,1)S(1)}, bf16[264,768]{1,0:T(8,128)(2,1)}, u32[]{:S(2)}) copy-start(bf16[264,768]{1,0:T(8,128)(2,1)} %get-tuple-element.104.refs_0_.tok_ref) | copy-start | bytes 1216516
  36.0 31.7 %copy-start.2 = (bf16[288,768]{1,0:T(8,128)(2,1)S(1)}, bf16[288,768]{1,0:T(8,128)(2,1)}, u32[]{:S(2)}) copy-start(bf16[288,768]{1,0:T(8,128)(2,1)} %get-tuple-element.112.refs_8_) | copy-start | bytes 1327108
  36.0 31.6 %copy-start.3 = (bf16[288,768]{1,0:T(8,128)(2,1)S(1)}, bf16[288,768]{1,0:T(8,128)(2,1)}, u32[]{:S(2)}) copy-start(bf16[288,768]{1,0:T(8,128)(2,1)} %get-tuple-element.116.refs_12_) | copy-start | bytes 1327108
  36.0 2.0 %collective-permute-start.9 = (bf16[520,192]{1,0:T(8,128)(2,1)S(1)}, bf16[520,192]{1,0:T(8,128)(2,1)S(1)}, u32[]{:S(2)}, u32[]{:S(2)}) collective-permute-start(bf16[520,192]{1,0:T(8,128)(2,1)S(1)} %get-tuple-element.108.refs_0_), channel_id=1, source_target_pairs={{0,1},{1,0},{2,3},{3,2},{4,5},{5,4},{6,7},{7,6},{8,9},{9,8},{10,11... | collective-permute-start | bytes 599048 | tf_op jit(solution)/shard_map/ppermute | solution.py:373
  36.1 1.9 %collective-permute-start.10 = (bf16[512,192]{1,0:T(8,128)(2,1)S(1)}, bf16[512,192]{1,0:T(8,128)(2,1)S(1)}, u32[]{:S(2)}, u32[]{:S(2)}) collective-permute-start(bf16[512,192]{1,0:T(8,128)(2,1)S(1)} %get-tuple-element.109.refs_1_), channel_id=1, source_target_pairs={{0,1},{1,0},{2,3},{3,2},{4,5},{5,4},{6,7},{7,6},{8,9},{9,8},{10,11... | collective-permute-start | bytes 589832 | tf_op jit(solution)/shard_map/ppermute | solution.py:373
  42.1 22.4 %collective-permute-start.13 = (bf16[512,192]{1,0:T(8,128)(2,1)S(1)}, bf16[512,192]{1,0:T(8,128)(2,1)S(1)}, u32[]{:S(2)}, u32[]{:S(2)}) collective-permute-start(bf16[512,192]{1,0:T(8,128)(2,1)S(1)} %get-tuple-element.110.refs_4_.refs_0_), channel_id=1, source_target_pairs={{0,6},{1,7},{2,4},{3,5},{4,2},{5,3},{6,0},{7,1},{8,14},{9,15},{10,... | collective-permute-start | bytes 589832 | tf_op jit(solution)/shard_map/ppermute | solution.py:377
  44.2 20.3 %collective-permute-start.12 = (bf16[512,192]{1,0:T(8,128)(2,1)S(1)}, bf16[512,192]{1,0:T(8,128)(2,1)S(1)}, u32[]{:S(2)}, u32[]{:S(2)}) collective-permute-start(bf16[512,192]{1,0:T(8,128)(2,1)S(1)} %get-tuple-element.110.refs_4_.refs_0_), channel_id=1, source_target_pairs={{0,4},{1,5},{2,6},{3,7},{4,0},{5,1},{6,2},{7,3},{8,12},{9,13},{10,... | collective-permute-start | bytes 589832 | tf_op jit(solution)/shard_map/ppermute | solution.py:377
  45.2 19.4 %collective-permute-start.11 = (bf16[512,192]{1,0:T(8,128)(2,1)S(1)}, bf16[512,192]{1,0:T(8,128)(2,1)S(1)}, u32[]{:S(2)}, u32[]{:S(2)}) collective-permute-start(bf16[512,192]{1,0:T(8,128)(2,1)S(1)} %get-tuple-element.110.refs_4_.refs_0_), channel_id=1, source_target_pairs={{0,2},{1,3},{2,0},{3,1},{4,6},{5,7},{6,4},{7,5},{8,10},{9,11},{10,... | collective-permute-start | bytes 589832 | tf_op jit(solution)/shard_map/ppermute | solution.py:377
  64.5 1.9 %collective-permute-start.17 = (bf16[288,768]{1,0:T(8,128)(2,1)S(1)}, bf16[288,768]{1,0:T(8,128)(2,1)S(1)}, u32[]{:S(2)}, u32[]{:S(2)}) collective-permute-start(bf16[288,768]{1,0:T(8,128)(2,1)S(1)} %collective-permute-done.14.refs_9_), channel_id=1, source_target_pairs={{0,1},{1,0},{2,3},{3,2},{4,5},{5,4},{6,7},{7,6},{8,9},{9,8},{10,11... | collective-permute-start | bytes 1327112 | tf_op jit(solution)/shard_map/ppermute | solution.py:373
  64.6 2.4 %collective-permute-start.18 = (bf16[288,768]{1,0:T(8,128)(2,1)S(1)}, bf16[288,768]{1,0:T(8,128)(2,1)S(1)}, u32[]{:S(2)}, u32[]{:S(2)}) collective-permute-start(bf16[288,768]{1,0:T(8,128)(2,1)S(1)} %collective-permute-done.15.refs_10_), channel_id=1, source_target_pairs={{0,1},{1,0},{2,3},{3,2},{4,5},{5,4},{6,7},{7,6},{8,9},{9,8},{10,11... | collective-permute-start | bytes 1327112 | tf_op jit(solution)/shard_map/ppermute | solution.py:373
  65.1 2.5 %collective-permute-start.19 = (bf16[288,768]{1,0:T(8,128)(2,1)S(1)}, bf16[288,768]{1,0:T(8,128)(2,1)S(1)}, u32[]{:S(2)}, u32[]{:S(2)}) collective-permute-start(bf16[288,768]{1,0:T(8,128)(2,1)S(1)} %collective-permute-done.16.refs_11_), channel_id=1, source_target_pairs={{0,1},{1,0},{2,3},{3,2},{4,5},{5,4},{6,7},{7,6},{8,9},{9,8},{10,11... | collective-permute-start | bytes 1327112 | tf_op jit(solution)/shard_map/ppermute | solution.py:373
  74.7 3.7 %collective-permute-start.20 = (bf16[4,192,768]{2,1,0:T(8,128)(2,1)S(1)}, bf16[4,192,768]{2,1,0:T(8,128)(2,1)S(1)}, u32[]{:S(2)}, u32[]{:S(2)}) collective-permute-start(bf16[4,192,768]{2,1,0:T(8,128)(2,1)S(1)} %get-tuple-element.120), channel_id=1, source_target_pairs={{0,1},{1,0},{2,3},{3,2},{4,5},{5,4},{6,7},{7,6},{8,9},{9,8},{10,11... | collective-permute-start | bytes 3538952 | tf_op jit(solution)/shard_map/ppermute | solution.py:373
  74.9 7.7 %collective-permute-start.21 = (bf16[128,768]{1,0:T(8,128)(2,1)S(1)}, bf16[128,768]{1,0:T(8,128)(2,1)S(1)}, u32[]{:S(2)}, u32[]{:S(2)}) collective-permute-start(bf16[128,768]{1,0:T(8,128)(2,1)S(1)} %get-tuple-element.123), channel_id=1, source_target_pairs={{0,2},{1,3},{2,0},{3,1},{4,6},{5,7},{6,4},{7,5},{8,10},{9,11},{10,... | collective-permute-start | bytes 589832 | tf_op jit(solution)/shard_map/ppermute | solution.py:377
  76.1 10.2 %collective-permute-start.22 = (bf16[128,768]{1,0:T(8,128)(2,1)S(1)}, bf16[128,768]{1,0:T(8,128)(2,1)S(1)}, u32[]{:S(2)}, u32[]{:S(2)}) collective-permute-start(bf16[128,768]{1,0:T(8,128)(2,1)S(1)} %get-tuple-element.124), channel_id=1, source_target_pairs={{0,4},{1,5},{2,6},{3,7},{4,0},{5,1},{6,2},{7,3},{8,12},{9,13},{10,... | collective-permute-start | bytes 589832 | tf_op jit(solution)/shard_map/ppermute | solution.py:377
  77.7 9.6 %collective-permute-start.23 = (bf16[128,768]{1,0:T(8,128)(2,1)S(1)}, bf16[128,768]{1,0:T(8,128)(2,1)S(1)}, u32[]{:S(2)}, u32[]{:S(2)}) collective-permute-start(bf16[128,768]{1,0:T(8,128)(2,1)S(1)} %get-tuple-element.125), channel_id=1, source_target_pairs={{0,6},{1,7},{2,4},{3,5},{4,2},{5,3},{6,0},{7,1},{8,14},{9,15},{10,... | collective-permute-start | bytes 589832 | tf_op jit(solution)/shard_map/ppermute | solution.py:377
  79.3 26.1 %collective-permute-start.27 = (bf16[192,768]{1,0:T(8,128)(2,1)S(1)}, bf16[192,768]{1,0:T(8,128)(2,1)S(1)}, u32[]{:S(2)}, u32[]{:S(2)}) collective-permute-start(bf16[192,768]{1,0:T(8,128)(2,1)S(1)} %get-tuple-element.134), channel_id=1, source_target_pairs={{0,16},{8,24},{16,0},{24,8},{1,17},{9,25},{17,1},{25,9},{2,18},{10... | collective-permute-start | bytes 884744 | tf_op jit(solution)/shard_map/ppermute | solution.py:381
  79.4 26.0 %collective-permute-start.28 = (bf16[192,768]{1,0:T(8,128)(2,1)S(1)}, bf16[192,768]{1,0:T(8,128)(2,1)S(1)}, u32[]{:S(2)}, u32[]{:S(2)}) collective-permute-start(bf16[192,768]{1,0:T(8,128)(2,1)S(1)} %get-tuple-element.135), channel_id=1, source_target_pairs={{0,24},{8,16},{16,8},{24,0},{1,25},{9,17},{17,9},{25,1},{2,26},{10... | collective-permute-start | bytes 884744 | tf_op jit(solution)/shard_map/ppermute | solution.py:381
  88.2 8.8 %collective-permute-start.26 = (bf16[128,768]{1,0:T(8,128)(2,1)S(1)}, bf16[128,768]{1,0:T(8,128)(2,1)S(1)}, u32[]{:S(2)}, u32[]{:S(2)}) collective-permute-start(bf16[128,768]{1,0:T(8,128)(2,1)S(1)} %get-tuple-element.127.a0.refs_4_.refs_6_), channel_id=1, source_target_pairs={{0,6},{1,7},{2,4},{3,5},{4,2},{5,3},{6,0},{7,1},{8,14},{9,15},{10,... | collective-permute-start | bytes 589832 | tf_op jit(solution)/shard_map/ppermute | solution.py:377
  90.0 9.8 %collective-permute-start.25 = (bf16[128,768]{1,0:T(8,128)(2,1)S(1)}, bf16[128,768]{1,0:T(8,128)(2,1)S(1)}, u32[]{:S(2)}, u32[]{:S(2)}) collective-permute-start(bf16[128,768]{1,0:T(8,128)(2,1)S(1)} %get-tuple-element.127.a0.refs_4_.refs_6_), channel_id=1, source_target_pairs={{0,4},{1,5},{2,6},{3,7},{4,0},{5,1},{6,2},{7,3},{8,12},{9,13},{10,... | collective-permute-start | bytes 589832 | tf_op jit(solution)/shard_map/ppermute | solution.py:377
  91.0 8.8 %collective-permute-start.24 = (bf16[128,768]{1,0:T(8,128)(2,1)S(1)}, bf16[128,768]{1,0:T(8,128)(2,1)S(1)}, u32[]{:S(2)}, u32[]{:S(2)}) collective-permute-start(bf16[128,768]{1,0:T(8,128)(2,1)S(1)} %get-tuple-element.127.a0.refs_4_.refs_6_), channel_id=1, source_target_pairs={{0,2},{1,3},{2,0},{3,1},{4,6},{5,7},{6,4},{7,5},{8,10},{9,11},{10,... | collective-permute-start | bytes 589832 | tf_op jit(solution)/shard_map/ppermute | solution.py:377
  97.1 13.0 %collective-permute-start.31 = (bf16[192,768]{1,0:T(8,128)(2,1)S(1)}, bf16[192,768]{1,0:T(8,128)(2,1)S(1)}, u32[]{:S(2)}, u32[]{:S(2)}) collective-permute-start(bf16[192,768]{1,0:T(8,128)(2,1)S(1)} %get-tuple-element.145), channel_id=1, source_target_pairs={{0,8},{8,0},{16,24},{24,16},{1,9},{9,1},{17,25},{25,17},{2,10},{10... | collective-permute-start | bytes 884744 | tf_op jit(solution)/shard_map/ppermute | solution.py:381
  105.3 1.6 %collective-permute-start.30 = (bf16[512,192]{1,0:T(8,128)(2,1)S(1)}, bf16[512,192]{1,0:T(8,128)(2,1)S(1)}, u32[]{:S(2)}, u32[]{:S(2)}) collective-permute-start(bf16[512,192]{1,0:T(8,128)(2,1)S(1)} %get-tuple-element.137), channel_id=1, source_target_pairs={{0,1},{1,0},{2,3},{3,2},{4,5},{5,4},{6,7},{7,6},{8,9},{9,8},{10,11... | collective-permute-start | bytes 589832 | tf_op jit(solution)/shard_map/ppermute | solution.py:373
  105.4 1.9 %collective-permute-start.29 = (bf16[512,192]{1,0:T(8,128)(2,1)S(1)}, bf16[512,192]{1,0:T(8,128)(2,1)S(1)}, u32[]{:S(2)}, u32[]{:S(2)}) collective-permute-start(bf16[512,192]{1,0:T(8,128)(2,1)S(1)} %get-tuple-element.136), channel_id=1, source_target_pairs={{0,1},{1,0},{2,3},{3,2},{4,5},{5,4},{6,7},{7,6},{8,9},{9,8},{10,11... | collective-permute-start | bytes 589832 | tf_op jit(solution)/shard_map/ppermute | solution.py:373
  110.1 5.4 %collective-permute-start.32 = (bf16[4,96,768]{2,1,0:T(8,128)(2,1)S(1)}, bf16[4,96,768]{2,1,0:T(8,128)(2,1)S(1)}, u32[]{:S(2)}, u32[]{:S(2)}) collective-permute-start(bf16[4,96,768]{2,1,0:T(8,128)(2,1)S(1)} %get-tuple-element.146), channel_id=1, source_target_pairs={{0,1},{1,0},{2,3},{3,2},{4,5},{5,4},{6,7},{7,6},{8,9},{9,8},{10,11... | collective-permute-start | bytes 1769480 | tf_op jit(solution)/shard_map/ppermute | solution.py:373
  110.3 10.9 %collective-permute-start.33 = (bf16[128,768]{1,0:T(8,128)(2,1)S(1)}, bf16[128,768]{1,0:T(8,128)(2,1)S(1)}, u32[]{:S(2)}, u32[]{:S(2)}) collective-permute-start(bf16[128,768]{1,0:T(8,128)(2,1)S(1)} %get-tuple-element.154), channel_id=1, source_target_pairs={{0,2},{1,3},{2,0},{3,1},{4,6},{5,7},{6,4},{7,5},{8,10},{9,11},{10,... | collective-permute-start | bytes 589832 | tf_op jit(solution)/shard_map/ppermute | solution.py:377
  111.7 11.1 %collective-permute-start.34 = (bf16[128,768]{1,0:T(8,128)(2,1)S(1)}, bf16[128,768]{1,0:T(8,128)(2,1)S(1)}, u32[]{:S(2)}, u32[]{:S(2)}) collective-permute-start(bf16[128,768]{1,0:T(8,128)(2,1)S(1)} %get-tuple-element.156), channel_id=1, source_target_pairs={{0,4},{1,5},{2,6},{3,7},{4,0},{5,1},{6,2},{7,3},{8,12},{9,13},{10,... | collective-permute-start | bytes 589832 | tf_op jit(solution)/shard_map/ppermute | solution.py:377
  112.3 11.8 %collective-permute-start.35 = (bf16[128,768]{1,0:T(8,128)(2,1)S(1)}, bf16[128,768]{1,0:T(8,128)(2,1)S(1)}, u32[]{:S(2)}, u32[]{:S(2)}) collective-permute-start(bf16[128,768]{1,0:T(8,128)(2,1)S(1)} %get-tuple-element.158), channel_id=1, source_target_pairs={{0,6},{1,7},{2,4},{3,5},{4,2},{5,3},{6,0},{7,1},{8,14},{9,15},{10,... | collective-permute-start | bytes 589832 | tf_op jit(solution)/shard_map/ppermute | solution.py:377
  116.2 14.9 %collective-permute-start.37 = (bf16[104,768]{1,0:T(8,128)(2,1)S(1)}, bf16[104,768]{1,0:T(8,128)(2,1)S(1)}, u32[]{:S(2)}, u32[]{:S(2)}) collective-permute-start(bf16[104,768]{1,0:T(8,128)(2,1)S(1)} %get-tuple-element.160), channel_id=1, source_target_pairs={{0,16},{8,24},{16,0},{24,8},{1,17},{9,25},{17,1},{25,9},{2,18},{10... | collective-permute-start | bytes 479240 | tf_op jit(solution)/shard_map/ppermute | solution.py:381
  118.6 13.8 %collective-permute-start.38 = (bf16[104,768]{1,0:T(8,128)(2,1)S(1)}, bf16[104,768]{1,0:T(8,128)(2,1)S(1)}, u32[]{:S(2)}, u32[]{:S(2)}) collective-permute-start(bf16[104,768]{1,0:T(8,128)(2,1)S(1)} %get-tuple-element.161), channel_id=1, source_target_pairs={{0,24},{8,16},{16,8},{24,0},{1,25},{9,17},{17,9},{25,1},{2,26},{10... | collective-permute-start | bytes 479240 | tf_op jit(solution)/shard_map/ppermute | solution.py:381
  121.2 11.2 %collective-permute-start.36 = (bf16[104,768]{1,0:T(8,128)(2,1)S(1)}, bf16[104,768]{1,0:T(8,128)(2,1)S(1)}, u32[]{:S(2)}, u32[]{:S(2)}) collective-permute-start(bf16[104,768]{1,0:T(8,128)(2,1)S(1)} %get-tuple-element.147), channel_id=1, source_target_pairs={{0,8},{8,0},{16,24},{24,16},{1,9},{9,1},{17,25},{25,17},{2,10},{10... | collective-permute-start | bytes 479240 | tf_op jit(solution)/shard_map/ppermute | solution.py:381
  122.8 11.8 %collective-permute-start.41 = (bf16[192,768]{1,0:T(8,128)(2,1)S(1)}, bf16[192,768]{1,0:T(8,128)(2,1)S(1)}, u32[]{:S(2)}, u32[]{:S(2)}) collective-permute-start(bf16[192,768]{1,0:T(8,128)(2,1)S(1)} %shard_map.281.refs_0_), channel_id=1, source_target_pairs={{0,6},{1,7},{2,4},{3,5},{4,2},{5,3},{6,0},{7,1},{8,14},{9,15},{10,... | collective-permute-start | bytes 884744 | tf_op jit(solution)/shard_map/ppermute | solution.py:377
  124.1 12.9 %collective-permute-start.40 = (bf16[192,768]{1,0:T(8,128)(2,1)S(1)}, bf16[192,768]{1,0:T(8,128)(2,1)S(1)}, u32[]{:S(2)}, u32[]{:S(2)}) collective-permute-start(bf16[192,768]{1,0:T(8,128)(2,1)S(1)} %shard_map.281.refs_0_), channel_id=1, source_target_pairs={{0,4},{1,5},{2,6},{3,7},{4,0},{5,1},{6,2},{7,3},{8,12},{9,13},{10,... | collective-permute-start | bytes 884744 | tf_op jit(solution)/shard_map/ppermute | solution.py:377
  131.1 7.8 %collective-permute-start.39 = (bf16[192,768]{1,0:T(8,128)(2,1)S(1)}, bf16[192,768]{1,0:T(8,128)(2,1)S(1)}, u32[]{:S(2)}, u32[]{:S(2)}) collective-permute-start(bf16[192,768]{1,0:T(8,128)(2,1)S(1)} %shard_map.281.refs_0_), channel_id=1, source_target_pairs={{0,2},{1,3},{2,0},{3,1},{4,6},{5,7},{6,4},{7,5},{8,10},{9,11},{10,... | collective-permute-start | bytes 884744 | tf_op jit(solution)/shard_map/ppermute | solution.py:377
  133.1 7.5 %collective-permute-start.52 = (bf16[104,768]{1,0:T(8,128)(2,1)S(1)}, bf16[104,768]{1,0:T(8,128)(2,1)S(1)}, u32[]{:S(2)}, u32[]{:S(2)}) collective-permute-start(bf16[104,768]{1,0:T(8,128)(2,1)S(1)} %shard_map.282.refs_0_), channel_id=1, source_target_pairs={{0,1},{1,0},{2,3},{3,2},{4,5},{5,4},{6,7},{7,6},{8,9},{9,8},{10,11... | collective-permute-start | bytes 479240 | tf_op jit(solution)/shard_map/ppermute | solution.py:373
  133.2 9.9 %collective-permute-start.51 = (bf16[104,768]{1,0:T(8,128)(2,1)S(1)}, bf16[104,768]{1,0:T(8,128)(2,1)S(1)}, u32[]{:S(2)}, u32[]{:S(2)}) collective-permute-start(bf16[104,768]{1,0:T(8,128)(2,1)S(1)} %shard_map.282.refs_0_), channel_id=1, source_target_pairs={{0,6},{1,7},{2,4},{3,5},{4,2},{5,3},{6,0},{7,1},{8,14},{9,15},{10,... | collective-permute-start | bytes 479240 | tf_op jit(solution)/shard_map/ppermute | solution.py:377
  134.6 11.2 %collective-permute-start.42 = (bf16[192,768]{1,0:T(8,128)(2,1)S(1)}, bf16[192,768]{1,0:T(8,128)(2,1)S(1)}, u32[]{:S(2)}, u32[]{:S(2)}) collective-permute-start(bf16[192,768]{1,0:T(8,128)(2,1)S(1)} %shard_map.281.refs_0_), channel_id=1, source_target_pairs={{0,1},{1,0},{2,3},{3,2},{4,5},{5,4},{6,7},{7,6},{8,9},{9,8},{10,11... | collective-permute-start | bytes 884744 | tf_op jit(solution)/shard_map/ppermute | solution.py:373
  137.1 8.2 %collective-permute-start.50 = (bf16[104,768]{1,0:T(8,128)(2,1)S(1)}, bf16[104,768]{1,0:T(8,128)(2,1)S(1)}, u32[]{:S(2)}, u32[]{:S(2)}) collective-permute-start(bf16[104,768]{1,0:T(8,128)(2,1)S(1)} %shard_map.282.refs_0_), channel_id=1, source_target_pairs={{0,4},{1,5},{2,6},{3,7},{4,0},{5,1},{6,2},{7,3},{8,12},{9,13},{10,... | collective-permute-start | bytes 479240 | tf_op jit(solution)/shard_map/ppermute | solution.py:377
  138.9 6.4 %collective-permute-start.49 = (bf16[104,768]{1,0:T(8,128)(2,1)S(1)}, bf16[104,768]{1,0:T(8,128)(2,1)S(1)}, u32[]{:S(2)}, u32[]{:S(2)}) collective-permute-start(bf16[104,768]{1,0:T(8,128)(2,1)S(1)} %shard_map.282.refs_0_), channel_id=1, source_target_pairs={{0,2},{1,3},{2,0},{3,1},{4,6},{5,7},{6,4},{7,5},{8,10},{9,11},{10,... | collective-permute-start | bytes 479240 | tf_op jit(solution)/shard_map/ppermute | solution.py:377
  140.6 8.1 %collective-permute-start.45 = (bf16[192,768]{1,0:T(8,128)(2,1)S(1)}, bf16[192,768]{1,0:T(8,128)(2,1)S(1)}, u32[]{:S(2)}, u32[]{:S(2)}) collective-permute-start(bf16[192,768]{1,0:T(8,128)(2,1)S(1)} %collective-permute-done.41.refs_3_), channel_id=1, source_target_pairs={{0,1},{1,0},{2,3},{3,2},{4,5},{5,4},{6,7},{7,6},{8,9},{9,8},{10,11... | collective-permute-start | bytes 884744 | tf_op jit(solution)/shard_map/ppermute | solution.py:373
  143.0 2.9 %collective-permute-start.55 = (bf16[104,768]{1,0:T(8,128)(2,1)S(1)}, bf16[104,768]{1,0:T(8,128)(2,1)S(1)}, u32[]{:S(2)}, u32[]{:S(2)}) collective-permute-start(bf16[104,768]{1,0:T(8,128)(2,1)S(1)} %collective-permute-done.51.refs_3_), channel_id=1, source_target_pairs={{0,1},{1,0},{2,3},{3,2},{4,5},{5,4},{6,7},{7,6},{8,9},{9,8},{10,11... | collective-permute-start | bytes 479240 | tf_op jit(solution)/shard_map/ppermute | solution.py:373
  145.3 1.4 collective-permute-start.54
  145.3 2.0 %collective-permute-start.53 = (bf16[104,768]{1,0:T(8,128)(2,1)S(1)}, bf16[104,768]{1,0:T(8,128)(2,1)S(1)}, u32[]{:S(2)}, u32[]{:S(2)}) collective-permute-start(bf16[104,768]{1,0:T(8,128)(2,1)S(1)} %collective-permute-done.49.refs_1_), channel_id=1, source_target_pairs={{0,1},{1,0},{2,3},{3,2},{4,5},{5,4},{6,7},{7,6},{8,9},{9,8},{10,11... | collective-permute-start | bytes 479240 | tf_op jit(solution)/shard_map/ppermute | solution.py:373
  145.8 6.7 %collective-permute-start.44 = (bf16[192,768]{1,0:T(8,128)(2,1)S(1)}, bf16[192,768]{1,0:T(8,128)(2,1)S(1)}, u32[]{:S(2)}, u32[]{:S(2)}) collective-permute-start(bf16[192,768]{1,0:T(8,128)(2,1)S(1)} %collective-permute-done.40.refs_2_), channel_id=1, source_target_pairs={{0,1},{1,0},{2,3},{3,2},{4,5},{5,4},{6,7},{7,6},{8,9},{9,8},{10,11... | collective-permute-start | bytes 884744 | tf_op jit(solution)/shard_map/ppermute | solution.py:373
  145.9 6.6 %collective-permute-start.43 = (bf16[192,768]{1,0:T(8,128)(2,1)S(1)}, bf16[192,768]{1,0:T(8,128)(2,1)S(1)}, u32[]{:S(2)}, u32[]{:S(2)}) collective-permute-start(bf16[192,768]{1,0:T(8,128)(2,1)S(1)} %collective-permute-done.39.refs_1_), channel_id=1, source_target_pairs={{0,1},{1,0},{2,3},{3,2},{4,5},{5,4},{6,7},{7,6},{8,9},{9,8},{10,11... | collective-permute-start | bytes 884744 | tf_op jit(solution)/shard_map/ppermute | solution.py:373
  146.7 9.1 %collective-permute-start.46 = (bf16[128,768]{1,0:T(8,128)(2,1)S(1)}, bf16[128,768]{1,0:T(8,128)(2,1)S(1)}, u32[]{:S(2)}, u32[]{:S(2)}) collective-permute-start(bf16[128,768]{1,0:T(8,128)(2,1)S(1)} %get-tuple-element.169), channel_id=1, source_target_pairs={{0,2},{1,3},{2,0},{3,1},{4,6},{5,7},{6,4},{7,5},{8,10},{9,11},{10,... | collective-permute-start | bytes 589832 | tf_op jit(solution)/shard_map/ppermute | solution.py:377
  147.3 10.9 %collective-permute-start.47 = (bf16[128,768]{1,0:T(8,128)(2,1)S(1)}, bf16[128,768]{1,0:T(8,128)(2,1)S(1)}, u32[]{:S(2)}, u32[]{:S(2)}) collective-permute-start(bf16[128,768]{1,0:T(8,128)(2,1)S(1)} %get-tuple-element.171), channel_id=1, source_target_pairs={{0,4},{1,5},{2,6},{3,7},{4,0},{5,1},{6,2},{7,3},{8,12},{9,13},{10,... | collective-permute-start | bytes 589832 | tf_op jit(solution)/shard_map/ppermute | solution.py:377
  148.7 9.5 %collective-permute-start.48 = (bf16[128,768]{1,0:T(8,128)(2,1)S(1)}, bf16[128,768]{1,0:T(8,128)(2,1)S(1)}, u32[]{:S(2)}, u32[]{:S(2)}) collective-permute-start(bf16[128,768]{1,0:T(8,128)(2,1)S(1)} %get-tuple-element.173), channel_id=1, source_target_pairs={{0,6},{1,7},{2,4},{3,5},{4,2},{5,3},{6,0},{7,1},{8,14},{9,15},{10,... | collective-permute-start | bytes 589832 | tf_op jit(solution)/shard_map/ppermute | solution.py:377
